TPU v7x, 32 devices: a whole 2x2x4 slice. The times are simulated.
32 devices in a mesh: expert: 4 (over z), shard: 8 (over y, x, core).
Axes of the slice: x: 2, y: 2, z: 4, core: 2. Of those that a mesh axis runs over, the one named last changes fastest.
Arguments:
- token_ids: int32 [8192], P('expert'), may hold values from 0 to 49151
- positions: int32 [32, 32], P('expert'), may hold values from 0 to 254, as said below
- pair_index: int32 [16, 2], replicated, may hold values from 0 to 31, as said below
- ref_logps: float32 [32], replicated, may hold values from -64 to 64
- routes: int32 [8192, 8], P(('expert', 'shard')), may hold values from 0 to 31, all different within a row; in each aligned block of 256 rows (0 to 255, 256 to 511, ...) at most 88 rows name the same one
- step_count: int32 [], replicated, may hold values from 2 to 20
- embed_table: float32 [49152, 1536], P('shard', 'expert'), may hold values from -1.75 to 1.75
- embed_first: float32 [49152, 1536], P('shard', 'expert'), may hold values from -0.00015258789 to 0.00015258789
- embed_second: float32 [49152, 1536], P('shard', 'expert'), may hold values from 6.25e-11 to 2.5e-10
- qkv_weight: float32 [1536, 2560], P(('expert', 'shard')), may hold values from -0.21875 to 0.21875
- qkv_first: float32 [1536, 2560], P(('expert', 'shard')), may hold values from -0.00390625 to 0.00390625
- qkv_second: float32 [1536, 2560], P(('expert', 'shard')), may hold values from 1.8e-08 to 2.88e-07
- out_weight: float32 [1536, 1536], P(('expert', 'shard')), may hold values from -0.625 to 0.625
- out_first: float32 [1536, 1536], P(('expert', 'shard')), may hold values from -0.0009765625 to 0.0009765625
- out_second: float32 [1536, 1536], P(('expert', 'shard')), may hold values from 2.25e-09 to 9e-09
- router_weight: float32 [1536, 32], P(('expert', 'shard')), may hold values from -0.078125 to 0.078125
- router_first: float32 [1536, 32], P(('expert', 'shard')), may hold values from -0.00048828125 to 0.00048828125
- router_second: float32 [1536, 32], P(('expert', 'shard')), may hold values from 5.625e-10 to 2.25e-09
- norm_gains: float32 [3, 1536], P(None, ('expert', 'shard')), may hold values from 0.5 to 1.5
- gains_first: float32 [3, 1536], P(None, ('expert', 'shard')), may hold values from -0.0034179688 to 0.0034179688
- gains_second: float32 [3, 1536], P(None, ('expert', 'shard')), may hold values from 2.5e-08 to 1e-07
- in_weight: float32 [32, 1536, 2, 512], P('shard', None, None, 'expert'), may hold values from -0.15625 to 0.15625
- in_first: float32 [32, 1536, 2, 512], P('shard', None, None, 'expert'), may hold values from -0.00048828125 to 0.00048828125
- in_second: float32 [32, 1536, 2, 512], P('shard', None, None, 'expert'), may hold values from 5.625e-10 to 2.25e-09
- down_weight: float32 [32, 512, 1536], P('shard', 'expert'), may hold values from -1 to 1
- down_first: float32 [32, 512, 1536], P('shard', 'expert'), may hold values from -0.00024414062 to 0.00024414062
- down_second: float32 [32, 512, 1536], P('shard', 'expert'), may hold values from 6.125e-11 to 9.8e-10
Outputs:
- loss_value: float32 [], replicated
- new_table: float32 [49152, 1536], P('shard', 'expert')
- new_table_first: float32 [49152, 1536], P('shard', 'expert')
- new_table_second: float32 [49152, 1536], P('shard', 'expert')
- new_qkv: float32 [1536, 2560], P(('expert', 'shard'))
- new_qkv_first: float32 [1536, 2560], P(('expert', 'shard'))
- new_qkv_second: float32 [1536, 2560], P(('expert', 'shard'))
- new_out: float32 [1536, 1536], P(('expert', 'shard'))
- new_out_first: float32 [1536, 1536], P(('expert', 'shard'))
- new_out_second: float32 [1536, 1536], P(('expert', 'shard'))
- new_router: float32 [1536, 32], P(('expert', 'shard'))
- new_router_first: float32 [1536, 32], P(('expert', 'shard'))
- new_router_second: float32 [1536, 32], P(('expert', 'shard'))
- new_gains: float32 [3, 1536], P(None, ('expert', 'shard'))
- new_gains_first: float32 [3, 1536], P(None, ('expert', 'shard'))
- new_gains_second: float32 [3, 1536], P(None, ('expert', 'shard'))
- new_in: float32 [32, 1536, 2, 512], P('shard', None, None, 'expert')
- new_in_first: float32 [32, 1536, 2, 512], P('shard', None, None, 'expert')
- new_in_second: float32 [32, 1536, 2, 512], P('shard', None, None, 'expert')
- new_down: float32 [32, 512, 1536], P('shard', 'expert')
- new_down_first: float32 [32, 512, 1536], P('shard', 'expert')
- new_down_second: float32 [32, 512, 1536], P('shard', 'expert')
- lamb_stats: float32 [7, 3], replicated
Inputs may be any that keep to these rules, and one draw needn't show every extreme that they name: Each row holds 32 consecutive positions. `pair_index`: every sequence appears exactly once. `routes`: each token names 8 different experts; within the rows of one device no expert is named by more than 88 tokens.
All inputs are finite; a program needn't handle non-finite values.
Results may differ from a plain program's by a relative error of at most 0.028.
The roundings to bfloat16 on the way count: a program that leaves them out, or rounds other values in their place, can miss the bound.
Values may be sent and summed in bfloat16 or wider, within the bound.
A program may use at most 384 MiB of HBM per device.

v0:
```python
import jax
import jax.numpy as jnp
from jax import lax
from jax.sharding import PartitionSpec as P

D = 1536
QUERY_HEADS = 24
KEY_VALUE_HEADS = 8
HEAD_WIDTH = 64
TOP = 8
EXPERTS = 32
SEQUENCE_TOKENS = 256
COMP = 32
CAP = 88


BETA = 0.1
LOGIT_SCALE = 6.0
RATE_ONE = 0.9
RATE_TWO = 0.999
EPSILON = 1e-06
DECAY = 0.01
STEP_RATE = 0.3


def merged_2(part, axis, combine):
    gathered = jax.tree.map(lambda a: lax.all_gather(a, axis), part)

    def take(source):
        return jax.tree.map(lambda a: lax.dynamic_index_in_dim(a, source, 0, False), gathered)

    return lax.fori_loop(
        1, lax.axis_size(axis), lambda source, state: combine(state, take(source)), take(0)
    )


def norm_apply(values, gain):
    return values * lax.rsqrt(jnp.mean(values * values, axis=-1, keepdims=True) + 1e-06) * gain


def rotary_apply(values):
    half = values.shape[-1] // 2
    places = jnp.arange(values.shape[0], dtype=jnp.float32)
    freqs = jnp.exp(-jnp.log(10000.0) * jnp.arange(half, dtype=jnp.float32) / half)
    angles = places[:, None] * freqs[None, :]
    cosine = jnp.cos(angles)[:, None, :]
    sine = jnp.sin(angles)[:, None, :]
    first_half = values[..., :half]
    second_half = values[..., half:]
    return jnp.concatenate(
        [first_half * cosine - second_half * sine, second_half * cosine + first_half * sine],
        axis=-1,
    )


def slot_places(route_flat, expert_count, capacity):
    onehot = (route_flat[:, None] == jnp.arange(expert_count, dtype=jnp.int32)[None, :]).astype(
        jnp.int32
    )
    before = jnp.cumsum(onehot, axis=0, dtype=jnp.int32) - onehot
    return route_flat * capacity + jnp.sum(before * onehot, axis=1, dtype=jnp.int32)


def gate_soft(router_logits, route):
    chosen = jnp.take_along_axis(router_logits, route, axis=1)
    return jax.nn.softmax(chosen, axis=-1)


def pair_loss(seq_sums, ref_logps, pair_index):
    margin = seq_sums - ref_logps
    scaled = BETA * (margin[pair_index[:, 0]] - margin[pair_index[:, 1]])
    return -jnp.mean(jax.nn.log_sigmoid(scaled))


def lamb_parts(weight, moment_one, moment_two, gradient, step_value):
    moment_one = RATE_ONE * moment_one + (1.0 - RATE_ONE) * gradient
    moment_two = RATE_TWO * moment_two + (1.0 - RATE_TWO) * gradient * gradient
    fixed_one = moment_one / (1.0 - RATE_ONE**step_value)
    fixed_two = moment_two / (1.0 - RATE_TWO**step_value)
    update = fixed_one / (jnp.sqrt(fixed_two) + EPSILON) + DECAY * weight
    return (moment_one, moment_two, update)


def split_rotate(projected_rows):
    sequence_length = projected_rows.shape[0]
    query_matrix_rows = rotary_apply(
        projected_rows[:, : QUERY_HEADS * HEAD_WIDTH].reshape(
            sequence_length, QUERY_HEADS, HEAD_WIDTH
        )
    )
    key_matrix_rows = rotary_apply(
        projected_rows[
            :, QUERY_HEADS * HEAD_WIDTH : (QUERY_HEADS + KEY_VALUE_HEADS) * HEAD_WIDTH
        ].reshape(sequence_length, KEY_VALUE_HEADS, HEAD_WIDTH)
    )
    value_matrix_rows = projected_rows[:, (QUERY_HEADS + KEY_VALUE_HEADS) * HEAD_WIDTH :].reshape(
        sequence_length, KEY_VALUE_HEADS, HEAD_WIDTH
    )
    return (query_matrix_rows, key_matrix_rows, value_matrix_rows)


def masked_scores(query_brain_float, key_brain_float):
    sequence_length = query_brain_float.shape[0]
    scores = jnp.einsum(
        "qhgd,khd->hgqk", query_brain_float, key_brain_float, preferred_element_type=jnp.float32
    ) * HEAD_WIDTH ** (-0.5)
    causal = jnp.arange(sequence_length)[:, None] >= jnp.arange(sequence_length)[None, :]
    return jnp.where(causal, scores, -1000000000.0)


def attend_forward(query_brain_float, key_brain_float, value_brain_float):
    scores = masked_scores(query_brain_float, key_brain_float)
    row_top = jnp.max(scores, axis=-1, keepdims=True)
    expd = jnp.exp(scores - row_top)
    row_total = jnp.sum(expd, axis=-1, keepdims=True)
    attn_probs = (expd / row_total).astype(jnp.bfloat16)
    attended = jnp.einsum(
        "hgqk,khd->qhgd", attn_probs, value_brain_float, preferred_element_type=jnp.float32
    )
    return (attended, row_top + jnp.log(row_total))


def attend_backward(
    query_brain_float, key_brain_float, value_brain_float, logarithm_total, grad_out
):
    attn_probs = jnp.exp(masked_scores(query_brain_float, key_brain_float) - logarithm_total)
    probs_b = attn_probs.astype(jnp.bfloat16)
    grad_probs = jnp.einsum(
        "qhgd,khd->hgqk", grad_out, value_brain_float, preferred_element_type=jnp.float32
    )
    grad_probs = grad_probs.astype(jnp.bfloat16).astype(jnp.float32)
    inner = jnp.sum(grad_probs * attn_probs, axis=-1, keepdims=True)
    grad_scores = (attn_probs * (grad_probs - inner)).astype(jnp.bfloat16)
    grad_value = jnp.einsum("hgqk,qhgd->khd", probs_b, grad_out, preferred_element_type=jnp.float32)
    grad_query = jnp.einsum(
        "hgqk,khd->qhgd", grad_scores, key_brain_float, preferred_element_type=jnp.float32
    ) * HEAD_WIDTH ** (-0.5)
    grad_key = jnp.einsum(
        "hgqk,qhgd->khd", grad_scores, query_brain_float, preferred_element_type=jnp.float32
    ) * HEAD_WIDTH ** (-0.5)
    return (grad_query, grad_key, grad_value)


def on_device(
    token_ids,
    positions,
    pair_index,
    ref_logps,
    routes,
    step_count,
    embed_table,
    embed_first,
    embed_second,
    qkv_weight,
    qkv_first,
    qkv_second,
    out_weight,
    out_first,
    out_second,
    router_weight,
    router_first,
    router_second,
    norm_gains,
    gains_first,
    gains_second,
    in_weight,
    in_first,
    in_second,
    down_weight,
    down_first,
    down_second,
):
    brain_float_sixteen = jnp.bfloat16
    f32 = jnp.float32
    shard_id = lax.axis_index("shard")
    expert_id = lax.axis_index("expert")
    shard_count = lax.axis_size("shard")
    expert_count = lax.axis_size("expert")
    query_group_width = QUERY_HEADS // KEY_VALUE_HEADS
    vocab_rows = embed_table.shape[0]
    vocab_base = shard_id * vocab_rows
    own_places = lax.dynamic_index_in_dim(positions, shard_id, 0, keepdims=False)
    table_block, expert_in, expert_down = (
        lax.all_gather(embed_table.astype(brain_float_sixteen), "expert", axis=1, tiled=True),
        lax.all_gather(in_weight.astype(brain_float_sixteen), "expert", axis=3, tiled=True),
        lax.all_gather(down_weight.astype(brain_float_sixteen), "expert", axis=1, tiled=True),
    )
    qkv_full, out_full, router_full, gains_full = (
        lax.all_gather(
            qkv_weight.astype(brain_float_sixteen), ("expert", "shard"), axis=0, tiled=True
        ),
        lax.all_gather(
            out_weight.astype(brain_float_sixteen), ("expert", "shard"), axis=0, tiled=True
        ),
        lax.all_gather(
            router_weight.astype(brain_float_sixteen), ("expert", "shard"), axis=0, tiled=True
        ),
        lax.all_gather(
            norm_gains.astype(brain_float_sixteen), ("expert", "shard"), axis=1, tiled=True
        ),
    )
    gains_value = gains_full.astype(f32)
    picked = token_ids
    inside = (picked >= vocab_base) & (picked < vocab_base + vocab_rows)
    local_rows = jnp.clip(picked - vocab_base, 0, vocab_rows - 1)
    embedded = lax.psum_scatter(
        jnp.where(inside[:, None], table_block[local_rows].astype(f32), 0.0).astype(jnp.bfloat16),
        "shard",
        scatter_dimension=0,
        tiled=True,
    ).astype(jnp.float32)
    normed, norm_back_one = jax.vjp(norm_apply, embedded, gains_value[0])
    normed_b = normed.astype(brain_float_sixteen)
    projected_rows = jnp.dot(normed_b, qkv_full, preferred_element_type=f32)
    (query_matrix_rows, key_matrix_rows, value_matrix_rows), rotate_back = jax.vjp(
        split_rotate, projected_rows
    )
    query_brain_float = query_matrix_rows.astype(brain_float_sixteen).reshape(
        SEQUENCE_TOKENS, KEY_VALUE_HEADS, query_group_width, HEAD_WIDTH
    )
    key_brain_float = key_matrix_rows.astype(brain_float_sixteen)
    value_brain_float = value_matrix_rows.astype(brain_float_sixteen)
    attended, logarithm_total = attend_forward(
        query_brain_float, key_brain_float, value_brain_float
    )
    attended_b = attended.reshape(SEQUENCE_TOKENS, QUERY_HEADS * HEAD_WIDTH).astype(
        brain_float_sixteen
    )
    resid = embedded + jnp.dot(attended_b, out_full, preferred_element_type=f32)
    normed_two, norm_back_two = jax.vjp(norm_apply, resid, gains_value[1])
    normed_two_b = normed_two.astype(brain_float_sixteen)
    router_logits = jnp.dot(normed_two_b, router_full, preferred_element_type=f32)
    gate_probs, gate_back = jax.vjp(lambda logit_rows: gate_soft(logit_rows, routes), router_logits)
    slot_index = slot_places(routes.reshape(-1), EXPERTS, CAP)
    copies = jnp.repeat(normed_two_b, TOP, axis=0)
    outgoing = (
        jnp.zeros((EXPERTS * CAP, D), brain_float_sixteen)
        .at[slot_index]
        .set(copies)
        .reshape(shard_count, -1, D)
    )
    arrived = lax.all_to_all(outgoing, "shard", split_axis=0, concat_axis=0, tiled=True)
    local_experts = expert_in.shape[0]
    arrived = arrived.reshape(shard_count, local_experts, CAP, D)
    gate_up = jnp.einsum("secd,edjf->secjf", arrived, expert_in, preferred_element_type=f32)

    def swiglu(pair_rows):
        return jax.nn.silu(pair_rows[..., 0, :]) * pair_rows[..., 1, :]

    hidden, swiglu_back = jax.vjp(swiglu, gate_up)
    hidden_b = hidden.astype(brain_float_sixteen)
    produced = jnp.einsum(
        "secf,efd->secd", hidden_b, expert_down, preferred_element_type=f32
    ).astype(brain_float_sixteen)
    returned = lax.all_to_all(
        produced.reshape(shard_count, -1, D), "shard", split_axis=0, concat_axis=0, tiled=True
    )
    routed = returned.reshape(EXPERTS * CAP, D)[slot_index].reshape(SEQUENCE_TOKENS, TOP, D)
    resid_two = resid + jnp.einsum("st,std->sd", gate_probs, routed.astype(f32))
    picked_rows = resid_two[own_places]
    final_rows, norm_back_three = jax.vjp(norm_apply, picked_rows, gains_value[2])
    group_rows = lax.all_gather(final_rows.astype(brain_float_sixteen), "shard", axis=0, tiled=True)
    logits = (
        jnp.einsum("rd,vd->rv", group_rows, table_block, preferred_element_type=f32) / LOGIT_SCALE
    )
    targets = jnp.take_along_axis(
        token_ids.reshape(-1, SEQUENCE_TOKENS), positions + 1, axis=1
    ).reshape(-1)
    inside_target = (targets >= vocab_base) & (targets < vocab_base + vocab_rows)
    local_target = jnp.clip(targets - vocab_base, 0, vocab_rows - 1)
    row_top = jnp.max(logits, axis=1)
    row_total = jnp.sum(jnp.exp(logits - row_top[:, None]), axis=1)
    row_hit = jnp.where(
        inside_target, jnp.take_along_axis(logits, local_target[:, None], axis=1)[:, 0], 0.0
    )
    own_slot = (jnp.arange(expert_count) == expert_id)[:, None]
    stats = (
        jnp.where(own_slot, row_top[None, :], -1e30),
        jnp.where(own_slot, row_total[None, :], 0.0),
        jnp.where(own_slot, row_hit[None, :], 0.0),
    )

    def combine_stats(first_part, second_part):
        higher = jnp.maximum(first_part[0], second_part[0])
        summed = first_part[1] * jnp.exp(first_part[0] - higher) + second_part[1] * jnp.exp(
            second_part[0] - higher
        )
        return (higher, summed, first_part[2] + second_part[2])

    merged = merged_2(stats, ("expert", "shard"), combine_stats)
    row_lse = merged[0] + jnp.log(merged[1])
    seq_sums = jnp.sum((merged[2] - row_lse).reshape(-1, COMP), axis=1)
    loss_value, loss_back = jax.vjp(
        lambda sums_in: pair_loss(sums_in, ref_logps, pair_index), seq_sums
    )
    seq_grad = loss_back(jnp.ones((), f32))[0]
    row_grad = jnp.repeat(
        lax.dynamic_slice_in_dim(seq_grad, expert_id * shard_count, shard_count), COMP
    )
    own_lse = lax.dynamic_index_in_dim(row_lse, expert_id, 0, keepdims=False)
    target_hot = (
        (local_target[:, None] == jnp.arange(vocab_rows)[None, :]) & inside_target[:, None]
    ).astype(f32)
    grad_logits = (row_grad[:, None] * (target_hot - jnp.exp(logits - own_lse[:, None]))).astype(
        brain_float_sixteen
    )
    grad_rows = jnp.dot(grad_logits, table_block, preferred_element_type=f32) / LOGIT_SCALE
    table_grad = (
        jnp.einsum("rv,rd->vd", grad_logits, group_rows, preferred_element_type=f32) / LOGIT_SCALE
    )
    own_grad_rows = lax.psum_scatter(grad_rows, "shard", scatter_dimension=0, tiled=True)
    grad_picked, grad_gain_three = norm_back_three(own_grad_rows)
    grad_resid_two = jnp.zeros((SEQUENCE_TOKENS, D), f32).at[own_places].add(grad_picked)
    grad_gates = jnp.einsum("sd,std->st", grad_resid_two, routed.astype(f32))
    grad_routed = (
        (gate_probs[:, :, None] * grad_resid_two[:, None, :])
        .astype(brain_float_sixteen)
        .reshape(-1, D)
    )
    outgoing_grad = (
        jnp.zeros((EXPERTS * CAP, D), brain_float_sixteen)
        .at[slot_index]
        .set(grad_routed)
        .reshape(shard_count, -1, D)
    )
    arrived_grad = lax.all_to_all(outgoing_grad, "shard", split_axis=0, concat_axis=0, tiled=True)
    arrived_grad = arrived_grad.reshape(shard_count, local_experts, CAP, D)
    grad_down = jnp.einsum("secf,secd->efd", hidden_b, arrived_grad, preferred_element_type=f32)
    grad_hidden = jnp.einsum(
        "secd,efd->secf", arrived_grad, expert_down, preferred_element_type=f32
    ).astype(brain_float_sixteen)
    grad_gate_up = swiglu_back(grad_hidden.astype(f32))[0].astype(brain_float_sixteen)
    grad_in = jnp.einsum("secd,secjf->edjf", arrived, grad_gate_up, preferred_element_type=f32)
    grad_copies = jnp.einsum(
        "secjf,edjf->secd", grad_gate_up, expert_in, preferred_element_type=f32
    ).astype(brain_float_sixteen)
    back_rows = lax.all_to_all(
        grad_copies.reshape(shard_count, -1, D), "shard", split_axis=0, concat_axis=0, tiled=True
    )
    grad_normed_two = jnp.sum(
        back_rows.reshape(EXPERTS * CAP, D)[slot_index].reshape(SEQUENCE_TOKENS, TOP, D),
        axis=1,
        dtype=f32,
    )
    grad_router_logits = gate_back(grad_gates)[0]
    grad_normed_two = grad_normed_two + jnp.einsum(
        "se,de->sd", grad_router_logits, router_full.astype(f32)
    )
    grad_router = jnp.einsum("sd,se->de", normed_two_b.astype(f32), grad_router_logits)
    grad_resid, grad_gain_two = norm_back_two(grad_normed_two)
    grad_resid = grad_resid + grad_resid_two
    grad_branch = grad_resid.astype(brain_float_sixteen)
    grad_out = jnp.einsum("sk,sd->kd", attended_b, grad_branch, preferred_element_type=f32)
    attended_gradient = jnp.einsum(
        "sd,kd->sk", grad_branch, out_full, preferred_element_type=f32
    ).astype(brain_float_sixteen)
    grad_query, grad_key, grad_value = attend_backward(
        query_brain_float,
        key_brain_float,
        value_brain_float,
        logarithm_total,
        attended_gradient.reshape(SEQUENCE_TOKENS, KEY_VALUE_HEADS, query_group_width, HEAD_WIDTH),
    )
    grad_projected = rotate_back(
        (grad_query.reshape(SEQUENCE_TOKENS, QUERY_HEADS, HEAD_WIDTH), grad_key, grad_value)
    )[0].astype(brain_float_sixteen)
    grad_qkv = jnp.einsum("sd,sk->dk", normed_b, grad_projected, preferred_element_type=f32)
    grad_normed = jnp.einsum("sk,dk->sd", grad_projected, qkv_full, preferred_element_type=f32)
    grad_embedded, grad_gain_one = norm_back_one(grad_normed)
    grad_embedded = (grad_embedded + grad_resid).astype(brain_float_sixteen)
    picked = token_ids
    inside = (picked >= vocab_base) & (picked < vocab_base + vocab_rows)
    local_rows = jnp.where(inside, picked - vocab_base, vocab_rows)
    table_grad = table_grad.at[local_rows].add(
        lax.all_gather(grad_embedded, "shard", axis=0, tiled=True).astype(f32), mode="drop"
    )
    owner_sums = (
        lax.psum_scatter(
            table_grad.astype(jnp.bfloat16), "expert", scatter_dimension=1, tiled=True
        ).astype(jnp.float32),
        lax.psum_scatter(
            grad_in.astype(jnp.bfloat16), "expert", scatter_dimension=3, tiled=True
        ).astype(jnp.float32),
        lax.psum_scatter(
            grad_down.astype(jnp.bfloat16), "expert", scatter_dimension=1, tiled=True
        ).astype(jnp.float32),
    )
    gains_grad = jnp.stack([grad_gain_one, grad_gain_two, grad_gain_three])
    layer_sums = (
        lax.psum_scatter(grad_qkv, ("expert", "shard"), scatter_dimension=0, tiled=True),
        lax.psum_scatter(grad_out, ("expert", "shard"), scatter_dimension=0, tiled=True),
        lax.psum_scatter(grad_router, ("expert", "shard"), scatter_dimension=0, tiled=True),
        lax.psum_scatter(gains_grad, ("expert", "shard"), scatter_dimension=1, tiled=True),
    )
    weights = (
        embed_table,
        qkv_weight,
        out_weight,
        router_weight,
        norm_gains,
        in_weight,
        down_weight,
    )
    firsts = (embed_first, qkv_first, out_first, router_first, gains_first, in_first, down_first)
    seconds = (
        embed_second,
        qkv_second,
        out_second,
        router_second,
        gains_second,
        in_second,
        down_second,
    )
    gradients = (
        owner_sums[0],
        layer_sums[0],
        layer_sums[1],
        layer_sums[2],
        layer_sums[3],
        owner_sums[1],
        owner_sums[2],
    )
    step_value = step_count.astype(f32)
    moved = [
        lamb_parts(weight, moment_one, moment_two, gradient, step_value)
        for weight, moment_one, moment_two, gradient in zip(weights, firsts, seconds, gradients)
    ]
    partial_norms = jnp.stack(
        [
            jnp.stack([jnp.sum(weight * weight), jnp.sum(parts[2] * parts[2])])
            for weight, parts in zip(weights, moved)
        ]
    )
    norm_values = jnp.sqrt(lax.psum(partial_norms, ("expert", "shard")))
    trust_ratio = norm_values[:, 0] / norm_values[:, 1]
    results = [loss_value]
    for place, (weight, parts) in enumerate(zip(weights, moved)):
        results.extend([weight - STEP_RATE * trust_ratio[place] * parts[2], parts[0], parts[1]])
    results.append(jnp.stack([norm_values[:, 0], norm_values[:, 1], trust_ratio], axis=1))
    return tuple(results)


def solution(mesh):
    placed = (
        P("expert"),
        P("expert", None),
        P(),
        P(),
        P(("expert", "shard"), None),
        P(),
        P("shard", "expert"),
        P("shard", "expert"),
        P("shard", "expert"),
        P(("expert", "shard"), None),
        P(("expert", "shard"), None),
        P(("expert", "shard"), None),
        P(("expert", "shard"), None),
        P(("expert", "shard"), None),
        P(("expert", "shard"), None),
        P(("expert", "shard"), None),
        P(("expert", "shard"), None),
        P(("expert", "shard"), None),
        P(None, ("expert", "shard")),
        P(None, ("expert", "shard")),
        P(None, ("expert", "shard")),
        P("shard", None, None, "expert"),
        P("shard", None, None, "expert"),
        P("shard", None, None, "expert"),
        P("shard", "expert", None),
        P("shard", "expert", None),
        P("shard", "expert", None),
    )
    return jax.shard_map(
        on_device,
        mesh=mesh,
        in_specs=placed,
        out_specs=(
            P(),
            P("shard", "expert"),
            P("shard", "expert"),
            P("shard", "expert"),
            P(("expert", "shard"), None),
            P(("expert", "shard"), None),
            P(("expert", "shard"), None),
            P(("expert", "shard"), None),
            P(("expert", "shard"), None),
            P(("expert", "shard"), None),
            P(("expert", "shard"), None),
            P(("expert", "shard"), None),
            P(("expert", "shard"), None),
            P(None, ("expert", "shard")),
            P(None, ("expert", "shard")),
            P(None, ("expert", "shard")),
            P("shard", None, None, "expert"),
            P("shard", None, None, "expert"),
            P("shard", None, None, "expert"),
            P("shard", "expert", None),
            P("shard", "expert", None),
            P("shard", "expert", None),
            P(),
        ),
        check_vma=False,
    )
```

profile of v0, /device:TPU:0, one launch (start us, length us, event | category | flops | bytes accessed | tf_op | source)
XLA Modules:
  0.0 2872.6 jit_solution(10488199964256355711)
XLA Ops:
  8.1 11.9 multiply_reduce_fusion.1
  20.7 324.8 %all-gather.9.cloned.1.call-done = bf16[6144,1536]{1,0:T(8,128)(2,1)} async-done(((bf16[6144,384]{1,0:T(8,128)(2,1)}), bf16[6144,1536]{1,0:T(8,128)(2,1)}) %all-gather.9.cloned.1.call-update) | async-done | bytes 18874384 | tf_op jit(solution)/shard_map/all_gather | solution.py:184
  345.4 22.0 gather_fusion
  367.5 6.6 select_convert_fusion
  378.0 5.3 copy.325
  384.3 39.1 %all-gather = bf16[32,48,3]{1,2,0:T(4,128)(2,1)S(1)} all-gather(bf16[1,48,3]{1,2,0:T(4,128)(2,1)S(1)} %get-tuple-element.405), channel_id=1, replica_groups=mesh['expert'=4,'shard'=8] {'expert','shard'}, dimensions={0}, use_global_device_ids=true | all-gather | bytes 9504 | tf_op jit(solution)/shard_map/all_gather | solution.py:198
  424.4 9.5 reduce-window.6
  437.2 25.9 all-gather.11.cloned.1.call-done
  463.1 5.8 fusion.90
  478.8 50.6 %all-gather.13.cloned.1.call-done = bf16[1536,1536]{1,0:T(8,128)(2,1)} async-done(((bf16[48,1536]{1,0:T(8,128)(2,1)}), bf16[1536,1536]{1,0:T(8,128)(2,1)}) %all-gather.13.cloned.1.call-update) | async-done | bytes 4718608 | tf_op jit(solution)/shard_map/all_gather | solution.py:192
  533.5 15.3 scatter_custom_fusion
  553.9 5.5 multiply_reduce_fusion.5
  559.5 187.8 %all-gather.15.cloned.1.call-done = bf16[4,1536,2,512]{3,1,2,0:T(8,128)(2,1)} async-done(((bf16[4,1536,2,128]{3,1,2,0:T(8,128)(2,1)}), bf16[4,1536,2,512]{3,1,2,0:T(8,128)(2,1)}) %all-gather.15.cloned.1.call-update) | async-done | bytes 12582928 | tf_op jit(solution)/shard_map/all_gather | solution.py:185
  747.3 13.4 fusion.47
  768.0 95.0 %all-gather.17.cloned.1.call-done = bf16[4,512,1536]{2,1,0:T(8,128)(2,1)} async-done(((bf16[4,128,1536]{2,1,0:T(8,128)(2,1)}), bf16[4,512,1536]{2,1,0:T(8,128)(2,1)}) %all-gather.17.cloned.1.call-update) | async-done | bytes 6291472 | tf_op jit(solution)/shard_map/all_gather | solution.py:186
  862.9 11.8 convert_bitcast_fusion
  874.7 7.8 copy.226
  891.2 123.3 %all-gather.1 = bf16[32,48,32]{1,2,0:T(8,128)(2,1)S(1)} all-gather(bf16[1,48,32]{1,2,0:T(8,128)(2,1)S(1)} %get-tuple-element.399), channel_id=1, replica_groups=mesh['expert'=4,'shard'=8] {'expert','shard'}, dimensions={0}, use_global_device_ids=true | all-gather | bytes 101376 | tf_op jit(solution)/shard_map/all_gather | solution.py:195
  1015.4 16.8 gather_fusion.6
  1032.7 17.8 gather_fusion.1
  1056.2 9.4 all_gather.46
  1065.6 11.0 fusion.146
  1084.8 37.8 %all_gather.49 = f32[32,4,256]{2,1,0:T(4,128)S(1)} all-gather(f32[1,4,256]{2,1,0:T(4,128)S(1)} %get-tuple-element.415), channel_id=1, replica_groups=mesh['expert'=4,'shard'=8] {'expert','shard'}, dimensions={0}, use_global_device_ids=true | all-gather | bytes 135168 | tf_op jit(solution)/shard_map/all_gather | solution.py:27
  1122.5 37.5 %all_gather.48 = f32[32,4,256]{2,1,0:T(4,128)S(1)} all-gather(f32[1,4,256]{2,1,0:T(4,128)S(1)} %get-tuple-element.416), channel_id=1, replica_groups=mesh['expert'=4,'shard'=8] {'expert','shard'}, dimensions={0}, use_global_device_ids=true | all-gather | bytes 135168 | tf_op jit(solution)/shard_map/all_gather | solution.py:27
  1160.0 37.8 %all_gather.47 = f32[32,4,256]{2,1,0:T(4,128)S(1)} all-gather(f32[1,4,256]{2,1,0:T(4,128)S(1)} %get-tuple-element.417), channel_id=1, replica_groups=mesh['expert'=4,'shard'=8] {'expert','shard'}, dimensions={0}, use_global_device_ids=true | all-gather | bytes 135168 | tf_op jit(solution)/shard_map/all_gather | solution.py:27
  1203.4 15.0 convolution_multiply_fusion.2
  1218.7 35.0 %reduce-scatter.20.cloned.1.call-done = f32[32,1536]{1,0:T(8,128)} async-done(((f32[256,1536]{1,0:T(8,128)}), f32[32,1536]{1,0:T(8,128)}) %reduce-scatter.20.cloned.1.call-update) | async-done | bytes 196624 | tf_op jit(solution)/shard_map/reduce_scatter | solution.py:311
  1256.6 16.1 scatter_custom_fusion.4
  1272.8 102.7 %all_to_all.20 = bf16[8,352,1536]{2,1,0:T(8,128)(2,1)} all-to-all(bf16[8,352,1536]{2,1,0:T(8,128)(2,1)} %bitcast.316), channel_id=1, replica_groups=mesh['expert'=4,'shard'=8] {'shard'}, dimensions={0} | all-to-all | bytes 17301504 | tf_op jit(solution)/shard_map/all_to_all | solution.py:326
  1375.4 14.7 fusion.38
  1390.1 15.9 fusion.4
  1406.0 7.8 copy.331
  1419.6 6.1 fusion.26
  1426.1 11.3 scatter_custom_fusion.6
  1437.4 78.5 %all-to-all-done.3 = bf16[8,352,1536]{2,1,0:T(8,128)(2,1)} async-done(((bf16[8,352,1536]{2,1,0:T(8,128)(2,1)}), bf16[8,352,1536]{2,1,0:T(8,128)(2,1)}, u32[]{:S(2)}, u32[]{:S(2)}) %all-to-all-start.3) | async-done | bytes 8650784 | tf_op jit(solution)/shard_map/all_to_all | solution.py:337
  1515.9 18.0 gather_fusion.5
  1534.0 7.2 convert_reduce_fusion
  1560.0 6.6 fusion.67
  1570.7 10.2 bitcast_convert_fusion.2
  1587.3 19.7 bitcast_convert_fusion
  1607.0 31.8 %copy.288 = bf16[4,1536,2,512]{1,2,0,3:T(2,128)(2,1)} copy(bf16[4,1536,2,512]{3,1,2,0:T(8,128)(2,1)} %bitcast_convert_fusion) | data formatting | bytes 25165824
  1638.9 27.2 reshape.869
  1667.8 7.9 fusion.88
  1676.8 20.0 convolution_multiply_fusion
  1696.8 46.4 %scatter_custom_fusion.5 = f32[6144,1536]{1,0:T(8,128)} fusion(f32[6144,1536]{1,0:T(8,128)} %convolution_multiply_fusion, s32[2048]{0:T(1024)} %get-tuple-element.402, bf16[2048,1536]{1,0:T(8,128)(2,1)} %all-gather.19.cloned.1.call-done), kind=kCustom, calls=%fused_computation.34 | custom fusion | flops 6291456 | bytes 44040192 | tf_op jit(solution)/shard_map/scatter-add | solution.py:374
  1743.1 21.0 convert_element_type.213
  1764.2 24.5 copy.282
  1789.7 8.8 multiply_reduce_fusion.3
  1806.6 78.1 %reduce-scatter.26.cloned.1.call-done = bf16[4,128,1536]{2,1,0:T(8,128)(2,1)} async-done(((bf16[4,512,1536]{2,1,0:T(8,128)(2,1)}), bf16[4,128,1536]{2,1,0:T(8,128)(2,1)}) %reduce-scatter.26.cloned.1.call-update) | async-done | bytes 1572880 | tf_op jit(solution)/shard_map/reduce_scatter | solution.py:384
  1884.7 7.2 multiply_reduce_fusion.4
  1893.3 134.9 %reduce-scatter.24.cloned.1.call-done = f32[48,1536]{1,0:T(8,128)} async-done(((f32[1536,1536]{1,0:T(8,128)}), f32[48,1536]{1,0:T(8,128)}) %reduce-scatter.24.cloned.1.call-update) | async-done | bytes 294928 | tf_op jit(solution)/shard_map/reduce_scatter | solution.py:391
  2032.4 208.7 %reduce-scatter.34.cloned.1.call-done = bf16[128,12288]{1,0:T(8,128)(2,1)} async-done(((bf16[512,12288]{1,0:T(8,128)(2,1)}), bf16[128,12288]{1,0:T(8,128)(2,1)}) %reduce-scatter.34.cloned.1.call-update) | async-done | bytes 3145744
  2241.1 8.0 reshape.870
  2249.2 8.8 copy.289
  2258.0 18.3 multiply_reduce_fusion.2
  2277.8 12.2 copy.253
  2290.0 128.5 %reduce-scatter.22.cloned.1.call-done = f32[48,2560]{1,0:T(8,128)} async-done(((f32[1536,2560]{1,0:T(8,128)}), f32[48,2560]{1,0:T(8,128)}) %reduce-scatter.22.cloned.1.call-update) | async-done | bytes 491536 | tf_op jit(solution)/shard_map/reduce_scatter | solution.py:390
  2423.3 310.3 %reduce-scatter.28.cloned.1.call-done = bf16[384,6144]{1,0:T(8,128)(2,1)} async-done(((bf16[1536,6144]{1,0:T(8,128)(2,1)}), bf16[384,6144]{1,0:T(8,128)(2,1)}) %reduce-scatter.28.cloned.1.call-update) | async-done | bytes 4718608
  2733.6 6.6 copy.283
  2740.2 23.5 multiply_reduce_fusion
  2765.3 12.0 copy.252
  2777.3 41.2 %psum.7 = f32[7,2]{0,1:T(2,128)S(1)} all-reduce(f32[7,2]{0,1:T(2,128)S(1)} %stack.127), channel_id=1, replica_groups=mesh['expert'=4,'shard'=8] {'expert','shard'}, use_global_device_ids=true, to_apply=%region_55.56 | all-reduce | flops 14 | bytes 112 | tf_op jit(solution)/shard_map/psum | solution.py:434
  2829.5 18.1 copy.251
  2852.7 11.3 multiply_subtract_fusion
  (424 shorter events, 139.2 us)
Async XLA Ops:
  8.0 12.0 copy-start.54
  8.0 337.4 %all-gather.9.cloned.1.call-start = ((), (), s32[]{:S(2)}) async-start(), calls=%async_computation.13 | async-start | bytes 23592960 | tf_op jit(solution)/shard_map/all_gather | solution.py:184
  20.0 415.8 %reduce-scatter.18.cloned.1.call-start = ((), (), s32[]{:S(2)}) async-start(), calls=%async_computation.14 | async-start | bytes 7077888 | tf_op jit(solution)/shard_map/reduce_scatter | solution.py:206
  374.1 89.0 %all-gather.11.cloned.1.call-start = ((), (), s32[]{:S(2)}) async-start(), calls=%async_computation.15 | async-start | bytes 8110080 | tf_op jit(solution)/shard_map/all_gather | solution.py:189
  376.5 152.9 %all-gather.13.cloned.1.call-start = ((), (), s32[]{:S(2)}) async-start(), calls=%async_computation.16 | async-start | bytes 4866048 | tf_op jit(solution)/shard_map/all_gather | solution.py:192
  377.9 5.8 copy-start.58
  377.9 369.4 %all-gather.15.cloned.1.call-start = ((), (), s32[]{:S(2)}) async-start(), calls=%async_computation.17 | async-start | bytes 15728640 | tf_op jit(solution)/shard_map/all_gather | solution.py:185
  435.2 33.6 %copy-start.51 = (f32[1536]{0:T(1024)}, f32[1536]{0:T(1024)S(1)}, u32[]{:S(2)}) copy-start(f32[1536]{0:T(1024)S(1)} %get-tuple-element.327) | copy-start | bytes 18436
  435.2 98.0 %copy-start.44 = (f32[1536]{0:T(1024)}, f32[1536]{0:T(1024)S(1)}, u32[]{:S(2)}) copy-start(f32[1536]{0:T(1024)S(1)} %get-tuple-element.326) | copy-start | bytes 18436
  435.7 36.1 %copy-start.34 = (f32[256,32]{0,1:T(8,128)}, f32[256,32]{0,1:T(8,128)S(1)}, u32[]{:S(2)}) copy-start(f32[256,32]{0,1:T(8,128)S(1)} %get-tuple-element.418) | copy-start | bytes 98308
  435.7 36.1 %copy-start.36 = (f32[256,32]{0,1:T(8,128)}, f32[256,32]{0,1:T(8,128)S(1)}, u32[]{:S(2)}) copy-start(f32[256,32]{0,1:T(8,128)S(1)} %get-tuple-element.419) | copy-start | bytes 98308
  437.1 31.7 %copy-start.70 = (f32[256]{0:T(256)}, f32[256]{0:T(256)S(1)}, u32[]{:S(2)}) copy-start(f32[256]{0:T(256)S(1)} %fusion.71) | copy-start | bytes 3076
  437.1 31.7 %copy-start.62 = (f32[256]{0:T(256)}, f32[256]{0:T(256)S(1)}, u32[]{:S(2)}) copy-start(f32[256]{0:T(256)S(1)} %fusion.116) | copy-start | bytes 3076
  470.0 6.0 copy-start.30
  477.5 51.8 %copy-start.4 = (bf16[256,1536]{1,0:T(8,128)(2,1)S(1)}, bf16[256,1536]{1,0:T(8,128)(2,1)}, u32[]{:S(2)}) copy-start(bf16[256,1536]{1,0:T(8,128)(2,1)} %reduce-scatter.18.cloned.1.call-done) | copy-start | bytes 2359300
  478.8 54.5 %copy-start.10 = (bf16[8,64,3,256]{3,1,2,0:T(8,128)(2,1)}, bf16[8,64,3,256]{3,1,2,0:T(8,128)(2,1)S(1)}, u32[]{:S(2)}) copy-start(bf16[8,64,3,256]{3,1,2,0:T(8,128)(2,1)S(1)} %fusion.74) | copy-start | bytes 2359300
  533.2 15.6 copy-start.72
  533.2 15.6 copy-start.64
  533.5 481.7 %copy-start.7 = (bf16[256,1536]{1,0:T(8,128)(2,1)}, bf16[256,1536]{1,0:T(8,128)(2,1)S(1)}, u32[]{:S(2)}) copy-start(bf16[256,1536]{1,0:T(8,128)(2,1)S(1)} %multiply_convert_fusion.2) | copy-start | bytes 2359300
  548.8 198.5 %all-to-all-start = ((bf16[8,352,1536]{2,1,0:T(8,128)(2,1)}), bf16[8,352,1536]{2,1,0:T(8,128)(2,1)}, u32[]{:S(2)}, u32[]{:S(2)}) async-start(bf16[8,352,1536]{2,1,0:T(8,128)(2,1)} %bitcast.315), calls=%async_computation.1 | async-start | bytes 17301504 | tf_op jit(solution)/shard_map/all_to_all | solution.py:242
  553.9 309.1 %all-gather.17.cloned.1.call-start = ((), (), s32[]{:S(2)}) async-start(), calls=%async_computation.18 | async-start | bytes 7864320 | tf_op jit(solution)/shard_map/all_gather | solution.py:186
  882.5 8.0 copy-start.42
  882.5 132.5 %copy-start.78 = (s32[16,2]{0,1:T(2,128)S(1)}, s32[16,2]{0,1:T(2,128)}, u32[]{:S(2)}) copy-start(s32[16,2]{0,1:T(2,128)} %param.31) | copy-start | bytes 388
  882.5 150.1 %all-to-all-start.1 = ((bf16[8,352,1536]{2,1,0:T(8,128)(2,1)}), bf16[8,352,1536]{2,1,0:T(8,128)(2,1)}, u32[]{:S(2)}, u32[]{:S(2)}) async-start(bf16[8,352,1536]{2,1,0:T(8,128)(2,1)} %bitcast.313), calls=%async_computation.2 | async-start | bytes 17301504 | tf_op jit(solution)/shard_map/all_to_all | solution.py:255
  887.6 366.1 %reduce-scatter.20.cloned.1.call-start = ((), (), s32[]{:S(2)}) async-start(), calls=%async_computation.19 | async-start | bytes 1769472 | tf_op jit(solution)/shard_map/reduce_scatter | solution.py:311
  890.1 313.3 %copy-start.56 = (s32[256]{0:T(256)}, s32[256]{0:T(256)S(1)}, u32[]{:S(2)}) copy-start(s32[256]{0:T(256)S(1)} %min.26) | copy-start | bytes 3076
  890.3 313.2 %copy-start.74 = (pred[256]{0:T(512)(128)(4,1)}, pred[256]{0:T(512)(128)(4,1)S(1)}, u32[]{:S(2)}) copy-start(pred[256]{0:T(512)(128)(4,1)S(1)} %and.55) | copy-start | bytes 772
  1015.0 17.3 copy-start.32
  1065.6 11.0 copy-start.16
  1076.6 122.9 %copy-start.82 = (f32[32]{0:T(128)S(1)}, f32[32]{0:T(128)}, u32[]{:S(2)}) copy-start(f32[32]{0:T(128)} %param.32) | copy-start | bytes 388
  1203.4 15.0 copy-start.60
  1203.4 15.0 copy-start.66
  1256.6 163.0 %copy-start.2 = (f32[256,1536]{1,0:T(8,128)}, f32[256,1536]{1,0:T(8,128)S(1)}, u32[]{:S(2)}) copy-start(f32[256,1536]{1,0:T(8,128)S(1)} %scatter_custom_fusion.3) | copy-start | bytes 4718596
  1413.9 102.1 %all-to-all-start.3 = ((bf16[8,352,1536]{2,1,0:T(8,128)(2,1)}), bf16[8,352,1536]{2,1,0:T(8,128)(2,1)}, u32[]{:S(2)}, u32[]{:S(2)}) async-start(bf16[8,352,1536]{2,1,0:T(8,128)(2,1)} %bitcast.314), calls=%async_computation.5 | async-start | bytes 17301504 | tf_op jit(solution)/shard_map/all_to_all | solution.py:337
  1419.1 277.7 %all-gather.19.cloned.1.call-start = ((), (), s32[]{:S(2)}) async-start(), calls=%async_computation.20 | async-start | bytes 7077888 | tf_op jit(solution)/shard_map/all_gather | solution.py:375
  1534.0 7.3 copy-start.33
  1534.0 7.3 copy-start.45
  1534.0 7.3 copy-start.65
  1534.0 8.0 copy-start.73
  1534.0 8.0 copy-start.3
  1534.0 8.4 slice-start.2
  1547.2 8.6 slice-start
  1551.3 8.6 copy-start.22
  1559.8 6.8 copy-start.20
  1559.9 6.6 copy-start.12
  1559.9 6.6 copy-start.71
  1560.0 8.1 copy-start.8
  1568.0 231.8 %reduce-scatter.30.cloned.1.call-start = ((), (), s32[]{:S(2)}) async-start(), calls=%async_computation.25 | async-start | bytes 811008
  1569.3 233.9 %reduce-scatter.32.cloned.1.call-start = ((), (), s32[]{:S(2)}) async-start(), calls=%async_computation.26 | async-start | bytes 811008
  1570.7 314.0 %reduce-scatter.26.cloned.1.call-start = ((), (), s32[]{:S(2)}) async-start(), calls=%async_computation.23 | async-start | bytes 7864320 | tf_op jit(solution)/shard_map/reduce_scatter | solution.py:384
  1581.0 447.2 %reduce-scatter.24.cloned.1.call-start = ((), (), s32[]{:S(2)}) async-start(), calls=%async_computation.22 | async-start | bytes 9732096 | tf_op jit(solution)/shard_map/reduce_scatter | solution.py:391
  1587.3 653.9 %reduce-scatter.34.cloned.1.call-start = ((), (), s32[]{:S(2)}) async-start(), calls=%async_computation.27 | async-start | bytes 15728640
  1666.1 752.4 %reduce-scatter.22.cloned.1.call-start = ((), (), s32[]{:S(2)}) async-start(), calls=%async_computation.21 | async-start | bytes 16220160 | tf_op jit(solution)/shard_map/reduce_scatter | solution.py:390
  1675.7 1057.9 %reduce-scatter.28.cloned.1.call-start = ((), (), s32[]{:S(2)}) async-start(), calls=%async_computation.24 | async-start | bytes 23592960
  1788.7 9.8 copy-start.81
  1788.7 11.8 copy-start.43
  1788.7 11.8 copy-start.68
  1788.7 11.8 copy-start.69
  1788.8 15.3 copy-start.59
  1788.8 15.3 copy-start.76
  1788.8 15.3 copy-start.77
  1788.8 95.9 %copy-start.1 = (f32[4,128,1536]{2,1,0:T(8,128)S(1)}, f32[4,128,1536]{2,1,0:T(8,128)}, u32[]{:S(2)}) copy-start(f32[4,128,1536]{2,1,0:T(8,128)} %param.53) | copy-start | bytes 9437188
  1806.6 221.6 %copy-start.19 = (f32[48,1536]{1,0:T(8,128)S(1)}, f32[48,1536]{1,0:T(8,128)}, u32[]{:S(2)}) copy-start(f32[48,1536]{1,0:T(8,128)} %param.41) | copy-start | bytes 884740
  2829.5 18.1 copy-start.6
  (41 other events, 117.9 us)
Sparse Core Ops, SparseCore 0:
  20.1 325.2 all-gather.8
  374.2 60.9 reduce-scatter.17
  1218.6 35.1 reduce-scatter.19
  1568.1 44.6 all-gather.18
Sparse Core Ops, SparseCore 1:
  378.1 84.9 all-gather.10
  466.9 62.5 all-gather.12
  531.5 215.8 all-gather.14
  749.5 113.4 all-gather.16
  1575.2 96.1 reduce-scatter.29
  1677.3 94.6 reduce-scatter.31
  1774.9 109.7 reduce-scatter.25
  1892.0 136.1 reduce-scatter.23
  2030.4 210.6 reduce-scatter.33
  2247.1 171.3 reduce-scatter.21
  2420.7 312.8 reduce-scatter.27
where the time goes:
time: 2880 us; the launch traced here: 2870 us
  waiting for transfers between devices  1660 us (58%)
  blocking collectives  429 us (15%)
  local copies, waits for them, and re-layouts  293 us (10%)
  other arithmetic  261 us (9%)
  matrix products  190 us (7%)
    unnamed x19, waiting for transfers between devices  519 us
    all_gather x1, waiting for transfers between devices, on_device(): lax.all_gather(embed_table.astype(brain_float_sixteen), 'expert', axis=1,...  325 us
    all_gather x1, waiting for transfers between devices, on_device(): lax.all_gather(in_weight.astype(brain_float_sixteen), 'expert', axis=3, t...  188 us
    unnamed x193, local copies, waits for them, and re-layouts  171 us
    reduce_scatter x1, waiting for transfers between devices, on_device(): lax.psum_scatter(grad_out, ('expert', 'shard'), scatter_dimension=0, tile...  135 us
    reduce_scatter x1, waiting for transfers between devices, on_device(): lax.psum_scatter(grad_qkv, ('expert', 'shard'), scatter_dimension=0, tile...  128 us
    all_gather x1, blocking collectives, on_device(): lax.all_gather(router_weight.astype(brain_float_sixteen), ('expert', 'sha...  123 us
    all_gather x3, blocking collectives, merged_2(): gathered = jax.tree.map(lambda a: lax.all_gather(a, axis), part)  113 us
  transfers between devices with their start and end apart: 18, of which 12 were waited for; matrix products, arithmetic and copies ran while one was open for 15% of the time, Pallas kernels for 0%

commit v1 on v0

v1 whole, which is shorter than its diff:
```python
import jax
import jax.numpy as jnp
from jax import lax
from jax.experimental import pallas as pl
from jax.experimental.pallas import tpu as pltpu
from jax.sharding import PartitionSpec as P

D = 1536
QUERY_HEADS = 24
KEY_VALUE_HEADS = 8
GROUP = QUERY_HEADS // KEY_VALUE_HEADS
HEAD_WIDTH = 64
TOP = 8
EXPERTS = 32
SEQUENCE_TOKENS = 256
COMP = 32

BETA = 0.1
LOGIT_SCALE = 6.0
RATE_ONE = 0.9
RATE_TWO = 0.999
EPSILON = 1e-06
DECAY = 0.01
STEP_RATE = 0.3

BOTH = ("expert", "shard")
bf16 = jnp.bfloat16
f32 = jnp.float32


def norm_apply(values, gain):
    return values * lax.rsqrt(jnp.mean(values * values, axis=-1, keepdims=True) + 1e-06) * gain


def rotary_apply(values, places):
    half = values.shape[-1] // 2
    freqs = jnp.exp(-jnp.log(10000.0) * jnp.arange(half, dtype=f32) / half)
    angles = places[:, None] * freqs[None, :]
    cosine = jnp.cos(angles)[:, None, :]
    sine = jnp.sin(angles)[:, None, :]
    first_half = values[..., :half]
    second_half = values[..., half:]
    return jnp.concatenate(
        [first_half * cosine - second_half * sine, second_half * cosine + first_half * sine],
        axis=-1,
    )


def lamb_parts(weight, moment_one, moment_two, gradient, step_value):
    moment_one = RATE_ONE * moment_one + (1.0 - RATE_ONE) * gradient
    moment_two = RATE_TWO * moment_two + (1.0 - RATE_TWO) * gradient * gradient
    fixed_one = moment_one / (1.0 - RATE_ONE**step_value)
    fixed_two = moment_two / (1.0 - RATE_TWO**step_value)
    update = fixed_one / (jnp.sqrt(fixed_two) + EPSILON) + DECAY * weight
    return (moment_one, moment_two, update)


STEPS = 4


def row_lists(tokens, base, rows):
    inside = (tokens >= base) & (tokens < base + rows)
    count = jnp.sum(inside.astype(jnp.int32), axis=1)
    place = jnp.arange(SEQUENCE_TOKENS, dtype=jnp.int32)
    before = (place[:, None] < place[None, :]).astype(bf16)
    rank = jnp.dot(inside.astype(bf16), before, preferred_element_type=f32).astype(jnp.int32)
    packed = place[None, :] * 65536 + (tokens - base)
    hit = inside[:, :, None] & (rank[:, :, None] == place[None, None, :])
    entry = jnp.sum(jnp.where(hit, packed[:, :, None], 0), axis=1)
    empty = SEQUENCE_TOKENS * 65536
    return jnp.where(place[None, :] < count[:, None], entry, empty), count


def gather_kernel(list_ref, count_ref, table_ref, out_ref, rows_ref):
    b = pl.program_id(0)
    rows_ref[...] = jnp.zeros_like(rows_ref)

    def step(k, carry):
        for j in range(STEPS):
            entry = list_ref[b, k * STEPS + j]
            rows_ref[pl.ds(entry >> 16, 1), :] = table_ref[pl.ds(entry & 65535, 1), :]
        return carry

    lax.fori_loop(0, (count_ref[b] + STEPS - 1) // STEPS, step, 0)
    out_ref[0] = rows_ref[:SEQUENCE_TOKENS].astype(bf16)


def gather_rows(lists, counts, table):
    blocks = lists.shape[0]
    rows, columns = table.shape
    return pl.pallas_call(
        gather_kernel,
        grid_spec=pltpu.PrefetchScalarGridSpec(
            num_scalar_prefetch=2,
            grid=(blocks,),
            in_specs=[pl.BlockSpec((rows, columns), lambda b, *_: (0, 0))],
            out_specs=pl.BlockSpec((1, SEQUENCE_TOKENS, columns), lambda b, *_: (b, 0, 0)),
            scratch_shapes=[pltpu.VMEM((SEQUENCE_TOKENS + 8, columns), f32)],
        ),
        out_shape=jax.ShapeDtypeStruct((blocks, SEQUENCE_TOKENS, columns), bf16),
        compiler_params=pltpu.CompilerParams(vmem_limit_bytes=40 << 20),
        name="gather_rows",
    )(lists, counts, table)


def scatter_kernel(list_ref, count_ref, grad_ref, head_ref, out_ref, rows_ref):
    b = pl.program_id(0)

    @pl.when(b == 0)
    def _():
        out_ref[...] = head_ref[...].astype(f32)

    rows_ref[:SEQUENCE_TOKENS] = grad_ref[0].astype(f32)
    rows_ref[SEQUENCE_TOKENS:] = jnp.zeros((8, rows_ref.shape[1]), f32)

    def step(k, carry):
        for j in range(STEPS):
            entry = list_ref[b, k * STEPS + j]
            out_ref[pl.ds(entry & 65535, 1), :] += rows_ref[pl.ds(entry >> 16, 1), :]
        return carry

    lax.fori_loop(0, (count_ref[b] + STEPS - 1) // STEPS, step, 0)


def scatter_rows(lists, counts, grads, head):
    blocks = lists.shape[0]
    rows, columns = head.shape
    return pl.pallas_call(
        scatter_kernel,
        grid_spec=pltpu.PrefetchScalarGridSpec(
            num_scalar_prefetch=2,
            grid=(blocks,),
            in_specs=[
                pl.BlockSpec((1, SEQUENCE_TOKENS, columns), lambda b, *_: (b, 0, 0)),
                pl.BlockSpec((rows, columns), lambda b, *_: (0, 0)),
            ],
            out_specs=pl.BlockSpec((rows, columns), lambda b, *_: (0, 0)),
            scratch_shapes=[pltpu.VMEM((SEQUENCE_TOKENS + 8, columns), f32)],
        ),
        out_shape=jax.ShapeDtypeStruct((rows, columns), f32),
        compiler_params=pltpu.CompilerParams(vmem_limit_bytes=50 << 20),
        name="scatter_rows",
    )(lists, counts, grads, head)


def on_device(
    token_ids,
    positions,
    pair_index,
    ref_logps,
    routes,
    step_count,
    embed_table,
    embed_first,
    embed_second,
    qkv_weight,
    qkv_first,
    qkv_second,
    out_weight,
    out_first,
    out_second,
    router_weight,
    router_first,
    router_second,
    norm_gains,
    gains_first,
    gains_second,
    in_weight,
    in_first,
    in_second,
    down_weight,
    down_first,
    down_second,
):
    shard_id = lax.axis_index("shard")
    expert_id = lax.axis_index("expert")
    shards = lax.axis_size("shard")
    planes = lax.axis_size("expert")
    devices = shards * planes
    vocab_rows, columns = embed_table.shape
    vocab_base = shard_id * vocab_rows
    own_rows = vocab_rows // planes
    local_experts = in_weight.shape[0]
    hidden_units = in_weight.shape[3]
    head_cols = QUERY_HEADS * HEAD_WIDTH
    key_cols = KEY_VALUE_HEADS * HEAD_WIDTH
    rows_all = devices * COMP

    tokens_all = lax.all_gather(token_ids, "expert", axis=0, tiled=True).reshape(
        devices, SEQUENCE_TOKENS
    )
    places_all = lax.all_gather(positions, "expert", axis=0, tiled=True)
    own_places = lax.dynamic_index_in_dim(positions, shard_id, 0, keepdims=False)
    start = own_places[0]
    routes_all = lax.all_gather(
        lax.dynamic_slice_in_dim(routes, start, COMP, 0), BOTH, axis=0, tiled=True
    )
    spots = jnp.arange(SEQUENCE_TOKENS, dtype=jnp.int32)
    targets = jnp.sum(
        jnp.where(
            places_all[:, :, None] + 1 == spots[None, None, :], tokens_all[:, None, :], 0
        ),
        axis=2,
    ).reshape(-1)

    lists, counts = row_lists(tokens_all, vocab_base, vocab_rows)
    picked = gather_rows(lists, counts, embed_table).reshape(
        planes, shards, SEQUENCE_TOKENS, columns
    )
    picked = lax.psum_scatter(picked, "shard", scatter_dimension=1, tiled=True)
    picked = lax.all_to_all(picked[:, 0], "expert", split_axis=0, concat_axis=0, tiled=True)
    embedded = jnp.concatenate([picked[p] for p in range(planes)], axis=1).astype(f32)

    qkv_full, out_full, router_full, gains_full = (
        lax.all_gather(qkv_weight.astype(bf16), BOTH, axis=0, tiled=True),
        lax.all_gather(out_weight.astype(bf16), BOTH, axis=0, tiled=True),
        lax.all_gather(router_weight.astype(bf16), BOTH, axis=0, tiled=True),
        lax.all_gather(norm_gains.astype(bf16), BOTH, axis=1, tiled=True),
    )
    gains_value = gains_full.astype(f32)
    table_own = lax.all_to_all(
        embed_table.astype(bf16).reshape(planes, own_rows, columns),
        "expert",
        split_axis=0,
        concat_axis=0,
        tiled=True,
    )
    table_own = jnp.concatenate([table_own[p] for p in range(planes)], axis=1)

    normed, norm_back_one = jax.vjp(norm_apply, embedded, gains_value[0])
    normed_b = normed.astype(bf16)
    normed_rows = lax.dynamic_slice_in_dim(normed_b, start, COMP, 0)
    query_weight, pair_weight = qkv_full[:, :head_cols], qkv_full[:, head_cols:]
    places_f = own_places.astype(f32)
    spots_f = spots.astype(f32)

    def make_query(projected):
        return rotary_apply(projected.reshape(COMP, QUERY_HEADS, HEAD_WIDTH), places_f)

    def make_key(projected):
        return rotary_apply(
            projected.reshape(SEQUENCE_TOKENS, KEY_VALUE_HEADS, HEAD_WIDTH), spots_f
        )

    query_f, query_back = jax.vjp(
        make_query, jnp.dot(normed_rows, query_weight, preferred_element_type=f32)
    )
    projected_pair = jnp.dot(normed_b, pair_weight, preferred_element_type=f32)
    key_f, key_back = jax.vjp(make_key, projected_pair[:, :key_cols])
    query = query_f.astype(bf16).reshape(COMP, KEY_VALUE_HEADS, GROUP, HEAD_WIDTH)
    key = key_f.astype(bf16)
    value = (
        projected_pair[:, key_cols:]
        .reshape(SEQUENCE_TOKENS, KEY_VALUE_HEADS, HEAD_WIDTH)
        .astype(bf16)
    )
    scores = jnp.einsum("qhgd,khd->hgqk", query, key, preferred_element_type=f32) * HEAD_WIDTH ** (
        -0.5
    )
    scores = jnp.where(own_places[:, None] >= spots[None, :], scores, -1000000000.0)
    expd = jnp.exp(scores - jnp.max(scores, axis=-1, keepdims=True))
    probs = expd / jnp.sum(expd, axis=-1, keepdims=True)
    probs_b = probs.astype(bf16)
    attended = (
        jnp.einsum("hgqk,khd->qhgd", probs_b, value, preferred_element_type=f32)
        .reshape(COMP, head_cols)
        .astype(bf16)
    )
    resid = lax.dynamic_slice_in_dim(embedded, start, COMP, 0) + jnp.dot(
        attended, out_full, preferred_element_type=f32
    )
    normed_two, norm_back_two = jax.vjp(norm_apply, resid, gains_value[1])
    normed_two_b = normed_two.astype(bf16)

    expert_rows = lax.all_gather(normed_two_b, BOTH, axis=0, tiled=True)
    chosen = jnp.any(
        routes_all[:, :, None] == jnp.arange(EXPERTS, dtype=jnp.int32)[None, None, :], axis=1
    )

    def soft_gates(router_logits, mask):
        top = jnp.max(jnp.where(mask, router_logits, -3e38), axis=-1, keepdims=True)
        weight = jnp.where(mask, jnp.exp(jnp.where(mask, router_logits - top, 0.0)), 0.0)
        return weight / jnp.sum(weight, axis=-1, keepdims=True)

    gates = soft_gates(jnp.dot(expert_rows, router_full, preferred_element_type=f32), chosen)
    own_index = expert_id * shards + shard_id
    own_gates = lax.dynamic_slice_in_dim(gates, own_index * COMP, COMP, 0)
    local_gates = lax.dynamic_slice_in_dim(gates, shard_id * local_experts, local_experts, 1)
    in_b = in_weight.astype(bf16)
    down_b = down_weight.astype(bf16)
    gate_up = jnp.einsum("td,edjf->tejf", expert_rows, in_b, preferred_element_type=f32)

    def swiglu(both):
        return jax.nn.silu(both[:, :, 0]) * both[:, :, 1]

    hidden, swiglu_back = jax.vjp(swiglu, gate_up)
    gated_hidden = (hidden.astype(bf16).astype(f32) * local_gates[:, :, None]).astype(bf16)
    produced = jnp.einsum("tef,efd->td", gated_hidden, down_b, preferred_element_type=f32)
    combined = lax.psum_scatter(produced.astype(bf16), BOTH, scatter_dimension=0, tiled=True)
    resid_two = resid + combined.astype(f32)

    final_rows, norm_back_three = jax.vjp(norm_apply, resid_two, gains_value[2])
    head_rows = lax.all_gather(final_rows.astype(bf16), BOTH, axis=0, tiled=True)
    logits = jnp.einsum("rd,vd->rv", head_rows, table_own, preferred_element_type=f32) / LOGIT_SCALE
    own_base = vocab_base + expert_id * own_rows
    target_hot = targets[:, None] == own_base + jnp.arange(own_rows, dtype=jnp.int32)[None, :]
    row_top = jnp.max(logits, axis=1)
    row_total = jnp.sum(jnp.exp(logits - row_top[:, None]), axis=1)
    row_hit = jnp.sum(jnp.where(target_hot, logits, 0.0), axis=1)
    stats = lax.all_gather(jnp.stack([row_top, row_total, row_hit]), BOTH, axis=0, tiled=False)
    top_all = jnp.max(stats[:, 0], axis=0)
    total_all = jnp.sum(stats[:, 1] * jnp.exp(stats[:, 0] - top_all[None]), axis=0)
    row_lse = top_all + jnp.log(total_all)
    seq_sums = jnp.sum((jnp.sum(stats[:, 2], axis=0) - row_lse).reshape(-1, COMP), axis=1)

    sequences = jnp.arange(devices, dtype=jnp.int32)[None, :]
    pair_sign = (pair_index[:, :1] == sequences).astype(f32) - (
        pair_index[:, 1:] == sequences
    ).astype(f32)
    scaled = BETA * jnp.sum(pair_sign * (seq_sums - ref_logps)[None, :], axis=1)
    loss_value = -jnp.mean(jax.nn.log_sigmoid(scaled))
    pair_grad = jax.nn.sigmoid(-scaled) * (-BETA / scaled.shape[0])
    seq_grad = jnp.sum(pair_sign * pair_grad[:, None], axis=0)
    row_grad = jnp.repeat(seq_grad, COMP)
    grad_logits = (
        row_grad[:, None] * (target_hot.astype(f32) - jnp.exp(logits - row_lse[:, None]))
    ).astype(bf16)
    grad_rows = jnp.dot(grad_logits, table_own, preferred_element_type=f32) / LOGIT_SCALE
    head_grad = (
        jnp.einsum("rv,rd->vd", grad_logits, head_rows, preferred_element_type=f32) / LOGIT_SCALE
    ).astype(bf16)
    head_grad = lax.all_to_all(
        jnp.stack([head_grad[:, p * columns : (p + 1) * columns] for p in range(planes)]),
        "expert",
        split_axis=0,
        concat_axis=0,
        tiled=True,
    ).reshape(vocab_rows, columns)
    own_grad_rows = lax.psum_scatter(
        grad_rows.astype(bf16), BOTH, scatter_dimension=0, tiled=True
    ).astype(f32)
    grad_resid_two, grad_gain_three = norm_back_three(own_grad_rows)

    grad_all = lax.all_gather(grad_resid_two.astype(bf16), BOTH, axis=0, tiled=True)
    grad_down = jnp.einsum("tef,td->efd", gated_hidden, grad_all, preferred_element_type=f32)
    pulled = jnp.einsum("td,efd->tef", grad_all, down_b, preferred_element_type=f32)
    grad_gates_local = jnp.sum(hidden.astype(bf16).astype(f32) * pulled, axis=2)
    grad_hidden = (pulled * local_gates[:, :, None]).astype(bf16)
    grad_gate_up = swiglu_back(grad_hidden.astype(f32))[0].astype(bf16)
    grad_in = jnp.einsum("td,tejf->edjf", expert_rows, grad_gate_up, preferred_element_type=f32)
    grad_copies = jnp.einsum("tejf,edjf->td", grad_gate_up, in_b, preferred_element_type=f32)
    grad_gates_all = lax.dynamic_update_slice_in_dim(
        jnp.zeros((rows_all, 128), f32), grad_gates_local, shard_id * local_experts, 1
    )
    back = lax.psum_scatter(
        jnp.concatenate([grad_copies.astype(bf16), grad_gates_all.astype(bf16)], axis=1),
        BOTH,
        scatter_dimension=0,
        tiled=True,
    ).astype(f32)
    grad_gates = back[:, D : D + EXPERTS]
    grad_router_logits = own_gates * (
        grad_gates - jnp.sum(own_gates * grad_gates, axis=1, keepdims=True)
    )
    grad_normed_two = back[:, :D] + jnp.einsum(
        "se,de->sd", grad_router_logits, router_full.astype(f32)
    )
    grad_router = jnp.einsum("sd,se->de", normed_two_b.astype(f32), grad_router_logits)
    grad_resid, grad_gain_two = norm_back_two(grad_normed_two)
    grad_resid = grad_resid + grad_resid_two
    grad_branch = grad_resid.astype(bf16)
    grad_out = jnp.einsum("sk,sd->kd", attended, grad_branch, preferred_element_type=f32)
    grad_attended = (
        jnp.einsum("sd,kd->sk", grad_branch, out_full, preferred_element_type=f32)
        .astype(bf16)
        .reshape(COMP, KEY_VALUE_HEADS, GROUP, HEAD_WIDTH)
    )

    grad_probs = jnp.einsum("qhgd,khd->hgqk", grad_attended, value, preferred_element_type=f32)
    grad_probs = grad_probs.astype(bf16).astype(f32)
    inner = jnp.sum(grad_probs * probs, axis=-1, keepdims=True)
    grad_scores = (probs * (grad_probs - inner)).astype(bf16)
    grad_value = jnp.einsum("hgqk,qhgd->khd", probs_b, grad_attended, preferred_element_type=f32)
    grad_query = jnp.einsum(
        "hgqk,khd->qhgd", grad_scores, key, preferred_element_type=f32
    ) * HEAD_WIDTH ** (-0.5)
    grad_key = jnp.einsum(
        "hgqk,qhgd->khd", grad_scores, query, preferred_element_type=f32
    ) * HEAD_WIDTH ** (-0.5)
    grad_query_rows = query_back(grad_query.reshape(COMP, QUERY_HEADS, HEAD_WIDTH))[0].astype(bf16)
    grad_pair_rows = jnp.concatenate(
        [key_back(grad_key)[0], grad_value.reshape(SEQUENCE_TOKENS, key_cols)], axis=1
    ).astype(bf16)
    grad_qkv = jnp.concatenate(
        [
            jnp.einsum("sd,sk->dk", normed_rows, grad_query_rows, preferred_element_type=f32),
            jnp.einsum("sd,sk->dk", normed_b, grad_pair_rows, preferred_element_type=f32),
        ],
        axis=1,
    )
    grad_normed = jnp.einsum("sk,dk->sd", grad_pair_rows, pair_weight, preferred_element_type=f32)
    grad_normed_rows = jnp.einsum(
        "sk,dk->sd", grad_query_rows, query_weight, preferred_element_type=f32
    )

    def spread(rows):
        return lax.dynamic_update_slice_in_dim(
            jnp.zeros((SEQUENCE_TOKENS, D), f32), rows, start, 0
        )

    grad_embedded, grad_gain_one = norm_back_one(grad_normed + spread(grad_normed_rows))
    grad_embedded = (grad_embedded + spread(grad_resid)).astype(bf16)
    sent = jnp.stack([grad_embedded[:, p * columns : (p + 1) * columns] for p in range(planes)])
    sent = lax.all_to_all(sent, "expert", split_axis=0, concat_axis=0, tiled=True)
    sent = lax.all_gather(sent, "shard", axis=1, tiled=False).reshape(
        devices, SEQUENCE_TOKENS, columns
    )
    table_grad = scatter_rows(lists, counts, sent, head_grad)

    gains_grad = jnp.stack([grad_gain_one, grad_gain_two, grad_gain_three])
    layer_sums = (
        lax.psum_scatter(grad_qkv.astype(bf16), BOTH, scatter_dimension=0, tiled=True).astype(f32),
        lax.psum_scatter(grad_out.astype(bf16), BOTH, scatter_dimension=0, tiled=True).astype(f32),
        lax.psum_scatter(grad_router, BOTH, scatter_dimension=0, tiled=True),
        lax.psum_scatter(gains_grad, BOTH, scatter_dimension=1, tiled=True),
    )
    weights = (
        embed_table,
        qkv_weight,
        out_weight,
        router_weight,
        norm_gains,
        in_weight,
        down_weight,
    )
    firsts = (embed_first, qkv_first, out_first, router_first, gains_first, in_first, down_first)
    seconds = (
        embed_second,
        qkv_second,
        out_second,
        router_second,
        gains_second,
        in_second,
        down_second,
    )
    gradients = (
        table_grad,
        layer_sums[0],
        layer_sums[1],
        layer_sums[2],
        layer_sums[3],
        grad_in,
        grad_down,
    )
    step_value = step_count.astype(f32)
    moved = [
        lamb_parts(weight, moment_one, moment_two, gradient, step_value)
        for weight, moment_one, moment_two, gradient in zip(weights, firsts, seconds, gradients)
    ]
    partial_norms = jnp.stack(
        [
            jnp.stack([jnp.sum(weight * weight), jnp.sum(parts[2] * parts[2])])
            for weight, parts in zip(weights, moved)
        ]
    )
    norm_values = jnp.sqrt(lax.psum(partial_norms, BOTH))
    trust_ratio = norm_values[:, 0] / norm_values[:, 1]
    results = [loss_value]
    for place, (weight, parts) in enumerate(zip(weights, moved)):
        results.extend([weight - STEP_RATE * trust_ratio[place] * parts[2], parts[0], parts[1]])
    results.append(jnp.stack([norm_values[:, 0], norm_values[:, 1], trust_ratio], axis=1))
    return tuple(results)


def solution(mesh):
    rows = P(BOTH, None)
    vocab = P("shard", "expert")
    gains = P(None, BOTH)
    inner = P("shard", None, None, "expert")
    outer = P("shard", "expert", None)
    state = (vocab,) * 3 + (rows,) * 9 + (gains,) * 3 + (inner,) * 3 + (outer,) * 3
    return jax.shard_map(
        on_device,
        mesh=mesh,
        in_specs=(P("expert"), P("expert", None), P(), P(), rows, P()) + state,
        out_specs=(P(),) + state + (P(),),
        check_vma=False,
    )
```

time: 2880 us -> 1640 us (0.57)
  waiting for transfers between devices: 1660 us -> 917 us
  blocking collectives: 429 us -> 249 us
  local copies, waits for them, and re-layouts: 293 us -> 115 us
  other arithmetic: 261 us -> 141 us
  matrix products: 190 us -> 128 us
  Pallas kernels: 0 us -> 41.4 us
    all_gather x6, waiting for transfers between devices: 684 us -> 152 us  [the longest x1 58.7 us: on_device(): lax.all_gather(grad_resid_two.astype(bf16), BOTH, axis=0, tiled=True)]
    unnamed x19 -> x16, waiting for transfers between devices: 519 us -> 111 us
    reduce_scatter x5 -> x6, waiting for transfers between devices: 376 us -> 620 us  [the longest x1 137 us: on_device(): lax.psum_scatter(jnp.concatenate([grad_copies.astype(bf16), grad_gates_al...]
    all_gather x6, blocking collectives: 285 us -> 189 us  [the longest x1 42.7 us: on_device(): lax.all_gather(norm_gains.astype(bf16), BOTH, axis=1, tiled=True)]
    unnamed x193 -> x238, local copies, waits for them, and re-layouts: 171 us -> 84.3 us
    gather x16 -> x0, local copies, waits for them, and re-layouts: 83.6 us -> none  [the longest x1 22 us: on_device(): table_block[local_rows].astype(f32)]
    all_to_all x1, blocking collectives: 103 us -> 20.5 us  [on_device(): lax.all_to_all(sent, 'expert', split_axis=0, concat_axis=0, tiled=True)]
    dot_general x23, matrix products: 185 us -> 114 us  [the longest x1 17.3 us: on_device(): jnp.einsum('td,tejf->edjf', expert_rows, grad_gate_up, preferred_element_...]
  transfers between devices with their start and end apart: 18 -> 17, of which waited for: 12 -> 13; matrix products, arithmetic and copies ran while one was open for 15% -> 12% of each run, Pallas kernels for 0% -> 0%
where the time goes in v1:
time: 1640 us; the launch traced here: 1630 us
  waiting for transfers between devices  917 us (56%)
  blocking collectives  249 us (15%)
  other arithmetic  141 us (9%)
  matrix products  128 us (8%)
  local copies, waits for them, and re-layouts  115 us (7%)
  Pallas kernels  41.4 us (3%)
  between operations  24.7 us (2%)
    reduce_scatter x1, waiting for transfers between devices, on_device(): lax.psum_scatter(jnp.concatenate([grad_copies.astype(bf16), grad_gates_al...  137 us
    reduce_scatter x1, waiting for transfers between devices, on_device(): lax.psum_scatter(produced.astype(bf16), BOTH, scatter_dimension=0, tiled=...  135 us
    reduce_scatter x1, waiting for transfers between devices, on_device(): lax.psum_scatter(grad_qkv.astype(bf16), BOTH, scatter_dimension=0, tiled=...  125 us
    unnamed x16, waiting for transfers between devices  111 us
    reduce_scatter x1, waiting for transfers between devices, on_device(): lax.psum_scatter(grad_out.astype(bf16), BOTH, scatter_dimension=0, tiled=...  108 us
    reduce_scatter x1, waiting for transfers between devices, on_device(): lax.psum_scatter(grad_rows.astype(bf16), BOTH, scatter_dimension=0, tiled...  97.7 us
    unnamed x238, local copies, waits for them, and re-layouts  84.3 us
    all_gather x1, waiting for transfers between devices, on_device(): lax.all_gather(grad_resid_two.astype(bf16), BOTH, axis=0, tiled=True)  58.7 us
  transfers between devices with their start and end apart: 17, of which 13 were waited for; matrix products, arithmetic and copies ran while one was open for 12% of the time, Pallas kernels for 0%

profile of v1, /device:TPU:0, one launch (start us, length us, event | category | flops | bytes accessed | tf_op | source)
XLA Modules:
  0.0 1632.6 jit_solution(2426244576024037946)
XLA Ops:
  8.1 15.0 all_gather.42
  23.4 4.8 select_reduce_fusion
  28.3 14.3 gather_rows.1
  42.7 3.5 copy.216
  51.4 42.7 %all-gather.2 = bf16[32,48,3]{1,2,0:T(4,128)(2,1)S(1)} all-gather(bf16[1,48,3]{1,2,0:T(4,128)(2,1)S(1)} %get-tuple-element.229), channel_id=1, replica_groups=mesh['expert'=4,'shard'=8] {'expert','shard'}, dimensions={0}, use_global_device_ids=true | all-gather | bytes 9504 | tf_op jit(solution)/shard_map/all_gather | solution.py:218
  94.1 17.5 %reduce-scatter.15.cloned.1.call-done = bf16[4,1,256,384]{3,2,0,1:T(8,128)(2,1)} async-done(((bf16[4,8,256,384]{3,2,0,1:T(8,128)(2,1)}), bf16[4,1,256,384]{3,2,0,1:T(8,128)(2,1)}) %reduce-scatter.15.cloned.1.call-update) | async-done | bytes 786448 | tf_op jit(solution)/shard_map/reduce_scatter | solution.py:210
  111.6 4.6 all-to-all-start
  119.2 32.8 %all-to-all-done = bf16[4,256,384]{2,1,0:T(8,128)(2,1)S(1)} async-done(((bf16[4,256,384]{2,1,0:T(8,128)(2,1)}), bf16[4,256,384]{2,1,0:T(8,128)(2,1)S(1)}, u32[]{:S(2)}, u32[]{:S(2)}) %all-to-all-start) | async-done | bytes 786464 | tf_op jit(solution)/shard_map/all_to_all | solution.py:211
  153.3 3.0 fusion.23
  156.4 3.2 fusion.12
  166.6 53.3 %all-gather.15.cloned.1.call-done = bf16[1536,1536]{1,0:T(8,128)(2,1)} async-done(((bf16[48,1536]{1,0:T(8,128)(2,1)}), bf16[1536,1536]{1,0:T(8,128)(2,1)}) %all-gather.15.cloned.1.call-update) | async-done | bytes 4718608 | tf_op jit(solution)/shard_map/all_gather | solution.py:216
  219.9 3.4 multiply_reduce_fusion.18
  224.2 39.1 %all-gather.3 = s32[32,32,8]{1,2,0:T(8,128)S(1)} all-gather(s32[1,32,8]{1,2,0:T(8,128)S(1)} %dynamic-slice_bitcast_fusion), channel_id=1, replica_groups=mesh['expert'=4,'shard'=8] {'expert','shard'}, dimensions={0}, use_global_device_ids=true | all-gather | bytes 33792 | tf_op jit(solution)/shard_map/all_gather | solution.py:195
  265.2 37.7 %all-gather.4 = bf16[32,48,32]{1,2,0:T(8,128)(2,1)S(1)} all-gather(bf16[1,48,32]{1,2,0:T(8,128)(2,1)S(1)} %get-tuple-element.227), channel_id=1, replica_groups=mesh['expert'=4,'shard'=8] {'expert','shard'}, dimensions={0}, use_global_device_ids=true | all-gather | bytes 101376 | tf_op jit(solution)/shard_map/all_gather | solution.py:217
  304.0 9.8 multiply_reduce_fusion.3
  313.8 5.5 copy.223
  319.3 3.6 select_reduce_fusion.2
  331.6 5.3 fusion.118
  340.7 3.5 bitcast_convert_fusion.1
  344.2 11.8 multiply_reduce_fusion.1
  356.0 5.1 all-to-all-start.1
  361.2 135.2 %reduce-scatter.17.cloned.1.call-done = bf16[32,1536]{1,0:T(8,128)(2,1)} async-done(((bf16[1024,1536]{1,0:T(8,128)(2,1)}), bf16[32,1536]{1,0:T(8,128)(2,1)}) %reduce-scatter.17.cloned.1.call-update) | async-done | bytes 98320 | tf_op jit(solution)/shard_map/reduce_scatter | solution.py:299
  499.1 13.5 all_gather.50
  514.1 4.2 slice_bitcast_fusion.9
  518.3 40.2 %all-gather.19.cloned.1.call-done = bf16[1024,1536]{1,0:T(8,128)(2,1)} async-done(((bf16[32,1536]{1,0:T(8,128)(2,1)}), bf16[1024,1536]{1,0:T(8,128)(2,1)}) %all-gather.19.cloned.1.call-update) | async-done | bytes 3145744 | tf_op jit(solution)/shard_map/all_gather | solution.py:303
  558.5 8.0 multiply_reduce_fusion.4
  566.5 3.1 exponential_reduce_fusion
  569.6 40.5 %all-gather.5 = f32[32,3,1024]{2,1,0:T(4,128)S(1)} all-gather(f32[1,3,1024]{2,1,0:T(4,128)S(1)} %maximum_bitcast_fusion.5), channel_id=2, replica_groups=mesh['expert'=4,'shard'=8] {'expert','shard'}, dimensions={0}, use_global_device_ids=true | all-gather | bytes 405504 | tf_op jit(solution)/shard_map/all_gather | solution.py:310
  613.9 10.4 multiply_convert_fusion
  624.4 97.7 %reduce-scatter.19.cloned.1.call-done = bf16[32,1536]{1,0:T(8,128)(2,1)} async-done(((bf16[1024,1536]{1,0:T(8,128)(2,1)}), bf16[32,1536]{1,0:T(8,128)(2,1)}) %reduce-scatter.19.cloned.1.call-update) | async-done | bytes 98320 | tf_op jit(solution)/shard_map/reduce_scatter | solution.py:339
  725.4 58.7 %all-gather.21.cloned.1.call-done = bf16[1024,1536]{1,0:T(8,128)(2,1)} async-done(((bf16[32,1536]{1,0:T(8,128)(2,1)}), bf16[1024,1536]{1,0:T(8,128)(2,1)}) %all-gather.21.cloned.1.call-update) | async-done | bytes 3145744 | tf_op jit(solution)/shard_map/all_gather | solution.py:344
  784.1 8.9 fusion.30
  793.9 7.2 bitcast_convert_fusion
  803.6 3.9 pad_maximum_fusion.3
  808.8 136.9 %reduce-scatter.21.cloned.1.call-done = bf16[32,1664]{1,0:T(8,128)(2,1)} async-done(((bf16[1024,1664]{1,0:T(8,128)(2,1)}), bf16[32,1664]{1,0:T(8,128)(2,1)}) %reduce-scatter.21.cloned.1.call-update) | async-done | bytes 106512 | tf_op jit(solution)/shard_map/reduce_scatter | solution.py:355
  948.9 3.9 convolution_convert_fusion.3
  953.1 3.2 fusion.45
  959.6 3.0 fusion.21
  962.7 3.9 fusion.25
  972.1 3.6 convolution_convert_fusion
  978.1 4.5 convolution_convert_fusion.1
  982.7 6.1 pad_maximum_fusion
  988.8 10.7 copy.265
  1003.7 20.5 %all_to_all.20 = bf16[4,256,384]{2,1,0:T(8,128)(2,1)} all-to-all(bf16[4,256,384]{2,1,0:T(8,128)(2,1)S(1)} %pad_maximum_fusion.7), channel_id=1, replica_groups=mesh['expert'=4,'shard'=8] {'expert'}, dimensions={0} | all-to-all | bytes 1572864 | tf_op jit(solution)/shard_map/all_to_all | solution.py:414
  1024.3 8.8 fusion.3
  1036.1 5.4 all-to-all-start.3
  1041.5 10.2 copy.244
  1052.4 10.1 copy.241
  1062.5 10.4 copy.243
  1073.6 17.3 %multiply_reduce_fusion.2 = (f32[]{:T(128)}, f32[4,1536,2,128]{1,3,2,0:T(8,128)}, f32[4,1536,2,128]{1,3,2,0:T(8,128)}, f32[4,1536,2,128]{1,3,2,0:T(8,128)}) fusion(f32[4,1536,2,128]{1,3,2,0:T(8,128)} %copy.244, f32[]{:T(128)S(6)} %sub.153, f32[]{:T(128)S(6)} %sub.152, f32[4,1536,2,128]{1,3,2,0:T(8,128)} %copy.243, f32[4,1536,2,128]{1,3,2,0:T(8,128)} %copy.241, ...), kind=kOutput, calls=%fused_computation.29 | convolution fusion | flops 3246915584 | bytes 45088780 | tf_op jit(solution)/shard_map/td,tejf->edjf/dot_general | solution.py:350
  1092.3 13.0 multiply_reduce_fusion.5
  1106.9 10.3 copy.255
  1117.2 8.6 reduce-scatter.29.cloned.1.call-done
  1129.2 102.7 %reduce-scatter.27.cloned.1.call-done = f32[48,32]{1,0:T(8,128)} async-done(((f32[1536,32]{1,0:T(8,128)}), f32[48,32]{1,0:T(8,128)}) %reduce-scatter.27.cloned.1.call-update) | async-done | bytes 6160
  1235.5 108.3 %reduce-scatter.23.cloned.1.call-done = bf16[48,1536]{1,0:T(8,128)(2,1)} async-done(((bf16[1536,1536]{1,0:T(8,128)(2,1)}), bf16[48,1536]{1,0:T(8,128)(2,1)}) %reduce-scatter.23.cloned.1.call-update) | async-done | bytes 147472 | tf_op jit(solution)/shard_map/reduce_scatter | solution.py:423
  1347.8 124.9 %reduce-scatter.25.cloned.1.call-done = bf16[48,2560]{1,0:T(8,128)(2,1)} async-done(((bf16[1536,2560]{1,0:T(8,128)(2,1)}), bf16[48,2560]{1,0:T(8,128)(2,1)}) %reduce-scatter.25.cloned.1.call-update) | async-done | bytes 245776 | tf_op jit(solution)/shard_map/reduce_scatter | solution.py:422
  1476.9 27.1 %scatter_rows.1 = f32[6144,384]{1,0:T(8,128)} custom-call(s32[32,256]{1,0:T(8,128)S(1)} %copy-done.3, s32[32]{0:T(128)S(1)} %copy-done.5, bf16[32,256,384]{2,1,0:T(8,128)(2,1)} %bitcast.266, bf16[6144,384]{1,0:T(8,128)(2,1)} %bitcast.71.head_ref), custom_call_target="tpu_custom_call" | custom-call | tf_op jit(solution)/shard_map/scatter_rows/pallas_call | solution.py:128
  1504.0 24.5 %multiply_reduce_fusion = (f32[]{:T(128)}, f32[6144,384]{1,0:T(8,128)}, f32[6144,384]{1,0:T(8,128)}, f32[6144,384]{1,0:T(8,128)}) fusion(f32[6144,384]{1,0:T(8,128)} %table_ref.1, f32[]{:T(128)S(6)} %sub.153, f32[]{:T(128)S(6)} %sub.152, f32[6144,384]{1,0:T(8,128)} %scatter_rows.1, f32[6144,384]{1,0:T(8,128)} %param.35, f32[6144,384]{1,0:T(8,128)} %param.34), kind=kLoop, calls=%fused_computation.6 | loop fusion | flops 35389440 | bytes 66060300 | tf_op jit(solution)/shard_map/reduce_sum | solution.py:462
  1530.1 10.1 copy.254
  1540.2 40.1 %psum.7 = f32[7,2]{0,1:T(2,128)S(1)} all-reduce(f32[7,2]{0,1:T(2,128)S(1)} %stack.183), channel_id=1, replica_groups=mesh['expert'=4,'shard'=8] {'expert','shard'}, use_global_device_ids=true, to_apply=%region_52.53 | all-reduce | flops 14 | bytes 112 | tf_op jit(solution)/shard_map/psum | solution.py:466
  1586.1 8.7 multiply_subtract_fusion.1
  1594.7 10.1 copy.253
  1604.9 5.1 multiply_subtract_fusion.2
  1612.8 11.1 multiply_subtract_fusion
  (398 shorter events, 94.1 us)
Async XLA Ops:
  8.0 216.1 %copy-start = (s32[256,8]{0,1:T(8,128)S(1)}, s32[256,8]{0,1:T(8,128)}, u32[]{:S(2)}) copy-start(s32[256,8]{0,1:T(8,128)} %param.31) | copy-start | bytes 24580
  8.0 103.5 %reduce-scatter.15.cloned.1.call-start = ((), (), s32[]{:S(2)}) async-start(), calls=%async_computation.12 | async-start | bytes 7077888 | tf_op jit(solution)/shard_map/reduce_scatter | solution.py:210
  23.1 19.5 %copy-start.52 = (s32[32,256]{1,0:T(8,128)}, s32[32,256]{1,0:T(8,128)S(1)}, u32[]{:S(2)}) copy-start(s32[32,256]{1,0:T(8,128)S(1)} %reshape.386) | copy-start | bytes 98308
  23.3 19.4 %copy-start.4 = (s32[32]{0:T(128)}, s32[32]{0:T(128)S(1)}, u32[]{:S(2)}) copy-start(s32[32]{0:T(128)S(1)} %get-tuple-element.183.count_ref) | copy-start | bytes 388
  46.2 107.1 %all-gather.13.cloned.1.call-start = ((), (), s32[]{:S(2)}) async-start(), calls=%async_computation.13 | async-start | bytes 8110080 | tf_op jit(solution)/shard_map/all_gather | solution.py:215
  48.6 171.4 %all-gather.15.cloned.1.call-start = ((), (), s32[]{:S(2)}) async-start(), calls=%async_computation.14 | async-start | bytes 4866048 | tf_op jit(solution)/shard_map/all_gather | solution.py:216
  111.6 40.4 %all-to-all-start = ((bf16[4,256,384]{2,1,0:T(8,128)(2,1)}), bf16[4,256,384]{2,1,0:T(8,128)(2,1)S(1)}, u32[]{:S(2)}, u32[]{:S(2)}) async-start(bf16[4,256,384]{2,1,0:T(8,128)(2,1)} %bitcast.283), calls=%async_computation.1 | async-start | bytes 1572864 | tf_op jit(solution)/shard_map/all_to_all | solution.py:211
  116.2 203.1 %all-gather.17.cloned.1.call-start = ((), (), s32[]{:S(2)}) async-start(), calls=%async_computation.15 | async-start | bytes 3244032 | tf_op jit(solution)/shard_map/all_gather | solution.py:275
  117.0 36.2 %copy-start.66 = (f32[1536]{0:T(1024)}, f32[1536]{0:T(1024)S(1)}, u32[]{:S(2)}) copy-start(f32[1536]{0:T(1024)S(1)} %get-tuple-element.150) | copy-start | bytes 18436
  166.2 57.2 %copy-start.68 = (f32[1536]{0:T(1024)S(1)}, f32[1536]{0:T(1024)}, u32[]{:S(2)}) copy-start(f32[1536]{0:T(1024)} %get-tuple-element.148) | copy-start | bytes 18436
  166.6 97.9 %copy-start.37 = (bf16[32,1536]{1,0:T(8,128)(2,1)}, bf16[32,1536]{1,0:T(8,128)(2,1)S(1)}, u32[]{:S(2)}) copy-start(bf16[32,1536]{1,0:T(8,128)(2,1)S(1)} %convert_element_type.209) | copy-start | bytes 294916
  166.6 97.9 %copy-start.64 = (f32[48,32]{0,1:T(8,128)S(1)}, f32[48,32]{0,1:T(8,128)}, u32[]{:S(2)}) copy-start(f32[48,32]{0,1:T(8,128)} %param.42) | copy-start | bytes 18436
  223.3 40.1 %copy-start.107 = (f32[32]{0:T(128)}, f32[32]{0:T(128)S(1)}, u32[]{:S(2)}) copy-start(f32[32]{0:T(128)S(1)} %get-tuple-element.247) | copy-start | bytes 388
  224.1 272.3 %reduce-scatter.17.cloned.1.call-start = ((), (), s32[]{:S(2)}) async-start(), calls=%async_computation.16 | async-start | bytes 3244032 | tf_op jit(solution)/shard_map/reduce_scatter | solution.py:299
  263.7 39.3 %copy-start.50 = (pred[1024,32]{0,1:T(8,128)(4,1)}, pred[1024,32]{0,1:T(8,128)(4,1)S(1)}, u32[]{:S(2)}) copy-start(pred[1024,32]{0,1:T(8,128)(4,1)S(1)} %fusion.47) | copy-start | bytes 98308
  356.0 143.2 %copy-start.92 = (s32[8,32]{1,0:T(8,128)S(1)}, s32[8,32]{1,0:T(8,128)}, u32[]{:S(2)}) copy-start(s32[8,32]{1,0:T(8,128)} %param.28) | copy-start | bytes 3076
  356.0 156.7 %copy-start.53 = (s32[32,256]{1,0:T(8,128)S(1)}, s32[32,256]{1,0:T(8,128)}, u32[]{:S(2)}) copy-start(s32[32,256]{1,0:T(8,128)} %copy-done.52) | copy-start | bytes 98308
  356.0 157.6 %copy-start.106 = (s32[16,2]{0,1:T(2,128)S(1)}, s32[16,2]{0,1:T(2,128)}, u32[]{:S(2)}) copy-start(s32[16,2]{0,1:T(2,128)} %param.29) | copy-start | bytes 388
  356.0 158.1 %all-to-all-start.1 = ((bf16[4,1536,384]{2,1,0:T(8,128)(2,1)}), bf16[4,1536,384]{2,1,0:T(8,128)(2,1)}, u32[]{:S(2)}, u32[]{:S(2)}) async-start(bf16[4,1536,384]{2,1,0:T(8,128)(2,1)} %bitcast.265), calls=%async_computation.3 | async-start | bytes 9437184 | tf_op jit(solution)/shard_map/all_to_all | solution.py:221
  361.1 197.4 %all-gather.19.cloned.1.call-start = ((), (), s32[]{:S(2)}) async-start(), calls=%async_computation.17 | async-start | bytes 3244032 | tf_op jit(solution)/shard_map/all_gather | solution.py:303
  499.1 223.0 %reduce-scatter.19.cloned.1.call-start = ((), (), s32[]{:S(2)}) async-start(), calls=%async_computation.18 | async-start | bytes 3244032 | tf_op jit(solution)/shard_map/reduce_scatter | solution.py:339
  513.6 52.9 %copy-start.78 = (s32[1024]{0:T(1024)}, s32[1024]{0:T(1024)S(1)}, u32[]{:S(2)}) copy-start(s32[1024]{0:T(1024)S(1)} %eq.101) | copy-start | bytes 12292
  513.6 52.9 %copy-start.70 = (s32[1536]{0:T(1024)}, s32[1536]{0:T(1024)S(1)}, u32[]{:S(2)}) copy-start(s32[1536]{0:T(1024)S(1)} %iota_add_fusion) | copy-start | bytes 18436
  624.3 97.8 %copy-start.27 = (bf16[32,1536]{1,0:T(8,128)(2,1)S(1)}, bf16[32,1536]{1,0:T(8,128)(2,1)}, u32[]{:S(2)}) copy-start(bf16[32,1536]{1,0:T(8,128)(2,1)} %reduce-scatter.17.cloned.1.call-done) | copy-start | bytes 294916
  624.3 97.8 %copy-start.90 = (f32[32]{0:T(128)S(1)}, f32[32]{0:T(128)}, u32[]{:S(2)}) copy-start(f32[32]{0:T(128)} %copy-done.89) | copy-start | bytes 388
  624.3 99.4 %copy-start.110 = (f32[32]{0:T(128)S(1)}, f32[32]{0:T(128)}, u32[]{:S(2)}) copy-start(f32[32]{0:T(128)} %copy-done.109) | copy-start | bytes 388
  624.4 159.8 %all-gather.21.cloned.1.call-start = ((), (), s32[]{:S(2)}) async-start(), calls=%async_computation.19 | async-start | bytes 3244032 | tf_op jit(solution)/shard_map/all_gather | solution.py:344
  725.4 220.3 %reduce-scatter.21.cloned.1.call-start = ((), (), s32[]{:S(2)}) async-start(), calls=%async_computation.20 | async-start | bytes 3514368 | tf_op jit(solution)/shard_map/reduce_scatter | solution.py:355
  725.4 68.5 %copy-start.23 = (bf16[4,1536,2,128]{1,3,2,0:T(8,128)(2,1)S(1)}, bf16[4,1536,2,128]{1,3,2,0:T(8,128)(2,1)}, u32[]{:S(2)}) copy-start(bf16[4,1536,2,128]{1,3,2,0:T(8,128)(2,1)} %copy.223) | copy-start | bytes 9437188
  807.5 140.0 %copy-start.36 = (bf16[1536,32]{0,1:T(8,128)(2,1)S(1)}, bf16[1536,32]{0,1:T(8,128)(2,1)}, u32[]{:S(2)}) copy-start(bf16[1536,32]{0,1:T(8,128)(2,1)} %reshape.408) | copy-start | bytes 294916
  807.5 140.0 %copy-start.69 = (f32[1536]{0:T(1024)S(1)}, f32[1536]{0:T(1024)}, u32[]{:S(2)}) copy-start(f32[1536]{0:T(1024)} %get-tuple-element.148) | copy-start | bytes 18436
  807.5 140.0 %copy-start.94 = (f32[32]{0:T(128)S(1)}, f32[32]{0:T(128)}, u32[]{:S(2)}) copy-start(f32[32]{0:T(128)} %copy-done.93) | copy-start | bytes 388
  807.5 141.2 %copy-start.108 = (f32[32]{0:T(128)S(1)}, f32[32]{0:T(128)}, u32[]{:S(2)}) copy-start(f32[32]{0:T(128)} %copy-done.107) | copy-start | bytes 388
  807.5 141.2 %copy-start.28 = (bf16[32,1536]{1,0:T(8,128)(2,1)S(1)}, bf16[32,1536]{1,0:T(8,128)(2,1)}, u32[]{:S(2)}) copy-start(bf16[32,1536]{1,0:T(8,128)(2,1)} %reduce-scatter.17.cloned.1.call-done) | copy-start | bytes 294916
  807.5 141.2 %copy-start.34 = (bf16[32,1536]{1,0:T(8,128)(2,1)S(1)}, bf16[32,1536]{1,0:T(8,128)(2,1)}, u32[]{:S(2)}) copy-start(bf16[32,1536]{1,0:T(8,128)(2,1)} %reduce-scatter.19.cloned.1.call-done) | copy-start | bytes 294916
  807.5 141.2 %copy-start.91 = (f32[32]{0:T(128)S(1)}, f32[32]{0:T(128)}, u32[]{:S(2)}) copy-start(f32[32]{0:T(128)} %copy-done.89) | copy-start | bytes 388
  807.5 141.2 %copy-start.105 = (f32[32]{0:T(128)S(1)}, f32[32]{0:T(128)}, u32[]{:S(2)}) copy-start(f32[32]{0:T(128)} %copy-done.104) | copy-start | bytes 388
  807.6 318.2 %reduce-scatter.29.cloned.1.call-start = ((), (), s32[]{:S(2)}) async-start(), calls=%async_computation.25 | async-start | bytes 811008
  948.9 23.2 %copy-start.21 = (f32[32,1536]{1,0:T(8,128)}, f32[32,1536]{1,0:T(8,128)S(1)}, u32[]{:S(2)}) copy-start(f32[32,1536]{1,0:T(8,128)S(1)} %fusion.63) | copy-start | bytes 589828
  970.0 262.0 %reduce-scatter.27.cloned.1.call-start = ((), (), s32[]{:S(2)}) async-start(), calls=%async_computation.24 | async-start | bytes 811008
  972.0 371.8 %reduce-scatter.23.cloned.1.call-start = ((), (), s32[]{:S(2)}) async-start(), calls=%async_computation.21 | async-start | bytes 4866048 | tf_op jit(solution)/shard_map/reduce_scatter | solution.py:423
  975.7 496.9 %reduce-scatter.25.cloned.1.call-start = ((), (), s32[]{:S(2)}) async-start(), calls=%async_computation.23 | async-start | bytes 8110080 | tf_op jit(solution)/shard_map/reduce_scatter | solution.py:422
  999.5 477.4 %all-gather.23.cloned.1.call-start = ((), (), s32[]{:S(2)}) async-start(), calls=%async_computation.22 | async-start | bytes 7077888 | tf_op jit(solution)/shard_map/all_gather | solution.py:415
  1003.4 20.8 %copy-start.71 = (s32[1536]{0:T(1024)S(1)}, s32[1536]{0:T(1024)}, u32[]{:S(2)}) copy-start(s32[1536]{0:T(1024)} %copy-done.70) | copy-start | bytes 18436
  1003.4 20.8 %copy-start.79 = (s32[1024]{0:T(1024)S(1)}, s32[1024]{0:T(1024)}, u32[]{:S(2)}) copy-start(s32[1024]{0:T(1024)} %copy-done.78) | copy-start | bytes 12292
  1003.5 20.8 %copy-start.99 = (f32[1024]{0:T(1024)S(1)}, f32[1024]{0:T(1024)}, u32[]{:S(2)}) copy-start(f32[1024]{0:T(1024)} %copy-done.98) | copy-start | bytes 12292
  1003.5 20.8 %copy-start.101 = (f32[1024]{0:T(1024)S(1)}, f32[1024]{0:T(1024)}, u32[]{:S(2)}) copy-start(f32[1024]{0:T(1024)} %copy-done.100) | copy-start | bytes 12292
  1003.5 20.8 %copy-start.111 = (bf16[1024,1536]{1,0:T(8,128)(2,1)S(1)}, bf16[1024,1536]{1,0:T(8,128)(2,1)}, u32[]{:S(2)}) copy-start(bf16[1024,1536]{1,0:T(8,128)(2,1)} %all-gather.19.cloned.1.call-done) | copy-start | bytes 9437188
  1036.1 440.8 %all-to-all-start.3 = ((bf16[4,1536,384]{2,1,0:T(8,128)(2,1)}), bf16[4,1536,384]{2,1,0:T(8,128)(2,1)}, u32[]{:S(2)}, u32[]{:S(2)}) async-start(bf16[4,1536,384]{2,1,0:T(8,128)(2,1)} %pad_maximum_fusion.2), calls=%async_computation.7 | async-start | bytes 9437184 | tf_op jit(solution)/shard_map/all_to_all | solution.py:332
  1073.6 18.8 %copy-start.83 = (f32[1024,4]{0,1:T(4,128)S(1)}, f32[1024,4]{0,1:T(4,128)}, u32[]{:S(2)}) copy-start(f32[1024,4]{0,1:T(4,128)} %copy.230) | copy-start | bytes 49156
  1106.8 19.8 %copy-start.75 = (f32[3,48]{1,0:T(4,128)S(1)}, f32[3,48]{1,0:T(4,128)}, u32[]{:S(2)}) copy-start(f32[3,48]{1,0:T(4,128)} %param.45) | copy-start | bytes 1732
  1106.8 19.8 %copy-start.102 = (f32[3,48]{1,0:T(4,128)S(1)}, f32[3,48]{1,0:T(4,128)}, u32[]{:S(2)}) copy-start(f32[3,48]{1,0:T(4,128)} %param.47) | copy-start | bytes 1732
  1106.8 19.8 %copy-start.103 = (f32[3,48]{1,0:T(4,128)S(1)}, f32[3,48]{1,0:T(4,128)}, u32[]{:S(2)}) copy-start(f32[3,48]{1,0:T(4,128)} %param.46) | copy-start | bytes 1732
  1106.8 126.0 %copy-start.65 = (f32[48,32]{0,1:T(8,128)S(1)}, f32[48,32]{0,1:T(8,128)}, u32[]{:S(2)}) copy-start(f32[48,32]{0,1:T(8,128)} %param.42) | copy-start | bytes 18436
  1106.8 126.0 %copy-start.80 = (f32[48,32]{0,1:T(8,128)S(1)}, f32[48,32]{0,1:T(8,128)}, u32[]{:S(2)}) copy-start(f32[48,32]{0,1:T(8,128)} %param.44) | copy-start | bytes 18436
  1106.8 126.0 %copy-start.81 = (f32[48,32]{0,1:T(8,128)S(1)}, f32[48,32]{0,1:T(8,128)}, u32[]{:S(2)}) copy-start(f32[48,32]{0,1:T(8,128)} %param.43) | copy-start | bytes 18436
  1106.8 237.0 %copy-start.26 = (f32[48,1536]{1,0:T(8,128)S(1)}, f32[48,1536]{1,0:T(8,128)}, u32[]{:S(2)}) copy-start(f32[48,1536]{1,0:T(8,128)} %param.39) | copy-start | bytes 884740
  1106.8 237.0 %copy-start.54 = (f32[48,1536]{1,0:T(8,128)S(1)}, f32[48,1536]{1,0:T(8,128)}, u32[]{:S(2)}) copy-start(f32[48,1536]{1,0:T(8,128)} %param.41) | copy-start | bytes 884740
  1106.8 237.0 %copy-start.55 = (f32[48,1536]{1,0:T(8,128)S(1)}, f32[48,1536]{1,0:T(8,128)}, u32[]{:S(2)}) copy-start(f32[48,1536]{1,0:T(8,128)} %param.40) | copy-start | bytes 884740
  1106.8 365.8 %copy-start.18 = (f32[48,2560]{1,0:T(8,128)S(1)}, f32[48,2560]{1,0:T(8,128)}, u32[]{:S(2)}) copy-start(f32[48,2560]{1,0:T(8,128)} %param.36) | copy-start | bytes 1474564
  1106.8 365.8 %copy-start.48 = (f32[48,2560]{1,0:T(8,128)S(1)}, f32[48,2560]{1,0:T(8,128)}, u32[]{:S(2)}) copy-start(f32[48,2560]{1,0:T(8,128)} %param.38) | copy-start | bytes 1474564
  1106.9 365.8 %copy-start.49 = (f32[48,2560]{1,0:T(8,128)S(1)}, f32[48,2560]{1,0:T(8,128)}, u32[]{:S(2)}) copy-start(f32[48,2560]{1,0:T(8,128)} %param.37) | copy-start | bytes 1474564
  1117.2 359.7 %copy-start.3 = (s32[32,256]{1,0:T(8,128)S(1)}, s32[32,256]{1,0:T(8,128)}, u32[]{:S(2)}) copy-start(s32[32,256]{1,0:T(8,128)} %copy-done.2) | copy-start | bytes 98308
  1117.2 359.7 %copy-start.5 = (s32[32]{0:T(128)S(1)}, s32[32]{0:T(128)}, u32[]{:S(2)}) copy-start(s32[32]{0:T(128)} %copy-done.4) | copy-start | bytes 388
  (65 other events, 250.1 us)
Sparse Core Ops, SparseCore 0:
  46.3 65.2 reduce-scatter.14
  1024.3 47.2 all-gather.22
Sparse Core Ops, SparseCore 1:
  50.2 103.1 all-gather.12
  156.7 63.2 all-gather.14
  224.2 57.8 all-gather.16
  344.3 152.0 reduce-scatter.16
  500.2 58.2 all-gather.18
  624.5 97.6 reduce-scatter.18
  725.8 58.3 all-gather.20
  807.6 138.0 reduce-scatter.20
  970.1 155.6 reduce-scatter.28
  1130.8 101.0 reduce-scatter.26
  1237.9 105.9 reduce-scatter.22
  1351.0 121.6 reduce-scatter.24

commit v2 on v1

v2 whole, which is shorter than its diff:
```python
import functools
import math

import jax
import jax.numpy as jnp
from jax import lax
from jax.experimental import pallas as pl
from jax.experimental.pallas import tpu as pltpu
from jax.sharding import PartitionSpec as P

D = 1536
QUERY_HEADS = 24
KEY_VALUE_HEADS = 8
GROUP = QUERY_HEADS // KEY_VALUE_HEADS
HEAD_WIDTH = 64
TOP = 8
EXPERTS = 32
SEQUENCE_TOKENS = 256
COMP = 32
QKV = 2560

BETA = 0.1
LOGIT_SCALE = 6.0
RATE_ONE = 0.9
RATE_TWO = 0.999
EPSILON = 1e-06
DECAY = 0.01
STEP_RATE = 0.3

BOTH = ("expert", "shard")
bf16 = jnp.bfloat16
f32 = jnp.float32


MESH = pl.DeviceIdType.MESH


class Spot:
    def __init__(self, planes, side):
        self.planes, self.side = planes, side
        self.z = lax.axis_index("expert")
        self.shard = lax.axis_index("shard")
        self.core = lax.rem(self.shard, 2)
        self.b = lax.rem(lax.div(self.shard, 2), side)
        self.a = lax.div(self.shard, 2 * side)

    def plane(self, k):
        z = lax.rem(self.z + k, self.planes)
        return z, (z, self.shard)

    def along_a(self, k):
        a = lax.rem(self.a + k, self.side)
        return a, (self.z, (a * self.side + self.b) * 2 + self.core)

    def along_b(self, k):
        b = lax.rem(self.b + k, self.side)
        return b, (self.z, (self.a * self.side + b) * 2 + self.core)

    def along(self, first, k):
        return self.along_a(k) if first else self.along_b(k)

    def mate(self):
        other = 1 - self.core
        return other, (self.z, (self.a * self.side + self.b) * 2 + other)

    def near(self, k):
        return self.z, lax.rem(self.shard + k, 2 * self.side * self.side)

    def greet(self, flat):
        targets = [self.plane(k)[1] for k in range(1, self.planes)]
        if flat:
            targets += [self.near(k) for k in range(1, 2 * self.side * self.side)]
        else:
            targets.append(self.mate()[1])
            for k in range(1, self.side):
                targets += [self.along_a(k)[1], self.along_b(k)[1]]
        barrier = pltpu.get_barrier_semaphore()
        for target in targets:
            pl.semaphore_signal(barrier, inc=1, device_id=target, device_id_type=MESH)
        pl.semaphore_wait(barrier, len(targets))


class Mail:
    def __init__(self, send, recv):
        self.send, self.recv, self.count, self.open = send, recv, 0, []

    def start(self, src, dst, target):
        copy = pltpu.make_async_remote_copy(
            src_ref=src,
            dst_ref=dst,
            send_sem=self.send.at[self.count],
            recv_sem=self.recv.at[self.count],
            device_id=target,
            device_id_type=MESH,
        )
        self.count += 1
        copy.start()
        self.open.append(copy)
        return copy

    def finish(self):
        for copy in self.open:
            copy.wait_send()


def arrive(copies):
    for copy in copies:
        copy.wait_recv()


class Tiny:
    flat = True
    scratch = ()

    def __init__(self, x, planes, side):
        self.planes, self.side, self.inputs = planes, side, [x]
        shape = (planes, 2 * side * side) + x.shape
        self.outputs = [jax.ShapeDtypeStruct(shape, x.dtype)]
        self.copies = planes + 2 * side * side - 2

    def steps(self, spot, mail, x, out):
        out[spot.z, spot.shard] = x[...]
        sent = []
        for k in range(1, self.planes):
            sent.append(mail.start(x, out.at[spot.z, spot.shard], spot.plane(k)[1]))
        yield
        arrive(sent)
        part = out.at[:, spot.shard]
        yield
        arrive([mail.start(part, part, spot.near(k)) for k in range(1, 2 * self.side**2)])


def split(array, rows, columns, row_parts, column_parts):
    r, c = rows // row_parts, columns // column_parts
    cuts = [
        (array, slice(i * r, i * r + r), slice(j * c, j * c + c))
        for j in range(column_parts)
        for i in range(row_parts)
    ]
    cuts = [cut + (n % 2 == 0,) for n, cut in enumerate(cuts)]
    return [cuts[n : n + 2] for n in range(0, len(cuts), 2)]


def pipeline(groups, stage, last):
    sent = [[[] for _ in group] for group in groups]
    for tick in range(len(groups) + last):
        for step in range(last, -1, -1):
            turn = tick - step
            if 0 <= turn < len(groups):
                for n, cut in enumerate(groups[turn]):
                    for copy in sent[turn][n]:
                        copy.wait_recv()
                    sent[turn][n] = stage(step, (turn, n), cut)
        yield


class Gather:
    flat = False
    scratch = ()

    def __init__(self, xs, groups, planes, side, exchange=False):
        self.planes, self.side, self.inputs, self.groups = planes, side, xs, groups
        self.exchange = exchange
        grid = (planes, side, side, 2)
        self.outputs = [jax.ShapeDtypeStruct(grid + x.shape[-2:], x.dtype) for x in xs]
        self.copies = sum(map(len, groups)) * (planes - 1 + 2 * (side - 1) + 1)

    def steps(self, spot, mail, *refs):
        xs, outs = refs[: len(self.inputs)], refs[len(self.inputs) :]
        z, a, b, core = spot.z, spot.a, spot.b, spot.core
        for x, out in zip(xs, outs):
            out[z, a, b, core] = x[z] if self.exchange else x[...]

        def stage(step, key, cut):
            i, rows, columns, first = cut
            x, out = xs[i], outs[i]
            if step == 0:
                place = out.at[z, a, b, core, rows, columns]
                sent = []
                for k in range(1, self.planes):
                    peer, target = spot.plane(k)
                    own = x.at[peer, rows, columns] if self.exchange else x.at[rows, columns]
                    sent.append(mail.start(own, place, target))
                return sent
            if step in (1, 2):
                if step == 1:
                    part = out.at[:, a, b, core, rows, columns]
                elif first:
                    part = out.at[:, :, b, core, rows, columns]
                else:
                    part = out.at[:, a, :, core, rows, columns]
                return [
                    mail.start(part, part, spot.along(first == (step == 1), k)[1])
                    for k in range(1, self.side)
                ]
            if step == 3:
                part = out.at[:, :, :, core, rows, columns]
                return [mail.start(part, part, spot.mate()[1])]
            return []

        return pipeline(self.groups, stage, 4)


class Reduce:
    flat = False

    def __init__(self, xs, groups, planes, side, exchange=False):
        self.planes, self.side, self.inputs, self.groups = planes, side, xs, groups
        self.exchange = exchange
        self.outputs = [
            jax.ShapeDtypeStruct((planes,) + x.shape[-2:], x.dtype)
            if exchange
            else jax.ShapeDtypeStruct(x.shape[-2:], f32)
            for x in xs
        ]
        self.scratch = []
        for i, rows, columns, _ in [cut for group in groups for cut in group]:
            block = (rows.stop - rows.start, columns.stop - columns.start)
            self.scratch += [
                pltpu.VMEM(shape + block, xs[i].dtype)
                for shape in (
                    (planes, side, side),
                    (side - 1, planes, side),
                    (planes, side),
                    (side - 1, planes),
                    (planes,),
                )
                + (() if exchange else ((planes - 1,),))
            ]
        self.copies = sum(map(len, groups)) * (planes - 1 + 2 * (side - 1) + 1)

    def steps(self, spot, mail, *refs):
        planes, side, number = self.planes, self.side, len(self.inputs)
        xs, outs, rest = refs[:number], refs[number : 2 * number], refs[2 * number :]
        each = 5 if self.exchange else 6
        order = [(t, n) for t, group in enumerate(self.groups) for n in range(len(group))]
        held = {key: rest[each * p : each * (p + 1)] for p, key in enumerate(order)}
        core, z = spot.core, spot.z
        other, mate = spot.mate()

        def stage(step, key, cut):
            i, rows, columns, first = cut
            x, out = xs[i], outs[i]
            one, hop_two, two, hop_three, three = held[key][:5]
            if step == 0:
                return [mail.start(x.at[:, :, :, other, rows, columns], one, mate)]
            sent = []
            if step == 1:

                def add(n, carry):
                    ia, ib = lax.rem(lax.div(n, side), side), lax.rem(n, side)
                    iz = lax.div(n, side * side)
                    total = x[iz, ia, ib, core, rows, columns].astype(f32)
                    one[iz, ia, ib] = (total + one[iz, ia, ib].astype(f32)).astype(one.dtype)
                    return carry

                lax.fori_loop(0, planes * side * side, add, 0)
                for k in range(1, side):
                    peer, target = spot.along(first, k)
                    part = one.at[:, peer] if first else one.at[:, :, peer]
                    sent.append(mail.start(part, hop_two.at[k - 1], target))
            elif step == 2:

                def add(n, carry):
                    iz, ir = lax.div(n, side), lax.rem(n, side)
                    total = (one[iz, spot.a, ir] if first else one[iz, ir, spot.b]).astype(f32)
                    for k in range(side - 1):
                        total += hop_two[k, iz, ir].astype(f32)
                    two[iz, ir] = total.astype(two.dtype)
                    return carry

                lax.fori_loop(0, planes * side, add, 0)
                for k in range(1, side):
                    peer, target = spot.along(not first, k)
                    sent.append(mail.start(two.at[:, peer], hop_three.at[k - 1], target))
            elif step == 3:
                mine = spot.b if first else spot.a

                def add(iz, carry):
                    total = two[iz, mine].astype(f32)
                    for k in range(side - 1):
                        total += hop_three[k, iz].astype(f32)
                    three[iz] = total.astype(three.dtype)
                    return carry

                lax.fori_loop(0, planes, add, 0)
                for k in range(1, planes):
                    peer, target = spot.plane(k)
                    if self.exchange:
                        place = out.at[z, rows, columns]
                    else:
                        place = held[key][5].at[k - 1]
                    sent.append(mail.start(three.at[peer], place, target))
                if self.exchange:
                    out[z, rows, columns] = three[z]
            elif not self.exchange:
                total = three[z].astype(f32)
                for k in range(planes - 1):
                    total += held[key][5][k].astype(f32)
                out[rows, columns] = total
            return sent

        return pipeline(self.groups, stage, 4)


def communicate(parts, ident):
    planes, side = parts[0].planes, parts[0].side
    counts = [(len(p.inputs), len(p.outputs), len(p.scratch)) for p in parts]
    n_in, n_out = (sum(c[i] for c in counts) for i in range(2))
    copies = sum(p.copies for p in parts)

    def kernel(*refs):
        ins, outs, rest = refs[:n_in], refs[n_in : n_in + n_out], refs[n_in + n_out :]
        send, recv = rest[-2:]
        spot = Spot(planes, side)
        spot.greet(parts[0].flat)
        mail = Mail(send, recv)
        running, i, o, s = [], 0, 0, 0
        for part, (ci, co, cs) in zip(parts, counts):
            running.append(
                part.steps(spot, mail, *ins[i : i + ci], *outs[o : o + co], *rest[s : s + cs])
            )
            i, o, s = i + ci, o + co, s + cs
        while running:
            running = [steps for steps in running if next(steps, True) is None]
        mail.finish()

    size = sum(x.size * x.dtype.itemsize for p in parts for x in p.inputs + p.outputs)
    return pl.pallas_call(
        kernel,
        out_shape=[x for p in parts for x in p.outputs],
        in_specs=[pl.BlockSpec(memory_space=pltpu.VMEM)] * n_in,
        out_specs=[pl.BlockSpec(memory_space=pltpu.VMEM)] * n_out,
        scratch_shapes=[s for p in parts for s in p.scratch]
        + [pltpu.SemaphoreType.DMA((copies,)), pltpu.SemaphoreType.DMA((copies,))],
        compiler_params=pltpu.CompilerParams(
            collective_id=ident, has_side_effects=True, vmem_limit_bytes=62 << 20
        ),
        cost_estimate=pl.CostEstimate(flops=0, bytes_accessed=20 * size, transcendentals=0),
        name="exchange_" + str(ident),
    )(*[x for p in parts for x in p.inputs])

def expert_weights(in_ref, cat_ref):
    units = in_ref.shape[1]
    for j in range(2):
        cat_ref[:, j * units : (j + 1) * units] = in_ref[pl.ds(j, D, stride=2), :].astype(bf16)


def expert_gate(gates, lane):
    lanes = lax.broadcasted_iota(jnp.int32, gates.shape, 1)
    return jnp.sum(jnp.where(lanes == lane, gates, 0.0), axis=1, keepdims=True)


CHUNK = 256
BLOCK = 1024


def forward_kernel(
    lane_ref, rows_ref, routes_ref, router_ref, in_ref, down_ref, out_ref, mid_ref, gates_ref, sums, cat
):
    e = pl.program_id(1)
    units = in_ref.shape[1]
    expert_weights(in_ref, cat)
    down = down_ref[0].astype(bf16)

    def chunk(i, carry):
        here = pl.ds(pl.multiple_of(i * CHUNK, CHUNK), CHUNK)
        rows = rows_ref[here, :]

        @pl.when(e == 0)
        def _():
            logits = jnp.dot(rows, router_ref[...], preferred_element_type=f32)
            lanes = lax.broadcasted_iota(jnp.int32, logits.shape, 1)
            mask = lanes == routes_ref[here, 0:1]
            for j in range(1, TOP):
                mask |= lanes == routes_ref[here, j : j + 1]
            top = jnp.max(jnp.where(mask, logits, -3e38), axis=1, keepdims=True)
            weight = jnp.where(mask, jnp.exp(jnp.where(mask, logits - top, 0.0)), 0.0)
            gates_ref[here, :] = weight / jnp.sum(weight, axis=1, keepdims=True)

        mid = jnp.dot(rows, cat[...], preferred_element_type=f32)
        mid_ref[here, :] = mid
        gate, up = mid[:, :units], mid[:, units:]
        hidden = (gate * jax.nn.sigmoid(gate) * up).astype(bf16).astype(f32)
        hidden = (hidden * expert_gate(gates_ref[here, :], lane_ref[0] + e)).astype(bf16)
        part = jnp.dot(hidden, down, preferred_element_type=f32)

        @pl.when(e == 0)
        def _():
            sums[here, :] = part

        @pl.when(e > 0)
        def _():
            sums[here, :] += part

        @pl.when(e == pl.num_programs(1) - 1)
        def _():
            out_ref[here, :] = sums[here, :].astype(bf16)

        return carry

    lax.fori_loop(0, rows_ref.shape[0] // CHUNK, chunk, 0)


def experts_forward(lane, rows, routes, router, in_rows, down):
    number, units = down.shape[:2]
    total = rows.shape[0]
    block = min(total, BLOCK)
    return pl.pallas_call(
        forward_kernel,
        grid_spec=pltpu.PrefetchScalarGridSpec(
            num_scalar_prefetch=1,
            grid=(total // block, number),
            in_specs=[
                pl.BlockSpec((block, D), lambda r, e, *_: (r, 0)),
                pl.BlockSpec((block, TOP), lambda r, e, *_: (r, 0)),
                pl.BlockSpec((D, 128), lambda r, e, *_: (0, 0)),
                pl.BlockSpec((2 * D, units), lambda r, e, *_: (e, 0)),
                pl.BlockSpec((1, units, D), lambda r, e, *_: (e, 0, 0)),
            ],
            out_specs=[
                pl.BlockSpec((block, D), lambda r, e, *_: (r, 0)),
                pl.BlockSpec((block, 2 * units), lambda r, e, *_: (r, e)),
                pl.BlockSpec((block, 128), lambda r, e, *_: (r, 0)),
            ],
            scratch_shapes=[pltpu.VMEM((block, D), f32), pltpu.VMEM((D, 2 * units), bf16)],
        ),
        out_shape=[
            jax.ShapeDtypeStruct((total, D), bf16),
            jax.ShapeDtypeStruct((total, 2 * units * number), f32),
            jax.ShapeDtypeStruct((total, 128), f32),
        ],
        compiler_params=pltpu.CompilerParams(vmem_limit_bytes=62 << 20),
        name="experts_forward",
    )(lane, rows, routes, router, in_rows, down)


def backward_kernel(
    lane_ref, grad_ref, mid_ref, gates_ref, in_ref, down_ref, out_ref, mid_grad_ref, hidden_ref, sums, cat, gate_sums
):
    e = pl.program_id(1)
    units = in_ref.shape[1]
    expert_weights(in_ref, cat)
    down = down_ref[0].astype(bf16)
    across = (((1,), (1,)), ((), ()))

    def chunk(i, carry):
        here = pl.ds(pl.multiple_of(i * CHUNK, CHUNK), CHUNK)
        weight = expert_gate(gates_ref[here, :], lane_ref[0] + e)
        mid = mid_ref[here, :]
        gate, up = mid[:, :units], mid[:, units:]
        soft = jax.nn.sigmoid(gate)
        silu = gate * soft
        hidden = (silu * up).astype(bf16).astype(f32)
        hidden_ref[here, :] = (hidden * weight).astype(bf16)
        pulled = lax.dot_general(grad_ref[here, :], down, across, preferred_element_type=f32)
        gate_grad = jnp.sum(hidden * pulled, axis=1, keepdims=True)
        hidden_grad = (pulled * weight).astype(bf16).astype(f32)
        turned = jnp.concatenate(
            [hidden_grad * up * (soft * (1.0 + gate * (1.0 - soft))), hidden_grad * silu], axis=1
        ).astype(bf16)
        mid_grad_ref[here, :] = turned
        part = lax.dot_general(turned, cat[...], across, preferred_element_type=f32)
        lanes = lax.broadcasted_iota(jnp.int32, (CHUNK, 128), 1)
        gate_part = jnp.where(lanes == lane_ref[0] + e, gate_grad, 0.0)

        @pl.when(e == 0)
        def _():
            sums[here, :] = part
            gate_sums[here, :] = gate_part

        @pl.when(e > 0)
        def _():
            sums[here, :] += part
            gate_sums[here, :] += gate_part

        @pl.when(e == pl.num_programs(1) - 1)
        def _():
            out_ref[here, :D] = sums[here, :].astype(bf16)
            out_ref[here, D:] = gate_sums[here, :].astype(bf16)

        return carry

    lax.fori_loop(0, grad_ref.shape[0] // CHUNK, chunk, 0)


def experts_backward(lane, grad, mid, gates, in_rows, down):
    number, units = down.shape[:2]
    total = grad.shape[0]
    block = min(total, BLOCK)
    return pl.pallas_call(
        backward_kernel,
        grid_spec=pltpu.PrefetchScalarGridSpec(
            num_scalar_prefetch=1,
            grid=(total // block, number),
            in_specs=[
                pl.BlockSpec((block, D), lambda r, e, *_: (r, 0)),
                pl.BlockSpec((block, 2 * units), lambda r, e, *_: (r, e)),
                pl.BlockSpec((block, 128), lambda r, e, *_: (r, 0)),
                pl.BlockSpec((2 * D, units), lambda r, e, *_: (e, 0)),
                pl.BlockSpec((1, units, D), lambda r, e, *_: (e, 0, 0)),
            ],
            out_specs=[
                pl.BlockSpec((block, D + 128), lambda r, e, *_: (r, 0)),
                pl.BlockSpec((block, 2 * units), lambda r, e, *_: (r, e)),
                pl.BlockSpec((block, units), lambda r, e, *_: (r, e)),
            ],
            scratch_shapes=[
                pltpu.VMEM((block, D), f32),
                pltpu.VMEM((D, 2 * units), bf16),
                pltpu.VMEM((block, 128), f32),
            ],
        ),
        out_shape=[
            jax.ShapeDtypeStruct((total, D + 128), bf16),
            jax.ShapeDtypeStruct((total, 2 * units * number), bf16),
            jax.ShapeDtypeStruct((total, units * number), bf16),
        ],
        compiler_params=pltpu.CompilerParams(vmem_limit_bytes=62 << 20),
        name="experts_backward",
    )(lane, grad, mid, gates, in_rows, down)


def moments_kernel(scale_ref, grad_ref, w_ref, first_ref, second_ref, new_first, new_second, norms):
    units = w_ref.shape[1]
    part = w_ref.shape[0] // 2

    @pl.when((pl.program_id(0) == 0) & (pl.program_id(1) == 0))
    def _():
        norms[...] = jnp.zeros_like(norms)

    for j in range(2):
        here = pl.ds(j, part, stride=2)
        grad = grad_ref[:, j * units : (j + 1) * units]
        weight = w_ref[here, :]
        one = RATE_ONE * first_ref[here, :] + (1.0 - RATE_ONE) * grad
        two = RATE_TWO * second_ref[here, :] + (1.0 - RATE_TWO) * grad * grad
        update = lamb_update(weight, one, two, scale_ref[0], scale_ref[1])
        new_first[here, :] = one
        new_second[here, :] = two
        norms[0] += jnp.sum((weight * weight).reshape(-1, 8, units), axis=0)
        norms[1] += jnp.sum((update * update).reshape(-1, 8, units), axis=0)


def in_moments(scales, grad, weight, first, second):
    units = weight.shape[1]
    number = grad.shape[1] // (2 * units)
    parts = 2
    row = pl.BlockSpec((2 * D // parts, units), lambda e, p, *_: (e * parts + p, 0))
    return pl.pallas_call(
        moments_kernel,
        grid_spec=pltpu.PrefetchScalarGridSpec(
            num_scalar_prefetch=1,
            grid=(number, parts),
            in_specs=[pl.BlockSpec((D // parts, 2 * units), lambda e, p, *_: (p, e)), row, row, row],
            out_specs=[row, row, pl.BlockSpec((2, 8, units), lambda e, p, *_: (0, 0, 0))],
        ),
        out_shape=[jax.ShapeDtypeStruct(weight.shape, f32)] * 2
        + [jax.ShapeDtypeStruct((2, 8, units), f32)],
        compiler_params=pltpu.CompilerParams(vmem_limit_bytes=40 << 20),
        name="in_moments",
    )(scales, grad, weight, first, second)


def norm_apply(values, gain):
    return values * lax.rsqrt(jnp.mean(values * values, axis=-1, keepdims=True) + 1e-06) * gain


def rotary_apply(values, places):
    half = values.shape[-1] // 2
    freqs = jnp.exp(-jnp.log(10000.0) * jnp.arange(half, dtype=f32) / half)
    angles = places[:, None] * freqs[None, :]
    cosine = jnp.cos(angles)[:, None, :]
    sine = jnp.sin(angles)[:, None, :]
    first_half = values[..., :half]
    second_half = values[..., half:]
    return jnp.concatenate(
        [first_half * cosine - second_half * sine, second_half * cosine + first_half * sine],
        axis=-1,
    )


def lamb_update(weight, moment_one, moment_two, scale_one, scale_two):
    return (moment_one * scale_one) / (jnp.sqrt(moment_two * scale_two) + EPSILON) + DECAY * weight


def lamb_parts(weight, moment_one, moment_two, gradient, scales):
    moment_one = RATE_ONE * moment_one + (1.0 - RATE_ONE) * gradient
    moment_two = RATE_TWO * moment_two + (1.0 - RATE_TWO) * gradient * gradient
    return (moment_one, moment_two, lamb_update(weight, moment_one, moment_two, *scales))


STEPS = 4


def row_lists(tokens, base, rows):
    inside = (tokens >= base) & (tokens < base + rows)
    count = jnp.sum(inside.astype(jnp.int32), axis=1)
    place = jnp.arange(SEQUENCE_TOKENS, dtype=jnp.int32)
    before = (place[:, None] < place[None, :]).astype(bf16)
    rank = jnp.dot(inside.astype(bf16), before, preferred_element_type=f32).astype(jnp.int32)
    packed = place[None, :] * 65536 + (tokens - base)
    hit = inside[:, :, None] & (rank[:, :, None] == place[None, None, :])
    entry = jnp.sum(jnp.where(hit, packed[:, :, None], 0), axis=1)
    empty = SEQUENCE_TOKENS * 65536
    return jnp.where(place[None, :] < count[:, None], entry, empty), count


def gather_kernel(list_ref, count_ref, table_ref, out_ref, rows_ref):
    b = pl.program_id(0)
    rows_ref[...] = jnp.zeros_like(rows_ref)

    def step(k, carry):
        for j in range(STEPS):
            entry = list_ref[b, k * STEPS + j]
            rows_ref[pl.ds(entry >> 16, 1), :] = table_ref[pl.ds(entry & 65535, 1), :]
        return carry

    lax.fori_loop(0, (count_ref[b] + STEPS - 1) // STEPS, step, 0)
    out_ref[0] = rows_ref[:SEQUENCE_TOKENS].astype(bf16)


def gather_rows(lists, counts, table):
    blocks = lists.shape[0]
    rows, columns = table.shape
    return pl.pallas_call(
        gather_kernel,
        grid_spec=pltpu.PrefetchScalarGridSpec(
            num_scalar_prefetch=2,
            grid=(blocks,),
            in_specs=[pl.BlockSpec((rows, columns), lambda b, *_: (0, 0))],
            out_specs=pl.BlockSpec((1, SEQUENCE_TOKENS, columns), lambda b, *_: (b, 0, 0)),
            scratch_shapes=[pltpu.VMEM((SEQUENCE_TOKENS + 8, columns), f32)],
        ),
        out_shape=jax.ShapeDtypeStruct((blocks, SEQUENCE_TOKENS, columns), bf16),
        compiler_params=pltpu.CompilerParams(vmem_limit_bytes=40 << 20),
        name="gather_rows",
    )(lists, counts, table)


def scatter_kernel(list_ref, count_ref, grad_ref, head_ref, out_ref, rows_ref):
    b = pl.program_id(0)

    @pl.when(b == 0)
    def _():
        out_ref[...] = head_ref[...].astype(f32)

    rows_ref[:SEQUENCE_TOKENS] = grad_ref[0].astype(f32)
    rows_ref[SEQUENCE_TOKENS:] = jnp.zeros((8, rows_ref.shape[1]), f32)

    def step(k, carry):
        for j in range(STEPS):
            entry = list_ref[b, k * STEPS + j]
            out_ref[pl.ds(entry & 65535, 1), :] += rows_ref[pl.ds(entry >> 16, 1), :]
        return carry

    lax.fori_loop(0, (count_ref[b] + STEPS - 1) // STEPS, step, 0)


def scatter_rows(lists, counts, grads, head):
    blocks = lists.shape[0]
    rows, columns = head.shape
    return pl.pallas_call(
        scatter_kernel,
        grid_spec=pltpu.PrefetchScalarGridSpec(
            num_scalar_prefetch=2,
            grid=(blocks,),
            in_specs=[
                pl.BlockSpec((1, SEQUENCE_TOKENS, columns), lambda b, *_: (b, 0, 0)),
                pl.BlockSpec((rows, columns), lambda b, *_: (0, 0)),
            ],
            out_specs=pl.BlockSpec((rows, columns), lambda b, *_: (0, 0)),
            scratch_shapes=[pltpu.VMEM((SEQUENCE_TOKENS + 8, columns), f32)],
        ),
        out_shape=jax.ShapeDtypeStruct((rows, columns), f32),
        compiler_params=pltpu.CompilerParams(vmem_limit_bytes=50 << 20),
        name="scatter_rows",
    )(lists, counts, grads, head)


def on_device(
    token_ids,
    positions,
    pair_index,
    ref_logps,
    routes,
    step_count,
    embed_table,
    embed_first,
    embed_second,
    qkv_weight,
    qkv_first,
    qkv_second,
    out_weight,
    out_first,
    out_second,
    router_weight,
    router_first,
    router_second,
    norm_gains,
    gains_first,
    gains_second,
    in_weight,
    in_first,
    in_second,
    down_weight,
    down_first,
    down_second,
):
    shard_id = lax.axis_index("shard")
    expert_id = lax.axis_index("expert")
    shards = lax.axis_size("shard")
    planes = lax.axis_size("expert")
    devices = shards * planes
    vocab_rows, columns = embed_table.shape
    vocab_base = shard_id * vocab_rows
    own_rows = vocab_rows // planes
    local_experts = in_weight.shape[0]
    hidden_units = in_weight.shape[3]
    head_cols = QUERY_HEADS * HEAD_WIDTH
    key_cols = KEY_VALUE_HEADS * HEAD_WIDTH
    rows_all = devices * COMP

    side = math.isqrt(shards // 2)
    grid = (planes, side, side, 2)
    together = devices <= 32

    def send(parts, ident):
        if together:
            return communicate(parts, ident)
        return [
            out for n, part in enumerate(parts) for out in communicate([part], ident + 20 * n)
        ]

    def gather_completion(rows, ident):
        part = Gather([rows], split(0, COMP, rows.shape[1], 2, 2), planes, side)
        return communicate([part], ident)[0].reshape(rows_all, rows.shape[1])

    def reduce_completion(rows, ident, cuts=2):
        rows = rows.reshape(grid + (COMP, rows.shape[1]))
        part = Reduce([rows], split(0, COMP, rows.shape[-1], 2, cuts), planes, side)
        return communicate([part], ident)[0]

    def gather_tiny(block, ident):
        return communicate([Tiny(block, planes, side)], ident)[0].reshape((devices,) + block.shape)

    weight_rows = qkv_weight.shape[0]
    weight_cols = head_cols + key_cols + 128
    cuts = 3 if weight_rows % 48 == 0 else 1
    weight_groups = [
        [
            (i, slice(n * (weight_rows // cuts), (n + 1) * (weight_rows // cuts)), slice(0, weight_cols), i == 0)
            for i in range(2)
        ]
        for n in range(cuts)
    ]
    embed_groups = split(0, SEQUENCE_TOKENS, columns, 8, 1)

    own_places = lax.dynamic_index_in_dim(positions, shard_id, 0, keepdims=False)
    start = own_places[0]
    own_tokens = lax.dynamic_slice_in_dim(token_ids, shard_id * SEQUENCE_TOKENS, SEQUENCE_TOKENS, 0)
    own_routes = lax.dynamic_slice_in_dim(routes, start, COMP, 0)
    sheet = jnp.concatenate(
        [
            own_tokens,
            own_routes.reshape(-1),
            own_places,
            jnp.zeros((1024 - SEQUENCE_TOKENS - COMP * TOP - COMP,), jnp.int32),
        ]
    )
    sheets = gather_tiny(sheet.reshape(8, 128), 0).reshape(devices, 1024)
    tokens_all = sheets[:, :SEQUENCE_TOKENS]
    routes_all = sheets[:, SEQUENCE_TOKENS : SEQUENCE_TOKENS + COMP * TOP].reshape(rows_all, TOP)
    places_all = sheets[:, SEQUENCE_TOKENS + COMP * TOP : SEQUENCE_TOKENS + COMP * TOP + COMP]
    spots = jnp.arange(SEQUENCE_TOKENS, dtype=jnp.int32)
    targets = jnp.sum(
        jnp.where(
            places_all[:, :, None] + 1 == spots[None, None, :], tokens_all[:, None, :], 0
        ),
        axis=2,
    ).reshape(-1)

    lists, counts = row_lists(tokens_all, vocab_base, vocab_rows)
    picked = gather_rows(lists, counts, embed_table).reshape(grid + (SEQUENCE_TOKENS, columns))
    packs = [
        jnp.concatenate(
            [
                qkv_weight[:, : head_cols + key_cols],
                router_weight,
                norm_gains.T,
                jnp.zeros((weight_rows, 128 - EXPERTS - 3), f32),
            ],
            axis=1,
        ).astype(bf16),
        jnp.concatenate(
            [
                qkv_weight[:, head_cols + key_cols :],
                out_weight,
                jnp.zeros((weight_rows, 128), f32),
            ],
            axis=1,
        ).astype(bf16),
    ]
    picked, first_pack, second_pack = send(
        [
            Reduce([picked], embed_groups, planes, side, exchange=True),
            Gather(packs, weight_groups, planes, side),
        ],
        1,
    )
    first_pack = first_pack.reshape(D, weight_cols)
    second_pack = second_pack.reshape(D, weight_cols)
    table_sent, picked = lax.optimization_barrier(
        (embed_table.astype(bf16).reshape(planes, own_rows, columns), picked)
    )
    table_own = lax.all_to_all(table_sent, "expert", split_axis=0, concat_axis=0, tiled=True)
    table_own = jnp.concatenate([table_own[p] for p in range(planes)], axis=1)
    embedded = jnp.concatenate([picked[p] for p in range(planes)], axis=1).astype(f32)
    router_block = first_pack[:, head_cols + key_cols :]
    gains_value = router_block[:, EXPERTS : EXPERTS + 3].T.astype(f32)
    out_full = second_pack[:, key_cols : key_cols + D]

    normed, norm_back_one = jax.vjp(norm_apply, embedded, gains_value[0])
    normed_b = normed.astype(bf16)
    places_f = own_places.astype(f32)
    spots_f = spots.astype(f32)

    def make_query(projected):
        return rotary_apply(projected.reshape(COMP, QUERY_HEADS, HEAD_WIDTH), places_f)

    def make_key(projected):
        return rotary_apply(
            projected.reshape(SEQUENCE_TOKENS, KEY_VALUE_HEADS, HEAD_WIDTH), spots_f
        )

    projected = jnp.dot(normed_b, first_pack, preferred_element_type=f32)
    query_f, query_back = jax.vjp(
        make_query, lax.dynamic_slice(projected, (start, 0), (COMP, head_cols))
    )
    key_f, key_back = jax.vjp(make_key, projected[:, head_cols : head_cols + key_cols])
    query = query_f.astype(bf16).reshape(COMP, KEY_VALUE_HEADS, GROUP, HEAD_WIDTH)
    key = key_f.astype(bf16)
    value = (
        jnp.dot(normed_b, second_pack[:, :key_cols], preferred_element_type=f32)
        .reshape(SEQUENCE_TOKENS, KEY_VALUE_HEADS, HEAD_WIDTH)
        .astype(bf16)
    )
    scores = jnp.einsum("qhgd,khd->hgqk", query, key, preferred_element_type=f32) * HEAD_WIDTH ** (
        -0.5
    )
    scores = jnp.where(own_places[:, None] >= spots[None, :], scores, -1000000000.0)
    expd = jnp.exp(scores - jnp.max(scores, axis=-1, keepdims=True))
    probs = expd / jnp.sum(expd, axis=-1, keepdims=True)
    probs_b = probs.astype(bf16)
    attended = (
        jnp.einsum("hgqk,khd->qhgd", probs_b, value, preferred_element_type=f32)
        .reshape(COMP, head_cols)
        .astype(bf16)
    )
    resid = lax.dynamic_slice_in_dim(embedded, start, COMP, 0) + jnp.dot(
        attended, out_full, preferred_element_type=f32
    )
    normed_two, norm_back_two = jax.vjp(norm_apply, resid, gains_value[1])
    normed_two_b = normed_two.astype(bf16)

    expert_rows = gather_completion(normed_two_b, 2)
    lane = (shard_id * local_experts).astype(jnp.int32).reshape(1)
    in_rows = in_weight.reshape(-1, hidden_units)
    produced, mid, gates = experts_forward(
        lane, expert_rows, routes_all, router_block, in_rows, down_weight
    )
    own_index = expert_id * shards + shard_id
    own_gates = lax.dynamic_slice(gates, (own_index * COMP, 0), (COMP, 128))[:, :EXPERTS]
    resid_two = resid + reduce_completion(produced, 3)

    final_rows, norm_back_three = jax.vjp(norm_apply, resid_two, gains_value[2])
    head_rows = gather_completion(final_rows.astype(bf16), 4)
    logits = jnp.einsum("rd,vd->rv", head_rows, table_own, preferred_element_type=f32) / LOGIT_SCALE
    own_base = vocab_base + expert_id * own_rows
    target_hot = targets[:, None] == own_base + jnp.arange(own_rows, dtype=jnp.int32)[None, :]
    row_top = jnp.max(logits, axis=1)
    row_total = jnp.sum(jnp.exp(logits - row_top[:, None]), axis=1)
    row_hit = jnp.sum(jnp.where(target_hot, logits, 0.0), axis=1)
    stats = jnp.stack([row_top, row_total, row_hit]).reshape(8, 3 * rows_all // 8)
    stats = gather_tiny(stats, 5).reshape(devices, 3, rows_all)
    top_all = jnp.max(stats[:, 0], axis=0)
    total_all = jnp.sum(stats[:, 1] * jnp.exp(stats[:, 0] - top_all[None]), axis=0)
    row_lse = top_all + jnp.log(total_all)
    seq_sums = jnp.sum((jnp.sum(stats[:, 2], axis=0) - row_lse).reshape(-1, COMP), axis=1)

    sequences = jnp.arange(devices, dtype=jnp.int32)[None, :]
    pair_sign = (pair_index[:, :1] == sequences).astype(f32) - (
        pair_index[:, 1:] == sequences
    ).astype(f32)
    scaled = BETA * jnp.sum(pair_sign * (seq_sums - ref_logps)[None, :], axis=1)
    loss_value = -jnp.mean(jax.nn.log_sigmoid(scaled))
    pair_grad = jax.nn.sigmoid(-scaled) * (-BETA / scaled.shape[0])
    seq_grad = jnp.sum(pair_sign * pair_grad[:, None], axis=0)
    row_grad = jnp.repeat(seq_grad, COMP)
    grad_logits = (
        row_grad[:, None] * (target_hot.astype(f32) - jnp.exp(logits - row_lse[:, None]))
    ).astype(bf16)
    grad_rows = jnp.dot(grad_logits, table_own, preferred_element_type=f32) / LOGIT_SCALE
    own_grad_rows = reduce_completion(grad_rows.astype(bf16), 6)
    grad_resid_two, grad_gain_three = norm_back_three(own_grad_rows)

    grad_all = gather_completion(grad_resid_two.astype(bf16), 7)
    head_grad = (
        jnp.einsum("rv,rd->vd", grad_logits, head_rows, preferred_element_type=f32) / LOGIT_SCALE
    ).astype(bf16)
    head_sent = jnp.stack([head_grad[:, p * columns : (p + 1) * columns] for p in range(planes)])
    head_sent, grad_all = lax.optimization_barrier((head_sent, grad_all))
    head_grad = lax.all_to_all(
        head_sent, "expert", split_axis=0, concat_axis=0, tiled=True
    ).reshape(vocab_rows, columns)
    back, mid_grad, gated_hidden = experts_backward(
        lane, grad_all, mid, gates, in_rows, down_weight
    )
    back = reduce_completion(back, 8, 1)
    grad_gates = back[:, D : D + EXPERTS]
    grad_router_logits = own_gates * (
        grad_gates - jnp.sum(own_gates * grad_gates, axis=1, keepdims=True)
    )
    grad_router_logits = jnp.pad(grad_router_logits, ((0, 0), (0, 128 - EXPERTS)))
    grad_normed_two = back[:, :D] + jnp.einsum(
        "se,de->sd", grad_router_logits, router_block.astype(f32)
    )
    grad_resid, grad_gain_two = norm_back_two(grad_normed_two)
    grad_resid = grad_resid + grad_resid_two
    grad_branch = grad_resid.astype(bf16)
    grad_attended = (
        jnp.einsum("sd,kd->sk", grad_branch, out_full, preferred_element_type=f32)
        .astype(bf16)
        .reshape(COMP, KEY_VALUE_HEADS, GROUP, HEAD_WIDTH)
    )

    grad_probs = jnp.einsum("qhgd,khd->hgqk", grad_attended, value, preferred_element_type=f32)
    grad_probs = grad_probs.astype(bf16).astype(f32)
    inner = jnp.sum(grad_probs * probs, axis=-1, keepdims=True)
    grad_scores = (probs * (grad_probs - inner)).astype(bf16)
    grad_value = jnp.einsum("hgqk,qhgd->khd", probs_b, grad_attended, preferred_element_type=f32)
    grad_query = jnp.einsum(
        "hgqk,khd->qhgd", grad_scores, key, preferred_element_type=f32
    ) * HEAD_WIDTH ** (-0.5)
    grad_key = jnp.einsum(
        "hgqk,qhgd->khd", grad_scores, query, preferred_element_type=f32
    ) * HEAD_WIDTH ** (-0.5)

    def spread(rows):
        return lax.dynamic_update_slice_in_dim(
            jnp.zeros((SEQUENCE_TOKENS, rows.shape[1]), rows.dtype), rows, start, 0
        )

    grad_query_rows = query_back(grad_query.reshape(COMP, QUERY_HEADS, HEAD_WIDTH))[0].astype(bf16)
    grad_first = jnp.concatenate(
        [
            spread(grad_query_rows),
            key_back(grad_key)[0].astype(bf16),
            jnp.zeros((SEQUENCE_TOKENS, 128), bf16),
        ],
        axis=1,
    )
    grad_value = grad_value.reshape(SEQUENCE_TOKENS, key_cols).astype(bf16)
    across = "sk,dk->sd"
    grad_normed = jnp.einsum(across, grad_first, first_pack, preferred_element_type=f32)
    grad_normed += jnp.einsum(
        across, grad_value, second_pack[:, :key_cols], preferred_element_type=f32
    )
    grad_embedded, grad_gain_one = norm_back_one(grad_normed)
    grad_embedded = (grad_embedded + spread(grad_resid)).astype(bf16)
    grad_embedded = jnp.stack(
        [grad_embedded[:, p * columns : (p + 1) * columns] for p in range(planes)]
    )

    gains_grad = jnp.pad(
        jnp.stack([grad_gain_one, grad_gain_two, grad_gain_three]), ((0, 13), (0, 0))
    ).astype(bf16)
    gains_lanes = (
        jnp.arange(16)[:, None] + EXPERTS == jnp.arange(128)[None, :]
    ).astype(bf16)
    wide = head_cols + key_cols
    first_left = jnp.concatenate([normed_b, normed_two_b, gains_grad], axis=0)
    first_right = jnp.concatenate(
        [
            grad_first,
            jnp.pad(
                jnp.concatenate([grad_router_logits.astype(bf16), gains_lanes], axis=0),
                ((0, 0), (wide, 0)),
            ),
        ],
        axis=0,
    )
    second_left = jnp.concatenate([normed_b, attended], axis=0)
    second_right = jnp.concatenate(
        [
            jnp.pad(grad_value, ((0, 0), (0, D + 128))),
            jnp.pad(grad_branch, ((0, 0), (key_cols, 128))),
        ],
        axis=0,
    )
    grad_packs = [
        jnp.einsum("sd,sk->dk", left, right, preferred_element_type=f32)
        .astype(bf16)
        .reshape(grid + (weight_rows, weight_cols))
        for left, right in ((first_left, first_right), (second_left, second_right))
    ]
    sent, first_grad, second_grad = send(
        [
            Gather([grad_embedded], embed_groups, planes, side, exchange=True),
            Reduce(grad_packs, weight_groups, planes, side),
        ],
        9,
    )
    table_grad = scatter_rows(
        lists, counts, sent.reshape(devices, SEQUENCE_TOKENS, columns), head_grad
    )

    step_value = step_count.astype(f32)
    scales = (1.0 / (1.0 - RATE_ONE**step_value), 1.0 / (1.0 - RATE_TWO**step_value))
    grad_in = jnp.einsum("td,tk->dk", expert_rows, mid_grad, preferred_element_type=f32)
    grad_down = jnp.einsum(
        "tk,td->kd", gated_hidden, grad_all, preferred_element_type=f32
    ).reshape(down_weight.shape)
    in_first_new, in_second_new, in_norms = in_moments(
        jnp.stack(scales),
        grad_in,
        in_rows,
        in_first.reshape(in_rows.shape),
        in_second.reshape(in_rows.shape),
    )
    weights = (embed_table, qkv_weight, out_weight, router_weight, norm_gains, down_weight)
    firsts = (embed_first, qkv_first, out_first, router_first, gains_first, down_first)
    seconds = (embed_second, qkv_second, out_second, router_second, gains_second, down_second)
    gradients = (
        table_grad,
        jnp.concatenate([first_grad[:, :wide], second_grad[:, :key_cols]], axis=1),
        second_grad[:, key_cols : key_cols + D],
        first_grad[:, wide : wide + EXPERTS],
        first_grad[:, wide + EXPERTS : wide + EXPERTS + 3].T,
        grad_down,
    )
    moved = [
        lamb_parts(weight, moment_one, moment_two, gradient, scales)
        for weight, moment_one, moment_two, gradient in zip(weights, firsts, seconds, gradients)
    ]
    partial_norms = [
        jnp.stack([jnp.sum(weight * weight), jnp.sum(parts[2] * parts[2])])
        for weight, parts in zip(weights, moved)
    ]
    partial_norms.insert(5, jnp.sum(in_norms, axis=(1, 2)))
    partial_norms = jnp.pad(jnp.stack(partial_norms), ((0, 1), (0, 126)))
    norm_values = jnp.sqrt(jnp.sum(gather_tiny(partial_norms, 10), axis=0))[:7, :2]
    trust_ratio = norm_values[:, 0] / norm_values[:, 1]
    moved.insert(
        5, (in_first_new, in_second_new, lamb_update(in_rows, in_first_new, in_second_new, *scales))
    )
    weights = weights[:5] + (in_rows,) + weights[5:]
    results = [loss_value]
    for place, (weight, parts) in enumerate(zip(weights, moved)):
        made = [weight - STEP_RATE * trust_ratio[place] * parts[2], parts[0], parts[1]]
        if place == 5:
            made = [x.reshape(in_weight.shape) for x in made]
        results.extend(made)
    results.append(jnp.stack([norm_values[:, 0], norm_values[:, 1], trust_ratio], axis=1))
    return tuple(results)


def solution(mesh):
    rows = P(BOTH, None)
    vocab = P("shard", "expert")
    gains = P(None, BOTH)
    inner = P("shard", None, None, "expert")
    outer = P("shard", "expert", None)
    state = (vocab,) * 3 + (rows,) * 9 + (gains,) * 3 + (inner,) * 3 + (outer,) * 3
    return jax.shard_map(
        on_device,
        mesh=mesh,
        in_specs=(P("expert"), P("expert", None), P(), P(), rows, P()) + state,
        out_specs=(P(),) + state + (P(),),
        check_vma=False,
    )
```

time: 1640 us -> 944 us (0.58)
  waiting for transfers between devices: 917 us -> 0.01 us
  Pallas kernels: 41.4 us -> 672 us
  blocking collectives: 249 us -> 0 us
  local copies, waits for them, and re-layouts: 115 us -> 46.4 us
  matrix products: 128 us -> 80.9 us
  other arithmetic: 141 us -> 118 us
    pallas_call x0 -> x14, Pallas kernels: none -> 631 us  [the longest x11 563 us: communicate(): pl.pallas_call(kernel, out_shape=[x for p in parts for x in p.outputs], i...]
    reduce_scatter x6 -> x0, waiting for transfers between devices: 620 us -> none  [the longest x1 137 us: on_device(): lax.psum_scatter(jnp.concatenate([grad_copies.astype(bf16), grad_gates_al...]
    all_gather x6 -> x0, blocking collectives: 189 us -> none  [the longest x1 42.7 us: on_device(): lax.all_gather(norm_gains.astype(bf16), BOTH, axis=1, tiled=True)]
    all_gather x6 -> x0, waiting for transfers between devices: 152 us -> none  [the longest x1 58.7 us: on_device(): lax.all_gather(grad_resid_two.astype(bf16), BOTH, axis=0, tiled=True)]
    unnamed x16 -> x0, waiting for transfers between devices: 111 us -> none
    unnamed x238 -> x236, local copies, waits for them, and re-layouts: 84.3 us -> 18.8 us
    psum x1 -> x0, blocking collectives: 40.1 us -> none  [on_device(): norm_values = jnp.sqrt(lax.psum(partial_norms, BOTH))]
    dot_general x14 -> x9, matrix products: 78.1 us -> 39.9 us  [the longest x2 11.4 us: on_device(): jnp.einsum('sd,sk->dk', left, right, preferred_element_type=f32)]
  transfers between devices with their start and end apart: 17 -> 2, of which waited for: 13 -> 0; matrix products, arithmetic and copies ran while one was open for 12% -> 10% of each run, Pallas kernels for 0% -> 38%
where the time goes in v2:
time: 944 us; the launch traced here: 938 us
  Pallas kernels  672 us (71%)
  other arithmetic  118 us (12%)
  matrix products  80.9 us (9%)
  local copies, waits for them, and re-layouts  46.4 us (5%)
  starting transfers between devices  10.3 us (1%)
  between operations  10 us (1%)
    pallas_call x11, Pallas kernels, communicate(): pl.pallas_call(kernel, out_shape=[x for p in parts for x in p.outputs], i...  563 us
    reduce_sum x6, other arithmetic, on_device(): jnp.sum(weight * weight)  33.9 us
    sub x7, other arithmetic, on_device(): weight - STEP_RATE * trust_ratio[place] * parts[2]  30.6 us
    pallas_call x1, Pallas kernels, experts_forward(): pl.pallas_call(forward_kernel, grid_spec=pltpu.PrefetchScalarGridSpec(num...  28.6 us
    pallas_call x1, Pallas kernels, scatter_rows(): pl.pallas_call(scatter_kernel, grid_spec=pltpu.PrefetchScalarGridSpec(num...  27.2 us
    pallas_call x1, Pallas kernels, experts_backward(): pl.pallas_call(backward_kernel, grid_spec=pltpu.PrefetchScalarGridSpec(nu...  25.7 us
  transfers between devices with their start and end apart: 2, of which 0 were waited for; matrix products, arithmetic and copies ran while one was open for 10% of the time, Pallas kernels for 38%

profile of v2, /device:TPU:0, one launch (start us, length us, event | category | flops | bytes accessed | tf_op | source)
XLA Modules:
  0.0 937.6 jit_solution(18207457196268423824)
XLA Ops:
  3.2 13.2 %exchange_0.1 = s32[4,8,8,128]{3,2,1,0:T(8,128)} custom-call(s32[8,128]{1,0:T(8,128)} %add_bitcast_fusion.refs_0_), custom_call_target="tpu_custom_call" | custom-call | bytes 2703360 | tf_op jit(solution)/shard_map/exchange_0/pallas_call | solution.py:329
  18.7 1.4 multiply_reduce_fusion.25
  20.2 1.4 multiply_reduce_fusion.21
  22.8 6.4 convert_element_type.175
  29.1 4.7 select_reduce_fusion
  34.0 14.6 %gather_rows.1 = bf16[32,256,384]{2,1,0:T(8,128)(2,1)S(1)} custom-call(s32[32,256]{1,0:T(8,128)S(1)} %fusion.85.list_ref, s32[32]{0:T(128)S(1)} %get-tuple-element.220.count_ref, f32[6144,384]{1,0:T(8,128)} %table_ref.1), custom_call_target="tpu_custom_call" | custom-call | tf_op jit(solution)/shard_map/gather_rows/pallas_call | solution.py:626
  48.6 2.7 copy-done.2
  52.8 108.6 %exchange_1.1 = (bf16[4,256,384]{2,1,0:T(8,128)(2,1)}, bf16[4,2,2,2,48,2176]{5,4,3,2,1,0:T(8,128)(2,1)}, bf16[4,2,2,2,48,2176]{5,4,3,2,1,0:T(8,128)(2,1)}) custom-call(bf16[4,2,2,2,256,384]{5,4,3,2,1,0:T(8,128)(2,1)} %bitcast.228, bf16[48,2176]{1,0:T(8,128)(2,1)} %concatenate.52.refs_1_, bf16[48,2176]{1,0:T(8,128)(2,1)} %maximum_maximum_fusion.refs_2_), custom_call_target="tpu_custom_call" | custom-call | bytes 417300480 | tf_op jit(solution)/shard_map/exchange_1/pallas_call | solution.py:329
  161.5 5.3 all-to-all-start
  167.6 1.8 slice.260.router_ref
  177.8 1.3 slice_reduce_fusion
  179.7 2.0 fusion.46
  181.9 5.0 fusion.129
  186.9 1.4 copy-done.49
  190.8 1.3 fusion.128
  192.2 1.5 fusion.49
  194.4 3.4 multiply_reduce_fusion.18
  198.5 98.0 %exchange_2.1 = bf16[4,2,2,2,32,1536]{5,4,3,2,1,0:T(8,128)(2,1)} custom-call(bf16[32,1536]{1,0:T(8,128)(2,1)} %multiply_convert_fusion.4.refs_0_), custom_call_target="tpu_custom_call" | custom-call | bytes 64880640 | tf_op jit(solution)/shard_map/exchange_2/pallas_call | solution.py:329
  296.5 28.6 %experts_forward.1 = (bf16[1024,1536]{1,0:T(8,128)(2,1)}, f32[1024,1024]{1,0:T(8,128)}, f32[1024,128]{1,0:T(8,128)}) custom-call(s32[1]{0:T(128)} %bitcast.25.lane_ref, bf16[1024,1536]{1,0:T(8,128)(2,1)} %bitcast.236, s32[1024,8]{1,0:T(8,128)} %reshape.431.routes_ref, bf16[1536,128]{1,0:T(8,128)(2,1)} %slice.260.router_ref, f32[12288,128]{1,0:T(8,128)} %bitcast.220, ...), custom_call_target="tpu_custom_call" | custom-call | tf_op jit(solution)/shard_map/experts_forward/pallas_call | solution.py:409
  325.2 29.0 %exchange_3.1 = f32[32,1536]{1,0:T(8,128)} custom-call(bf16[4,2,2,2,32,1536]{5,4,3,2,1,0:T(8,128)(2,1)} %bitcast.252), custom_call_target="tpu_custom_call" | custom-call | bytes 66846720 | tf_op jit(solution)/shard_map/exchange_3/pallas_call | solution.py:329
  356.0 29.3 %exchange_4.1 = bf16[4,2,2,2,32,1536]{5,4,3,2,1,0:T(8,128)(2,1)} custom-call(bf16[32,1536]{1,0:T(8,128)(2,1)} %multiply_convert_fusion.3.refs_0_), custom_call_target="tpu_custom_call" | custom-call | bytes 64880640 | tf_op jit(solution)/shard_map/exchange_4/pallas_call | solution.py:329
  386.6 3.0 slice_bitcast_fusion.7
  389.9 5.1 multiply_reduce_fusion.2
  395.2 3.1 exponential_reduce_fusion
  398.9 11.8 %exchange_5.1 = f32[4,8,8,384]{3,2,1,0:T(8,128)} custom-call(f32[8,384]{1,0:T(8,128)} %reshape.435.refs_0_), custom_call_target="tpu_custom_call" | custom-call | bytes 8110080 | tf_op jit(solution)/shard_map/exchange_5/pallas_call | solution.py:329
  415.5 11.2 %multiply_convert_fusion = bf16[1024,1536]{1,0:T(8,128)(2,1)} fusion(bf16[1536,384]{1,0:T(8,128)(2,1)} %copy-done.16, bf16[1536,384]{1,0:T(8,128)(2,1)} %copy-done.17, bf16[1536,384]{1,0:T(8,128)(2,1)} %copy-done.18, bf16[1536,384]{1,0:T(8,128)(2,1)} %copy-done.15, f32[1024,1536]{1,0:T(8,128)} %copy-done.5, f32[1024]{0:T(1024)S(1)} %get-tuple-element.215, ...), kind=kOutput, calls=%fused_computation.22 | convolution fusion | flops 4864868352 | bytes 14174208 | tf_op jit(solution)/shard_map/dot_general | solution.py:903
  426.8 11.0 %fusion.3 = bf16[1536,1536]{1,0:T(8,128)(2,1)} fusion(bf16[1024,1536]{1,0:T(8,128)(2,1)S(1)} %bitcast.250, f32[1024,1536]{1,0:T(8,128)} %copy-done.5, f32[1024]{0:T(1024)S(1)} %get-tuple-element.215, f32[1024]{0:T(1024)S(1)} %mul.950, s32[1536]{0:T(1024)S(1)} %copy-done.71, s32[1024]{0:T(1024)S(1)} %copy-done.76), kind=kOutput, calls=%fused_computation.16 | convolution fusion | flops 4847566848 | bytes 14174208 | tf_op jit(solution)/shard_map/rv,rd->vd/dot_general | solution.py:909
  437.7 30.5 %exchange_6.1 = f32[32,1536]{1,0:T(8,128)} custom-call(bf16[4,2,2,2,32,1536]{5,4,3,2,1,0:T(8,128)(2,1)} %bitcast.251), custom_call_target="tpu_custom_call" | custom-call | bytes 66846720 | tf_op jit(solution)/shard_map/exchange_6/pallas_call | solution.py:329
  468.3 4.7 slice_bitcast_fusion.3
  474.5 29.1 %exchange_7.1 = bf16[4,2,2,2,32,1536]{5,4,3,2,1,0:T(8,128)(2,1)} custom-call(bf16[32,1536]{1,0:T(8,128)(2,1)} %fusion.86.refs_0_), custom_call_target="tpu_custom_call" | custom-call | bytes 64880640 | tf_op jit(solution)/shard_map/exchange_7/pallas_call | solution.py:329
  503.7 4.3 pad_maximum_fusion.1
  508.0 25.7 %experts_backward.1 = (bf16[1024,1664]{1,0:T(8,128)(2,1)}, bf16[1024,1024]{1,0:T(8,128)(2,1)}, bf16[1024,512]{1,0:T(8,128)(2,1)}) custom-call(s32[1]{0:T(128)} %bitcast.25.lane_ref, bf16[1024,1536]{1,0:T(8,128)(2,1)} %bitcast.234, f32[1024,1024]{1,0:T(8,128)} %get-tuple-element.49.mid_ref, f32[1024,128]{1,0:T(8,128)} %get-tuple-element.50.gates_ref, ...), custom_call_target="tpu_custom_call" | custom-call | tf_op jit(solution)/shard_map/experts_backward/pallas_call | solution.py:491
  533.8 35.3 %exchange_8.1 = f32[32,1664]{1,0:T(8,128)} custom-call(bf16[4,2,2,2,32,1664]{5,4,3,2,1,0:T(8,128)(2,1)} %bitcast.247), custom_call_target="tpu_custom_call" | custom-call | bytes 72417280 | tf_op jit(solution)/shard_map/exchange_8/pallas_call | solution.py:329
  570.8 1.9 multiply_reduce_fusion.14
  573.5 3.8 fusion.18
  579.4 5.0 all-to-all-start.1
  587.7 6.2 fusion.50
  594.1 2.5 fusion.45
  598.1 2.9 multiply_reduce_fusion.5
  601.1 1.5 add_add_fusion
  605.0 5.8 convolution_convert_fusion.1
  610.8 5.6 convolution_convert_fusion
  616.5 162.1 %exchange_9.1 = (bf16[4,2,2,2,256,384]{5,4,3,2,1,0:T(8,128)(2,1)}, f32[48,2176]{1,0:T(8,128)}, f32[48,2176]{1,0:T(8,128)}) custom-call(bf16[4,256,384]{2,1,0:T(8,128)(2,1)} %pad_maximum_fusion.5.refs_0_, bf16[4,2,2,2,48,2176]{5,4,3,2,1,0:T(8,128)(2,1)} %bitcast.238, bf16[4,2,2,2,48,2176]{5,4,3,2,1,0:T(8,128)(2,1)} %bitcast.239), custom_call_target="tpu_custom_call" | custom-call | bytes 425656320 | tf_op jit(solution)/shard_map/exchange_9/pallas_call | solution.py:329
  779.7 2.0 multiply_reduce_fusion.19
  783.0 1.4 multiply_reduce_fusion.20
  786.7 6.3 fusion.130.grad_ref
  793.0 13.5 %in_moments.1 = (f32[12288,128]{1,0:T(8,128)}, f32[12288,128]{1,0:T(8,128)}, f32[2,8,128]{2,1,0:T(8,128)S(1)}) custom-call(f32[2]{0:T(128)S(1)} %pad_maximum_fusion.10.scale_ref, f32[1536,1024]{1,0:T(8,128)S(1)} %fusion.130.grad_ref, f32[12288,128]{1,0:T(8,128)S(1)} %bitcast.224, f32[12288,128]{1,0:T(8,128)} %bitcast.240, f32[12288,128]{1,0:T(8,128)} %bitcast.241), custom_call_target="tpu_custom_call" | custom-call | tf_op jit(solution)/shard_map/in_moments/pallas_call | solution.py:550
  806.6 4.2 fusion.131
  811.7 4.8 multiply_reduce_fusion.4
  816.5 2.6 maximum_bitcast_fusion.9
  819.2 1.6 multiply_reduce_fusion.12
  820.8 2.7 maximum_bitcast_fusion.7
  823.5 1.9 multiply_reduce_fusion.10
  825.4 27.2 %scatter_rows.1 = f32[6144,384]{1,0:T(8,128)} custom-call(s32[32,256]{1,0:T(8,128)S(1)} %fusion.85.list_ref, s32[32]{0:T(128)S(1)} %get-tuple-element.220.count_ref, bf16[32,256,384]{2,1,0:T(8,128)(2,1)} %bitcast.244, bf16[6144,384]{1,0:T(8,128)(2,1)} %bitcast.69.head_ref), custom_call_target="tpu_custom_call" | custom-call | tf_op jit(solution)/shard_map/scatter_rows/pallas_call | solution.py:663
  852.6 22.6 %multiply_reduce_fusion.1 = (f32[]{:T(128)}, f32[]{:T(128)}, f32[6144,384]{1,0:T(8,128)}, f32[6144,384]{1,0:T(8,128)}) fusion(f32[6144,384]{1,0:T(8,128)} %table_ref.1, f32[]{:T(128)} %div.140, f32[]{:T(128)} %div.139, f32[6144,384]{1,0:T(8,128)} %scatter_rows.1, f32[6144,384]{1,0:T(8,128)} %param.34, f32[6144,384]{1,0:T(8,128)} %param.35), kind=kLoop, calls=%fused_computation.10 | loop fusion | flops 40108032 | bytes 56623120 | tf_op jit(solution)/shard_map/reduce_sum | solution.py:1047
  875.2 2.7 maximum_bitcast_fusion.5
  878.5 15.5 %exchange_10.1 = f32[4,8,8,128]{3,2,1,0:T(8,128)} custom-call(f32[8,128]{1,0:T(8,128)} %pad.46.refs_0_), custom_call_target="tpu_custom_call" | custom-call | bytes 2703360 | tf_op jit(solution)/shard_map/exchange_10/pallas_call | solution.py:329
  903.2 1.9 multiply_subtract_fusion.4
  905.2 2.4 multiply_subtract_fusion.3
  907.5 6.5 multiply_subtract_fusion.2
  914.1 8.1 multiply_subtract_fusion.1
  922.2 1.2 slice-done.4
  923.4 1.2 slice-done.5
  925.1 10.9 %multiply_subtract_fusion = f32[6144,384]{1,0:T(8,128)} fusion(f32[6144,384]{1,0:T(8,128)S(1)} %bitcast.230, f32[]{:T(128)} %bitcast.94, f32[6144,384]{1,0:T(8,128)} %get-tuple-element.211, f32[]{:T(128)} %div.140, f32[6144,384]{1,0:T(8,128)S(1)} %bitcast.232, f32[]{:T(128)} %div.139), kind=kLoop, calls=%fused_computation.6 | loop fusion | flops 18874368 | bytes 37748748 | tf_op jit(solution)/shard_map/sub | solution.py:1060
  (363 shorter events, 53.1 us)
Async XLA Ops:
  18.7 10.4 %copy-start.19 = (bf16[48,2560]{1,0:T(8,128)(2,1)}, bf16[48,2560]{1,0:T(8,128)(2,1)S(1)}, u32[]{:S(2)}) copy-start(bf16[48,2560]{1,0:T(8,128)(2,1)S(1)} %convert.50) | copy-start | bytes 737284
  34.0 17.4 %slice-start.10 = ((bf16[48,2560]{1,0:T(8,128)(2,1)}), bf16[48,512]{1,0:T(8,128)(2,1)S(1)}, s32[]{:S(2)}) async-start(bf16[48,2560]{1,0:T(8,128)(2,1)} %copy-done.19), calls=%async_computation.12 | async-start | bytes 98304 | tf_op jit(solution)/shard_map/slice | solution.py:797
  34.0 18.1 %slice-start.11 = ((bf16[48,2560]{1,0:T(8,128)(2,1)}), bf16[48,2048]{1,0:T(8,128)(2,1)S(1)}, s32[]{:S(2)}) async-start(bf16[48,2560]{1,0:T(8,128)(2,1)} %copy-done.19), calls=%async_computation.13 | async-start | bytes 393216 | tf_op jit(solution)/shard_map/slice | solution.py:788
  161.5 5.5 copy-start.87
  161.5 9.9 %copy-start.92 = (f32[3,48]{1,0:T(4,128)S(1)}, f32[3,48]{1,0:T(4,128)}, u32[]{:S(2)}) copy-start(f32[3,48]{1,0:T(4,128)} %param.46) | copy-start | bytes 1732
  161.5 9.9 %copy-start.93 = (f32[3,48]{1,0:T(4,128)S(1)}, f32[3,48]{1,0:T(4,128)}, u32[]{:S(2)}) copy-start(f32[3,48]{1,0:T(4,128)} %param.47) | copy-start | bytes 1732
  161.5 12.0 %copy-start.80 = (f32[48,32]{0,1:T(8,128)S(1)}, f32[48,32]{0,1:T(8,128)}, u32[]{:S(2)}) copy-start(f32[48,32]{0,1:T(8,128)} %param.43) | copy-start | bytes 18436
  161.5 12.7 %copy-start.81 = (f32[48,32]{0,1:T(8,128)S(1)}, f32[48,32]{0,1:T(8,128)}, u32[]{:S(2)}) copy-start(f32[48,32]{0,1:T(8,128)} %param.44) | copy-start | bytes 18436
  161.5 13.4 %copy-start.24 = (bf16[4,256,384]{2,1,0:T(8,128)(2,1)S(1)}, bf16[4,256,384]{2,1,0:T(8,128)(2,1)}, u32[]{:S(2)}) copy-start(bf16[4,256,384]{2,1,0:T(8,128)(2,1)} %get-tuple-element.43) | copy-start | bytes 2359300
  161.5 225.1 %all-to-all-start = ((bf16[4,1536,384]{2,1,0:T(8,128)(2,1)}), bf16[4,1536,384]{2,1,0:T(8,128)(2,1)}, u32[]{:S(2)}, u32[]{:S(2)}) async-start(bf16[4,1536,384]{2,1,0:T(8,128)(2,1)} %bitcast.233), calls=%async_computation | async-start | bytes 9437184 | tf_op jit(solution)/shard_map/all_to_all | solution.py:816
  175.0 423.1 %copy-start.6 = (bf16[256,384]{1,0:T(8,128)(2,1)}, bf16[256,384]{1,0:T(8,128)(2,1)S(1)}, u32[]{:S(2)}) copy-start(bf16[256,384]{1,0:T(8,128)(2,1)S(1)} %get-tuple-element.238) | copy-start | bytes 589828
  175.0 423.1 %copy-start.7 = (bf16[256,384]{1,0:T(8,128)(2,1)}, bf16[256,384]{1,0:T(8,128)(2,1)S(1)}, u32[]{:S(2)}) copy-start(bf16[256,384]{1,0:T(8,128)(2,1)S(1)} %get-tuple-element.239) | copy-start | bytes 589828
  179.1 18.7 %copy-start.56 = (f32[1536]{0:T(1024)}, f32[1536]{0:T(1024)S(1)}, u32[]{:S(2)}) copy-start(f32[1536]{0:T(1024)S(1)} %get-tuple-element.185) | copy-start | bytes 18436
  179.4 7.4 copy-start.25
  181.8 10.3 %copy-start.44 = (bf16[256,512]{0,1:T(8,128)(2,1)}, bf16[256,512]{0,1:T(8,128)(2,1)S(1)}, u32[]{:S(2)}) copy-start(bf16[256,512]{0,1:T(8,128)(2,1)S(1)} %copy.188) | copy-start | bytes 786436
  190.4 388.2 %copy-start.20 = (bf16[32,24,32]{2,0,1:T(8,128)(2,1)}, bf16[32,24,32]{2,0,1:T(8,128)(2,1)S(1)}, u32[]{:S(2)}) copy-start(bf16[32,24,32]{2,0,1:T(8,128)(2,1)S(1)} %copy.190) | copy-start | bytes 147460
  197.8 127.4 %copy-start.99 = (f32[32]{0:T(128)}, f32[32]{0:T(128)S(1)}, u32[]{:S(2)}) copy-start(f32[32]{0:T(128)S(1)} %get-tuple-element.277) | copy-start | bytes 388
  197.8 127.4 %copy-start.90 = (f32[32]{0:T(128)}, f32[32]{0:T(128)S(1)}, u32[]{:S(2)}) copy-start(f32[32]{0:T(128)S(1)} %fusion.94) | copy-start | bytes 388
  325.1 30.1 %copy-start.50 = (f32[1536]{0:T(1024)S(1)}, f32[1536]{0:T(1024)}, u32[]{:S(2)}) copy-start(f32[1536]{0:T(1024)} %get-tuple-element.184) | copy-start | bytes 18436
  325.1 60.3 %copy-start.94 = (s32[16,2]{0,1:T(2,128)S(1)}, s32[16,2]{0,1:T(2,128)}, u32[]{:S(2)}) copy-start(s32[16,2]{0,1:T(2,128)} %param.29) | copy-start | bytes 388
  355.2 30.1 %copy-start.95 = (f32[32]{0:T(128)}, f32[32]{0:T(128)S(1)}, u32[]{:S(2)}) copy-start(f32[32]{0:T(128)S(1)} %get-tuple-element.216) | copy-start | bytes 388
  355.3 34.3 %copy-start.88 = (f32[32]{0:T(128)}, f32[32]{0:T(128)S(1)}, u32[]{:S(2)}) copy-start(f32[32]{0:T(128)S(1)} %fusion.95) | copy-start | bytes 388
  385.4 9.7 %copy-start.70 = (s32[1536]{0:T(1024)}, s32[1536]{0:T(1024)S(1)}, u32[]{:S(2)}) copy-start(s32[1536]{0:T(1024)S(1)} %iota_add_fusion) | copy-start | bytes 18436
  389.6 5.5 copy-start.15
  415.5 11.2 %copy-start.12 = (bf16[4,2,2,2,32,1536]{5,4,3,2,1,0:T(8,128)(2,1)S(1)}, bf16[4,2,2,2,32,1536]{5,4,3,2,1,0:T(8,128)(2,1)}, u32[]{:S(2)}) copy-start(bf16[4,2,2,2,32,1536]{5,4,3,2,1,0:T(8,128)(2,1)} %exchange_4.1) | copy-start | bytes 9437188
  415.5 11.2 %copy-start.71 = (s32[1536]{0:T(1024)S(1)}, s32[1536]{0:T(1024)}, u32[]{:S(2)}) copy-start(s32[1536]{0:T(1024)} %copy-done.70) | copy-start | bytes 18436
  415.5 11.2 %copy-start.76 = (s32[1024]{0:T(1024)S(1)}, s32[1024]{0:T(1024)}, u32[]{:S(2)}) copy-start(s32[1024]{0:T(1024)} %eq.98) | copy-start | bytes 12292
  468.3 5.5 copy-start.96
  533.8 37.0 %copy-start.57 = (f32[1536]{0:T(1024)S(1)}, f32[1536]{0:T(1024)}, u32[]{:S(2)}) copy-start(f32[1536]{0:T(1024)} %copy-done.56) | copy-start | bytes 18436
  533.8 37.0 %copy-start.91 = (f32[32]{0:T(128)S(1)}, f32[32]{0:T(128)}, u32[]{:S(2)}) copy-start(f32[32]{0:T(128)} %copy-done.90) | copy-start | bytes 388
  533.8 38.9 %copy-start.100 = (f32[32]{0:T(128)S(1)}, f32[32]{0:T(128)}, u32[]{:S(2)}) copy-start(f32[32]{0:T(128)} %copy-done.99) | copy-start | bytes 388
  579.4 246.1 %all-to-all-start.1 = ((bf16[4,1536,384]{2,1,0:T(8,128)(2,1)}), bf16[4,1536,384]{2,1,0:T(8,128)(2,1)}, u32[]{:S(2)}, u32[]{:S(2)}) async-start(bf16[4,1536,384]{2,1,0:T(8,128)(2,1)} %pad_maximum_fusion.1), calls=%async_computation.1 | async-start | bytes 9437184 | tf_op jit(solution)/shard_map/all_to_all | solution.py:913
  587.7 6.3 copy-start.21
  587.7 6.3 copy-start.31
  587.7 6.3 copy-start.34
  587.7 6.3 copy-start.48
  587.7 6.3 copy-start.74
  605.0 5.8 copy-start.38
  605.0 5.8 copy-start.61
  605.0 5.8 copy-start.98
  616.5 163.2 %copy-start.62 = (f32[3,48]{0,1:T(8,128)S(1)}, f32[3,48]{0,1:T(8,128)}, u32[]{:S(2)}) copy-start(f32[3,48]{0,1:T(8,128)} %copy.206) | copy-start | bytes 1732
  616.5 163.2 %copy-start.63 = (f32[3,48]{0,1:T(8,128)S(1)}, f32[3,48]{0,1:T(8,128)}, u32[]{:S(2)}) copy-start(f32[3,48]{0,1:T(8,128)} %copy.205) | copy-start | bytes 1732
  616.5 163.2 %copy-start.64 = (f32[3,48]{0,1:T(8,128)S(1)}, f32[3,48]{0,1:T(8,128)}, u32[]{:S(2)}) copy-start(f32[3,48]{0,1:T(8,128)} %copy.207) | copy-start | bytes 1732
  616.5 166.6 %copy-start.58 = (f32[48,32]{1,0:T(8,128)S(1)}, f32[48,32]{1,0:T(8,128)}, u32[]{:S(2)}) copy-start(f32[48,32]{1,0:T(8,128)} %copy.200) | copy-start | bytes 18436
  616.5 166.6 %copy-start.59 = (f32[48,32]{1,0:T(8,128)S(1)}, f32[48,32]{1,0:T(8,128)}, u32[]{:S(2)}) copy-start(f32[48,32]{1,0:T(8,128)} %copy.202) | copy-start | bytes 18436
  786.7 6.3 slice-start
  786.7 6.3 slice-start.1
  811.6 7.5 copy-start.14
  811.6 7.5 copy-start.41
  811.6 7.5 copy-start.42
  811.6 7.5 copy-start.43
  811.6 11.8 %copy-start.8 = (f32[48,2560]{1,0:T(8,128)S(1)}, f32[48,2560]{1,0:T(8,128)}, u32[]{:S(2)}) copy-start(f32[48,2560]{1,0:T(8,128)} %param.36) | copy-start | bytes 1474564
  811.7 11.8 %copy-start.35 = (f32[48,2560]{1,0:T(8,128)S(1)}, f32[48,2560]{1,0:T(8,128)}, u32[]{:S(2)}) copy-start(f32[48,2560]{1,0:T(8,128)} %param.37) | copy-start | bytes 1474564
  811.7 11.8 %copy-start.36 = (f32[48,2560]{1,0:T(8,128)S(1)}, f32[48,2560]{1,0:T(8,128)}, u32[]{:S(2)}) copy-start(f32[48,2560]{1,0:T(8,128)} %param.38) | copy-start | bytes 1474564
  894.0 13.5 %copy-start.4 = (f32[4,128,1536]{2,1,0:T(8,128)S(1)}, f32[4,128,1536]{2,1,0:T(8,128)}, u32[]{:S(2)}) copy-start(f32[4,128,1536]{2,1,0:T(8,128)} %down_ref.3) | copy-start | bytes 9437188
  907.5 6.5 slice-start.2
  907.5 6.5 slice-start.3
  907.5 14.7 %slice-start.7 = ((s8[9437184]{0:T(1024)(128)(4,1)}), s8[4194304]{0:T(1024)(128)(4,1)S(1)}, s32[]{:S(2)}) async-start(s8[9437184]{0:T(1024)(128)(4,1)} %bitcast.231), calls=%async_computation.9 | async-start | bytes 8388608
  914.0 8.2 slice-start.8
  914.0 9.4 %slice-start.4 = ((s8[9437184]{0:T(1024)(128)(4,1)}), s8[4194304]{0:T(1024)(128)(4,1)S(1)}, s32[]{:S(2)}) async-start(s8[9437184]{0:T(1024)(128)(4,1)} %bitcast.229), calls=%async_computation.6 | async-start | bytes 8388608
  914.0 10.6 %slice-start.5 = ((s8[9437184]{0:T(1024)(128)(4,1)}), s8[4194304]{0:T(1024)(128)(4,1)S(1)}, s32[]{:S(2)}) async-start(s8[9437184]{0:T(1024)(128)(4,1)} %bitcast.229), calls=%async_computation.7 | async-start | bytes 8388608
  914.1 10.8 %slice-start.6 = ((s8[9437184]{0:T(1024)(128)(4,1)}), s8[1048576]{0:T(1024)(128)(4,1)S(1)}, s32[]{:S(2)}) async-start(s8[9437184]{0:T(1024)(128)(4,1)} %bitcast.229), calls=%async_computation.8 | async-start | bytes 2097152
  914.1 11.1 %slice-start.9 = ((s8[9437184]{0:T(1024)(128)(4,1)}), s8[1048576]{0:T(1024)(128)(4,1)S(1)}, s32[]{:S(2)}) async-start(s8[9437184]{0:T(1024)(128)(4,1)} %bitcast.231), calls=%async_computation.11 | async-start | bytes 2097152
  925.1 10.9 %copy-start.1 = (s32[256,8]{0,1:T(8,128)S(1)}, s32[256,8]{0,1:T(8,128)}, u32[]{:S(2)}) copy-start(s32[256,8]{0,1:T(8,128)} %param.31) | copy-start | bytes 24580
  (51 other events, 148.2 us)

commit v3 on v2

--- a/solution.py
+++ b/solution.py
@@ -303,6 +303,45 @@
         return pipeline(self.groups, stage, 4)
 
 
+class Swap:
+    flat = False
+    scratch = (pltpu.SemaphoreType.DMA(()),)
+    spaces = (pl.ANY,)
+
+    def __init__(self, x, start, size, planes, side, rounds, back=False):
+        self.planes, self.side, self.inputs = planes, side, [x]
+        self.begin, self.size, self.rounds, self.back = start, size, rounds, back
+        self.columns = x.shape[1] // planes if back else x.shape[1]
+        shape = (planes, size, self.columns) if back else (size, planes * self.columns)
+        self.outputs = [jax.ShapeDtypeStruct(shape, x.dtype)]
+        self.copies = planes - 1
+
+    def steps(self, spot, mail, x, out, own_sem):
+        def block(z):
+            return pl.ds(pl.multiple_of(z * self.columns, 128), self.columns)
+
+        def source(z):
+            if self.back:
+                return x.at[pl.ds(self.begin, self.size), block(z)]
+            first = z * (x.shape[0] // self.planes) + self.begin
+            return x.at[pl.ds(pl.multiple_of(first, 16), self.size), :]
+
+        for _ in range(self.rounds):
+            yield
+        place = out.at[spot.z] if self.back else out.at[:, block(spot.z)]
+        sent = []
+        for k in range(1, self.planes):
+            peer, target = spot.plane(k)
+            sent.append(mail.start(source(peer), place, target))
+        own = pltpu.make_async_copy(source(spot.z), place, own_sem)
+        own.start()
+        for _ in range(20):
+            yield
+        own.wait()
+        for copy in sent:
+            copy.wait_recv()
+
+
 def communicate(parts, ident):
     planes, side = parts[0].planes, parts[0].side
     counts = [(len(p.inputs), len(p.outputs), len(p.scratch)) for p in parts]
@@ -326,10 +365,14 @@
         mail.finish()
 
     size = sum(x.size * x.dtype.itemsize for p in parts for x in p.inputs + p.outputs)
-    return pl.pallas_call(
+    out = pl.pallas_call(
         kernel,
         out_shape=[x for p in parts for x in p.outputs],
-        in_specs=[pl.BlockSpec(memory_space=pltpu.VMEM)] * n_in,
+        in_specs=[
+            pl.BlockSpec(memory_space=space)
+            for p in parts
+            for space in getattr(p, "spaces", (pltpu.VMEM,) * len(p.inputs))
+        ],
         out_specs=[pl.BlockSpec(memory_space=pltpu.VMEM)] * n_out,
         scratch_shapes=[s for p in parts for s in p.scratch]
         + [pltpu.SemaphoreType.DMA((copies,)), pltpu.SemaphoreType.DMA((copies,))],
@@ -339,29 +382,26 @@
         cost_estimate=pl.CostEstimate(flops=0, bytes_accessed=20 * size, transcendentals=0),
         name="exchange_" + str(ident),
     )(*[x for p in parts for x in p.inputs])
-
-def expert_weights(in_ref, cat_ref):
+    return list(out)
+
+def expert_gate(gates, lane):
+    lanes = lax.broadcasted_iota(jnp.int32, gates.shape, 1)
+    return jnp.sum(jnp.where(lanes == lane, gates, 0.0), axis=1, keepdims=True)
+
+
+CHUNK = 512
+BLOCK = 1024
+ACROSS = (((1,), (1,)), ((), ()))
+
+
+def forward_kernel(
+    lane_ref, rows_ref, routes_ref, router_ref, in_ref, down_ref, out_ref, mid_ref, gates_ref, cat_ref, down_out, hidden_ref
+):
+    e, number = pl.program_id(1), pl.num_programs(1)
     units = in_ref.shape[1]
     for j in range(2):
         cat_ref[:, j * units : (j + 1) * units] = in_ref[pl.ds(j, D, stride=2), :].astype(bf16)
-
-
-def expert_gate(gates, lane):
-    lanes = lax.broadcasted_iota(jnp.int32, gates.shape, 1)
-    return jnp.sum(jnp.where(lanes == lane, gates, 0.0), axis=1, keepdims=True)
-
-
-CHUNK = 256
-BLOCK = 1024
-
-
-def forward_kernel(
-    lane_ref, rows_ref, routes_ref, router_ref, in_ref, down_ref, out_ref, mid_ref, gates_ref, sums, cat
-):
-    e = pl.program_id(1)
-    units = in_ref.shape[1]
-    expert_weights(in_ref, cat)
-    down = down_ref[0].astype(bf16)
+    down_out[pl.ds(pl.multiple_of(e * units, units), units), :] = down_ref[0].astype(bf16)
 
     def chunk(i, carry):
         here = pl.ds(pl.multiple_of(i * CHUNK, CHUNK), CHUNK)
@@ -378,24 +418,18 @@
             weight = jnp.where(mask, jnp.exp(jnp.where(mask, logits - top, 0.0)), 0.0)
             gates_ref[here, :] = weight / jnp.sum(weight, axis=1, keepdims=True)
 
-        mid = jnp.dot(rows, cat[...], preferred_element_type=f32)
+        mid = jnp.dot(rows, cat_ref[...], preferred_element_type=f32)
         mid_ref[here, :] = mid
         gate, up = mid[:, :units], mid[:, units:]
         hidden = (gate * jax.nn.sigmoid(gate) * up).astype(bf16).astype(f32)
         hidden = (hidden * expert_gate(gates_ref[here, :], lane_ref[0] + e)).astype(bf16)
-        part = jnp.dot(hidden, down, preferred_element_type=f32)
-
-        @pl.when(e == 0)
+        hidden_ref[here, pl.ds(pl.multiple_of(e * units, units), units)] = hidden
+
+        @pl.when(e == number - 1)
         def _():
-            sums[here, :] = part
-
-        @pl.when(e > 0)
-        def _():
-            sums[here, :] += part
-
-        @pl.when(e == pl.num_programs(1) - 1)
-        def _():
-            out_ref[here, :] = sums[here, :].astype(bf16)
+            out_ref[here, :] = jnp.dot(
+                hidden_ref[here, :], down_out[...], preferred_element_type=f32
+            ).astype(bf16)
 
         return carry
 
@@ -406,119 +440,112 @@
     number, units = down.shape[:2]
     total = rows.shape[0]
     block = min(total, BLOCK)
+    row = lambda r, e, *_: (r, 0)
+    still = lambda r, e, *_: (0, 0)
     return pl.pallas_call(
         forward_kernel,
         grid_spec=pltpu.PrefetchScalarGridSpec(
             num_scalar_prefetch=1,
             grid=(total // block, number),
             in_specs=[
-                pl.BlockSpec((block, D), lambda r, e, *_: (r, 0)),
-                pl.BlockSpec((block, TOP), lambda r, e, *_: (r, 0)),
-                pl.BlockSpec((D, 128), lambda r, e, *_: (0, 0)),
+                pl.BlockSpec((block, D), row),
+                pl.BlockSpec((block, TOP), row),
+                pl.BlockSpec((D, 128), still),
                 pl.BlockSpec((2 * D, units), lambda r, e, *_: (e, 0)),
                 pl.BlockSpec((1, units, D), lambda r, e, *_: (e, 0, 0)),
             ],
             out_specs=[
-                pl.BlockSpec((block, D), lambda r, e, *_: (r, 0)),
+                pl.BlockSpec((block, D), row),
                 pl.BlockSpec((block, 2 * units), lambda r, e, *_: (r, e)),
-                pl.BlockSpec((block, 128), lambda r, e, *_: (r, 0)),
+                pl.BlockSpec((block, 128), row),
+                pl.BlockSpec((D, 2 * units), lambda r, e, *_: (0, e)),
+                pl.BlockSpec((number * units, D), still),
+                pl.BlockSpec((block, number * units), row),
             ],
-            scratch_shapes=[pltpu.VMEM((block, D), f32), pltpu.VMEM((D, 2 * units), bf16)],
         ),
         out_shape=[
             jax.ShapeDtypeStruct((total, D), bf16),
             jax.ShapeDtypeStruct((total, 2 * units * number), f32),
             jax.ShapeDtypeStruct((total, 128), f32),
+            jax.ShapeDtypeStruct((D, 2 * units * number), bf16),
+            jax.ShapeDtypeStruct((number * units, D), bf16),
+            jax.ShapeDtypeStruct((total, number * units), bf16),
         ],
-        compiler_params=pltpu.CompilerParams(vmem_limit_bytes=62 << 20),
+        compiler_params=pltpu.CompilerParams(vmem_limit_bytes=60 << 20),
         name="experts_forward",
     )(lane, rows, routes, router, in_rows, down)
 
 
 def backward_kernel(
-    lane_ref, grad_ref, mid_ref, gates_ref, in_ref, down_ref, out_ref, mid_grad_ref, hidden_ref, sums, cat, gate_sums
+    lane_ref, grad_ref, mid_ref, gates_ref, cat_ref, down_ref, out_ref, mid_grad_ref, pulled_ref
 ):
-    e = pl.program_id(1)
-    units = in_ref.shape[1]
-    expert_weights(in_ref, cat)
-    down = down_ref[0].astype(bf16)
-    across = (((1,), (1,)), ((), ()))
+    number = lane_ref.shape[0]
+    units = pulled_ref.shape[1] // number
 
     def chunk(i, carry):
         here = pl.ds(pl.multiple_of(i * CHUNK, CHUNK), CHUNK)
-        weight = expert_gate(gates_ref[here, :], lane_ref[0] + e)
-        mid = mid_ref[here, :]
-        gate, up = mid[:, :units], mid[:, units:]
-        soft = jax.nn.sigmoid(gate)
-        silu = gate * soft
-        hidden = (silu * up).astype(bf16).astype(f32)
-        hidden_ref[here, :] = (hidden * weight).astype(bf16)
-        pulled = lax.dot_general(grad_ref[here, :], down, across, preferred_element_type=f32)
-        gate_grad = jnp.sum(hidden * pulled, axis=1, keepdims=True)
-        hidden_grad = (pulled * weight).astype(bf16).astype(f32)
-        turned = jnp.concatenate(
-            [hidden_grad * up * (soft * (1.0 + gate * (1.0 - soft))), hidden_grad * silu], axis=1
+        pulled_ref[...] = lax.dot_general(
+            grad_ref[here, :], down_ref[...], ACROSS, preferred_element_type=f32
+        )
+        lanes = lax.broadcasted_iota(jnp.int32, (CHUNK, 128), 1)
+        gate_part = jnp.zeros((CHUNK, 128), f32)
+        for e in range(number):
+            lane = lane_ref[e]
+            weight = expert_gate(gates_ref[here, :], lane)
+            gate = mid_ref[here, 2 * e * units : (2 * e + 1) * units]
+            up = mid_ref[here, (2 * e + 1) * units : (2 * e + 2) * units]
+            pulled = pulled_ref[:, e * units : (e + 1) * units]
+            soft = jax.nn.sigmoid(gate)
+            silu = gate * soft
+            hidden = (silu * up).astype(bf16).astype(f32)
+            gate_grad = jnp.sum(hidden * pulled, axis=1, keepdims=True)
+            gate_part = jnp.where(lanes == lane, gate_grad, gate_part)
+            hidden_grad = (pulled * weight).astype(bf16).astype(f32)
+            turned = hidden_grad * up * (soft * (1.0 + gate * (1.0 - soft)))
+            mid_grad_ref[here, 2 * e * units : (2 * e + 1) * units] = turned.astype(bf16)
+            mid_grad_ref[here, (2 * e + 1) * units : (2 * e + 2) * units] = (
+                hidden_grad * silu
+            ).astype(bf16)
+        out_ref[here, D:] = gate_part.astype(bf16)
+        out_ref[here, :D] = lax.dot_general(
+            mid_grad_ref[here, :], cat_ref[...], ACROSS, preferred_element_type=f32
         ).astype(bf16)
-        mid_grad_ref[here, :] = turned
-        part = lax.dot_general(turned, cat[...], across, preferred_element_type=f32)
-        lanes = lax.broadcasted_iota(jnp.int32, (CHUNK, 128), 1)
-        gate_part = jnp.where(lanes == lane_ref[0] + e, gate_grad, 0.0)
-
-        @pl.when(e == 0)
-        def _():
-            sums[here, :] = part
-            gate_sums[here, :] = gate_part
-
-        @pl.when(e > 0)
-        def _():
-            sums[here, :] += part
-            gate_sums[here, :] += gate_part
-
-        @pl.when(e == pl.num_programs(1) - 1)
-        def _():
-            out_ref[here, :D] = sums[here, :].astype(bf16)
-            out_ref[here, D:] = gate_sums[here, :].astype(bf16)
-
         return carry
 
     lax.fori_loop(0, grad_ref.shape[0] // CHUNK, chunk, 0)
 
 
-def experts_backward(lane, grad, mid, gates, in_rows, down):
-    number, units = down.shape[:2]
+def experts_backward(lanes, grad, mid, gates, cat, down):
+    number = lanes.shape[0]
     total = grad.shape[0]
     block = min(total, BLOCK)
+    row = lambda r, *_: (r, 0)
+    still = lambda r, *_: (0, 0)
     return pl.pallas_call(
         backward_kernel,
         grid_spec=pltpu.PrefetchScalarGridSpec(
             num_scalar_prefetch=1,
-            grid=(total // block, number),
+            grid=(total // block,),
             in_specs=[
-                pl.BlockSpec((block, D), lambda r, e, *_: (r, 0)),
-                pl.BlockSpec((block, 2 * units), lambda r, e, *_: (r, e)),
-                pl.BlockSpec((block, 128), lambda r, e, *_: (r, 0)),
-                pl.BlockSpec((2 * D, units), lambda r, e, *_: (e, 0)),
-                pl.BlockSpec((1, units, D), lambda r, e, *_: (e, 0, 0)),
+                pl.BlockSpec((block, D), row),
+                pl.BlockSpec((block, mid.shape[1]), row),
+                pl.BlockSpec((block, 128), row),
+                pl.BlockSpec(cat.shape, still),
+                pl.BlockSpec(down.shape, still),
             ],
             out_specs=[
-                pl.BlockSpec((block, D + 128), lambda r, e, *_: (r, 0)),
-                pl.BlockSpec((block, 2 * units), lambda r, e, *_: (r, e)),
-                pl.BlockSpec((block, units), lambda r, e, *_: (r, e)),
+                pl.BlockSpec((block, D + 128), row),
+                pl.BlockSpec((block, mid.shape[1]), row),
             ],
-            scratch_shapes=[
-                pltpu.VMEM((block, D), f32),
-                pltpu.VMEM((D, 2 * units), bf16),
-                pltpu.VMEM((block, 128), f32),
-            ],
+            scratch_shapes=[pltpu.VMEM((CHUNK, down.shape[0]), f32)],
         ),
         out_shape=[
             jax.ShapeDtypeStruct((total, D + 128), bf16),
-            jax.ShapeDtypeStruct((total, 2 * units * number), bf16),
-            jax.ShapeDtypeStruct((total, units * number), bf16),
+            jax.ShapeDtypeStruct(mid.shape, bf16),
         ],
-        compiler_params=pltpu.CompilerParams(vmem_limit_bytes=62 << 20),
+        compiler_params=pltpu.CompilerParams(vmem_limit_bytes=60 << 20),
         name="experts_backward",
-    )(lane, grad, mid, gates, in_rows, down)
+    )(lanes, grad, mid, gates, cat, down)
 
 
 def moments_kernel(scale_ref, grad_ref, w_ref, first_ref, second_ref, new_first, new_second, norms):
@@ -732,14 +759,20 @@
             out for n, part in enumerate(parts) for out in communicate([part], ident + 20 * n)
         ]
 
-    def gather_completion(rows, ident):
+    unit = own_rows // 24
+
+    def swap(x, start, size, rounds, back=False):
+        return Swap(x, start * unit, size * unit, planes, side, rounds, back)
+
+    def gather_completion(rows, ident, *beside):
         part = Gather([rows], split(0, COMP, rows.shape[1], 2, 2), planes, side)
-        return communicate([part], ident)[0].reshape(rows_all, rows.shape[1])
-
-    def reduce_completion(rows, ident, cuts=2):
+        out = communicate([part, *beside], ident)
+        return (out[0].reshape(rows_all, rows.shape[1]), *out[1:])
+
+    def reduce_completion(rows, ident, cuts, *beside):
         rows = rows.reshape(grid + (COMP, rows.shape[1]))
         part = Reduce([rows], split(0, COMP, rows.shape[-1], 2, cuts), planes, side)
-        return communicate([part], ident)[0]
+        return communicate([part, *beside], ident)
 
     def gather_tiny(block, ident):
         return communicate([Tiny(block, planes, side)], ident)[0].reshape((devices,) + block.shape)
@@ -801,20 +834,17 @@
             axis=1,
         ).astype(bf16),
     ]
-    picked, first_pack, second_pack = send(
+    table_b = embed_table.astype(bf16)
+    picked, first_pack, second_pack, table_one = send(
         [
             Reduce([picked], embed_groups, planes, side, exchange=True),
             Gather(packs, weight_groups, planes, side),
+            swap(table_b, 0, 12, 3),
         ],
         1,
     )
     first_pack = first_pack.reshape(D, weight_cols)
     second_pack = second_pack.reshape(D, weight_cols)
-    table_sent, picked = lax.optimization_barrier(
-        (embed_table.astype(bf16).reshape(planes, own_rows, columns), picked)
-    )
-    table_own = lax.all_to_all(table_sent, "expert", split_axis=0, concat_axis=0, tiled=True)
-    table_own = jnp.concatenate([table_own[p] for p in range(planes)], axis=1)
     embedded = jnp.concatenate([picked[p] for p in range(planes)], axis=1).astype(f32)
     router_block = first_pack[:, head_cols + key_cols :]
     gains_value = router_block[:, EXPERTS : EXPERTS + 3].T.astype(f32)
@@ -863,18 +893,22 @@
     normed_two, norm_back_two = jax.vjp(norm_apply, resid, gains_value[1])
     normed_two_b = normed_two.astype(bf16)
 
-    expert_rows = gather_completion(normed_two_b, 2)
-    lane = (shard_id * local_experts).astype(jnp.int32).reshape(1)
+    expert_rows, table_two = gather_completion(normed_two_b, 2, swap(table_b, 12, 4, 2))
+    lanes = shard_id * local_experts + jnp.arange(local_experts, dtype=jnp.int32)
     in_rows = in_weight.reshape(-1, hidden_units)
-    produced, mid, gates = experts_forward(
-        lane, expert_rows, routes_all, router_block, in_rows, down_weight
+    produced, mid, gates, in_cat, down_b, gated_hidden = experts_forward(
+        lanes, expert_rows, routes_all, router_block, in_rows, down_weight
     )
     own_index = expert_id * shards + shard_id
     own_gates = lax.dynamic_slice(gates, (own_index * COMP, 0), (COMP, 128))[:, :EXPERTS]
-    resid_two = resid + reduce_completion(produced, 3)
+    combined, table_three = reduce_completion(produced, 3, 2, swap(table_b, 16, 4, 0))
+    resid_two = resid + combined
 
     final_rows, norm_back_three = jax.vjp(norm_apply, resid_two, gains_value[2])
-    head_rows = gather_completion(final_rows.astype(bf16), 4)
+    head_rows, table_four = gather_completion(
+        final_rows.astype(bf16), 4, swap(table_b, 20, 4, 2)
+    )
+    table_own = jnp.concatenate([table_one, table_two, table_three, table_four], axis=0)
     logits = jnp.einsum("rd,vd->rv", head_rows, table_own, preferred_element_type=f32) / LOGIT_SCALE
     own_base = vocab_base + expert_id * own_rows
     target_hot = targets[:, None] == own_base + jnp.arange(own_rows, dtype=jnp.int32)[None, :]
@@ -901,22 +935,19 @@
         row_grad[:, None] * (target_hot.astype(f32) - jnp.exp(logits - row_lse[:, None]))
     ).astype(bf16)
     grad_rows = jnp.dot(grad_logits, table_own, preferred_element_type=f32) / LOGIT_SCALE
-    own_grad_rows = reduce_completion(grad_rows.astype(bf16), 6)
-    grad_resid_two, grad_gain_three = norm_back_three(own_grad_rows)
-
-    grad_all = gather_completion(grad_resid_two.astype(bf16), 7)
     head_grad = (
         jnp.einsum("rv,rd->vd", grad_logits, head_rows, preferred_element_type=f32) / LOGIT_SCALE
     ).astype(bf16)
-    head_sent = jnp.stack([head_grad[:, p * columns : (p + 1) * columns] for p in range(planes)])
-    head_sent, grad_all = lax.optimization_barrier((head_sent, grad_all))
-    head_grad = lax.all_to_all(
-        head_sent, "expert", split_axis=0, concat_axis=0, tiled=True
-    ).reshape(vocab_rows, columns)
-    back, mid_grad, gated_hidden = experts_backward(
-        lane, grad_all, mid, gates, in_rows, down_weight
-    )
-    back = reduce_completion(back, 8, 1)
+    own_grad_rows, head_one = reduce_completion(
+        grad_rows.astype(bf16), 6, 2, swap(head_grad, 0, 5, 0, back=True)
+    )
+    grad_resid_two, grad_gain_three = norm_back_three(own_grad_rows)
+
+    grad_all, head_two = gather_completion(
+        grad_resid_two.astype(bf16), 7, swap(head_grad, 5, 5, 2, back=True)
+    )
+    back, mid_grad = experts_backward(lanes, grad_all, mid, gates, in_cat, down_b)
+    back, head_three = reduce_completion(back, 8, 1, swap(head_grad, 10, 5, 0, back=True))
     grad_gates = back[:, D : D + EXPERTS]
     grad_router_logits = own_gates * (
         grad_gates - jnp.sum(own_gates * grad_gates, axis=1, keepdims=True)
@@ -1004,15 +1035,20 @@
         .reshape(grid + (weight_rows, weight_cols))
         for left, right in ((first_left, first_right), (second_left, second_right))
     ]
-    sent, first_grad, second_grad = send(
+    sent, first_grad, second_grad, head_four = send(
         [
             Gather([grad_embedded], embed_groups, planes, side, exchange=True),
             Reduce(grad_packs, weight_groups, planes, side),
+            swap(head_grad, 15, 9, 3, back=True),
         ],
         9,
     )
+    head_grad = jnp.concatenate([head_one, head_two, head_three, head_four], axis=1)
     table_grad = scatter_rows(
-        lists, counts, sent.reshape(devices, SEQUENCE_TOKENS, columns), head_grad
+        lists,
+        counts,
+        sent.reshape(devices, SEQUENCE_TOKENS, columns),
+        head_grad.reshape(vocab_rows, columns),
     )
 
     step_value = step_count.astype(f32)
@@ -1044,12 +1080,17 @@
         for weight, moment_one, moment_two, gradient in zip(weights, firsts, seconds, gradients)
     ]
     partial_norms = [
-        jnp.stack([jnp.sum(weight * weight), jnp.sum(parts[2] * parts[2])])
+        (jnp.sum(weight * weight), jnp.sum(parts[2] * parts[2]))
         for weight, parts in zip(weights, moved)
     ]
-    partial_norms.insert(5, jnp.sum(in_norms, axis=(1, 2)))
-    partial_norms = jnp.pad(jnp.stack(partial_norms), ((0, 1), (0, 126)))
-    norm_values = jnp.sqrt(jnp.sum(gather_tiny(partial_norms, 10), axis=0))[:7, :2]
+    partial_norms.insert(5, (jnp.sum(in_norms[0]), jnp.sum(in_norms[1])))
+    norm_row = lax.broadcasted_iota(jnp.int32, (8, 128), 0)
+    norm_lane = lax.broadcasted_iota(jnp.int32, (8, 128), 1)
+    norm_block = jnp.zeros((8, 128), f32)
+    for n, pair in enumerate(partial_norms):
+        for lane, part in enumerate(pair):
+            norm_block = jnp.where((norm_row == n) & (norm_lane == lane), part, norm_block)
+    norm_values = jnp.sqrt(jnp.sum(gather_tiny(norm_block, 10), axis=0))[:7, :2]
     trust_ratio = norm_values[:, 0] / norm_values[:, 1]
     moved.insert(
         5, (in_first_new, in_second_new, lamb_update(in_rows, in_first_new, in_second_new, *scales))

time: 944 us -> 873 us (0.925)
  Pallas kernels: 672 us -> 581 us
  local copies, waits for them, and re-layouts: 46.4 us -> 61.9 us
  starting transfers between devices: 10.3 us -> 0 us
    pallas_call x11, Pallas kernels: 563 us -> 493 us  [communicate(): pl.pallas_call(kernel, out_shape=[x for p in parts for x in p.outputs], i...]
    reduce_sum x6 -> x1, other arithmetic: 33.9 us -> 1.4 us  [on_device(): jnp.sum(weight * weight)]
    reduce_sum x2 -> x5, other arithmetic: 3.42 us -> 32.4 us  [on_device(): jnp.sum(parts[2] * parts[2])]
    unnamed x236 -> x235, local copies, waits for them, and re-layouts: 18.8 us -> 32.6 us
    pallas_call x1, Pallas kernels: 25.7 us -> 13.4 us  [experts_backward(): pl.pallas_call(backward_kernel, grid_spec=pltpu.PrefetchScalarGridSpec(nu...]
    another operation x8 -> x4, other arithmetic: 14.6 us -> 2.3 us  [the longest x3 7.95 us: on_device(): partial_norms = jnp.pad(jnp.stack(partial_norms), ((0, 1), (0, 126)))]
    pallas_call x1, Pallas kernels: 28.6 us -> 18 us  [experts_forward(): pl.pallas_call(forward_kernel, grid_spec=pltpu.PrefetchScalarGridSpec(num...]
    all_to_all x2 -> x0, starting transfers between devices: 10.3 us -> none  [the longest x1 5.31 us: on_device(): lax.all_to_all(table_sent, 'expert', split_axis=0, concat_axis=0, tiled=T...]
  transfers between devices with their start and end apart: 2 -> 0, of which waited for: 0 -> 0; matrix products, arithmetic and copies ran while one was open for 10% -> 0% of each run, Pallas kernels for 38% -> 0%
where the time goes in v3:
time: 873 us; the launch traced here: 859 us
  Pallas kernels  581 us (67%)
  other arithmetic  124 us (14%)
  matrix products  83.2 us (10%)
  local copies, waits for them, and re-layouts  61.9 us (7%)
  between operations  9.75 us (1%)
    pallas_call x11, Pallas kernels, communicate(): pl.pallas_call(kernel, out_shape=[x for p in parts for x in p.outputs], i...  493 us
    unnamed x235, local copies, waits for them, and re-layouts  32.6 us
    reduce_sum x5, other arithmetic, on_device(): jnp.sum(parts[2] * parts[2])  32.4 us
    sub x7, other arithmetic, on_device(): weight - STEP_RATE * trust_ratio[place] * parts[2]  28.9 us
    pallas_call x1, Pallas kernels, scatter_rows(): pl.pallas_call(scatter_kernel, grid_spec=pltpu.PrefetchScalarGridSpec(num...  27.8 us
    pallas_call x1, Pallas kernels, experts_forward(): pl.pallas_call(forward_kernel, grid_spec=pltpu.PrefetchScalarGridSpec(num...  18 us

profile of v3, /device:TPU:0, one launch (start us, length us, event | category | flops | bytes accessed | tf_op | source)
XLA Modules:
  0.0 858.9 jit_solution(14754337440144430165)
XLA Ops:
  11.5 1.4 multiply_reduce_fusion.21
  16.0 1.4 copy.204
  17.4 1.4 copy.201
  18.8 1.4 copy.203
  22.0 13.3 %exchange_0.1 = s32[4,8,8,128]{3,2,1,0:T(8,128)} custom-call(s32[8,128]{1,0:T(8,128)} %add_bitcast_fusion.refs_0_), custom_call_target="tpu_custom_call" | custom-call | bytes 2703360 | tf_op jit(solution)/shard_map/exchange_0/pallas_call | solution.py:368
  37.4 4.8 select_reduce_fusion
  46.9 6.4 convert_element_type.175.refs_3_.refs_1_
  53.3 14.6 %gather_rows.1 = bf16[32,256,384]{2,1,0:T(8,128)(2,1)S(1)} custom-call(s32[32,256]{1,0:T(8,128)S(1)} %fusion.84.list_ref, s32[32]{0:T(128)S(1)} %get-tuple-element.246.count_ref, f32[6144,384]{1,0:T(8,128)} %table_ref.1), custom_call_target="tpu_custom_call" | custom-call | tf_op jit(solution)/shard_map/gather_rows/pallas_call | solution.py:653
  67.9 2.7 copy-done.2
  70.6 127.9 %exchange_1.1 = (bf16[4,256,384]{2,1,0:T(8,128)(2,1)}, bf16[4,2,2,2,48,2176]{5,4,3,2,1,0:T(8,128)(2,1)}, bf16[4,2,2,2,48,2176]{5,4,3,2,1,0:T(8,128)(2,1)}, bf16[768,1536]{1,0:T(8,128)(2,1)}) custom-call(bf16[4,2,2,2,256,384]{5,4,3,2,1,0:T(8,128)(2,1)} %bitcast.187, bf16[48,2176]{1,0:T(8,128)(2,1)} %concatenate.55.refs_1_, ...), custom_call_target="tpu_custom_call" | custom-call | bytes 558858240 | tf_op jit(solution)/shard_map/exchange_1/pallas_call | solution.py:368
  200.1 1.8 slice.236.router_ref
  204.4 2.3 fusion.46
  208.2 4.9 fusion.126
  215.3 1.5 fusion.49
  217.3 3.4 multiply_reduce_fusion.18
  221.5 29.5 %exchange_2.1 = (bf16[4,2,2,2,32,1536]{5,4,3,2,1,0:T(8,128)(2,1)}, bf16[256,1536]{1,0:T(8,128)(2,1)}) custom-call(bf16[32,1536]{1,0:T(8,128)(2,1)} %multiply_convert_fusion.4.refs_0_, bf16[6144,384]{1,0:T(8,128)(2,1)} %convert_element_type.175.refs_3_.refs_1_), custom_call_target="tpu_custom_call" | custom-call | bytes 174981120 | tf_op jit(solution)/shard_map/exchange_2/pallas_call | solution.py:368
  251.1 3.3 constant_dynamic-update-slice_fusion.3
  255.3 18.0 %experts_forward.1 = (bf16[1024,1536]{1,0:T(8,128)(2,1)}, f32[1024,1024]{1,0:T(8,128)}, f32[1024,128]{1,0:T(8,128)}, bf16[1536,1024]{1,0:T(8,128)(2,1)}, bf16[51...) custom-call(s32[4]{0:T(128)} %iota_add_fusion.2.lane_ref, bf16[1024,1536]{1,0:T(8,128)(2,1)} %bitcast.207, ...), custom_call_target="tpu_custom_call" | custom-call | tf_op jit(solution)/shard_map/experts_forward/pallas_call | solution.py:445
  273.4 35.7 %exchange_3.1 = (f32[32,1536]{1,0:T(8,128)}, bf16[256,1536]{1,0:T(8,128)(2,1)}) custom-call(bf16[4,2,2,2,32,1536]{5,4,3,2,1,0:T(8,128)(2,1)} %bitcast.211, bf16[6144,384]{1,0:T(8,128)(2,1)} %convert_element_type.175.refs_3_.refs_1_), custom_call_target="tpu_custom_call" | custom-call | bytes 176947200 | tf_op jit(solution)/shard_map/exchange_3/pallas_call | solution.py:368
  309.0 2.1 constant_dynamic-update-slice_fusion.1
  311.1 2.3 copy.218
  314.3 29.4 %exchange_4.1 = (bf16[4,2,2,2,32,1536]{5,4,3,2,1,0:T(8,128)(2,1)}, bf16[256,1536]{1,0:T(8,128)(2,1)}) custom-call(bf16[32,1536]{1,0:T(8,128)(2,1)} %multiply_convert_fusion.3.refs_0_, bf16[6144,384]{1,0:T(8,128)(2,1)} %convert_element_type.175.refs_3_.refs_1_), custom_call_target="tpu_custom_call" | custom-call | bytes 174981120 | tf_op jit(solution)/shard_map/exchange_4/pallas_call | solution.py:368
  343.7 2.1 constant_dynamic-update-slice_fusion
  345.8 8.3 multiply_reduce_fusion.2
  354.1 3.1 exponential_reduce_fusion
  357.8 15.5 %exchange_5.1 = f32[4,8,8,384]{3,2,1,0:T(8,128)} custom-call(f32[8,384]{1,0:T(8,128)} %reshape.426.refs_0_), custom_call_target="tpu_custom_call" | custom-call | bytes 8110080 | tf_op jit(solution)/shard_map/exchange_5/pallas_call | solution.py:368
  373.3 2.0 reshape_reshape.7
  375.3 2.0 fusion.122
  386.3 10.9 %multiply_convert_fusion = bf16[1024,1536]{1,0:T(8,128)(2,1)} fusion(bf16[1536,1536]{1,0:T(8,128)(2,1)} %constant_dynamic-update-slice_fusion, f32[1024,1536]{1,0:T(8,128)} %copy-done.6, f32[1024]{0:T(1024)} %get-tuple-element.241, f32[1024]{0:T(1024)} %mul.949, s32[1536]{0:T(1024)} %copy-done.61, s32[1024]{0:T(1024)S(1)} %eq.191), kind=kOutput, calls=%fused_computation.22 | convolution fusion | flops 4845993984 | bytes 14174208 | tf_op jit(solution)/shard_map/dot_general | solution.py:937
  397.2 8.2 fusion.3.refs_1_.refs_3_
  405.4 37.8 %exchange_6.1 = (f32[32,1536]{1,0:T(8,128)}, bf16[4,320,384]{2,1,0:T(8,128)(2,1)}) custom-call(bf16[4,2,2,2,32,1536]{5,4,3,2,1,0:T(8,128)(2,1)} %bitcast.212, bf16[1536,1536]{1,0:T(8,128)(2,1)} %fusion.3.refs_1_.refs_3_), custom_call_target="tpu_custom_call" | custom-call | bytes 180879360 | tf_op jit(solution)/shard_map/exchange_6/pallas_call | solution.py:368
  445.0 1.7 fusion.85.refs_0_
  446.6 32.2 %exchange_7.1 = (bf16[4,2,2,2,32,1536]{5,4,3,2,1,0:T(8,128)(2,1)}, bf16[4,320,384]{2,1,0:T(8,128)(2,1)}) custom-call(bf16[32,1536]{1,0:T(8,128)(2,1)} %fusion.85.refs_0_, bf16[1536,1536]{1,0:T(8,128)(2,1)} %fusion.3.refs_1_.refs_3_), custom_call_target="tpu_custom_call" | custom-call | bytes 178913280 | tf_op jit(solution)/shard_map/exchange_7/pallas_call | solution.py:368
  478.9 13.4 %experts_backward.1 = (bf16[1024,1664]{1,0:T(8,128)(2,1)}, bf16[1024,1024]{1,0:T(8,128)(2,1)}) custom-call(s32[4]{0:T(128)} %iota_add_fusion.2.lane_ref, bf16[1024,1536]{1,0:T(8,128)(2,1)} %bitcast.209, f32[1024,1024]{1,0:T(8,128)} %get-tuple-element.68.mid_ref, f32[1024,128]{1,0:T(8,128)} %get-tuple-element.69.gates_ref, ...), custom_call_target="tpu_custom_call" | custom-call | tf_op jit(solution)/shard_map/experts_backward/pallas_call | solution.py:524
  492.3 39.7 %exchange_8.1 = (f32[32,1664]{1,0:T(8,128)}, bf16[4,320,384]{2,1,0:T(8,128)(2,1)}) custom-call(bf16[4,2,2,2,32,1664]{5,4,3,2,1,0:T(8,128)(2,1)} %bitcast.206, bf16[1536,1536]{1,0:T(8,128)(2,1)} %fusion.3.refs_1_.refs_3_), custom_call_target="tpu_custom_call" | custom-call | bytes 186449920 | tf_op jit(solution)/shard_map/exchange_8/pallas_call | solution.py:368
  533.7 1.4 multiply_reduce_fusion.14
  536.7 3.8 fusion.18
  541.5 3.1 fusion.45
  550.8 5.3 fusion.50
  556.2 2.4 multiply_reduce_fusion.5
  563.4 5.4 fusion.127.grad_ref
  568.9 5.8 convolution_convert_fusion.1
  574.7 5.6 convolution_convert_fusion
  580.3 119.8 %exchange_9.1 = (bf16[4,2,2,2,256,384]{5,4,3,2,1,0:T(8,128)(2,1)}, f32[48,2176]{1,0:T(8,128)}, f32[48,2176]{1,0:T(8,128)}, bf16[4,576,384]{2,1,0:T(8,128)(2,1)}) custom-call(bf16[4,256,384]{2,1,0:T(8,128)(2,1)} %pad_maximum_fusion.2.refs_0_, bf16[4,2,2,2,48,2176]{5,4,3,2,1,0:T(8,128)(2,1)} %bitcast.195, bf16[4,2,2,2,48,2176]{5,4,3,2,1,0:T(8,128)(2,1)} %bitcast.196, ...), custom_call_target="tpu_custom_call" | custom-call | bytes 555417600 | tf_op jit(solution)/shard_map/exchange_9/pallas_call | solution.py:368
  700.2 2.2 multiply_reduce_fusion.20
  702.5 1.9 multiply_reduce_fusion.19
  708.9 1.4 copy.209
  711.4 2.8 multiply_reduce_fusion.12
  714.2 3.0 multiply_reduce_fusion.10
  717.2 2.4 pad_maximum_fusion
  719.7 27.8 %scatter_rows.1 = f32[6144,384]{1,0:T(8,128)} custom-call(s32[32,256]{1,0:T(8,128)S(1)} %fusion.84.list_ref, s32[32]{0:T(128)S(1)} %get-tuple-element.246.count_ref, bf16[32,256,384]{2,1,0:T(8,128)(2,1)} %bitcast.204, bf16[6144,384]{1,0:T(8,128)(2,1)} %bitcast.194), custom_call_target="tpu_custom_call" | custom-call | tf_op jit(solution)/shard_map/scatter_rows/pallas_call | solution.py:690
  747.5 8.3 multiply_reduce_fusion.4
  755.8 2.8 copy-done.3
  758.6 13.5 %in_moments.1 = (f32[12288,128]{1,0:T(8,128)}, f32[12288,128]{1,0:T(8,128)}, f32[2,8,128]{2,1,0:T(8,128)S(1)}) custom-call(f32[2]{0:T(128)S(1)} %pad_maximum_fusion.7.scale_ref, f32[1536,1024]{1,0:T(8,128)S(1)} %copy-done.3, f32[12288,128]{1,0:T(8,128)S(1)} %bitcast.186, f32[12288,128]{1,0:T(8,128)} %bitcast.199, f32[12288,128]{1,0:T(8,128)} %bitcast.200), custom_call_target="tpu_custom_call" | custom-call | tf_op jit(solution)/shard_map/in_moments/pallas_call | solution.py:577
  772.8 22.4 %multiply_reduce_fusion.1 = (f32[]{:T(128)}, f32[]{:T(128)}, f32[6144,384]{1,0:T(8,128)}, f32[6144,384]{1,0:T(8,128)}) fusion(f32[6144,384]{1,0:T(8,128)} %table_ref.1, f32[]{:T(128)} %div.136, f32[]{:T(128)} %div.135, f32[6144,384]{1,0:T(8,128)} %scatter_rows.1, f32[6144,384]{1,0:T(8,128)} %param.34, f32[6144,384]{1,0:T(8,128)} %param.35), kind=kLoop, calls=%fused_computation.8 | loop fusion | flops 40108032 | bytes 56623120 | tf_op jit(solution)/shard_map/reduce_sum | solution.py:1083
  795.3 9.4 %select_select_fusion.refs_0_ = f32[8,128]{1,0:T(8,128)} fusion(f32[]{:T(128)} %get-tuple-element.201, f32[]{:T(128)} %get-tuple-element.200, f32[]{:T(128)} %get-tuple-element.214, f32[]{:T(128)} %get-tuple-element.213, f32[]{:T(128)} %get-tuple-element.220, f32[]{:T(128)} %get-tuple-element.219, f32[]{:T(128)} %get-tuple-element.273, ...), kind=kLoop, calls=%fused_computation.225 | loop fusion | flops 28672 | bytes 4464 | tf_op jit(solution)/shard_map/jit(_where)/select_n | solution.py:1092
  804.7 12.5 %exchange_10.1 = f32[4,8,8,128]{3,2,1,0:T(8,128)} custom-call(f32[8,128]{1,0:T(8,128)} %select_select_fusion.refs_0_), custom_call_target="tpu_custom_call" | custom-call | bytes 2703360 | tf_op jit(solution)/shard_map/exchange_10/pallas_call | solution.py:368
  826.2 1.4 copy.207
  827.6 1.9 multiply_subtract_fusion.4
  829.5 2.5 multiply_subtract_fusion.3
  832.1 6.5 multiply_subtract_fusion.2
  838.6 10.0 %multiply_subtract_fusion.1 = f32[12288,128]{1,0:T(8,128)} fusion(f32[12288,128]{1,0:T(8,128)} %bitcast.183, f32[12288,128]{1,0:T(8,128)} %get-tuple-element.84, f32[12288,128]{1,0:T(8,128)} %get-tuple-element.83, f32[]{:T(128)} %div.136, f32[]{:T(128)} %div.135, f32[]{:T(128)} %bitcast.72), kind=kLoop, calls=%fused_computation.21 | loop fusion | flops 12582912 | bytes 25165836 | tf_op jit(solution)/shard_map/sub | solution.py:1101
  848.6 1.6 slice-done.6
  850.8 6.6 multiply_subtract_fusion
  (358 shorter events, 69.2 us)
Async XLA Ops:
  0.7 10.7 %copy-start = (s32[256,8]{0,1:T(8,128)S(1)}, s32[256,8]{0,1:T(8,128)}, u32[]{:S(2)}) copy-start(s32[256,8]{0,1:T(8,128)} %param.31) | copy-start | bytes 24580
  11.4 342.7 %copy-start.61 = (s32[1536]{0:T(1024)}, s32[1536]{0:T(1024)S(1)}, u32[]{:S(2)}) copy-start(s32[1536]{0:T(1024)S(1)} %iota_add_fusion) | copy-start | bytes 18436
  11.5 203.8 %copy-start.72 = (pred[32,256]{1,0:T(8,128)(4,1)}, pred[32,256]{1,0:T(8,128)(4,1)S(1)}, u32[]{:S(2)}) copy-start(pred[32,256]{1,0:T(8,128)(4,1)S(1)} %iota_compare_fusion.8) | copy-start | bytes 24580
  21.8 191.9 %copy-start.46 = (f32[32,32]{1,0:T(8,128)}, f32[32,32]{1,0:T(8,128)S(1)}, u32[]{:S(2)}) copy-start(f32[32,32]{1,0:T(8,128)S(1)} %get-tuple-element.289) | copy-start | bytes 12292
  21.8 191.9 %copy-start.48 = (f32[32,32]{1,0:T(8,128)}, f32[32,32]{1,0:T(8,128)S(1)}, u32[]{:S(2)}) copy-start(f32[32,32]{1,0:T(8,128)S(1)} %get-tuple-element.290) | copy-start | bytes 12292
  22.0 191.4 %copy-start.35 = (f32[256,32]{0,1:T(8,128)}, f32[256,32]{0,1:T(8,128)S(1)}, u32[]{:S(2)}) copy-start(f32[256,32]{0,1:T(8,128)S(1)} %get-tuple-element.286) | copy-start | bytes 98308
  204.1 16.7 %copy-start.50 = (f32[1536]{0:T(1024)}, f32[1536]{0:T(1024)S(1)}, u32[]{:S(2)}) copy-start(f32[1536]{0:T(1024)S(1)} %get-tuple-element.209) | copy-start | bytes 18436
  204.1 109.4 %copy-start.43 = (f32[1536]{0:T(1024)}, f32[1536]{0:T(1024)S(1)}, u32[]{:S(2)}) copy-start(f32[1536]{0:T(1024)S(1)} %get-tuple-element.208) | copy-start | bytes 18436
  206.8 8.5 copy-start.37
  217.3 33.8 %copy-start.54 = (bf16[32,1536]{1,0:T(8,128)(2,1)}, bf16[32,1536]{1,0:T(8,128)(2,1)S(1)}, u32[]{:S(2)}) copy-start(bf16[32,1536]{1,0:T(8,128)(2,1)S(1)} %convert_element_type.187) | copy-start | bytes 294916
  220.8 33.6 %copy-start.94 = (f32[32]{0:T(128)}, f32[32]{0:T(128)S(1)}, u32[]{:S(2)}) copy-start(f32[32]{0:T(128)S(1)} %get-tuple-element.295) | copy-start | bytes 388
  220.8 33.6 %copy-start.75 = (f32[32]{0:T(128)}, f32[32]{0:T(128)S(1)}, u32[]{:S(2)}) copy-start(f32[32]{0:T(128)S(1)} %fusion.93) | copy-start | bytes 388
  313.5 32.2 %copy-start.88 = (f32[32]{0:T(128)}, f32[32]{0:T(128)S(1)}, u32[]{:S(2)}) copy-start(f32[32]{0:T(128)S(1)} %get-tuple-element.242) | copy-start | bytes 388
  313.6 30.1 %copy-start.73 = (f32[32]{0:T(128)}, f32[32]{0:T(128)S(1)}, u32[]{:S(2)}) copy-start(f32[32]{0:T(128)S(1)} %fusion.94) | copy-start | bytes 388
  375.3 21.8 %slice-start.11 = ((s8[6291456]{0:T(1024)(128)(4,1)}), s8[2097152]{0:T(1024)(128)(4,1)S(1)}, s32[]{:S(2)}) async-start(s8[6291456]{0:T(1024)(128)(4,1)} %bitcast.197), calls=%async_computation.11 | async-start | bytes 4194304
  386.3 10.9 %slice-start.12 = ((s8[6291456]{0:T(1024)(128)(4,1)}), s8[4194304]{0:T(1024)(128)(4,1)S(1)}, s32[]{:S(2)}) async-start(s8[6291456]{0:T(1024)(128)(4,1)} %bitcast.197), calls=%async_computation.12 | async-start | bytes 8388608
  386.3 10.9 %copy-start.62 = (s32[1536]{0:T(1024)S(1)}, s32[1536]{0:T(1024)}, u32[]{:S(2)}) copy-start(s32[1536]{0:T(1024)} %copy-done.61) | copy-start | bytes 18436
  386.3 10.9 %copy-start.77 = (f32[1024]{0:T(1024)S(1)}, f32[1024]{0:T(1024)}, u32[]{:S(2)}) copy-start(f32[1024]{0:T(1024)} %get-tuple-element.241) | copy-start | bytes 12292
  386.3 10.9 %copy-start.78 = (f32[1024]{0:T(1024)S(1)}, f32[1024]{0:T(1024)}, u32[]{:S(2)}) copy-start(f32[1024]{0:T(1024)} %mul.949) | copy-start | bytes 12292
  386.3 10.9 %copy-start.90 = (bf16[4,2,2,2,32,1536]{5,4,3,2,1,0:T(8,128)(2,1)S(1)}, bf16[4,2,2,2,32,1536]{5,4,3,2,1,0:T(8,128)(2,1)}, u32[]{:S(2)}) copy-start(bf16[4,2,2,2,32,1536]{5,4,3,2,1,0:T(8,128)(2,1)} %get-tuple-element.60) | copy-start | bytes 9437188
  405.4 37.8 %copy-start.44 = (f32[1536]{0:T(1024)S(1)}, f32[1536]{0:T(1024)}, u32[]{:S(2)}) copy-start(f32[1536]{0:T(1024)} %copy-done.43) | copy-start | bytes 18436
  405.4 37.8 %copy-start.74 = (f32[32]{0:T(128)S(1)}, f32[32]{0:T(128)}, u32[]{:S(2)}) copy-start(f32[32]{0:T(128)} %copy-done.73) | copy-start | bytes 388
  405.4 38.9 %copy-start.89 = (f32[32]{0:T(128)S(1)}, f32[32]{0:T(128)}, u32[]{:S(2)}) copy-start(f32[32]{0:T(128)} %copy-done.88) | copy-start | bytes 388
  492.2 41.5 %copy-start.51 = (f32[1536]{0:T(1024)S(1)}, f32[1536]{0:T(1024)}, u32[]{:S(2)}) copy-start(f32[1536]{0:T(1024)} %copy-done.50) | copy-start | bytes 18436
  492.2 41.5 %copy-start.76 = (f32[32]{0:T(128)S(1)}, f32[32]{0:T(128)}, u32[]{:S(2)}) copy-start(f32[32]{0:T(128)} %copy-done.75) | copy-start | bytes 388
  492.2 42.9 %copy-start.95 = (f32[32]{0:T(128)S(1)}, f32[32]{0:T(128)}, u32[]{:S(2)}) copy-start(f32[32]{0:T(128)} %copy-done.94) | copy-start | bytes 388
  492.3 42.9 %copy-start.12 = (f32[32,1536]{1,0:T(8,128)S(1)}, f32[32,1536]{1,0:T(8,128)}, u32[]{:S(2)}) copy-start(f32[32,1536]{1,0:T(8,128)} %get-tuple-element.66) | copy-start | bytes 589828
  536.1 8.5 copy-start.33
  580.3 119.9 %copy-start.56 = (f32[3,48]{0,1:T(8,128)S(1)}, f32[3,48]{0,1:T(8,128)}, u32[]{:S(2)}) copy-start(f32[3,48]{0,1:T(8,128)} %copy.200) | copy-start | bytes 1732
  580.3 119.9 %copy-start.57 = (f32[3,48]{0,1:T(8,128)S(1)}, f32[3,48]{0,1:T(8,128)}, u32[]{:S(2)}) copy-start(f32[3,48]{0,1:T(8,128)} %copy.199) | copy-start | bytes 1732
  580.3 119.9 %copy-start.58 = (f32[3,48]{0,1:T(8,128)S(1)}, f32[3,48]{0,1:T(8,128)}, u32[]{:S(2)}) copy-start(f32[3,48]{0,1:T(8,128)} %copy.198) | copy-start | bytes 1732
  580.3 122.2 %copy-start.40 = (f32[48,32]{1,0:T(8,128)S(1)}, f32[48,32]{1,0:T(8,128)}, u32[]{:S(2)}) copy-start(f32[48,32]{1,0:T(8,128)} %copy.204) | copy-start | bytes 18436
  580.3 122.2 %copy-start.52 = (f32[48,32]{1,0:T(8,128)S(1)}, f32[48,32]{1,0:T(8,128)}, u32[]{:S(2)}) copy-start(f32[48,32]{1,0:T(8,128)} %copy.201) | copy-start | bytes 18436
  580.3 122.1 %copy-start.53 = (f32[48,32]{1,0:T(8,128)S(1)}, f32[48,32]{1,0:T(8,128)}, u32[]{:S(2)}) copy-start(f32[48,32]{1,0:T(8,128)} %copy.203) | copy-start | bytes 18436
  580.3 131.0 %copy-start.10 = (f32[48,1536]{1,0:T(8,128)S(1)}, f32[48,1536]{1,0:T(8,128)}, u32[]{:S(2)}) copy-start(f32[48,1536]{1,0:T(8,128)} %param.39) | copy-start | bytes 884740
  700.1 14.0 %copy-start.7 = (f32[48,2560]{1,0:T(8,128)S(1)}, f32[48,2560]{1,0:T(8,128)}, u32[]{:S(2)}) copy-start(f32[48,2560]{1,0:T(8,128)} %param.36) | copy-start | bytes 1474564
  700.1 14.0 %copy-start.32 = (f32[48,2560]{1,0:T(8,128)S(1)}, f32[48,2560]{1,0:T(8,128)}, u32[]{:S(2)}) copy-start(f32[48,2560]{1,0:T(8,128)} %param.37) | copy-start | bytes 1474564
  700.2 17.0 %copy-start.11 = (bf16[4,576,384]{2,1,0:T(8,128)(2,1)S(1)}, bf16[4,576,384]{2,1,0:T(8,128)(2,1)}, u32[]{:S(2)}) copy-start(bf16[4,576,384]{2,1,0:T(8,128)(2,1)} %get-tuple-element.82) | copy-start | bytes 5308420
  710.3 6.9 copy-start.16
  719.6 27.8 %copy-start.4 = (f32[4,128,1536]{2,1,0:T(8,128)S(1)}, f32[4,128,1536]{2,1,0:T(8,128)}, u32[]{:S(2)}) copy-start(f32[4,128,1536]{2,1,0:T(8,128)} %down_ref.1) | copy-start | bytes 9437188
  719.7 27.8 %copy-start.9 = (bf16[4,2,2,2,32,1536]{5,4,3,2,1,0:T(8,128)(2,1)S(1)}, bf16[4,2,2,2,32,1536]{5,4,3,2,1,0:T(8,128)(2,1)}, u32[]{:S(2)}) copy-start(bf16[4,2,2,2,32,1536]{5,4,3,2,1,0:T(8,128)(2,1)} %get-tuple-element.67) | copy-start | bytes 9437188
  719.7 27.8 %copy-start.13 = (bf16[512,1024]{1,0:T(8,128)(2,1)S(1)}, bf16[512,1024]{1,0:T(8,128)(2,1)}, u32[]{:S(2)}) copy-start(bf16[512,1024]{1,0:T(8,128)(2,1)} %copy.218) | copy-start | bytes 3145732
  719.7 36.2 %slice-start = ((s8[6291456]{0:T(1024)(128)(4,1)}), s8[4194304]{0:T(1024)(128)(4,1)S(1)}, s32[]{:S(2)}) async-start(s8[6291456]{0:T(1024)(128)(4,1)} %bitcast.184), calls=%async_computation | async-start | bytes 8388608
  747.5 8.3 slice-start.1
  772.8 22.5 %copy-start.79 = (pred[8]{0:T(512)(128)(4,1)S(1)}, pred[8]{0:T(512)(128)(4,1)}, u32[]{:S(2)}) copy-start(pred[8]{0:T(512)(128)(4,1)} %iota_compare_fusion.21) | copy-start | bytes 28
  772.8 22.5 %copy-start.80 = (pred[128]{0:T(512)(128)(4,1)S(1)}, pred[128]{0:T(512)(128)(4,1)}, u32[]{:S(2)}) copy-start(pred[128]{0:T(512)(128)(4,1)} %get-tuple-element.309) | copy-start | bytes 388
  772.8 22.5 %copy-start.81 = (pred[128]{0:T(512)(128)(4,1)S(1)}, pred[128]{0:T(512)(128)(4,1)}, u32[]{:S(2)}) copy-start(pred[128]{0:T(512)(128)(4,1)} %get-tuple-element.310) | copy-start | bytes 388
  772.8 22.5 %copy-start.82 = (pred[8]{0:T(512)(128)(4,1)S(1)}, pred[8]{0:T(512)(128)(4,1)}, u32[]{:S(2)}) copy-start(pred[8]{0:T(512)(128)(4,1)} %get-tuple-element.307) | copy-start | bytes 28
  772.8 22.5 %copy-start.83 = (pred[8]{0:T(512)(128)(4,1)S(1)}, pred[8]{0:T(512)(128)(4,1)}, u32[]{:S(2)}) copy-start(pred[8]{0:T(512)(128)(4,1)} %get-tuple-element.308) | copy-start | bytes 28
  772.8 22.5 %copy-start.84 = (pred[8]{0:T(512)(128)(4,1)S(1)}, pred[8]{0:T(512)(128)(4,1)}, u32[]{:S(2)}) copy-start(pred[8]{0:T(512)(128)(4,1)} %get-tuple-element.305) | copy-start | bytes 28
  772.8 22.5 %copy-start.85 = (pred[8]{0:T(512)(128)(4,1)S(1)}, pred[8]{0:T(512)(128)(4,1)}, u32[]{:S(2)}) copy-start(pred[8]{0:T(512)(128)(4,1)} %get-tuple-element.306) | copy-start | bytes 28
  772.8 22.5 %copy-start.86 = (pred[8]{0:T(512)(128)(4,1)S(1)}, pred[8]{0:T(512)(128)(4,1)}, u32[]{:S(2)}) copy-start(pred[8]{0:T(512)(128)(4,1)} %get-tuple-element.303) | copy-start | bytes 28
  772.8 22.5 %copy-start.87 = (pred[8]{0:T(512)(128)(4,1)S(1)}, pred[8]{0:T(512)(128)(4,1)}, u32[]{:S(2)}) copy-start(pred[8]{0:T(512)(128)(4,1)} %get-tuple-element.304) | copy-start | bytes 28
  772.8 51.3 %copy-start.41 = (f32[48,32]{1,0:T(8,128)S(1)}, f32[48,32]{1,0:T(8,128)}, u32[]{:S(2)}) copy-start(f32[48,32]{1,0:T(8,128)} %get-tuple-element.231) | copy-start | bytes 18436
  817.2 14.9 %copy-start.5 = (f32[4,128,1536]{2,1,0:T(8,128)S(1)}, f32[4,128,1536]{2,1,0:T(8,128)}, u32[]{:S(2)}) copy-start(f32[4,128,1536]{2,1,0:T(8,128)} %down_ref.1) | copy-start | bytes 9437188
  829.5 19.0 %slice-start.8 = ((s8[9437184]{0:T(1024)(128)(4,1)}), s8[4194304]{0:T(1024)(128)(4,1)S(1)}, s32[]{:S(2)}) async-start(s8[9437184]{0:T(1024)(128)(4,1)} %bitcast.192), calls=%async_computation.8 | async-start | bytes 8388608
  832.1 16.5 %slice-start.2 = ((s8[9437184]{0:T(1024)(128)(4,1)}), s8[4194304]{0:T(1024)(128)(4,1)S(1)}, s32[]{:S(2)}) async-start(s8[9437184]{0:T(1024)(128)(4,1)} %bitcast.188), calls=%async_computation.2 | async-start | bytes 8388608
  832.1 16.5 %slice-start.5 = ((s8[9437184]{0:T(1024)(128)(4,1)}), s8[4194304]{0:T(1024)(128)(4,1)S(1)}, s32[]{:S(2)}) async-start(s8[9437184]{0:T(1024)(128)(4,1)} %bitcast.190), calls=%async_computation.5 | async-start | bytes 8388608
  832.1 16.5 %slice-start.9 = ((s8[9437184]{0:T(1024)(128)(4,1)}), s8[4194304]{0:T(1024)(128)(4,1)S(1)}, s32[]{:S(2)}) async-start(s8[9437184]{0:T(1024)(128)(4,1)} %bitcast.192), calls=%async_computation.9 | async-start | bytes 8388608
  838.6 10.0 %slice-start.3 = ((s8[9437184]{0:T(1024)(128)(4,1)}), s8[4194304]{0:T(1024)(128)(4,1)S(1)}, s32[]{:S(2)}) async-start(s8[9437184]{0:T(1024)(128)(4,1)} %bitcast.188), calls=%async_computation.3 | async-start | bytes 8388608
  838.6 10.1 %slice-start.4 = ((s8[9437184]{0:T(1024)(128)(4,1)}), s8[1048576]{0:T(1024)(128)(4,1)S(1)}, s32[]{:S(2)}) async-start(s8[9437184]{0:T(1024)(128)(4,1)} %bitcast.188), calls=%async_computation.4 | async-start | bytes 2097152
  838.6 11.7 %slice-start.6 = ((s8[9437184]{0:T(1024)(128)(4,1)}), s8[4194304]{0:T(1024)(128)(4,1)S(1)}, s32[]{:S(2)}) async-start(s8[9437184]{0:T(1024)(128)(4,1)} %bitcast.190), calls=%async_computation.6 | async-start | bytes 8388608
  838.6 11.9 %slice-start.7 = ((s8[9437184]{0:T(1024)(128)(4,1)}), s8[1048576]{0:T(1024)(128)(4,1)S(1)}, s32[]{:S(2)}) async-start(s8[9437184]{0:T(1024)(128)(4,1)} %bitcast.190), calls=%async_computation.7 | async-start | bytes 2097152
  838.6 12.2 %slice-start.10 = ((s8[9437184]{0:T(1024)(128)(4,1)}), s8[1048576]{0:T(1024)(128)(4,1)S(1)}, s32[]{:S(2)}) async-start(s8[9437184]{0:T(1024)(128)(4,1)} %bitcast.192), calls=%async_computation.10 | async-start | bytes 2097152
  (45 other events, 195.2 us)

commit v4 on v3

--- a/solution.py
+++ b/solution.py
@@ -306,29 +306,34 @@
 class Swap:
     flat = False
     scratch = (pltpu.SemaphoreType.DMA(()),)
-    spaces = (pl.ANY,)
-
-    def __init__(self, x, start, size, planes, side, rounds, back=False):
-        self.planes, self.side, self.inputs = planes, side, [x]
+
+    def __init__(self, x, start, size, planes, side, rounds, back=False, held=None):
+        self.planes, self.side = planes, side
+        self.inputs = [x] if held is None else [x, held]
+        self.in_spaces, self.out_spaces = (pl.ANY,) * len(self.inputs), (pl.ANY,)
+        self.aliases = {} if held is None else {1: 0}
         self.begin, self.size, self.rounds, self.back = start, size, rounds, back
         self.columns = x.shape[1] // planes if back else x.shape[1]
-        shape = (planes, size, self.columns) if back else (size, planes * self.columns)
+        self.rows = x.shape[0] if back else x.shape[0] // planes
+        shape = (planes, self.rows, self.columns) if back else (self.rows, planes * self.columns)
         self.outputs = [jax.ShapeDtypeStruct(shape, x.dtype)]
         self.copies = planes - 1
 
-    def steps(self, spot, mail, x, out, own_sem):
+    def steps(self, spot, mail, *refs):
+        x, out, own_sem = refs[0], refs[-2], refs[-1]
+        rows = pl.ds(self.begin, self.size)
+
         def block(z):
             return pl.ds(pl.multiple_of(z * self.columns, 128), self.columns)
 
         def source(z):
             if self.back:
-                return x.at[pl.ds(self.begin, self.size), block(z)]
-            first = z * (x.shape[0] // self.planes) + self.begin
-            return x.at[pl.ds(pl.multiple_of(first, 16), self.size), :]
+                return x.at[rows, block(z)]
+            return x.at[pl.ds(pl.multiple_of(z * self.rows + self.begin, 16), self.size), :]
 
         for _ in range(self.rounds):
             yield
-        place = out.at[spot.z] if self.back else out.at[:, block(spot.z)]
+        place = out.at[spot.z, rows] if self.back else out.at[rows, block(spot.z)]
         sent = []
         for k in range(1, self.planes):
             peer, target = spot.plane(k)
@@ -347,6 +352,10 @@
     counts = [(len(p.inputs), len(p.outputs), len(p.scratch)) for p in parts]
     n_in, n_out = (sum(c[i] for c in counts) for i in range(2))
     copies = sum(p.copies for p in parts)
+    aliases, i, o = {}, 0, 0
+    for part, (ci, co, _) in zip(parts, counts):
+        aliases.update({i + a: o + b for a, b in getattr(part, "aliases", {}).items()})
+        i, o = i + ci, o + co
 
     def kernel(*refs):
         ins, outs, rest = refs[:n_in], refs[n_in : n_in + n_out], refs[n_in + n_out :]
@@ -371,9 +380,14 @@
         in_specs=[
             pl.BlockSpec(memory_space=space)
             for p in parts
-            for space in getattr(p, "spaces", (pltpu.VMEM,) * len(p.inputs))
+            for space in getattr(p, "in_spaces", (pltpu.VMEM,) * len(p.inputs))
         ],
-        out_specs=[pl.BlockSpec(memory_space=pltpu.VMEM)] * n_out,
+        out_specs=[
+            pl.BlockSpec(memory_space=space)
+            for p in parts
+            for space in getattr(p, "out_spaces", (pltpu.VMEM,) * len(p.outputs))
+        ],
+        input_output_aliases=aliases,
         scratch_shapes=[s for p in parts for s in p.scratch]
         + [pltpu.SemaphoreType.DMA((copies,)), pltpu.SemaphoreType.DMA((copies,))],
         compiler_params=pltpu.CompilerParams(
@@ -450,7 +464,7 @@
             in_specs=[
                 pl.BlockSpec((block, D), row),
                 pl.BlockSpec((block, TOP), row),
-                pl.BlockSpec((D, 128), still),
+                pl.BlockSpec((D, 128), lambda r, e, *_: (0, PACK // 128 - 1)),
                 pl.BlockSpec((2 * D, units), lambda r, e, *_: (e, 0)),
                 pl.BlockSpec((1, units, D), lambda r, e, *_: (e, 0, 0)),
             ],
@@ -589,22 +603,224 @@
     )(scales, grad, weight, first, second)
 
 
-def norm_apply(values, gain):
-    return values * lax.rsqrt(jnp.mean(values * values, axis=-1, keepdims=True) + 1e-06) * gain
-
-
-def rotary_apply(values, places):
-    half = values.shape[-1] // 2
+HEAD_COLS = QUERY_HEADS * HEAD_WIDTH
+KEY_COLS = KEY_VALUE_HEADS * HEAD_WIDTH
+PACK = HEAD_COLS + KEY_COLS + 128
+ROOT = HEAD_WIDTH ** (-0.5)
+
+
+def turn(u, cosine, sine):
+    width = u.shape[1]
+    lanes = lax.broadcasted_iota(jnp.int32, u.shape, 1)
+    ahead = pltpu.roll(u, width - HEAD_WIDTH // 2, 1)
+    behind = pltpu.roll(u, HEAD_WIDTH // 2, 1)
+    other = jnp.where(lax.rem(lanes, HEAD_WIDTH) < HEAD_WIDTH // 2, ahead, behind)
+    return u * jnp.tile(cosine, (1, width // 128)) + other * jnp.tile(sine, (1, width // 128))
+
+
+def rotary_tables():
+    half = HEAD_WIDTH // 2
     freqs = jnp.exp(-jnp.log(10000.0) * jnp.arange(half, dtype=f32) / half)
-    angles = places[:, None] * freqs[None, :]
-    cosine = jnp.cos(angles)[:, None, :]
-    sine = jnp.sin(angles)[:, None, :]
-    first_half = values[..., :half]
-    second_half = values[..., half:]
+    angles = jnp.arange(SEQUENCE_TOKENS, dtype=f32)[:, None] * freqs[None, :]
+    cosine, sine = jnp.cos(angles), jnp.sin(angles)
+    return jnp.tile(cosine, (1, 4)), jnp.tile(jnp.concatenate([-sine, sine], axis=1), (1, 2))
+
+
+def inverse_root(values):
+    return lax.rsqrt(jnp.mean(values * values, axis=-1, keepdims=True) + 1e-06)
+
+
+def norm_back(values, gain, grad):
+    root = inverse_root(values)
+    scaled = grad * gain
+    inner = jnp.mean(scaled * values, axis=-1, keepdims=True)
+    return root * scaled - values * (root * root * root * inner), jnp.sum(
+        grad * values * root, axis=0, keepdims=True
+    )
+
+
+def dot(a, b):
+    return jnp.dot(a, b, preferred_element_type=f32)
+
+
+def dot_across(a, b):
+    return lax.dot_general(a, b, ACROSS, preferred_element_type=f32)
+
+
+def selector(start, shape, axis):
+    row = lax.broadcasted_iota(jnp.int32, shape, 1 - axis) + start
+    return (row == lax.broadcasted_iota(jnp.int32, shape, axis)).astype(f32)
+
+
+def spread(start, rows):
+    pick = selector(start, (SEQUENCE_TOKENS, COMP), 0)
+    return jnp.dot(pick, rows, preferred_element_type=f32, precision=lax.Precision.HIGHEST)
+
+
+def head_rows(ref_value, h):
+    first = h * GROUP * HEAD_WIDTH
     return jnp.concatenate(
-        [first_half * cosine - second_half * sine, second_half * cosine + first_half * sine],
-        axis=-1,
-    )
+        [
+            ref_value[:, first + g * HEAD_WIDTH : first + (g + 1) * HEAD_WIDTH]
+            for g in range(GROUP)
+        ],
+        axis=0,
+    )
+
+
+def head_lanes(parts):
+    return jnp.concatenate(
+        [part[g * COMP : (g + 1) * COMP] for part in parts for g in range(GROUP)], axis=1
+    )
+
+
+def attend_kernel(
+    start_ref, picked_ref, one_ref, two_ref, cos_ref, sin_ref, cos_rows, sin_rows,
+    c_ref, resid_ref, probs_ref, query_ref, key_ref, value_ref, mixed_ref, normed_ref, gains_ref,
+    embedded,
+):
+    start = start_ref[0]
+    pick_rows = selector(start, (COMP, SEQUENCE_TOKENS), 1).astype(bf16)
+    planes, _, columns = picked_ref.shape
+    for p in range(planes):
+        embedded[:, p * columns : (p + 1) * columns] = picked_ref[p].astype(f32)
+    pick = lax.broadcasted_iota(jnp.int32, (8, 128), 0) + EXPERTS
+    pick = (pick == lax.broadcasted_iota(jnp.int32, (8, 128), 1)).astype(f32).astype(bf16)
+    gains = dot_across(pick, one_ref[:, HEAD_COLS + KEY_COLS :])
+    gains_ref[...] = gains
+    x = embedded[...]
+    a = (x * inverse_root(x) * gains[0:1]).astype(bf16)
+    normed_ref[...] = a
+    a_rows = dot(pick_rows, a).astype(bf16)
+    cosine, sine = cos_ref[...], sin_ref[...]
+    query = turn(dot(a_rows, one_ref[:, :HEAD_COLS]), cos_rows[...], sin_rows[...])
+    query = query.astype(bf16)
+    key = turn(dot(a, one_ref[:, HEAD_COLS : HEAD_COLS + KEY_COLS]), cosine, sine).astype(bf16)
+    value = dot(a, two_ref[:, :KEY_COLS]).astype(bf16)
+    query_ref[...], key_ref[...], value_ref[...] = query, key, value
+    rows = GROUP * COMP
+    place = lax.rem(lax.broadcasted_iota(jnp.int32, (rows, SEQUENCE_TOKENS), 0), COMP) + start
+    seen = place >= lax.broadcasted_iota(jnp.int32, (rows, SEQUENCE_TOKENS), 1)
+    parts = []
+    for h in range(KEY_VALUE_HEADS):
+        lanes = slice(h * HEAD_WIDTH, (h + 1) * HEAD_WIDTH)
+        scores = dot_across(head_rows(query, h), key[:, lanes]) * ROOT
+        scores = jnp.where(seen, scores, -1000000000.0)
+        expd = jnp.exp(scores - jnp.max(scores, axis=-1, keepdims=True))
+        probs = expd / jnp.sum(expd, axis=-1, keepdims=True)
+        probs_ref[h] = probs
+        parts.append(dot(probs.astype(bf16), value[:, lanes]))
+    mixed = head_lanes(parts).astype(bf16)
+    mixed_ref[...] = mixed
+    resid = dot(pick_rows, embedded[...].astype(bf16)) + dot(mixed, two_ref[:, KEY_COLS : KEY_COLS + D])
+    resid_ref[...] = resid
+    c_ref[...] = (resid * inverse_root(resid) * gains[1:2]).astype(bf16)
+
+
+def attend(start, picked, one, two, *tables):
+    vm = pl.BlockSpec(memory_space=pltpu.VMEM)
+    rows = GROUP * COMP
+    return pl.pallas_call(
+        attend_kernel,
+        in_specs=[pl.BlockSpec(memory_space=pltpu.SMEM)] + [vm] * 7,
+        out_specs=[vm] * 9,
+        out_shape=[
+            jax.ShapeDtypeStruct((COMP, D), bf16),
+            jax.ShapeDtypeStruct((COMP, D), f32),
+            jax.ShapeDtypeStruct((KEY_VALUE_HEADS, rows, SEQUENCE_TOKENS), f32),
+            jax.ShapeDtypeStruct((COMP, HEAD_COLS), bf16),
+            jax.ShapeDtypeStruct((SEQUENCE_TOKENS, KEY_COLS), bf16),
+            jax.ShapeDtypeStruct((SEQUENCE_TOKENS, KEY_COLS), bf16),
+            jax.ShapeDtypeStruct((COMP, HEAD_COLS), bf16),
+            jax.ShapeDtypeStruct((SEQUENCE_TOKENS, D), bf16),
+            jax.ShapeDtypeStruct((8, D), f32),
+        ],
+        scratch_shapes=[pltpu.VMEM((SEQUENCE_TOKENS, D), f32)],
+        compiler_params=pltpu.CompilerParams(vmem_limit_bytes=56 << 20),
+        name="attend",
+    )(start, picked, one, two, *tables)
+
+
+def attend_back_kernel(
+    start_ref, back_ref, gates_ref, grad_two_ref, gain_three_ref, c_ref, resid_ref, probs_ref, query_ref,
+    key_ref, value_ref, mixed_ref, normed_ref, gains_ref, picked_ref, one_ref, two_ref, cos_ref, sin_ref, cos_rows, sin_rows,
+    out_ref, grad_one_ref, grad_pack_ref,
+    total,
+):
+    start = start_ref[0]
+    planes, _, columns = picked_ref.shape
+    gains = gains_ref[...]
+    wide = HEAD_COLS + KEY_COLS
+    gates = gates_ref[...]
+    gate_grad = back_ref[:, D:]
+    router_grad = gates * (gate_grad - jnp.sum(gates * gate_grad, axis=1, keepdims=True))
+    router_grad = router_grad.astype(bf16)
+    grad = back_ref[:, :D] + dot_across(router_grad, one_ref[:, wide:])
+    grad_resid, gain_two = norm_back(resid_ref[...], gains[1:2], grad)
+    grad_resid = grad_resid + grad_two_ref[...]
+    branch = grad_resid.astype(bf16)
+    grad_mixed = dot_across(branch, two_ref[:, KEY_COLS : KEY_COLS + D]).astype(bf16)
+    query, key, value = query_ref[...], key_ref[...], value_ref[...]
+    query_parts, key_parts, value_parts = [], [], []
+    for h in range(KEY_VALUE_HEADS):
+        lanes = slice(h * HEAD_WIDTH, (h + 1) * HEAD_WIDTH)
+        probs = probs_ref[h]
+        grad_head = head_rows(grad_mixed, h)
+        grad_probs = dot_across(grad_head, value[:, lanes]).astype(bf16).astype(f32)
+        inner = jnp.sum(grad_probs * probs, axis=-1, keepdims=True)
+        grad_scores = probs * (grad_probs - inner)
+        value_parts.append(dot(probs.T.astype(bf16), grad_head))
+        query_parts.append(dot(grad_scores.astype(bf16), key[:, lanes]) * ROOT)
+        key_parts.append(dot(grad_scores.T.astype(bf16), head_rows(query, h)) * ROOT)
+    grad_query = turn(head_lanes(query_parts), cos_rows[...], -sin_rows[...]).astype(bf16)
+    grad_key = jnp.concatenate(key_parts, axis=1)
+    grad_key = turn(grad_key, cos_ref[...], -sin_ref[...]).astype(bf16)
+    grad_value = jnp.concatenate(value_parts, axis=1).astype(bf16)
+    grad_normed = dot_across(grad_key, one_ref[:, HEAD_COLS:wide])
+    grad_normed += dot_across(grad_value, two_ref[:, :KEY_COLS])
+    grad_normed += spread(start, dot_across(grad_query, one_ref[:, :HEAD_COLS]))
+    for p in range(planes):
+        total[:, p * columns : (p + 1) * columns] = picked_ref[p].astype(f32)
+    grad_embedded, gain_one = norm_back(total[...], gains[0:1], grad_normed)
+    total[...] = grad_embedded + spread(start, grad_resid)
+    for p in range(planes):
+        out_ref[p] = total[:, p * columns : (p + 1) * columns].astype(bf16)
+    pick_rows = selector(start, (COMP, SEQUENCE_TOKENS), 1).astype(bf16)
+    a_rows = dot(pick_rows, normed_ref[...])
+    turned = normed_ref[...].astype(f32).T.astype(bf16)
+    grad_one_ref[:, HEAD_COLS:wide] = dot(turned, grad_key).astype(bf16)
+    grad_pack_ref[:, :KEY_COLS] = dot(turned, grad_value).astype(bf16)
+    grad_one_ref[:, :HEAD_COLS] = dot(a_rows.T.astype(bf16), grad_query).astype(bf16)
+    grad_pack_ref[:, KEY_COLS : KEY_COLS + D] = dot(
+        mixed_ref[...].astype(f32).T.astype(bf16), branch
+    ).astype(bf16)
+    grad_pack_ref[:, KEY_COLS + D :] = jnp.zeros((D, PACK - KEY_COLS - D), bf16)
+    left = jnp.concatenate(
+        [c_ref[...].astype(f32), gain_one, gain_two, gain_three_ref[...], jnp.zeros((5, D), f32)],
+        axis=0,
+    )
+    lane = lax.broadcasted_iota(jnp.int32, (8, 128), 0) + EXPERTS
+    lane = (lane == lax.broadcasted_iota(jnp.int32, (8, 128), 1)).astype(f32)
+    right = jnp.concatenate([router_grad.astype(f32), lane], axis=0).astype(bf16)
+    grad_one_ref[:, wide:] = dot(left.T.astype(bf16), right).astype(bf16)
+
+
+def attend_back(start, *operands):
+    vm = pl.BlockSpec(memory_space=pltpu.VMEM)
+    picked = operands[13]
+    return pl.pallas_call(
+        attend_back_kernel,
+        in_specs=[pl.BlockSpec(memory_space=pltpu.SMEM)] + [vm] * len(operands),
+        out_specs=[vm] * 3,
+        out_shape=[
+            jax.ShapeDtypeStruct(picked.shape, bf16),
+            jax.ShapeDtypeStruct((D, PACK), bf16),
+            jax.ShapeDtypeStruct((D, PACK), bf16),
+        ],
+        scratch_shapes=[pltpu.VMEM((SEQUENCE_TOKENS, D), f32)],
+        compiler_params=pltpu.CompilerParams(vmem_limit_bytes=60 << 20),
+        name="attend_back",
+    )(start, *operands)
 
 
 def lamb_update(weight, moment_one, moment_two, scale_one, scale_two):
@@ -761,8 +977,8 @@
 
     unit = own_rows // 24
 
-    def swap(x, start, size, rounds, back=False):
-        return Swap(x, start * unit, size * unit, planes, side, rounds, back)
+    def swap(x, start, size, rounds, back=False, held=None):
+        return Swap(x, start * unit, size * unit, planes, side, rounds, back, held)
 
     def gather_completion(rows, ident, *beside):
         part = Gather([rows], split(0, COMP, rows.shape[1], 2, 2), planes, side)
@@ -778,7 +994,7 @@
         return communicate([Tiny(block, planes, side)], ident)[0].reshape((devices,) + block.shape)
 
     weight_rows = qkv_weight.shape[0]
-    weight_cols = head_cols + key_cols + 128
+    weight_cols = PACK
     cuts = 3 if weight_rows % 48 == 0 else 1
     weight_groups = [
         [
@@ -845,70 +1061,33 @@
     )
     first_pack = first_pack.reshape(D, weight_cols)
     second_pack = second_pack.reshape(D, weight_cols)
-    embedded = jnp.concatenate([picked[p] for p in range(planes)], axis=1).astype(f32)
-    router_block = first_pack[:, head_cols + key_cols :]
-    gains_value = router_block[:, EXPERTS : EXPERTS + 3].T.astype(f32)
-    out_full = second_pack[:, key_cols : key_cols + D]
-
-    normed, norm_back_one = jax.vjp(norm_apply, embedded, gains_value[0])
-    normed_b = normed.astype(bf16)
-    places_f = own_places.astype(f32)
-    spots_f = spots.astype(f32)
-
-    def make_query(projected):
-        return rotary_apply(projected.reshape(COMP, QUERY_HEADS, HEAD_WIDTH), places_f)
-
-    def make_key(projected):
-        return rotary_apply(
-            projected.reshape(SEQUENCE_TOKENS, KEY_VALUE_HEADS, HEAD_WIDTH), spots_f
-        )
-
-    projected = jnp.dot(normed_b, first_pack, preferred_element_type=f32)
-    query_f, query_back = jax.vjp(
-        make_query, lax.dynamic_slice(projected, (start, 0), (COMP, head_cols))
-    )
-    key_f, key_back = jax.vjp(make_key, projected[:, head_cols : head_cols + key_cols])
-    query = query_f.astype(bf16).reshape(COMP, KEY_VALUE_HEADS, GROUP, HEAD_WIDTH)
-    key = key_f.astype(bf16)
-    value = (
-        jnp.dot(normed_b, second_pack[:, :key_cols], preferred_element_type=f32)
-        .reshape(SEQUENCE_TOKENS, KEY_VALUE_HEADS, HEAD_WIDTH)
-        .astype(bf16)
-    )
-    scores = jnp.einsum("qhgd,khd->hgqk", query, key, preferred_element_type=f32) * HEAD_WIDTH ** (
-        -0.5
-    )
-    scores = jnp.where(own_places[:, None] >= spots[None, :], scores, -1000000000.0)
-    expd = jnp.exp(scores - jnp.max(scores, axis=-1, keepdims=True))
-    probs = expd / jnp.sum(expd, axis=-1, keepdims=True)
-    probs_b = probs.astype(bf16)
-    attended = (
-        jnp.einsum("hgqk,khd->qhgd", probs_b, value, preferred_element_type=f32)
-        .reshape(COMP, head_cols)
-        .astype(bf16)
-    )
-    resid = lax.dynamic_slice_in_dim(embedded, start, COMP, 0) + jnp.dot(
-        attended, out_full, preferred_element_type=f32
-    )
-    normed_two, norm_back_two = jax.vjp(norm_apply, resid, gains_value[1])
-    normed_two_b = normed_two.astype(bf16)
-
-    expert_rows, table_two = gather_completion(normed_two_b, 2, swap(table_b, 12, 4, 2))
+
+    start_at = start.reshape(1)
+    tables = rotary_tables()
+    tables += tuple(lax.dynamic_slice_in_dim(table, start, COMP, 0) for table in tables)
+    normed_two_b, resid, probs, query, key, value, attended, normed_b, gains = attend(
+        start_at, picked, first_pack, second_pack, *tables
+    )
+
+    expert_rows, table_own = gather_completion(
+        normed_two_b, 2, swap(table_b, 12, 4, 2, held=table_one)
+    )
     lanes = shard_id * local_experts + jnp.arange(local_experts, dtype=jnp.int32)
     in_rows = in_weight.reshape(-1, hidden_units)
     produced, mid, gates, in_cat, down_b, gated_hidden = experts_forward(
-        lanes, expert_rows, routes_all, router_block, in_rows, down_weight
+        lanes, expert_rows, routes_all, first_pack, in_rows, down_weight
     )
     own_index = expert_id * shards + shard_id
-    own_gates = lax.dynamic_slice(gates, (own_index * COMP, 0), (COMP, 128))[:, :EXPERTS]
-    combined, table_three = reduce_completion(produced, 3, 2, swap(table_b, 16, 4, 0))
+    own_gates = lax.dynamic_slice(gates, (own_index * COMP, 0), (COMP, 128))
+    combined, table_own = reduce_completion(
+        produced, 3, 2, swap(table_b, 16, 4, 0, held=table_own)
+    )
     resid_two = resid + combined
 
-    final_rows, norm_back_three = jax.vjp(norm_apply, resid_two, gains_value[2])
-    head_rows, table_four = gather_completion(
-        final_rows.astype(bf16), 4, swap(table_b, 20, 4, 2)
-    )
-    table_own = jnp.concatenate([table_one, table_two, table_three, table_four], axis=0)
+    final_rows = resid_two * inverse_root(resid_two) * gains[2:3]
+    head_rows, table_own = gather_completion(
+        final_rows.astype(bf16), 4, swap(table_b, 20, 4, 2, held=table_own)
+    )
     logits = jnp.einsum("rd,vd->rv", head_rows, table_own, preferred_element_type=f32) / LOGIT_SCALE
     own_base = vocab_base + expert_id * own_rows
     target_hot = targets[:, None] == own_base + jnp.arange(own_rows, dtype=jnp.int32)[None, :]
@@ -938,117 +1117,54 @@
     head_grad = (
         jnp.einsum("rv,rd->vd", grad_logits, head_rows, preferred_element_type=f32) / LOGIT_SCALE
     ).astype(bf16)
-    own_grad_rows, head_one = reduce_completion(
+    own_grad_rows, head_back = reduce_completion(
         grad_rows.astype(bf16), 6, 2, swap(head_grad, 0, 5, 0, back=True)
     )
-    grad_resid_two, grad_gain_three = norm_back_three(own_grad_rows)
-
-    grad_all, head_two = gather_completion(
-        grad_resid_two.astype(bf16), 7, swap(head_grad, 5, 5, 2, back=True)
+    grad_resid_two, grad_gain_three = norm_back(resid_two, gains[2:3], own_grad_rows)
+
+    grad_all, head_back = gather_completion(
+        grad_resid_two.astype(bf16), 7, swap(head_grad, 5, 5, 2, back=True, held=head_back)
     )
     back, mid_grad = experts_backward(lanes, grad_all, mid, gates, in_cat, down_b)
-    back, head_three = reduce_completion(back, 8, 1, swap(head_grad, 10, 5, 0, back=True))
-    grad_gates = back[:, D : D + EXPERTS]
-    grad_router_logits = own_gates * (
-        grad_gates - jnp.sum(own_gates * grad_gates, axis=1, keepdims=True)
-    )
-    grad_router_logits = jnp.pad(grad_router_logits, ((0, 0), (0, 128 - EXPERTS)))
-    grad_normed_two = back[:, :D] + jnp.einsum(
-        "se,de->sd", grad_router_logits, router_block.astype(f32)
-    )
-    grad_resid, grad_gain_two = norm_back_two(grad_normed_two)
-    grad_resid = grad_resid + grad_resid_two
-    grad_branch = grad_resid.astype(bf16)
-    grad_attended = (
-        jnp.einsum("sd,kd->sk", grad_branch, out_full, preferred_element_type=f32)
-        .astype(bf16)
-        .reshape(COMP, KEY_VALUE_HEADS, GROUP, HEAD_WIDTH)
-    )
-
-    grad_probs = jnp.einsum("qhgd,khd->hgqk", grad_attended, value, preferred_element_type=f32)
-    grad_probs = grad_probs.astype(bf16).astype(f32)
-    inner = jnp.sum(grad_probs * probs, axis=-1, keepdims=True)
-    grad_scores = (probs * (grad_probs - inner)).astype(bf16)
-    grad_value = jnp.einsum("hgqk,qhgd->khd", probs_b, grad_attended, preferred_element_type=f32)
-    grad_query = jnp.einsum(
-        "hgqk,khd->qhgd", grad_scores, key, preferred_element_type=f32
-    ) * HEAD_WIDTH ** (-0.5)
-    grad_key = jnp.einsum(
-        "hgqk,qhgd->khd", grad_scores, query, preferred_element_type=f32
-    ) * HEAD_WIDTH ** (-0.5)
-
-    def spread(rows):
-        return lax.dynamic_update_slice_in_dim(
-            jnp.zeros((SEQUENCE_TOKENS, rows.shape[1]), rows.dtype), rows, start, 0
-        )
-
-    grad_query_rows = query_back(grad_query.reshape(COMP, QUERY_HEADS, HEAD_WIDTH))[0].astype(bf16)
-    grad_first = jnp.concatenate(
-        [
-            spread(grad_query_rows),
-            key_back(grad_key)[0].astype(bf16),
-            jnp.zeros((SEQUENCE_TOKENS, 128), bf16),
-        ],
-        axis=1,
-    )
-    grad_value = grad_value.reshape(SEQUENCE_TOKENS, key_cols).astype(bf16)
-    across = "sk,dk->sd"
-    grad_normed = jnp.einsum(across, grad_first, first_pack, preferred_element_type=f32)
-    grad_normed += jnp.einsum(
-        across, grad_value, second_pack[:, :key_cols], preferred_element_type=f32
-    )
-    grad_embedded, grad_gain_one = norm_back_one(grad_normed)
-    grad_embedded = (grad_embedded + spread(grad_resid)).astype(bf16)
-    grad_embedded = jnp.stack(
-        [grad_embedded[:, p * columns : (p + 1) * columns] for p in range(planes)]
-    )
-
-    gains_grad = jnp.pad(
-        jnp.stack([grad_gain_one, grad_gain_two, grad_gain_three]), ((0, 13), (0, 0))
-    ).astype(bf16)
-    gains_lanes = (
-        jnp.arange(16)[:, None] + EXPERTS == jnp.arange(128)[None, :]
-    ).astype(bf16)
+    back, head_back = reduce_completion(
+        back, 8, 1, swap(head_grad, 10, 5, 0, back=True, held=head_back)
+    )
+
+    grad_embedded, *grad_packs = attend_back(
+        start_at,
+        back,
+        own_gates,
+        grad_resid_two,
+        grad_gain_three,
+        normed_two_b,
+        resid,
+        probs,
+        query,
+        key,
+        value,
+        attended,
+        normed_b,
+        gains,
+        picked,
+        first_pack,
+        second_pack,
+        *tables,
+    )
+    grad_packs = [pack.reshape(grid + (weight_rows, weight_cols)) for pack in grad_packs]
     wide = head_cols + key_cols
-    first_left = jnp.concatenate([normed_b, normed_two_b, gains_grad], axis=0)
-    first_right = jnp.concatenate(
-        [
-            grad_first,
-            jnp.pad(
-                jnp.concatenate([grad_router_logits.astype(bf16), gains_lanes], axis=0),
-                ((0, 0), (wide, 0)),
-            ),
-        ],
-        axis=0,
-    )
-    second_left = jnp.concatenate([normed_b, attended], axis=0)
-    second_right = jnp.concatenate(
-        [
-            jnp.pad(grad_value, ((0, 0), (0, D + 128))),
-            jnp.pad(grad_branch, ((0, 0), (key_cols, 128))),
-        ],
-        axis=0,
-    )
-    grad_packs = [
-        jnp.einsum("sd,sk->dk", left, right, preferred_element_type=f32)
-        .astype(bf16)
-        .reshape(grid + (weight_rows, weight_cols))
-        for left, right in ((first_left, first_right), (second_left, second_right))
-    ]
-    sent, first_grad, second_grad, head_four = send(
+    sent, first_grad, second_grad, head_back = send(
         [
             Gather([grad_embedded], embed_groups, planes, side, exchange=True),
             Reduce(grad_packs, weight_groups, planes, side),
-            swap(head_grad, 15, 9, 3, back=True),
+            swap(head_grad, 15, 9, 3, back=True, held=head_back),
         ],
         9,
     )
-    head_grad = jnp.concatenate([head_one, head_two, head_three, head_four], axis=1)
     table_grad = scatter_rows(
         lists,
         counts,
         sent.reshape(devices, SEQUENCE_TOKENS, columns),
-        head_grad.reshape(vocab_rows, columns),
+        head_back.reshape(vocab_rows, columns),
     )
 
     step_value = step_count.astype(f32)

time: 873 us -> 803 us (0.920)
  matrix products: 83.2 us -> 42.4 us
  local copies, waits for them, and re-layouts: 61.9 us -> 29.9 us
  Pallas kernels: 581 us -> 612 us
  other arithmetic: 124 us -> 95.8 us
    dot_general x14 -> x0, matrix products: 40.7 us -> none  [the longest x2 11.4 us: on_device(): jnp.einsum('sd,sk->dk', left, right, preferred_element_type=f32)]
    pallas_call x0 -> x2, Pallas kernels: none -> 36.2 us  [the longest x1 23.9 us: attend_back(): pl.pallas_call(attend_back_kernel, in_specs=[pl.BlockSpec(memory_space=pl...]
    unnamed x235 -> x103, local copies, waits for them, and re-layouts: 32.6 us -> 16.8 us
    pallas_call x11, Pallas kernels: 493 us -> 484 us  [communicate(): pl.pallas_call(kernel, out_shape=[x for p in parts for x in p.outputs], i...]
where the time goes in v4:
time: 803 us; the launch traced here: 790 us
  Pallas kernels  612 us (76%)
  other arithmetic  95.8 us (12%)
  matrix products  42.4 us (5%)
  local copies, waits for them, and re-layouts  29.9 us (4%)
  between operations  9.01 us (1%)
    pallas_call x11, Pallas kernels, communicate(): pl.pallas_call(kernel, out_shape=[x for p in parts for x in p.outputs], i...  484 us
    pallas_call x1, Pallas kernels, scatter_rows(): pl.pallas_call(scatter_kernel, grid_spec=pltpu.PrefetchScalarGridSpec(num...  28.8 us
    sub x7, other arithmetic, on_device(): weight - STEP_RATE * trust_ratio[place] * parts[2]  27.3 us
    reduce_sum x5, other arithmetic, on_device(): jnp.sum(parts[2] * parts[2])  26 us
    pallas_call x1, Pallas kernels, attend_back(): pl.pallas_call(attend_back_kernel, in_specs=[pl.BlockSpec(memory_space=pl...  23.9 us
    pallas_call x1, Pallas kernels, experts_forward(): pl.pallas_call(forward_kernel, grid_spec=pltpu.PrefetchScalarGridSpec(num...  17.8 us
    pallas_call x1, Pallas kernels, gather_rows(): pl.pallas_call(gather_kernel, grid_spec=pltpu.PrefetchScalarGridSpec(num_...  17.6 us
    unnamed x103, local copies, waits for them, and re-layouts  16.8 us

profile of v4, /device:TPU:0, one launch (start us, length us, event | category | flops | bytes accessed | tf_op | source)
XLA Modules:
  0.0 789.5 jit_solution(2524447562763508793)
XLA Ops:
  2.0 0.8 dynamic_slice.20
  2.8 0.7 fusion.46
  4.4 0.8 slice_bitcast_fusion.1
  7.6 1.4 broadcast_multiply_fusion
  9.1 1.4 multiply_reduce_fusion.14
  11.9 0.8 copy.181
  12.7 0.8 copy.178
  13.5 0.8 copy.180
  14.2 0.8 copy.183
  15.4 13.3 %exchange_0.1 = s32[4,8,8,128]{3,2,1,0:T(8,128)} custom-call(s32[8,128]{1,0:T(8,128)} %add_bitcast_fusion.refs_0_), custom_call_target="tpu_custom_call" | custom-call | bytes 2703360 | tf_op jit(solution)/shard_map/exchange_0/pallas_call | solution.py:377
  28.6 0.9 copy.208
  29.7 0.8 select_reduce_fusion.1
  30.7 4.8 select_reduce_fusion
  36.4 1.0 convert.23
  37.4 1.1 convert.20
  38.5 0.8 concatenate.18.refs_1_
  39.2 0.7 maximum_maximum_fusion.refs_2_
  40.0 1.1 reshape.264.routes_ref
  41.1 6.4 convert_element_type.44.refs_3_.refs_1_
  47.4 17.6 %gather_rows.1 = bf16[32,256,384]{2,1,0:T(8,128)(2,1)S(1)} custom-call(s32[32,256]{1,0:T(8,128)S(1)} %fusion.16.list_ref, s32[32]{0:T(128)S(1)} %get-tuple-element.261.count_ref, f32[6144,384]{1,0:T(8,128)} %table_ref.1), custom_call_target="tpu_custom_call" | custom-call | tf_op jit(solution)/shard_map/gather_rows/pallas_call | solution.py:869
  65.1 2.7 copy-done.2
  67.8 120.8 %exchange_1.1 = (bf16[4,256,384]{2,1,0:T(8,128)(2,1)}, bf16[4,2,2,2,48,2176]{5,4,3,2,1,0:T(8,128)(2,1)}, bf16[4,2,2,2,48,2176]{5,4,3,2,1,0:T(8,128)(2,1)}, bf16[1536,1536]{1,0:T(8,128)(2,1)}) custom-call(bf16[4,2,2,2,256,384]{5,4,3,2,1,0:T(8,128)(2,1)} %bitcast.90, bf16[48,2176]{1,0:T(8,128)(2,1)} %concatenate.18.refs_1_, ...), custom_call_target="tpu_custom_call" | custom-call | bytes 606044160 | tf_op jit(solution)/shard_map/exchange_1/pallas_call | solution.py:377
  188.6 12.2 %attend.1 = (bf16[32,1536]{1,0:T(8,128)(2,1)}, f32[32,1536]{1,0:T(8,128)}, f32[8,96,256]{2,1,0:T(8,128)}, bf16[32,1536]{1,0:T(8,128)(2,1)}, bf16[256,512]{1,0:T(...) custom-call(s32[1]{0:T(128)} %bitcast.134, ...), custom_call_target="tpu_custom_call" | custom-call | tf_op jit(solution)/shard_map/attend/pallas_call | solution.py:723
  200.8 0.8 slice_reduce_fusion.1
  201.6 32.4 %exchange_2.1 = (bf16[4,2,2,2,32,1536]{5,4,3,2,1,0:T(8,128)(2,1)}, bf16[1536,1536]{1,0:T(8,128)(2,1)}) custom-call(bf16[32,1536]{1,0:T(8,128)(2,1)} %get-tuple-element.70.refs_0_.c_ref, bf16[6144,384]{1,0:T(8,128)(2,1)} %convert_element_type.44.refs_3_.refs_1_, bf16[1536,1536]{1,0:T(8,128)(2,1)} %get-tuple-element.71.refs_2_), custom_call_target="tpu_custom_call", output_to_operand_aliasing={{1}: (2, {})} | custom-call | bytes 347996160 | tf_op jit(solution)/shard_map/exchange_2/pallas_call | solution.py:377
  234.0 17.8 %experts_forward.1 = (bf16[1024,1536]{1,0:T(8,128)(2,1)}, f32[1024,1024]{1,0:T(8,128)}, f32[1024,128]{1,0:T(8,128)}, bf16[1536,1024]{1,0:T(8,128)(2,1)}, bf16[51...) custom-call(s32[4]{0:T(128)} %iota_add_fusion.1.lane_ref, bf16[1024,1536]{1,0:T(8,128)(2,1)} %bitcast.118, ...), custom_call_target="tpu_custom_call" | custom-call | tf_op jit(solution)/shard_map/experts_forward/pallas_call | solution.py:459
  251.8 33.8 %exchange_3.1 = (f32[32,1536]{1,0:T(8,128)}, bf16[1536,1536]{1,0:T(8,128)(2,1)}) custom-call(bf16[4,2,2,2,32,1536]{5,4,3,2,1,0:T(8,128)(2,1)} %bitcast.116, bf16[6144,384]{1,0:T(8,128)(2,1)} %convert_element_type.44.refs_3_.refs_1_, bf16[1536,1536]{1,0:T(8,128)(2,1)} %get-tuple-element.74.refs_2_), custom_call_target="tpu_custom_call", output_to_operand_aliasing={{1}: (2, {})} | custom-call | bytes 349962240 | tf_op jit(solution)/shard_map/exchange_3/pallas_call | solution.py:377
  285.7 1.3 copy.191
  287.0 1.1 multiply_reduce_fusion.11
  288.1 1.3 constant_dynamic-slice_fusion.gates_ref
  289.4 0.7 multiply_convert_fusion.1.refs_0_
  290.1 28.7 %exchange_4.1 = (bf16[4,2,2,2,32,1536]{5,4,3,2,1,0:T(8,128)(2,1)}, bf16[1536,1536]{1,0:T(8,128)(2,1)}) custom-call(bf16[32,1536]{1,0:T(8,128)(2,1)} %multiply_convert_fusion.1.refs_0_, bf16[6144,384]{1,0:T(8,128)(2,1)} %convert_element_type.44.refs_3_.refs_1_, bf16[1536,1536]{1,0:T(8,128)(2,1)} %get-tuple-element.77.refs_2_), custom_call_target="tpu_custom_call", output_to_operand_aliasing={{1}: (2, {})} | custom-call | bytes 347996160 | tf_op jit(solution)/shard_map/exchange_4/pallas_call | solution.py:377
  318.9 8.3 %multiply_reduce_fusion.2 = (f32[1024]{0:T(1024)S(1)}, f32[1024,1536]{1,0:T(8,128)S(1)}) fusion(bf16[1024,1536]{1,0:T(8,128)(2,1)} %bitcast.136, bf16[1536,1536]{1,0:T(8,128)(2,1)} %get-tuple-element.79), kind=kOutput, calls=%fused_computation.21 | convolution fusion | flops 4834982912 | bytes 14159872 | tf_op jit(solution)/shard_map/rd,vd->rv/dot_general | solution.py:1091
  327.2 2.7 copy-done.4
  329.8 3.4 exponential_reduce_fusion
  333.9 14.8 %exchange_5.1 = f32[4,8,8,384]{3,2,1,0:T(8,128)} custom-call(f32[8,384]{1,0:T(8,128)} %reshape.268.refs_0_), custom_call_target="tpu_custom_call" | custom-call | bytes 8110080 | tf_op jit(solution)/shard_map/exchange_5/pallas_call | solution.py:377
  348.7 1.2 reshape_reshape.7
  352.2 10.4 %multiply_convert_fusion = bf16[1024,1536]{1,0:T(8,128)(2,1)} fusion(bf16[1536,1536]{1,0:T(8,128)(2,1)} %get-tuple-element.79, f32[1024,1536]{1,0:T(8,128)} %copy-done.4, f32[1024]{0:T(1024)S(1)} %get-tuple-element.258, f32[1024]{0:T(1024)S(1)} %mul.633, s32[1536]{0:T(1024)S(1)} %iota_add_fusion, s32[1024]{0:T(1024)S(1)} %eq.178), kind=kOutput, calls=%fused_computation.19 | convolution fusion | flops 4845993984 | bytes 14174208 | tf_op jit(solution)/shard_map/dot_general | solution.py:1116
  362.6 10.9 %fusion.2.refs_1_.refs_3_ = bf16[1536,1536]{1,0:T(8,128)(2,1)} fusion(bf16[1024,1536]{1,0:T(8,128)(2,1)S(1)} %bitcast.137, f32[1024,1536]{1,0:T(8,128)} %copy-done.4, f32[1024]{0:T(1024)S(1)} %get-tuple-element.258, f32[1024]{0:T(1024)S(1)} %mul.633, s32[1536]{0:T(1024)S(1)} %iota_add_fusion, s32[1024]{0:T(1024)S(1)} %eq.178), kind=kOutput, calls=%fused_computation.13 | convolution fusion | flops 4847566848 | bytes 14174208 | tf_op jit(solution)/shard_map/rv,rd->vd/dot_general | solution.py:1118
  373.5 37.7 %exchange_6.1 = (f32[32,1536]{1,0:T(8,128)}, bf16[4,1536,384]{2,1,0:T(8,128)(2,1)}) custom-call(bf16[4,2,2,2,32,1536]{5,4,3,2,1,0:T(8,128)(2,1)} %bitcast.117, bf16[1536,1536]{1,0:T(8,128)(2,1)} %fusion.2.refs_1_.refs_3_), custom_call_target="tpu_custom_call" | custom-call | bytes 255590400 | tf_op jit(solution)/shard_map/exchange_6/pallas_call | solution.py:377
  411.2 1.1 multiply_reduce_fusion.9
  412.9 1.7 fusion.32
  414.6 31.8 %exchange_7.1 = (bf16[4,2,2,2,32,1536]{5,4,3,2,1,0:T(8,128)(2,1)}, bf16[4,1536,384]{2,1,0:T(8,128)(2,1)}) custom-call(bf16[32,1536]{1,0:T(8,128)(2,1)} %get-tuple-element.255.refs_0_, bf16[1536,1536]{1,0:T(8,128)(2,1)} %fusion.2.refs_1_.refs_3_, bf16[4,1536,384]{2,1,0:T(8,128)(2,1)} %get-tuple-element.82.refs_2_), custom_call_target="tpu_custom_call", output_to_operand_aliasing={{1}: (2, {})} | custom-call | bytes 347996160 | tf_op jit(solution)/shard_map/exchange_7/pallas_call | solution.py:377
  446.4 13.3 %experts_backward.1 = (bf16[1024,1664]{1,0:T(8,128)(2,1)}, bf16[1024,1024]{1,0:T(8,128)(2,1)}) custom-call(s32[4]{0:T(128)} %iota_add_fusion.1.lane_ref, bf16[1024,1536]{1,0:T(8,128)(2,1)} %bitcast.114, f32[1024,1024]{1,0:T(8,128)} %get-tuple-element.84.mid_ref, f32[1024,128]{1,0:T(8,128)} %get-tuple-element.85.gates_ref, ...), custom_call_target="tpu_custom_call" | custom-call | tf_op jit(solution)/shard_map/experts_backward/pallas_call | solution.py:538
  459.7 39.7 %exchange_8.1 = (f32[32,1664]{1,0:T(8,128)}, bf16[4,1536,384]{2,1,0:T(8,128)(2,1)}) custom-call(bf16[4,2,2,2,32,1664]{5,4,3,2,1,0:T(8,128)(2,1)} %bitcast.113, bf16[1536,1536]{1,0:T(8,128)(2,1)} %fusion.2.refs_1_.refs_3_, bf16[4,1536,384]{2,1,0:T(8,128)(2,1)} %get-tuple-element.91.refs_2_), custom_call_target="tpu_custom_call", output_to_operand_aliasing={{1}: (2, {})} | custom-call | bytes 355532800 | tf_op jit(solution)/shard_map/exchange_8/pallas_call | solution.py:377
  499.4 23.9 %attend_back.1 = (bf16[4,256,384]{2,1,0:T(8,128)(2,1)}, bf16[1536,2176]{1,0:T(8,128)(2,1)}, bf16[1536,2176]{1,0:T(8,128)(2,1)}) custom-call(s32[1]{0:T(128)} %bitcast.135, f32[32,1664]{1,0:T(8,128)} %get-tuple-element.92.back_ref, f32[32,128]{1,0:T(8,128)} %constant_dynamic-slice_fusion.gates_ref, f32[32,1536]{1,0:T(8,128)} %get-tuple-element.256.grad_two_ref, ...), custom_call_target="tpu_custom_call" | custom-call | tf_op jit(solution)/shard_map/attend_back/pallas_call | solution.py:811
  523.4 118.4 %exchange_9.1 = (bf16[4,2,2,2,256,384]{5,4,3,2,1,0:T(8,128)(2,1)}, f32[48,2176]{1,0:T(8,128)}, f32[48,2176]{1,0:T(8,128)}, bf16[4,1536,384]{2,1,0:T(8,128)(2,1)}) custom-call(bf16[4,256,384]{2,1,0:T(8,128)(2,1)} %get-tuple-element.99.refs_0_, bf16[4,2,2,2,48,2176]{5,4,3,2,1,0:T(8,128)(2,1)} %bitcast.105, ...), custom_call_target="tpu_custom_call", output_to_operand_aliasing={{3}: (4, {})} | custom-call | bytes 708771840 | tf_op jit(solution)/shard_map/exchange_9/pallas_call | solution.py:377
  641.9 28.8 %scatter_rows.1 = f32[6144,384]{1,0:T(8,128)} custom-call(s32[32,256]{1,0:T(8,128)S(1)} %fusion.16.list_ref, s32[32]{0:T(128)S(1)} %get-tuple-element.261.count_ref, bf16[32,256,384]{2,1,0:T(8,128)(2,1)} %bitcast.112, bf16[6144,384]{1,0:T(8,128)(2,1)} %bitcast.95), custom_call_target="tpu_custom_call" | custom-call | tf_op jit(solution)/shard_map/scatter_rows/pallas_call | solution.py:906
  670.7 1.3 multiply_reduce_fusion.13
  675.4 1.7 multiply_reduce_fusion.8
  677.2 1.2 multiply_reduce_fusion.6
  678.4 6.4 fusion.36.grad_ref
  685.2 6.3 multiply_reduce_fusion.4
  691.5 15.0 %in_moments.1 = (f32[12288,128]{1,0:T(8,128)}, f32[12288,128]{1,0:T(8,128)}, f32[2,8,128]{2,1,0:T(8,128)S(1)}) custom-call(f32[2]{0:T(128)S(1)} %pad_maximum_fusion.4.scale_ref, f32[1536,1024]{1,0:T(8,128)S(1)} %fusion.36.grad_ref, f32[12288,128]{1,0:T(8,128)S(1)} %bitcast.89, f32[12288,128]{1,0:T(8,128)} %bitcast.107, f32[12288,128]{1,0:T(8,128)} %bitcast.108), custom_call_target="tpu_custom_call" | custom-call | tf_op jit(solution)/shard_map/in_moments/pallas_call | solution.py:591
  707.2 21.0 %multiply_reduce_fusion.1 = (f32[]{:T(128)}, f32[]{:T(128)}, f32[6144,384]{1,0:T(8,128)}, f32[6144,384]{1,0:T(8,128)}) fusion(f32[6144,384]{1,0:T(8,128)S(1)} %bitcast.92, f32[]{:T(128)} %div.86, f32[]{:T(128)} %div.85, f32[6144,384]{1,0:T(8,128)} %scatter_rows.1, f32[6144,384]{1,0:T(8,128)} %param.34, f32[6144,384]{1,0:T(8,128)} %param.35), kind=kLoop, calls=%fused_computation.5 | loop fusion | flops 40108032 | bytes 56623120 | tf_op jit(solution)/shard_map/reduce_sum | solution.py:1199
  728.3 9.6 %select_select_fusion.refs_0_ = f32[8,128]{1,0:T(8,128)} fusion(f32[]{:T(128)} %get-tuple-element.225, f32[]{:T(128)} %get-tuple-element.224, f32[]{:T(128)} %get-tuple-element.233, f32[]{:T(128)} %get-tuple-element.232, f32[]{:T(128)} %get-tuple-element.237, f32[]{:T(128)} %get-tuple-element.236, f32[]{:T(128)} %get-tuple-element.270, ...), kind=kLoop, calls=%fused_computation.97 | loop fusion | flops 28672 | bytes 4464 | tf_op jit(solution)/shard_map/jit(_where)/select_n | solution.py:1208
  737.9 12.4 %exchange_10.1 = f32[4,8,8,128]{3,2,1,0:T(8,128)} custom-call(f32[8,128]{1,0:T(8,128)} %select_select_fusion.refs_0_), custom_call_target="tpu_custom_call" | custom-call | bytes 2703360 | tf_op jit(solution)/shard_map/exchange_10/pallas_call | solution.py:377
  750.3 0.9 reduce_sum.293
  758.5 1.9 multiply_subtract_fusion.4
  760.4 1.0 multiply_subtract_fusion.3
  761.5 7.4 multiply_subtract_fusion.2
  769.0 10.3 %multiply_subtract_fusion.1 = f32[12288,128]{1,0:T(8,128)} fusion(f32[12288,128]{1,0:T(8,128)} %bitcast.86, f32[12288,128]{1,0:T(8,128)} %get-tuple-element.108, f32[12288,128]{1,0:T(8,128)} %get-tuple-element.107, f32[]{:T(128)} %div.86, f32[]{:T(128)} %div.85, f32[]{:T(128)} %bitcast.40), kind=kLoop, calls=%fused_computation.18 | loop fusion | flops 12582912 | bytes 25165836 | tf_op jit(solution)/shard_map/sub | solution.py:1217
  779.3 1.6 slice-done.9
  781.4 6.6 multiply_subtract_fusion
  (166 shorter events, 17.4 us)
Async XLA Ops:
  0.7 8.4 %copy-start = (s32[256,8]{0,1:T(8,128)S(1)}, s32[256,8]{0,1:T(8,128)}, u32[]{:S(2)}) copy-start(s32[256,8]{0,1:T(8,128)} %param.31) | copy-start | bytes 24580
  4.2 43.3 %copy-start.22 = (s32[1,32]{1,0:T(1,128)}, s32[1,32]{1,0:T(1,128)S(1)}, u32[]{:S(2)}) copy-start(s32[1,32]{1,0:T(1,128)S(1)} %constant_dynamic-slice_fusion.4) | copy-start | bytes 388
  15.3 32.1 %copy-start.10 = (f32[256,128]{1,0:T(8,128)}, f32[256,128]{1,0:T(8,128)S(1)}, u32[]{:S(2)}) copy-start(f32[256,128]{1,0:T(8,128)S(1)} %copy.169.sin_ref) | copy-start | bytes 393220
  35.7 11.7 %copy-start.11 = (f32[256,128]{1,0:T(8,128)}, f32[256,128]{1,0:T(8,128)S(1)}, u32[]{:S(2)}) copy-start(f32[256,128]{1,0:T(8,128)S(1)} %copy.168.cos_ref) | copy-start | bytes 393220
  65.1 2.7 copy-start.2
  251.8 33.8 %copy-start.13 = (bf16[1024,512]{1,0:T(8,128)(2,1)S(1)}, bf16[1024,512]{1,0:T(8,128)(2,1)}, u32[]{:S(2)}) copy-start(bf16[1024,512]{1,0:T(8,128)(2,1)} %get-tuple-element.80) | copy-start | bytes 3145732
  251.8 35.2 %copy-start.14 = (f32[32,1536]{1,0:T(8,128)S(1)}, f32[32,1536]{1,0:T(8,128)}, u32[]{:S(2)}) copy-start(f32[32,1536]{1,0:T(8,128)} %get-tuple-element.69.resid_ref) | copy-start | bytes 589828
  327.1 2.7 copy-start.4
  327.1 23.3 %copy-start.30 = (f32[32]{0:T(128)S(1)}, f32[32]{0:T(128)}, u32[]{:S(2)}) copy-start(f32[32]{0:T(128)} %param.30) | copy-start | bytes 388
  352.2 10.4 %copy-start.29 = (bf16[4,2,2,2,32,1536]{5,4,3,2,1,0:T(8,128)(2,1)S(1)}, bf16[4,2,2,2,32,1536]{5,4,3,2,1,0:T(8,128)(2,1)}, u32[]{:S(2)}) copy-start(bf16[4,2,2,2,32,1536]{5,4,3,2,1,0:T(8,128)(2,1)} %get-tuple-element.78) | copy-start | bytes 9437188
  641.8 28.9 %copy-start.17 = (f32[48,2176]{1,0:T(8,128)S(1)}, f32[48,2176]{1,0:T(8,128)}, u32[]{:S(2)}) copy-start(f32[48,2176]{1,0:T(8,128)} %get-tuple-element.103) | copy-start | bytes 1253380
  641.8 33.6 %copy-start.18 = (f32[48,2176]{1,0:T(8,128)S(1)}, f32[48,2176]{1,0:T(8,128)}, u32[]{:S(2)}) copy-start(f32[48,2176]{1,0:T(8,128)} %get-tuple-element.104) | copy-start | bytes 1253380
  641.8 33.6 %copy-start.7 = (f32[48,1536]{1,0:T(8,128)S(1)}, f32[48,1536]{1,0:T(8,128)}, u32[]{:S(2)}) copy-start(f32[48,1536]{1,0:T(8,128)} %param.39) | copy-start | bytes 884740
  641.8 33.6 %copy-start.19 = (f32[48,1536]{1,0:T(8,128)S(1)}, f32[48,1536]{1,0:T(8,128)}, u32[]{:S(2)}) copy-start(f32[48,1536]{1,0:T(8,128)} %param.40) | copy-start | bytes 884740
  641.8 33.6 %copy-start.20 = (f32[48,1536]{1,0:T(8,128)S(1)}, f32[48,1536]{1,0:T(8,128)}, u32[]{:S(2)}) copy-start(f32[48,1536]{1,0:T(8,128)} %param.41) | copy-start | bytes 884740
  641.8 35.3 %copy-start.5 = (f32[48,2560]{1,0:T(8,128)S(1)}, f32[48,2560]{1,0:T(8,128)}, u32[]{:S(2)}) copy-start(f32[48,2560]{1,0:T(8,128)} %param.36) | copy-start | bytes 1474564
  641.8 35.3 %copy-start.15 = (f32[48,2560]{1,0:T(8,128)S(1)}, f32[48,2560]{1,0:T(8,128)}, u32[]{:S(2)}) copy-start(f32[48,2560]{1,0:T(8,128)} %param.37) | copy-start | bytes 1474564
  641.9 35.3 %copy-start.16 = (f32[48,2560]{1,0:T(8,128)S(1)}, f32[48,2560]{1,0:T(8,128)}, u32[]{:S(2)}) copy-start(f32[48,2560]{1,0:T(8,128)} %param.38) | copy-start | bytes 1474564
  678.4 82.1 %copy-start.8 = (f32[48,2560]{1,0:T(8,128)}, f32[48,2560]{1,0:T(8,128)S(1)}, u32[]{:S(2)}) copy-start(f32[48,2560]{1,0:T(8,128)S(1)} %get-tuple-element.251) | copy-start | bytes 1474564
  678.4 82.1 %copy-start.9 = (f32[48,2560]{1,0:T(8,128)}, f32[48,2560]{1,0:T(8,128)S(1)}, u32[]{:S(2)}) copy-start(f32[48,2560]{1,0:T(8,128)S(1)} %get-tuple-element.252) | copy-start | bytes 1474564
  678.4 6.5 copy-start.3
  678.4 6.5 copy-start.6
  678.4 6.5 copy-start.12
  678.4 6.5 copy-start.27
  678.4 6.8 copy-start.28
  678.4 13.1 %slice-start = ((s8[6291456]{0:T(1024)(128)(4,1)}), s8[4194304]{0:T(1024)(128)(4,1)S(1)}, s32[]{:S(2)}) async-start(s8[6291456]{0:T(1024)(128)(4,1)} %bitcast.87), calls=%async_computation | async-start | bytes 8388608
  685.2 6.3 slice-start.1
  691.5 15.7 %slice-start.2 = ((s8[9437184]{0:T(1024)(128)(4,1)}), s8[4194304]{0:T(1024)(128)(4,1)S(1)}, s32[]{:S(2)}) async-start(s8[9437184]{0:T(1024)(128)(4,1)} %bitcast.91), calls=%async_computation.2 | async-start | bytes 8388608
  691.5 15.6 %slice-start.3 = ((s8[9437184]{0:T(1024)(128)(4,1)}), s8[4194304]{0:T(1024)(128)(4,1)S(1)}, s32[]{:S(2)}) async-start(s8[9437184]{0:T(1024)(128)(4,1)} %bitcast.91), calls=%async_computation.3 | async-start | bytes 8388608
  691.5 15.6 %slice-start.4 = ((s8[9437184]{0:T(1024)(128)(4,1)}), s8[1048576]{0:T(1024)(128)(4,1)S(1)}, s32[]{:S(2)}) async-start(s8[9437184]{0:T(1024)(128)(4,1)} %bitcast.91), calls=%async_computation.4 | async-start | bytes 2097152
  707.2 21.1 %copy-start.23 = (pred[8]{0:T(512)(128)(4,1)S(1)}, pred[8]{0:T(512)(128)(4,1)}, u32[]{:S(2)}) copy-start(pred[8]{0:T(512)(128)(4,1)} %get-tuple-element.295) | copy-start | bytes 28
  707.2 21.1 %copy-start.24 = (pred[8]{0:T(512)(128)(4,1)S(1)}, pred[8]{0:T(512)(128)(4,1)}, u32[]{:S(2)}) copy-start(pred[8]{0:T(512)(128)(4,1)} %get-tuple-element.296) | copy-start | bytes 28
  707.2 21.1 %copy-start.25 = (pred[8]{0:T(512)(128)(4,1)S(1)}, pred[8]{0:T(512)(128)(4,1)}, u32[]{:S(2)}) copy-start(pred[8]{0:T(512)(128)(4,1)} %get-tuple-element.293) | copy-start | bytes 28
  707.2 21.1 %copy-start.26 = (pred[8]{0:T(512)(128)(4,1)S(1)}, pred[8]{0:T(512)(128)(4,1)}, u32[]{:S(2)}) copy-start(pred[8]{0:T(512)(128)(4,1)} %get-tuple-element.294) | copy-start | bytes 28
  707.2 49.9 %copy-start.21 = (f32[3,48]{0,1:T(8,128)S(1)}, f32[3,48]{0,1:T(8,128)}, u32[]{:S(2)}) copy-start(f32[3,48]{0,1:T(8,128)} %get-tuple-element.243) | copy-start | bytes 1732
  760.4 18.8 %slice-start.11 = ((s8[9437184]{0:T(1024)(128)(4,1)}), s8[4194304]{0:T(1024)(128)(4,1)S(1)}, s32[]{:S(2)}) async-start(s8[9437184]{0:T(1024)(128)(4,1)} %bitcast.101), calls=%async_computation.11 | async-start | bytes 8388608
  761.5 17.7 %slice-start.5 = ((s8[9437184]{0:T(1024)(128)(4,1)}), s8[4194304]{0:T(1024)(128)(4,1)S(1)}, s32[]{:S(2)}) async-start(s8[9437184]{0:T(1024)(128)(4,1)} %bitcast.93), calls=%async_computation.5 | async-start | bytes 8388608
  761.5 17.7 %slice-start.8 = ((s8[9437184]{0:T(1024)(128)(4,1)}), s8[4194304]{0:T(1024)(128)(4,1)S(1)}, s32[]{:S(2)}) async-start(s8[9437184]{0:T(1024)(128)(4,1)} %bitcast.99), calls=%async_computation.8 | async-start | bytes 8388608
  761.5 17.7 %slice-start.12 = ((s8[9437184]{0:T(1024)(128)(4,1)}), s8[4194304]{0:T(1024)(128)(4,1)S(1)}, s32[]{:S(2)}) async-start(s8[9437184]{0:T(1024)(128)(4,1)} %bitcast.101), calls=%async_computation.12 | async-start | bytes 8388608
  768.9 10.3 %slice-start.6 = ((s8[9437184]{0:T(1024)(128)(4,1)}), s8[4194304]{0:T(1024)(128)(4,1)S(1)}, s32[]{:S(2)}) async-start(s8[9437184]{0:T(1024)(128)(4,1)} %bitcast.93), calls=%async_computation.6 | async-start | bytes 8388608
  768.9 10.3 %slice-start.7 = ((s8[9437184]{0:T(1024)(128)(4,1)}), s8[1048576]{0:T(1024)(128)(4,1)S(1)}, s32[]{:S(2)}) async-start(s8[9437184]{0:T(1024)(128)(4,1)} %bitcast.93), calls=%async_computation.7 | async-start | bytes 2097152
  768.9 11.9 %slice-start.9 = ((s8[9437184]{0:T(1024)(128)(4,1)}), s8[4194304]{0:T(1024)(128)(4,1)S(1)}, s32[]{:S(2)}) async-start(s8[9437184]{0:T(1024)(128)(4,1)} %bitcast.99), calls=%async_computation.9 | async-start | bytes 8388608
  768.9 12.1 %slice-start.10 = ((s8[9437184]{0:T(1024)(128)(4,1)}), s8[1048576]{0:T(1024)(128)(4,1)S(1)}, s32[]{:S(2)}) async-start(s8[9437184]{0:T(1024)(128)(4,1)} %bitcast.99), calls=%async_computation.10 | async-start | bytes 2097152
  768.9 12.4 %slice-start.13 = ((s8[9437184]{0:T(1024)(128)(4,1)}), s8[1048576]{0:T(1024)(128)(4,1)S(1)}, s32[]{:S(2)}) async-start(s8[9437184]{0:T(1024)(128)(4,1)} %bitcast.101), calls=%async_computation.13 | async-start | bytes 2097152
  781.4 6.6 copy-start.1

commit v5 on v4

--- a/solution.py
+++ b/solution.py
@@ -158,9 +158,9 @@
     flat = False
     scratch = ()
 
-    def __init__(self, xs, groups, planes, side, exchange=False):
+    def __init__(self, xs, groups, planes, side, exchange=False, prior=False):
         self.planes, self.side, self.inputs, self.groups = planes, side, xs, groups
-        self.exchange = exchange
+        self.exchange, self.prior = exchange, prior
         grid = (planes, side, side, 2)
         self.outputs = [jax.ShapeDtypeStruct(grid + x.shape[-2:], x.dtype) for x in xs]
         self.copies = sum(map(len, groups)) * (planes - 1 + 2 * (side - 1) + 1)
@@ -169,11 +169,16 @@
         xs, outs = refs[: len(self.inputs)], refs[len(self.inputs) :]
         z, a, b, core = spot.z, spot.a, spot.b, spot.core
         for x, out in zip(xs, outs):
-            out[z, a, b, core] = x[z] if self.exchange else x[...]
+            if self.prior:
+                out[:, a, b, core] = x[...]
+            else:
+                out[z, a, b, core] = x[z] if self.exchange else x[...]
 
         def stage(step, key, cut):
             i, rows, columns, first = cut
             x, out = xs[i], outs[i]
+            if step == 0 and self.prior:
+                return []
             if step == 0:
                 place = out.at[z, a, b, core, rows, columns]
                 sent = []
@@ -204,12 +209,12 @@
 class Reduce:
     flat = False
 
-    def __init__(self, xs, groups, planes, side, exchange=False):
+    def __init__(self, xs, groups, planes, side, exchange=False, partial=False):
         self.planes, self.side, self.inputs, self.groups = planes, side, xs, groups
-        self.exchange = exchange
+        self.exchange, self.partial = exchange or partial, partial
         self.outputs = [
             jax.ShapeDtypeStruct((planes,) + x.shape[-2:], x.dtype)
-            if exchange
+            if self.exchange
             else jax.ShapeDtypeStruct(x.shape[-2:], f32)
             for x in xs
         ]
@@ -225,7 +230,7 @@
                     (side - 1, planes),
                     (planes,),
                 )
-                + (() if exchange else ((planes - 1,),))
+                + (() if self.exchange else ((planes - 1,),))
             ]
         self.copies = sum(map(len, groups)) * (planes - 1 + 2 * (side - 1) + 1)
 
@@ -280,10 +285,15 @@
                     total = two[iz, mine].astype(f32)
                     for k in range(side - 1):
                         total += hop_three[k, iz].astype(f32)
-                    three[iz] = total.astype(three.dtype)
+                    if self.partial:
+                        out[iz, rows, columns] = total.astype(out.dtype)
+                    else:
+                        three[iz] = total.astype(three.dtype)
                     return carry
 
                 lax.fori_loop(0, planes, add, 0)
+                if self.partial:
+                    return []
                 for k in range(1, planes):
                     peer, target = spot.plane(k)
                     if self.exchange:
@@ -305,46 +315,82 @@
 
 class Swap:
     flat = False
-    scratch = (pltpu.SemaphoreType.DMA(()),)
-
-    def __init__(self, x, start, size, planes, side, rounds, back=False, held=None):
+    def __init__(self, x, turns, planes, side, back=False, held=None):
         self.planes, self.side = planes, side
         self.inputs = [x] if held is None else [x, held]
         self.in_spaces, self.out_spaces = (pl.ANY,) * len(self.inputs), (pl.ANY,)
         self.aliases = {} if held is None else {1: 0}
-        self.begin, self.size, self.rounds, self.back = start, size, rounds, back
+        self.turns, self.back = turns, back
+        self.scratch = [pltpu.SemaphoreType.DMA((len(turns),))]
         self.columns = x.shape[1] // planes if back else x.shape[1]
         self.rows = x.shape[0] if back else x.shape[0] // planes
         shape = (planes, self.rows, self.columns) if back else (self.rows, planes * self.columns)
         self.outputs = [jax.ShapeDtypeStruct(shape, x.dtype)]
-        self.copies = planes - 1
+        self.copies = len(turns) * (planes - 1)
 
     def steps(self, spot, mail, *refs):
         x, out, own_sem = refs[0], refs[-2], refs[-1]
-        rows = pl.ds(self.begin, self.size)
-
         def block(z):
             return pl.ds(pl.multiple_of(z * self.columns, 128), self.columns)
 
-        def source(z):
+        def source(z, begin, size):
             if self.back:
-                return x.at[rows, block(z)]
-            return x.at[pl.ds(pl.multiple_of(z * self.rows + self.begin, 16), self.size), :]
-
-        for _ in range(self.rounds):
+                return x.at[pl.ds(begin, size), block(z)]
+            return x.at[pl.ds(pl.multiple_of(z * self.rows + begin, 16), size), :]
+
+        sent, own, now = [], [], 0
+        for n, (begin, size, rounds) in enumerate(self.turns):
+            while now < rounds:
+                now += 1
+                yield
+            rows = pl.ds(begin, size)
+            place = out.at[spot.z, rows] if self.back else out.at[rows, block(spot.z)]
+            for k in range(1, self.planes):
+                peer, target = spot.plane(k)
+                sent.append(mail.start(source(peer, begin, size), place, target))
+            own.append(pltpu.make_async_copy(source(spot.z, begin, size), place, own_sem.at[n]))
+            own[-1].start()
+        while now < 24:
+            now += 1
             yield
-        place = out.at[spot.z, rows] if self.back else out.at[rows, block(spot.z)]
-        sent = []
-        for k in range(1, self.planes):
-            peer, target = spot.plane(k)
-            sent.append(mail.start(source(peer), place, target))
-        own = pltpu.make_async_copy(source(spot.z), place, own_sem)
-        own.start()
-        for _ in range(20):
-            yield
-        own.wait()
+        for copy in own:
+            copy.wait()
         for copy in sent:
             copy.wait_recv()
+
+
+class Chain:
+    flat = False
+
+    def __init__(self, reduce, extra, extra_out, middle, gather):
+        self.planes, self.side = reduce.planes, reduce.side
+        self.reduce, self.middle, self.gather = reduce, middle, gather
+        self.inputs = reduce.inputs + extra
+        self.outputs = gather.outputs + extra_out
+        self.scratch = reduce.scratch + [
+            pltpu.VMEM(x.shape, x.dtype) for x in reduce.outputs + gather.inputs
+        ]
+        self.copies = reduce.copies + gather.copies
+
+    def steps(self, spot, mail, *refs):
+        n_in, n_out = len(self.inputs), len(self.outputs)
+        (x, *extra), (out, *extra_out) = refs[:n_in], refs[n_in : n_in + n_out]
+        *held, sums, made = refs[n_in + n_out :]
+        yield from self.reduce.steps(spot, mail, x, sums, *held)
+        self.middle(sums, made, *extra, *extra_out)
+        yield from self.gather.steps(spot, mail, made, out)
+
+
+def final_norm(sums, made, resid, gains, resid_two):
+    values = resid[...] + sums[...]
+    resid_two[...] = values
+    made[...] = (values * inverse_root(values) * gains[2:3]).astype(bf16)
+
+
+def final_norm_back(sums, made, resid_two, gains, grad_two, gain_grad):
+    grad, gain_grad[...] = norm_back(resid_two[...], gains[2:3], sums[...])
+    grad_two[...] = grad
+    made[...] = grad.astype(bf16)
 
 
 def communicate(parts, ident):
@@ -977,18 +1023,22 @@
 
     unit = own_rows // 24
 
-    def swap(x, start, size, rounds, back=False, held=None):
-        return Swap(x, start * unit, size * unit, planes, side, rounds, back, held)
-
-    def gather_completion(rows, ident, *beside):
-        part = Gather([rows], split(0, COMP, rows.shape[1], 2, 2), planes, side)
-        out = communicate([part, *beside], ident)
-        return (out[0].reshape(rows_all, rows.shape[1]), *out[1:])
-
-    def reduce_completion(rows, ident, cuts, *beside):
+    def swap(x, *turns, back=False, held=None):
+        turns = [(start * unit, size * unit, rounds) for start, size, rounds in turns]
+        return Swap(x, turns, planes, side, back, held)
+
+    def gather_part(rows):
+        return Gather([rows], split(0, COMP, rows.shape[1], 2, 2), planes, side)
+
+    def reduce_part(rows, cuts):
         rows = rows.reshape(grid + (COMP, rows.shape[1]))
-        part = Reduce([rows], split(0, COMP, rows.shape[-1], 2, cuts), planes, side)
-        return communicate([part, *beside], ident)
+        return Reduce([rows], split(0, COMP, rows.shape[-1], 2, cuts), planes, side)
+
+    def chain(rows, extra, extra_out, middle, beside, ident):
+        gather = gather_part(jax.ShapeDtypeStruct((COMP, D), bf16))
+        part = Chain(reduce_part(rows, 2), extra, extra_out, middle, gather)
+        out = communicate([part, beside], ident)
+        return (out[0].reshape(rows_all, D), *out[1:])
 
     def gather_tiny(block, ident):
         return communicate([Tiny(block, planes, side)], ident)[0].reshape((devices,) + block.shape)
@@ -1051,11 +1101,27 @@
         ).astype(bf16),
     ]
     table_b = embed_table.astype(bf16)
-    picked, first_pack, second_pack, table_one = send(
+    packs = jnp.concatenate(packs, axis=0)
+    packs, sheets = lax.optimization_barrier((packs, sheets))
+    packs = lax.all_to_all(
+        jnp.broadcast_to(packs[None], (planes,) + packs.shape),
+        "expert",
+        split_axis=0,
+        concat_axis=0,
+        tiled=True,
+    )
+    table_b = embed_table.astype(bf16)
+    picked, first_pack, second_pack, table_own = send(
         [
             Reduce([picked], embed_groups, planes, side, exchange=True),
-            Gather(packs, weight_groups, planes, side),
-            swap(table_b, 0, 12, 3),
+            Gather(
+                [packs[:, :weight_rows], packs[:, weight_rows:]],
+                weight_groups,
+                planes,
+                side,
+                prior=True,
+            ),
+            swap(table_b, (0, 16, 0)),
         ],
         1,
     )
@@ -1069,9 +1135,10 @@
         start_at, picked, first_pack, second_pack, *tables
     )
 
-    expert_rows, table_own = gather_completion(
-        normed_two_b, 2, swap(table_b, 12, 4, 2, held=table_one)
-    )
+    expert_rows, table_own = communicate(
+        [gather_part(normed_two_b), swap(table_b, (16, 2, 2), held=table_own)], 2
+    )
+    expert_rows = expert_rows.reshape(rows_all, D)
     lanes = shard_id * local_experts + jnp.arange(local_experts, dtype=jnp.int32)
     in_rows = in_weight.reshape(-1, hidden_units)
     produced, mid, gates, in_cat, down_b, gated_hidden = experts_forward(
@@ -1079,15 +1146,16 @@
     )
     own_index = expert_id * shards + shard_id
     own_gates = lax.dynamic_slice(gates, (own_index * COMP, 0), (COMP, 128))
-    combined, table_own = reduce_completion(
-        produced, 3, 2, swap(table_b, 16, 4, 0, held=table_own)
-    )
-    resid_two = resid + combined
-
-    final_rows = resid_two * inverse_root(resid_two) * gains[2:3]
-    head_rows, table_own = gather_completion(
-        final_rows.astype(bf16), 4, swap(table_b, 20, 4, 2, held=table_own)
-    )
+    row_block = jax.ShapeDtypeStruct((COMP, D), f32)
+    head_rows, resid_two, table_own = chain(
+        produced,
+        [resid, gains],
+        [row_block],
+        final_norm,
+        swap(table_b, (18, 3, 0), (21, 3, 8), held=table_own),
+        3,
+    )
+
     logits = jnp.einsum("rd,vd->rv", head_rows, table_own, preferred_element_type=f32) / LOGIT_SCALE
     own_base = vocab_base + expert_id * own_rows
     target_hot = targets[:, None] == own_base + jnp.arange(own_rows, dtype=jnp.int32)[None, :]
@@ -1113,21 +1181,23 @@
     grad_logits = (
         row_grad[:, None] * (target_hot.astype(f32) - jnp.exp(logits - row_lse[:, None]))
     ).astype(bf16)
+    grad_logits = lax.optimization_barrier(grad_logits)
     grad_rows = jnp.dot(grad_logits, table_own, preferred_element_type=f32) / LOGIT_SCALE
     head_grad = (
         jnp.einsum("rv,rd->vd", grad_logits, head_rows, preferred_element_type=f32) / LOGIT_SCALE
     ).astype(bf16)
-    own_grad_rows, head_back = reduce_completion(
-        grad_rows.astype(bf16), 6, 2, swap(head_grad, 0, 5, 0, back=True)
-    )
-    grad_resid_two, grad_gain_three = norm_back(resid_two, gains[2:3], own_grad_rows)
-
-    grad_all, head_back = gather_completion(
-        grad_resid_two.astype(bf16), 7, swap(head_grad, 5, 5, 2, back=True, held=head_back)
-    )
+    grad_all, grad_resid_two, grad_gain_three, head_back = chain(
+        grad_rows.astype(bf16),
+        [resid_two, gains],
+        [row_block, jax.ShapeDtypeStruct((1, D), f32)],
+        final_norm_back,
+        swap(head_grad, (0, 3, 0), (3, 3, 8), back=True),
+        6,
+    )
+
     back, mid_grad = experts_backward(lanes, grad_all, mid, gates, in_cat, down_b)
-    back, head_back = reduce_completion(
-        back, 8, 1, swap(head_grad, 10, 5, 0, back=True, held=head_back)
+    back, head_back = communicate(
+        [reduce_part(back, 1), swap(head_grad, (6, 3, 0), back=True, held=head_back)], 8
     )
 
     grad_embedded, *grad_packs = attend_back(
@@ -1155,11 +1225,20 @@
     sent, first_grad, second_grad, head_back = send(
         [
             Gather([grad_embedded], embed_groups, planes, side, exchange=True),
-            Reduce(grad_packs, weight_groups, planes, side),
-            swap(head_grad, 15, 9, 3, back=True, held=head_back),
+            Reduce(grad_packs, weight_groups, planes, side, partial=True),
+            swap(head_grad, (9, 15, 4), back=True, held=head_back),
         ],
         9,
     )
+    plane_sums = lax.all_to_all(
+        jnp.concatenate([first_grad, second_grad], axis=1),
+        "expert",
+        split_axis=0,
+        concat_axis=0,
+        tiled=True,
+    ).astype(f32)
+    first_grad = jnp.sum(plane_sums[:, :weight_rows], axis=0)
+    second_grad = jnp.sum(plane_sums[:, weight_rows:], axis=0)
     table_grad = scatter_rows(
         lists,
         counts,

time: 803 us -> 786 us (0.979)
  Pallas kernels: 612 us -> 578 us
  starting transfers between devices: 0 us -> 24.5 us
  local copies, waits for them, and re-layouts: 29.9 us -> 19.6 us
    pallas_call x11 -> x9, Pallas kernels: 484 us -> 457 us  [communicate(): pl.pallas_call(kernel, out_shape=[x for p in parts for x in p.outputs], i...]
    all_to_all x0 -> x2, starting transfers between devices: none -> 24.5 us  [the longest x1 20.2 us: on_device(): lax.all_to_all(jnp.concatenate([first_grad, second_grad], axis=1), 'exper...]
    unnamed x103 -> x91, local copies, waits for them, and re-layouts: 16.8 us -> 7.73 us
  transfers between devices with their start and end apart: 0 -> 2, of which waited for: 0 -> 1; matrix products, arithmetic and copies ran while one was open for 0% -> 7% of each run, Pallas kernels for 0% -> 7%
where the time goes in v5:
time: 786 us; the launch traced here: 774 us
  Pallas kernels  578 us (74%)
  other arithmetic  98.1 us (12%)
  matrix products  38 us (5%)
  starting transfers between devices  24.5 us (3%)
  local copies, waits for them, and re-layouts  19.6 us (2%)
  between operations  9.04 us (1%)
    pallas_call x9, Pallas kernels, communicate(): pl.pallas_call(kernel, out_shape=[x for p in parts for x in p.outputs], i...  457 us
    sub x7, other arithmetic, on_device(): weight - STEP_RATE * trust_ratio[place] * parts[2]  28.2 us
    pallas_call x1, Pallas kernels, scatter_rows(): pl.pallas_call(scatter_kernel, grid_spec=pltpu.PrefetchScalarGridSpec(num...  26.7 us
    reduce_sum x5, other arithmetic, on_device(): jnp.sum(parts[2] * parts[2])  26.6 us
    pallas_call x1, Pallas kernels, attend_back(): pl.pallas_call(attend_back_kernel, in_specs=[pl.BlockSpec(memory_space=pl...  23.9 us
    all_to_all x1, starting transfers between devices, on_device(): lax.all_to_all(jnp.concatenate([first_grad, second_grad], axis=1), 'exper...  20.2 us
    pallas_call x1, Pallas kernels, experts_forward(): pl.pallas_call(forward_kernel, grid_spec=pltpu.PrefetchScalarGridSpec(num...  17.8 us
  transfers between devices with their start and end apart: 2, of which 1 were waited for; matrix products, arithmetic and copies ran while one was open for 7% of the time, Pallas kernels for 7%

profile of v5, /device:TPU:0, one launch (start us, length us, event | category | flops | bytes accessed | tf_op | source)
XLA Modules:
  0.0 774.4 jit_solution(10896448338596642714)
XLA Ops:
  0.7 0.7 fusion.45
  1.4 0.7 constant_dynamic-slice_fusion.4
  2.1 1.1 convert.20
  3.2 0.7 convert_bitcast_fusion
  3.9 0.7 convert.21
  5.2 0.8 dynamic_slice.20
  5.9 0.7 add_bitcast_fusion.refs_0_
  6.6 13.2 %exchange_0.1 = s32[4,8,8,128]{3,2,1,0:T(8,128)} custom-call(s32[8,128]{1,0:T(8,128)} %add_bitcast_fusion.refs_0_), custom_call_target="tpu_custom_call" | custom-call | bytes 2703360 | tf_op jit(solution)/shard_map/exchange_0/pallas_call | solution.py:423
  19.9 0.9 copy.187
  20.8 1.0 convert.23
  21.9 1.3 broadcast_in_dim.123
  23.2 4.3 all-to-all-start
  28.8 0.8 select_reduce_fusion.1
  29.8 1.1 reshape.245.routes_ref
  30.9 6.4 convert_element_type.41.refs_3_.refs_1_
  37.5 4.8 select_reduce_fusion
  42.3 13.2 %gather_rows.1 = bf16[32,256,384]{2,1,0:T(8,128)(2,1)S(1)} custom-call(s32[32,256]{1,0:T(8,128)S(1)} %fusion.16.list_ref, s32[32]{0:T(128)S(1)} %get-tuple-element.258.count_ref, f32[6144,384]{1,0:T(8,128)} %table_ref.1), custom_call_target="tpu_custom_call" | custom-call | tf_op jit(solution)/shard_map/gather_rows/pallas_call | solution.py:915
  55.5 2.7 copy-done.2
  59.5 7.3 all-to-all-done
  66.8 1.3 fusion.30
  68.1 109.3 %exchange_1.1 = (bf16[4,256,384]{2,1,0:T(8,128)(2,1)}, bf16[4,2,2,2,48,2176]{5,4,3,2,1,0:T(8,128)(2,1)}, bf16[4,2,2,2,48,2176]{5,4,3,2,1,0:T(8,128)(2,1)}, bf16[1536,1536]{1,0:T(8,128)(2,1)}) custom-call(bf16[4,2,2,2,256,384]{5,4,3,2,1,0:T(8,128)(2,1)} %bitcast.93, bf16[4,48,2176]{2,1,0:T(8,128)(2,1)} %get-tuple-element.261.refs_1_, ...), custom_call_target="tpu_custom_call" | custom-call | bytes 631111680 | tf_op jit(solution)/shard_map/exchange_1/pallas_call | solution.py:423
  177.5 12.2 %attend.1 = (bf16[32,1536]{1,0:T(8,128)(2,1)}, f32[32,1536]{1,0:T(8,128)}, f32[8,96,256]{2,1,0:T(8,128)}, bf16[32,1536]{1,0:T(8,128)(2,1)}, bf16[256,512]{1,0:T(...) custom-call(s32[1]{0:T(128)} %bitcast.138, ...), custom_call_target="tpu_custom_call" | custom-call | tf_op jit(solution)/shard_map/attend/pallas_call | solution.py:769
  189.7 30.9 %exchange_2.1 = (bf16[4,2,2,2,32,1536]{5,4,3,2,1,0:T(8,128)(2,1)}, bf16[1536,1536]{1,0:T(8,128)(2,1)}) custom-call(bf16[32,1536]{1,0:T(8,128)(2,1)} %get-tuple-element.70.refs_0_.c_ref, bf16[6144,384]{1,0:T(8,128)(2,1)} %convert_element_type.41.refs_3_.refs_1_, bf16[1536,1536]{1,0:T(8,128)(2,1)} %get-tuple-element.71.refs_2_), custom_call_target="tpu_custom_call", output_to_operand_aliasing={{1}: (2, {})} | custom-call | bytes 347996160 | tf_op jit(solution)/shard_map/exchange_2/pallas_call | solution.py:423
  220.5 17.8 %experts_forward.1 = (bf16[1024,1536]{1,0:T(8,128)(2,1)}, f32[1024,1024]{1,0:T(8,128)}, f32[1024,128]{1,0:T(8,128)}, bf16[1536,1024]{1,0:T(8,128)(2,1)}, bf16[51...) custom-call(s32[4]{0:T(128)} %iota_add_fusion.1.lane_ref, bf16[1024,1536]{1,0:T(8,128)(2,1)} %bitcast.123, ...), custom_call_target="tpu_custom_call" | custom-call | tf_op jit(solution)/shard_map/experts_forward/pallas_call | solution.py:505
  238.3 56.0 %exchange_3.1 = (bf16[4,2,2,2,32,1536]{5,4,3,2,1,0:T(8,128)(2,1)}, f32[32,1536]{1,0:T(8,128)}, bf16[1536,1536]{1,0:T(8,128)(2,1)}) custom-call(bf16[4,2,2,2,32,1536]{5,4,3,2,1,0:T(8,128)(2,1)} %bitcast.122, f32[32,1536]{1,0:T(8,128)} %get-tuple-element.74.refs_1_.resid_ref, ...), custom_call_target="tpu_custom_call", output_to_operand_aliasing={{2}: (4, {})} | custom-call | bytes 417792000 | tf_op jit(solution)/shard_map/exchange_3/pallas_call | solution.py:423
  294.4 10.2 %multiply_reduce_fusion.2 = (f32[1024]{0:T(1024)S(1)}, f32[1024,1536]{1,0:T(8,128)}) fusion(bf16[1024,1536]{1,0:T(8,128)(2,1)} %bitcast.140, bf16[1536,1536]{1,0:T(8,128)(2,1)} %get-tuple-element.78), kind=kOutput, calls=%fused_computation.21 | convolution fusion | flops 4834982912 | bytes 14159872 | tf_op jit(solution)/shard_map/rd,vd->rv/dot_general | solution.py:1159
  304.6 4.6 exponential_reduce_fusion
  309.8 13.1 %exchange_5.1 = f32[4,8,8,384]{3,2,1,0:T(8,128)} custom-call(f32[8,384]{1,0:T(8,128)} %reshape.249.refs_0_), custom_call_target="tpu_custom_call" | custom-call | bytes 8110080 | tf_op jit(solution)/shard_map/exchange_5/pallas_call | solution.py:423
  322.9 1.2 reshape_reshape.7
  324.9 0.6 divide_multiply_fusion
  325.8 4.0 fusion.6
  329.8 6.4 multiply_convert_fusion
  336.2 6.8 fusion.2.refs_3_.refs_1_
  344.2 1.3 constant_dynamic-slice_fusion.gates_ref
  345.6 57.0 %exchange_6.1 = (bf16[4,2,2,2,32,1536]{5,4,3,2,1,0:T(8,128)(2,1)}, f32[32,1536]{1,0:T(8,128)}, f32[1,1536]{1,0:T(1,128)}, bf16[4,1536,384]{2,1,0:T(8,128)(2,1)}) custom-call(bf16[4,2,2,2,32,1536]{5,4,3,2,1,0:T(8,128)(2,1)} %bitcast.121, f32[32,1536]{1,0:T(8,128)} %get-tuple-element.80.refs_1_, f32[8,1536]{1,0:T(8,128)} %get-tuple-element.75.refs_2_.gains_ref, ...), custom_call_target="tpu_custom_call" | custom-call | bytes 323543040 | tf_op jit(solution)/shard_map/exchange_6/pallas_call | solution.py:423
  402.5 13.4 %experts_backward.1 = (bf16[1024,1664]{1,0:T(8,128)(2,1)}, bf16[1024,1024]{1,0:T(8,128)(2,1)}) custom-call(s32[4]{0:T(128)} %iota_add_fusion.1.lane_ref, bf16[1024,1536]{1,0:T(8,128)(2,1)} %bitcast.119, f32[1024,1024]{1,0:T(8,128)} %get-tuple-element.82.mid_ref, f32[1024,128]{1,0:T(8,128)} %get-tuple-element.83.gates_ref, ...), custom_call_target="tpu_custom_call" | custom-call | tf_op jit(solution)/shard_map/experts_backward/pallas_call | solution.py:584
  415.9 35.4 %exchange_8.1 = (f32[32,1664]{1,0:T(8,128)}, bf16[4,1536,384]{2,1,0:T(8,128)(2,1)}) custom-call(bf16[4,2,2,2,32,1664]{5,4,3,2,1,0:T(8,128)(2,1)} %bitcast.118, bf16[1536,1536]{1,0:T(8,128)(2,1)} %fusion.2.refs_3_.refs_1_, bf16[4,1536,384]{2,1,0:T(8,128)(2,1)} %get-tuple-element.89.refs_2_), custom_call_target="tpu_custom_call", output_to_operand_aliasing={{1}: (2, {})} | custom-call | bytes 355532800 | tf_op jit(solution)/shard_map/exchange_8/pallas_call | solution.py:423
  451.3 23.9 %attend_back.1 = (bf16[4,256,384]{2,1,0:T(8,128)(2,1)}, bf16[1536,2176]{1,0:T(8,128)(2,1)}, bf16[1536,2176]{1,0:T(8,128)(2,1)}) custom-call(s32[1]{0:T(128)} %bitcast.139, f32[32,1664]{1,0:T(8,128)} %get-tuple-element.90.back_ref, f32[32,128]{1,0:T(8,128)} %constant_dynamic-slice_fusion.gates_ref, f32[32,1536]{1,0:T(8,128)} %get-tuple-element.91.grad_two_ref, ...), custom_call_target="tpu_custom_call" | custom-call | tf_op jit(solution)/shard_map/attend_back/pallas_call | solution.py:857
  475.2 127.5 %exchange_9.1 = (bf16[4,2,2,2,256,384]{5,4,3,2,1,0:T(8,128)(2,1)}, bf16[4,48,2176]{2,1,0:T(8,128)(2,1)}, bf16[4,48,2176]{2,1,0:T(8,128)(2,1)}, bf16[4,1536,384]{2,1,0:T(8,128)(2,1)}) custom-call(bf16[4,256,384]{2,1,0:T(8,128)(2,1)} %get-tuple-element.99.refs_0_, bf16[4,2,2,2,48,2176]{5,4,3,2,1,0:T(8,128)(2,1)} %bitcast.110, ...), custom_call_target="tpu_custom_call", output_to_operand_aliasing={{3}: (4, {})} | custom-call | bytes 725483520 | tf_op jit(solution)/shard_map/exchange_9/pallas_call | solution.py:423
  602.8 2.7 pad_maximum_fusion
  605.5 20.2 %all-to-all-start.1 = ((bf16[4,96,2176]{2,1,0:T(8,128)(2,1)}), bf16[4,96,2176]{2,1,0:T(8,128)(2,1)}, u32[]{:S(2)}, u32[]{:S(2)}) async-start(bf16[4,96,2176]{2,1,0:T(8,128)(2,1)} %pad_maximum_fusion), calls=%async_computation.1 | async-start | bytes 3342336 | tf_op jit(solution)/shard_map/all_to_all | solution.py:1233
  625.7 6.2 fusion.33.grad_ref
  631.9 13.6 %in_moments.1 = (f32[12288,128]{1,0:T(8,128)}, f32[12288,128]{1,0:T(8,128)}, f32[2,8,128]{2,1,0:T(8,128)S(1)}) custom-call(f32[2]{0:T(128)S(1)} %pad_maximum_fusion.5.scale_ref, f32[1536,1024]{1,0:T(8,128)S(1)} %fusion.33.grad_ref, f32[12288,128]{1,0:T(8,128)S(1)} %bitcast.92, f32[12288,128]{1,0:T(8,128)} %bitcast.112, f32[12288,128]{1,0:T(8,128)} %bitcast.113), custom_call_target="tpu_custom_call" | custom-call | tf_op jit(solution)/shard_map/in_moments/pallas_call | solution.py:637
  645.5 0.7 slice_reduce_fusion.4
  646.2 26.7 %scatter_rows.1 = f32[6144,384]{1,0:T(8,128)} custom-call(s32[32,256]{1,0:T(8,128)S(1)} %fusion.16.list_ref, s32[32]{0:T(128)S(1)} %get-tuple-element.258.count_ref, bf16[32,256,384]{2,1,0:T(8,128)(2,1)} %bitcast.117, bf16[6144,384]{1,0:T(8,128)(2,1)} %bitcast.101), custom_call_target="tpu_custom_call" | custom-call | tf_op jit(solution)/shard_map/scatter_rows/pallas_call | solution.py:952
  672.9 8.3 %multiply_reduce_fusion.4 = (f32[]{:T(128)}, f32[]{:T(128)}, f32[4,128,1536]{2,1,0:T(8,128)}, f32[4,128,1536]{2,1,0:T(8,128)}) fusion(f32[4,128,1536]{2,1,0:T(8,128)S(1)} %copy-done.3, f32[]{:T(128)} %div.77, f32[]{:T(128)} %div.76, f32[4,128,1536]{2,1,0:T(8,128)} %param.52, f32[4,128,1536]{2,1,0:T(8,128)} %param.53, ...), kind=kOutput, calls=%fused_computation.26 | convolution fusion | flops 1623982080 | bytes 19922960 | tf_op jit(solution)/shard_map/tk,td->kd/dot_general | solution.py:1252
  681.2 21.0 %multiply_reduce_fusion.1 = (f32[]{:T(128)}, f32[]{:T(128)}, f32[6144,384]{1,0:T(8,128)}, f32[6144,384]{1,0:T(8,128)}) fusion(f32[6144,384]{1,0:T(8,128)S(1)} %bitcast.95, f32[]{:T(128)} %div.77, f32[]{:T(128)} %div.76, f32[6144,384]{1,0:T(8,128)} %scatter_rows.1, f32[6144,384]{1,0:T(8,128)} %param.34, f32[6144,384]{1,0:T(8,128)} %param.35), kind=kLoop, calls=%fused_computation.5 | loop fusion | flops 40108032 | bytes 56623120 | tf_op jit(solution)/shard_map/reduce_sum | solution.py:1278
  702.3 1.8 convert_element_type.47
  704.6 1.6 multiply_reduce_fusion.8
  706.2 1.3 multiply_reduce_fusion.14
  707.5 0.6 multiply_reduce_fusion.10
  708.1 2.1 multiply_reduce_fusion.6
  710.2 9.7 %select_select_fusion.refs_0_ = f32[8,128]{1,0:T(8,128)} fusion(f32[]{:T(128)} %get-tuple-element.225, f32[]{:T(128)} %get-tuple-element.224, f32[]{:T(128)} %get-tuple-element.235, f32[]{:T(128)} %get-tuple-element.234, f32[]{:T(128)} %get-tuple-element.237, f32[]{:T(128)} %get-tuple-element.236, f32[]{:T(128)} %get-tuple-element.239, ...), kind=kLoop, calls=%fused_computation.87 | loop fusion | flops 28672 | bytes 4464 | tf_op jit(solution)/shard_map/jit(_where)/select_n | solution.py:1287
  719.9 14.6 %exchange_10.1 = f32[4,8,8,128]{3,2,1,0:T(8,128)} custom-call(f32[8,128]{1,0:T(8,128)} %select_select_fusion.refs_0_), custom_call_target="tpu_custom_call" | custom-call | bytes 2703360 | tf_op jit(solution)/shard_map/exchange_10/pallas_call | solution.py:423
  734.5 0.9 reduce_sum.279
  736.1 0.7 copy.168
  741.9 0.6 multiply_subtract_fusion.5
  742.6 1.9 multiply_subtract_fusion.4
  744.5 1.0 multiply_subtract_fusion.3
  745.5 7.4 multiply_subtract_fusion.2
  753.1 10.0 %multiply_subtract_fusion.1 = f32[12288,128]{1,0:T(8,128)} fusion(f32[12288,128]{1,0:T(8,128)} %bitcast.89, f32[12288,128]{1,0:T(8,128)} %get-tuple-element.108, f32[12288,128]{1,0:T(8,128)} %get-tuple-element.107, f32[]{:T(128)} %div.77, f32[]{:T(128)} %div.76, f32[]{:T(128)} %bitcast.40), kind=kLoop, calls=%fused_computation.18 | loop fusion | flops 12582912 | bytes 25165836 | tf_op jit(solution)/shard_map/sub | solution.py:1296
  763.1 1.1 slice-done.5
  764.2 1.2 slice-done.6
  766.2 6.6 multiply_subtract_fusion
  (151 shorter events, 7.6 us)
Async XLA Ops:
  0.7 4.2 copy-start
  2.1 35.2 %copy-start.21 = (s32[1,32]{1,0:T(1,128)}, s32[1,32]{1,0:T(1,128)S(1)}, u32[]{:S(2)}) copy-start(s32[1,32]{1,0:T(1,128)S(1)} %constant_dynamic-slice_fusion.4) | copy-start | bytes 388
  23.2 43.6 %all-to-all-start = ((bf16[4,96,2176]{2,1,0:T(8,128)(2,1)}), bf16[4,96,2176]{2,1,0:T(8,128)(2,1)S(1)}, u32[]{:S(2)}, u32[]{:S(2)}) async-start(bf16[4,96,2176]{2,1,0:T(8,128)(2,1)} %broadcast_in_dim.123), calls=%async_computation | async-start | bytes 3342336 | tf_op jit(solution)/shard_map/all_to_all | solution.py:1106
  28.7 30.2 %copy-start.9 = (f32[256,128]{1,0:T(8,128)}, f32[256,128]{1,0:T(8,128)S(1)}, u32[]{:S(2)}) copy-start(f32[256,128]{1,0:T(8,128)S(1)} %copy.161.sin_ref) | copy-start | bytes 393220
  29.8 29.1 %copy-start.10 = (f32[256,128]{1,0:T(8,128)}, f32[256,128]{1,0:T(8,128)S(1)}, u32[]{:S(2)}) copy-start(f32[256,128]{1,0:T(8,128)S(1)} %copy.160.cos_ref) | copy-start | bytes 393220
  42.3 17.2 %copy-start.24 = (s32[16,2]{0,1:T(2,128)S(1)}, s32[16,2]{0,1:T(2,128)}, u32[]{:S(2)}) copy-start(s32[16,2]{0,1:T(2,128)} %param.29) | copy-start | bytes 388
  55.5 2.7 copy-start.2
  304.6 20.1 %copy-start.26 = (f32[32]{0:T(128)S(1)}, f32[32]{0:T(128)}, u32[]{:S(2)}) copy-start(f32[32]{0:T(128)} %param.30) | copy-start | bytes 388
  309.1 20.7 %slice-start.14 = ((s8[4718592]{0:T(1024)(128)(4,1)}), s8[524288]{0:T(1024)(128)(4,1)S(1)}, s32[]{:S(2)}) async-start(s8[4718592]{0:T(1024)(128)(4,1)} %bitcast.108), calls=%async_computation.16 | async-start | bytes 1048576
  325.8 4.1 slice-start.15
  329.8 6.4 copy-start.25
  336.2 6.8 copy-start.11
  605.5 26.4 %slice-start = ((s8[6291456]{0:T(1024)(128)(4,1)}), s8[2097152]{0:T(1024)(128)(4,1)S(1)}, s32[]{:S(2)}) async-start(s8[6291456]{0:T(1024)(128)(4,1)} %bitcast.90), calls=%async_computation.2 | async-start | bytes 4194304
  605.5 96.8 %all-to-all-start.1 = ((bf16[4,96,2176]{2,1,0:T(8,128)(2,1)}), bf16[4,96,2176]{2,1,0:T(8,128)(2,1)}, u32[]{:S(2)}, u32[]{:S(2)}) async-start(bf16[4,96,2176]{2,1,0:T(8,128)(2,1)} %pad_maximum_fusion), calls=%async_computation.1 | async-start | bytes 3342336 | tf_op jit(solution)/shard_map/all_to_all | solution.py:1233
  625.7 6.2 slice-start.1
  646.2 26.7 %copy-start.3 = (f32[4,128,1536]{2,1,0:T(8,128)S(1)}, f32[4,128,1536]{2,1,0:T(8,128)}, u32[]{:S(2)}) copy-start(f32[4,128,1536]{2,1,0:T(8,128)} %down_ref.1) | copy-start | bytes 9437188
  646.2 26.7 %copy-start.5 = (bf16[4,2,2,2,32,1536]{5,4,3,2,1,0:T(8,128)(2,1)S(1)}, bf16[4,2,2,2,32,1536]{5,4,3,2,1,0:T(8,128)(2,1)}, u32[]{:S(2)}) copy-start(bf16[4,2,2,2,32,1536]{5,4,3,2,1,0:T(8,128)(2,1)} %get-tuple-element.81) | copy-start | bytes 9437188
  646.2 35.0 %slice-start.2 = ((s8[9437184]{0:T(1024)(128)(4,1)}), s8[1048576]{0:T(1024)(128)(4,1)S(1)}, s32[]{:S(2)}) async-start(s8[9437184]{0:T(1024)(128)(4,1)} %bitcast.94), calls=%async_computation.4 | async-start | bytes 2097152
  646.2 35.0 %slice-start.3 = ((s8[9437184]{0:T(1024)(128)(4,1)}), s8[4194304]{0:T(1024)(128)(4,1)S(1)}, s32[]{:S(2)}) async-start(s8[9437184]{0:T(1024)(128)(4,1)} %bitcast.94), calls=%async_computation.5 | async-start | bytes 8388608
  672.9 8.3 %slice-start.4 = ((s8[9437184]{0:T(1024)(128)(4,1)}), s8[4194304]{0:T(1024)(128)(4,1)S(1)}, s32[]{:S(2)}) async-start(s8[9437184]{0:T(1024)(128)(4,1)} %bitcast.94), calls=%async_computation.6 | async-start | bytes 8388608
  702.2 2.3 copy-start.6
  702.2 2.3 copy-start.13
  702.2 2.3 copy-start.14
  702.2 4.0 copy-start.18
  702.2 4.0 copy-start.22
  702.2 4.0 copy-start.23
  702.2 5.2 copy-start.15
  702.2 5.2 copy-start.19
  702.3 5.2 copy-start.20
  702.3 5.8 copy-start.4
  702.3 5.8 copy-start.12
  708.1 44.9 %copy-start.16 = (f32[48,32]{0,1:T(8,128)}, f32[48,32]{0,1:T(8,128)S(1)}, u32[]{:S(2)}) copy-start(f32[48,32]{0,1:T(8,128)S(1)} %get-tuple-element.248) | copy-start | bytes 18436
  708.1 44.9 %copy-start.17 = (f32[48,32]{0,1:T(8,128)}, f32[48,32]{0,1:T(8,128)S(1)}, u32[]{:S(2)}) copy-start(f32[48,32]{0,1:T(8,128)S(1)} %get-tuple-element.249) | copy-start | bytes 18436
  710.2 42.8 %copy-start.7 = (f32[48,2560]{1,0:T(8,128)}, f32[48,2560]{1,0:T(8,128)S(1)}, u32[]{:S(2)}) copy-start(f32[48,2560]{1,0:T(8,128)S(1)} %get-tuple-element.252) | copy-start | bytes 1474564
  710.2 42.8 %copy-start.8 = (f32[48,2560]{1,0:T(8,128)}, f32[48,2560]{1,0:T(8,128)S(1)}, u32[]{:S(2)}) copy-start(f32[48,2560]{1,0:T(8,128)S(1)} %get-tuple-element.253) | copy-start | bytes 1474564
  744.5 18.6 %slice-start.11 = ((s8[9437184]{0:T(1024)(128)(4,1)}), s8[4194304]{0:T(1024)(128)(4,1)S(1)}, s32[]{:S(2)}) async-start(s8[9437184]{0:T(1024)(128)(4,1)} %bitcast.104), calls=%async_computation.13 | async-start | bytes 8388608
  745.5 17.5 %slice-start.8 = ((s8[9437184]{0:T(1024)(128)(4,1)}), s8[4194304]{0:T(1024)(128)(4,1)S(1)}, s32[]{:S(2)}) async-start(s8[9437184]{0:T(1024)(128)(4,1)} %bitcast.102), calls=%async_computation.10 | async-start | bytes 8388608
  745.5 17.5 %slice-start.12 = ((s8[9437184]{0:T(1024)(128)(4,1)}), s8[4194304]{0:T(1024)(128)(4,1)S(1)}, s32[]{:S(2)}) async-start(s8[9437184]{0:T(1024)(128)(4,1)} %bitcast.104), calls=%async_computation.14 | async-start | bytes 8388608
  753.0 10.1 %slice-start.9 = ((s8[9437184]{0:T(1024)(128)(4,1)}), s8[4194304]{0:T(1024)(128)(4,1)S(1)}, s32[]{:S(2)}) async-start(s8[9437184]{0:T(1024)(128)(4,1)} %bitcast.102), calls=%async_computation.11 | async-start | bytes 8388608
  753.0 11.2 %slice-start.5 = ((s8[9437184]{0:T(1024)(128)(4,1)}), s8[4194304]{0:T(1024)(128)(4,1)S(1)}, s32[]{:S(2)}) async-start(s8[9437184]{0:T(1024)(128)(4,1)} %bitcast.96), calls=%async_computation.7 | async-start | bytes 8388608
  753.0 12.3 %slice-start.6 = ((s8[9437184]{0:T(1024)(128)(4,1)}), s8[4194304]{0:T(1024)(128)(4,1)S(1)}, s32[]{:S(2)}) async-start(s8[9437184]{0:T(1024)(128)(4,1)} %bitcast.96), calls=%async_computation.8 | async-start | bytes 8388608
  753.0 12.6 %slice-start.7 = ((s8[9437184]{0:T(1024)(128)(4,1)}), s8[1048576]{0:T(1024)(128)(4,1)S(1)}, s32[]{:S(2)}) async-start(s8[9437184]{0:T(1024)(128)(4,1)} %bitcast.96), calls=%async_computation.9 | async-start | bytes 2097152
  753.0 12.8 %slice-start.10 = ((s8[9437184]{0:T(1024)(128)(4,1)}), s8[1048576]{0:T(1024)(128)(4,1)S(1)}, s32[]{:S(2)}) async-start(s8[9437184]{0:T(1024)(128)(4,1)} %bitcast.102), calls=%async_computation.12 | async-start | bytes 2097152
  753.1 13.1 %slice-start.13 = ((s8[9437184]{0:T(1024)(128)(4,1)}), s8[1048576]{0:T(1024)(128)(4,1)S(1)}, s32[]{:S(2)}) async-start(s8[9437184]{0:T(1024)(128)(4,1)} %bitcast.104), calls=%async_computation.15 | async-start | bytes 2097152
  766.2 6.6 copy-start.1

commit v6 on v5

--- a/solution.py
+++ b/solution.py
@@ -420,6 +420,12 @@
         mail.finish()
 
     size = sum(x.size * x.dtype.itemsize for p in parts for x in p.inputs + p.outputs)
+    need = size + sum(
+        math.prod(x.shape) * x.dtype.itemsize
+        for p in parts
+        for x in p.scratch
+        if x.memory_space == pltpu.VMEM
+    )
     out = pl.pallas_call(
         kernel,
         out_shape=[x for p in parts for x in p.outputs],
@@ -437,7 +443,9 @@
         scratch_shapes=[s for p in parts for s in p.scratch]
         + [pltpu.SemaphoreType.DMA((copies,)), pltpu.SemaphoreType.DMA((copies,))],
         compiler_params=pltpu.CompilerParams(
-            collective_id=ident, has_side_effects=True, vmem_limit_bytes=62 << 20
+            collective_id=ident,
+            has_side_effects=True,
+            vmem_limit_bytes=min(62 << 20, need * 9 // 8 + (4 << 20)),
         ),
         cost_estimate=pl.CostEstimate(flops=0, bytes_accessed=20 * size, transcendentals=0),
         name="exchange_" + str(ident),
@@ -531,7 +539,7 @@
             jax.ShapeDtypeStruct((number * units, D), bf16),
             jax.ShapeDtypeStruct((total, number * units), bf16),
         ],
-        compiler_params=pltpu.CompilerParams(vmem_limit_bytes=60 << 20),
+        compiler_params=pltpu.CompilerParams(vmem_limit_bytes=42 << 20),
         name="experts_forward",
     )(lane, rows, routes, router, in_rows, down)
 
@@ -603,50 +611,70 @@
             jax.ShapeDtypeStruct((total, D + 128), bf16),
             jax.ShapeDtypeStruct(mid.shape, bf16),
         ],
-        compiler_params=pltpu.CompilerParams(vmem_limit_bytes=60 << 20),
+        compiler_params=pltpu.CompilerParams(vmem_limit_bytes=50 << 20),
         name="experts_backward",
     )(lanes, grad, mid, gates, cat, down)
 
 
-def moments_kernel(scale_ref, grad_ref, w_ref, first_ref, second_ref, new_first, new_second, norms):
+def moments_kernel(
+    scale_ref, grad_ref, w_ref, first_ref, second_ref, down_grad, down_w, down_first, down_second,
+    new_first, new_second, new_down_first, new_down_second, norms, sums, down_sums,
+):
     units = w_ref.shape[1]
     part = w_ref.shape[0] // 2
-
-    @pl.when((pl.program_id(0) == 0) & (pl.program_id(1) == 0))
+    scales = (scale_ref[0], scale_ref[1])
+    step = pl.program_id(0) * pl.num_programs(1) + pl.program_id(1)
+
+    @pl.when(step == 0)
     def _():
-        norms[...] = jnp.zeros_like(norms)
+        sums[...] = jnp.zeros_like(sums)
+        down_sums[...] = jnp.zeros_like(down_sums)
 
     for j in range(2):
         here = pl.ds(j, part, stride=2)
         grad = grad_ref[:, j * units : (j + 1) * units]
         weight = w_ref[here, :]
-        one = RATE_ONE * first_ref[here, :] + (1.0 - RATE_ONE) * grad
-        two = RATE_TWO * second_ref[here, :] + (1.0 - RATE_TWO) * grad * grad
-        update = lamb_update(weight, one, two, scale_ref[0], scale_ref[1])
+        one, two, update = lamb_parts(weight, first_ref[here, :], second_ref[here, :], grad, scales)
         new_first[here, :] = one
         new_second[here, :] = two
-        norms[0] += jnp.sum((weight * weight).reshape(-1, 8, units), axis=0)
-        norms[1] += jnp.sum((update * update).reshape(-1, 8, units), axis=0)
-
-
-def in_moments(scales, grad, weight, first, second):
+        sums[0] += fold(weight * weight)
+        sums[1] += fold(update * update)
+    weight = down_w[...]
+    one, two, update = lamb_parts(weight, down_first[...], down_second[...], down_grad[...], scales)
+    new_down_first[...] = one
+    new_down_second[...] = two
+    down_sums[0] += fold(weight * weight)
+    down_sums[1] += fold(update * update)
+
+    @pl.when(step == pl.num_programs(0) * pl.num_programs(1) - 1)
+    def _():
+        norms[...] = norm_cells(5, total_of(sums[0]), total_of(sums[1])) + norm_cells(
+            6, total_of(down_sums[0]), total_of(down_sums[1])
+        )
+
+
+def expert_moments(scales, grad, weight, first, second, down_grad, down, down_first, down_second):
     units = weight.shape[1]
     number = grad.shape[1] // (2 * units)
     parts = 2
     row = pl.BlockSpec((2 * D // parts, units), lambda e, p, *_: (e * parts + p, 0))
+    down_row = pl.BlockSpec((units // parts, D), lambda e, p, *_: (e * parts + p, 0))
     return pl.pallas_call(
         moments_kernel,
         grid_spec=pltpu.PrefetchScalarGridSpec(
             num_scalar_prefetch=1,
             grid=(number, parts),
-            in_specs=[pl.BlockSpec((D // parts, 2 * units), lambda e, p, *_: (p, e)), row, row, row],
-            out_specs=[row, row, pl.BlockSpec((2, 8, units), lambda e, p, *_: (0, 0, 0))],
+            in_specs=[pl.BlockSpec((D // parts, 2 * units), lambda e, p, *_: (p, e)), row, row, row]
+            + [down_row] * 4,
+            out_specs=[row, row, down_row, down_row, pl.BlockSpec((8, 128), lambda e, p, *_: (0, 0))],
+            scratch_shapes=[pltpu.VMEM((2, 8, units), f32), pltpu.VMEM((2, 8, D), f32)],
         ),
         out_shape=[jax.ShapeDtypeStruct(weight.shape, f32)] * 2
-        + [jax.ShapeDtypeStruct((2, 8, units), f32)],
-        compiler_params=pltpu.CompilerParams(vmem_limit_bytes=40 << 20),
-        name="in_moments",
-    )(scales, grad, weight, first, second)
+        + [jax.ShapeDtypeStruct(down.shape, f32)] * 2
+        + [jax.ShapeDtypeStruct((8, 128), f32)],
+        compiler_params=pltpu.CompilerParams(vmem_limit_bytes=36 << 20),
+        name="expert_moments",
+    )(scales, grad, weight, first, second, down_grad, down, down_first, down_second)
 
 
 HEAD_COLS = QUERY_HEADS * HEAD_WIDTH
@@ -927,44 +955,213 @@
     )(lists, counts, table)
 
 
-def scatter_kernel(list_ref, count_ref, grad_ref, head_ref, out_ref, rows_ref):
+TABLE_PARTS = 16
+
+
+def norm_cells(row, weight_sum, update_sum):
+    rows = lax.broadcasted_iota(jnp.int32, (8, 128), 0)
+    lanes = lax.broadcasted_iota(jnp.int32, (8, 128), 1)
+    block = jnp.where(lanes == 0, weight_sum, jnp.where(lanes == 1, update_sum, 0.0))
+    return jnp.where(rows == row, block, 0.0)
+
+
+def total_of(values):
+    return jnp.sum(jnp.sum(values, axis=1, keepdims=True), axis=0, keepdims=True)
+
+
+def fold(values):
+    return jnp.sum(values.reshape(-1, 8, values.shape[1]), axis=0)
+
+
+def table_kernel(
+    list_ref, count_ref, scale_ref, grad_ref, head_ref, w_in, first_in, second_in,
+    new_first, new_second, norms,
+    rows_ref, acc, w, first, second, sums, sems,
+):
     b = pl.program_id(0)
+    blocks = pl.num_programs(0) - TABLE_PARTS
+    loads = [
+        pltpu.make_async_copy(src, dst, sems.at[n])
+        for n, (src, dst) in enumerate([(w_in, w), (first_in, first), (second_in, second)])
+    ]
 
     @pl.when(b == 0)
     def _():
-        out_ref[...] = head_ref[...].astype(f32)
-
-    rows_ref[:SEQUENCE_TOKENS] = grad_ref[0].astype(f32)
-    rows_ref[SEQUENCE_TOKENS:] = jnp.zeros((8, rows_ref.shape[1]), f32)
-
-    def step(k, carry):
-        for j in range(STEPS):
-            entry = list_ref[b, k * STEPS + j]
-            out_ref[pl.ds(entry & 65535, 1), :] += rows_ref[pl.ds(entry >> 16, 1), :]
-        return carry
-
-    lax.fori_loop(0, (count_ref[b] + STEPS - 1) // STEPS, step, 0)
-
-
-def scatter_rows(lists, counts, grads, head):
+        for load in loads:
+            load.start()
+        acc[...] = head_ref[...].astype(f32)
+        sums[...] = jnp.zeros_like(sums)
+
+    @pl.when(b < blocks)
+    def _():
+        rows_ref[:SEQUENCE_TOKENS] = grad_ref[0].astype(f32)
+        rows_ref[SEQUENCE_TOKENS:] = jnp.zeros((8, rows_ref.shape[1]), f32)
+
+        def step(k, carry):
+            entries = [list_ref[b, k * STEPS + j] for j in range(STEPS)]
+            spots = [entry & 65535 for entry in entries]
+            grads = [rows_ref[pl.ds(entry >> 16, 1), :] for entry in entries]
+            olds = [acc[pl.ds(spot, 1), :] for spot in spots]
+            for j in range(STEPS):
+                total = olds[j] + grads[j]
+                for i in range(j):
+                    total += jnp.where(spots[i] == spots[j], grads[i], 0.0)
+                acc[pl.ds(spots[j], 1), :] = total
+            return carry
+
+        lax.fori_loop(0, (count_ref[b] + STEPS - 1) // STEPS, step, 0)
+
+    @pl.when(b == blocks)
+    def _():
+        for load in loads:
+            load.wait()
+
+    @pl.when(b >= blocks)
+    def _():
+        size = new_first.shape[0]
+        here = pl.ds(pl.multiple_of((b - blocks) * size, 8), size)
+        one, two, update = lamb_parts(
+            w[here, :], first[here, :], second[here, :], acc[here, :], (scale_ref[0], scale_ref[1])
+        )
+        new_first[...] = one
+        new_second[...] = two
+        sums[0] += fold(w[here, :] * w[here, :])
+        sums[1] += fold(update * update)
+
+    @pl.when(b == blocks + TABLE_PARTS - 1)
+    def _():
+        norms[...] = norm_cells(0, total_of(sums[0]), total_of(sums[1]))
+
+
+def table_moments(lists, counts, scales, grads, head, weight, first, second):
     blocks = lists.shape[0]
-    rows, columns = head.shape
+    rows, columns = weight.shape
+    part = rows // TABLE_PARTS
+    out = pl.BlockSpec((part, columns), lambda b, *_: (jnp.maximum(b - blocks, 0), 0))
     return pl.pallas_call(
-        scatter_kernel,
+        table_kernel,
         grid_spec=pltpu.PrefetchScalarGridSpec(
-            num_scalar_prefetch=2,
-            grid=(blocks,),
+            num_scalar_prefetch=3,
+            grid=(blocks + TABLE_PARTS,),
             in_specs=[
-                pl.BlockSpec((1, SEQUENCE_TOKENS, columns), lambda b, *_: (b, 0, 0)),
-                pl.BlockSpec((rows, columns), lambda b, *_: (0, 0)),
-            ],
-            out_specs=pl.BlockSpec((rows, columns), lambda b, *_: (0, 0)),
-            scratch_shapes=[pltpu.VMEM((SEQUENCE_TOKENS + 8, columns), f32)],
+                pl.BlockSpec(
+                    (1, SEQUENCE_TOKENS, columns),
+                    lambda b, *_: (jnp.minimum(b, blocks - 1), 0, 0),
+                ),
+                pl.BlockSpec(
+                    (rows, columns), lambda b, *_: (0, 0), pipeline_mode=pl.Buffered(1)
+                ),
+            ]
+            + [pl.BlockSpec(memory_space=pl.ANY)] * 3,
+            out_specs=[out, out, pl.BlockSpec((8, 128), lambda b, *_: (0, 0))],
+            scratch_shapes=[pltpu.VMEM((SEQUENCE_TOKENS + 8, columns), f32)]
+            + [pltpu.VMEM((rows, columns), f32)] * 4
+            + [pltpu.VMEM((2, 8, columns), f32), pltpu.SemaphoreType.DMA((3,))],
         ),
-        out_shape=jax.ShapeDtypeStruct((rows, columns), f32),
-        compiler_params=pltpu.CompilerParams(vmem_limit_bytes=50 << 20),
-        name="scatter_rows",
-    )(lists, counts, grads, head)
+        out_shape=[jax.ShapeDtypeStruct((rows, columns), f32)] * 2
+        + [jax.ShapeDtypeStruct((8, 128), f32)],
+        compiler_params=pltpu.CompilerParams(vmem_limit_bytes=54 << 20),
+        name="table_moments",
+    )(lists, counts, scales, grads, head, weight, first, second)
+
+
+def small_kernel(
+    scale_ref, grad_ref, qkv, qkv_one, qkv_two, out, out_one, out_two, router, router_one, router_two,
+    gains, gains_one, gains_two, *results
+):
+    scales = (scale_ref[0], scale_ref[1])
+    planes = grad_ref.shape[0]
+    packs = []
+    for n in range(2):
+        pack = grad_ref[0, n].astype(f32)
+        for z in range(1, planes):
+            pack += grad_ref[z, n].astype(f32)
+        packs.append(pack)
+    wide = HEAD_COLS + KEY_COLS
+    pick = lax.broadcasted_iota(jnp.int32, (8, 128), 0) + EXPERTS
+    pick = (pick == lax.broadcasted_iota(jnp.int32, (8, 128), 1)).astype(f32)
+    gains_grad = lax.dot_general(
+        pick,
+        packs[0][:, wide:],
+        ACROSS,
+        preferred_element_type=f32,
+        precision=lax.Precision.HIGHEST,
+    )[:3]
+    block = jnp.zeros((8, 128), f32)
+    sets = [
+        (qkv, qkv_one, qkv_two, jnp.concatenate([packs[0][:, :wide], packs[1][:, :KEY_COLS]], axis=1)),
+        (out, out_one, out_two, packs[1][:, KEY_COLS : KEY_COLS + D]),
+        (router, router_one, router_two, packs[0][:, wide : wide + EXPERTS]),
+        (gains, gains_one, gains_two, gains_grad),
+    ]
+    for n, (weight, first, second, grad) in enumerate(sets):
+        one, two, update = lamb_parts(weight[...], first[...], second[...], grad, scales)
+        results[2 * n][...] = one
+        results[2 * n + 1][...] = two
+        block += norm_cells(n + 1, total_of(weight[...] * weight[...]), total_of(update * update))
+    results[8][...] = block
+
+
+def small_moments(scales, sums, *state):
+    vm = pl.BlockSpec(memory_space=pltpu.VMEM)
+    return pl.pallas_call(
+        small_kernel,
+        in_specs=[pl.BlockSpec(memory_space=pltpu.SMEM)] + [vm] * (1 + len(state)),
+        out_specs=[vm] * 9,
+        out_shape=[jax.ShapeDtypeStruct(x.shape, f32) for x in state[::3] for _ in range(2)]
+        + [jax.ShapeDtypeStruct((8, 128), f32)],
+        compiler_params=pltpu.CompilerParams(vmem_limit_bytes=16 << 20),
+        name="small_moments",
+    )(scales, sums, *state)
+
+
+FINISH_PARTS = 16
+
+
+def finish_kernel(scale_ref, norms_ref, *refs):
+    norms = jnp.sqrt(jnp.sum(norms_ref[...], axis=0))
+    count = len(refs) // 4
+
+    def apply(n, row):
+        weight = refs[3 * n][...]
+        update = lamb_update(
+            weight, refs[3 * n + 1][...], refs[3 * n + 2][...], scale_ref[0], scale_ref[1]
+        )
+        ratio = norms[row : row + 1, 0:1] / norms[row : row + 1, 1:2]
+        refs[3 * count + n][...] = weight - (STEP_RATE * ratio) * update
+
+    apply(0, 0)
+    apply(1, 5)
+    apply(2, 6)
+
+    @pl.when(pl.program_id(0) == 0)
+    def _():
+        apply(3, 1)
+        apply(4, 2)
+
+
+def finish(scales, norms, *state):
+    weights = state[::3]
+
+    def spec(n):
+        rows, columns = weights[n].shape
+        if n < 3:
+            return pl.BlockSpec((rows // FINISH_PARTS, columns), lambda i, *_: (i, 0))
+        return pl.BlockSpec((rows, columns), lambda i, *_: (0, 0))
+
+    return pl.pallas_call(
+        finish_kernel,
+        grid_spec=pltpu.PrefetchScalarGridSpec(
+            num_scalar_prefetch=1,
+            grid=(FINISH_PARTS,),
+            in_specs=[pl.BlockSpec(norms.shape, lambda i, *_: (0, 0, 0))]
+            + [spec(n) for n in range(5) for _ in range(3)],
+            out_specs=[spec(n) for n in range(5)],
+        ),
+        out_shape=[jax.ShapeDtypeStruct(x.shape, f32) for x in weights],
+        compiler_params=pltpu.CompilerParams(vmem_limit_bytes=40 << 20),
+        name="finish",
+    )(scales, norms, *state)
 
 
 def on_device(
@@ -1053,7 +1250,7 @@
         ]
         for n in range(cuts)
     ]
-    embed_groups = split(0, SEQUENCE_TOKENS, columns, 8, 1)
+    embed_groups = split(0, SEQUENCE_TOKENS, columns, 4, 1)
 
     own_places = lax.dynamic_index_in_dim(positions, shard_id, 0, keepdims=False)
     start = own_places[0]
@@ -1111,9 +1308,8 @@
         tiled=True,
     )
     table_b = embed_table.astype(bf16)
-    picked, first_pack, second_pack, table_own = send(
+    first_pack, second_pack, picked, table_own = send(
         [
-            Reduce([picked], embed_groups, planes, side, exchange=True),
             Gather(
                 [packs[:, :weight_rows], packs[:, weight_rows:]],
                 weight_groups,
@@ -1121,6 +1317,7 @@
                 side,
                 prior=True,
             ),
+            Reduce([picked], embed_groups, planes, side, exchange=True),
             swap(table_b, (0, 16, 0)),
         ],
         1,
@@ -1222,11 +1419,11 @@
     )
     grad_packs = [pack.reshape(grid + (weight_rows, weight_cols)) for pack in grad_packs]
     wide = head_cols + key_cols
-    sent, first_grad, second_grad, head_back = send(
+    first_grad, second_grad, sent, head_back = send(
         [
+            Reduce(grad_packs, weight_groups, planes, side, partial=True),
             Gather([grad_embedded], embed_groups, planes, side, exchange=True),
-            Reduce(grad_packs, weight_groups, planes, side, partial=True),
-            swap(head_grad, (9, 15, 4), back=True, held=head_back),
+            swap(head_grad, (9, 5, 1), (14, 5, 2), (19, 5, 3), back=True, held=head_back),
         ],
         9,
     )
@@ -1236,69 +1433,105 @@
         split_axis=0,
         concat_axis=0,
         tiled=True,
-    ).astype(f32)
-    first_grad = jnp.sum(plane_sums[:, :weight_rows], axis=0)
-    second_grad = jnp.sum(plane_sums[:, weight_rows:], axis=0)
-    table_grad = scatter_rows(
-        lists,
-        counts,
-        sent.reshape(devices, SEQUENCE_TOKENS, columns),
-        head_back.reshape(vocab_rows, columns),
-    )
+    ).reshape(planes, 2, weight_rows, weight_cols)
 
     step_value = step_count.astype(f32)
-    scales = (1.0 / (1.0 - RATE_ONE**step_value), 1.0 / (1.0 - RATE_TWO**step_value))
+    scales = jnp.stack([1.0 / (1.0 - RATE_ONE**step_value), 1.0 / (1.0 - RATE_TWO**step_value)])
     grad_in = jnp.einsum("td,tk->dk", expert_rows, mid_grad, preferred_element_type=f32)
-    grad_down = jnp.einsum(
-        "tk,td->kd", gated_hidden, grad_all, preferred_element_type=f32
-    ).reshape(down_weight.shape)
-    in_first_new, in_second_new, in_norms = in_moments(
-        jnp.stack(scales),
+    grad_down = jnp.einsum("tk,td->kd", gated_hidden, grad_all, preferred_element_type=f32)
+    down_rows = down_weight.reshape(-1, D)
+    in_one, in_two, down_one, down_two, expert_norms = expert_moments(
+        scales,
         grad_in,
         in_rows,
         in_first.reshape(in_rows.shape),
         in_second.reshape(in_rows.shape),
-    )
-    weights = (embed_table, qkv_weight, out_weight, router_weight, norm_gains, down_weight)
-    firsts = (embed_first, qkv_first, out_first, router_first, gains_first, down_first)
-    seconds = (embed_second, qkv_second, out_second, router_second, gains_second, down_second)
-    gradients = (
-        table_grad,
-        jnp.concatenate([first_grad[:, :wide], second_grad[:, :key_cols]], axis=1),
-        second_grad[:, key_cols : key_cols + D],
-        first_grad[:, wide : wide + EXPERTS],
-        first_grad[:, wide + EXPERTS : wide + EXPERTS + 3].T,
         grad_down,
-    )
-    moved = [
-        lamb_parts(weight, moment_one, moment_two, gradient, scales)
-        for weight, moment_one, moment_two, gradient in zip(weights, firsts, seconds, gradients)
-    ]
-    partial_norms = [
-        (jnp.sum(weight * weight), jnp.sum(parts[2] * parts[2]))
-        for weight, parts in zip(weights, moved)
-    ]
-    partial_norms.insert(5, (jnp.sum(in_norms[0]), jnp.sum(in_norms[1])))
-    norm_row = lax.broadcasted_iota(jnp.int32, (8, 128), 0)
-    norm_lane = lax.broadcasted_iota(jnp.int32, (8, 128), 1)
-    norm_block = jnp.zeros((8, 128), f32)
-    for n, pair in enumerate(partial_norms):
-        for lane, part in enumerate(pair):
-            norm_block = jnp.where((norm_row == n) & (norm_lane == lane), part, norm_block)
-    norm_values = jnp.sqrt(jnp.sum(gather_tiny(norm_block, 10), axis=0))[:7, :2]
+        down_rows,
+        down_first.reshape(down_rows.shape),
+        down_second.reshape(down_rows.shape),
+    )
+    table_one, table_two, table_norms = table_moments(
+        lists,
+        counts,
+        scales,
+        sent.reshape(devices, SEQUENCE_TOKENS, columns),
+        head_back.reshape(vocab_rows, columns),
+        embed_table,
+        embed_first,
+        embed_second,
+    )
+    *small, small_norms = small_moments(
+        scales,
+        plane_sums,
+        qkv_weight,
+        qkv_first,
+        qkv_second,
+        out_weight,
+        out_first,
+        out_second,
+        router_weight,
+        router_first,
+        router_second,
+        norm_gains,
+        gains_first,
+        gains_second,
+    )
+    norm_blocks = gather_tiny(expert_norms + table_norms + small_norms, 10)
+    norm_values = jnp.sqrt(jnp.sum(norm_blocks, axis=0))[:7, :2]
     trust_ratio = norm_values[:, 0] / norm_values[:, 1]
-    moved.insert(
-        5, (in_first_new, in_second_new, lamb_update(in_rows, in_first_new, in_second_new, *scales))
-    )
-    weights = weights[:5] + (in_rows,) + weights[5:]
-    results = [loss_value]
-    for place, (weight, parts) in enumerate(zip(weights, moved)):
-        made = [weight - STEP_RATE * trust_ratio[place] * parts[2], parts[0], parts[1]]
-        if place == 5:
-            made = [x.reshape(in_weight.shape) for x in made]
-        results.extend(made)
-    results.append(jnp.stack([norm_values[:, 0], norm_values[:, 1], trust_ratio], axis=1))
-    return tuple(results)
+    new_table, new_in, new_down, new_qkv, new_out = finish(
+        scales,
+        norm_blocks,
+        embed_table,
+        table_one,
+        table_two,
+        in_rows,
+        in_one,
+        in_two,
+        down_rows,
+        down_one,
+        down_two,
+        qkv_weight,
+        small[0],
+        small[1],
+        out_weight,
+        small[2],
+        small[3],
+    )
+
+    def renew(place, weight, one, two):
+        update = lamb_update(weight, one, two, scales[0], scales[1])
+        return weight - STEP_RATE * trust_ratio[place] * update
+
+    new_router = renew(3, router_weight, small[4], small[5])
+    new_gains = renew(4, norm_gains, small[6], small[7])
+    stats = jnp.stack([norm_values[:, 0], norm_values[:, 1], trust_ratio], axis=1)
+    return (
+        loss_value,
+        new_table,
+        table_one,
+        table_two,
+        new_qkv,
+        small[0],
+        small[1],
+        new_out,
+        small[2],
+        small[3],
+        new_router,
+        small[4],
+        small[5],
+        new_gains,
+        small[6],
+        small[7],
+        new_in.reshape(in_weight.shape),
+        in_one.reshape(in_weight.shape),
+        in_two.reshape(in_weight.shape),
+        new_down.reshape(down_weight.shape),
+        down_one.reshape(down_weight.shape),
+        down_two.reshape(down_weight.shape),
+        stats,
+    )
 
 
 def solution(mesh):

time: 786 us -> 714 us (0.908)
  other arithmetic: 98.1 us -> 31.6 us
  local copies, waits for them, and re-layouts: 19.6 us -> 49.4 us
  starting transfers between devices: 24.5 us -> 9.26 us
  matrix products: 38 us -> 23.2 us
    pallas_call x9, Pallas kernels: 457 us -> 395 us  [communicate(): pl.pallas_call(kernel, out_shape=[x for p in parts for x in p.outputs], i...]
    pallas_call x2 -> x4, Pallas kernels: 40.3 us -> 99.2 us  [the longest x1 43.9 us: table_moments(): pl.pallas_call(table_kernel, grid_spec=pltpu.PrefetchScalarGridSpec(num_s...]
    unnamed x91 -> x145, local copies, waits for them, and re-layouts: 7.73 us -> 41.7 us
    reduce_sum x8 -> x1, other arithmetic: 28.4 us -> 0.94 us  [on_device(): norm_values = jnp.sqrt(jnp.sum(norm_blocks, axis=0))[:7, :2]]
    sub x7 -> x2, other arithmetic: 28.2 us -> 2.06 us  [renew(): return weight - STEP_RATE * trust_ratio[place] * update]
    all_to_all x1, starting transfers between devices: 20.2 us -> 5 us  [on_device(): lax.all_to_all(jnp.concatenate([first_grad, second_grad], axis=1), 'exper...]
    select_n x1 -> x0, other arithmetic: 9.69 us -> none  [on_device(): jnp.where((norm_row == n) & (norm_lane == lane), part, norm_block)]
    pallas_call x1, Pallas kernels: 13.4 us -> 22.7 us  [experts_backward(): pl.pallas_call(backward_kernel, grid_spec=pltpu.PrefetchScalarGridSpec(nu...]
  transfers between devices with their start and end apart: 2 -> 2, of which waited for: 1 -> 1; matrix products, arithmetic and copies ran while one was open for 7% -> 3% of each run, Pallas kernels for 7% -> 11%
where the time goes in v6:
time: 714 us; the launch traced here: 710 us
  Pallas kernels  581 us (81%)
  local copies, waits for them, and re-layouts  49.4 us (7%)
  other arithmetic  31.6 us (4%)
  matrix products  23.2 us (3%)
  waiting for transfers between devices  9.54 us (1%)
  starting transfers between devices  9.26 us (1%)
    pallas_call x9, Pallas kernels, communicate(): pl.pallas_call(kernel, out_shape=[x for p in parts for x in p.outputs], i...  395 us
    pallas_call x1, Pallas kernels, table_moments(): pl.pallas_call(table_kernel, grid_spec=pltpu.PrefetchScalarGridSpec(num_s...  43.9 us
    unnamed x145, local copies, waits for them, and re-layouts  41.7 us
    pallas_call x1, Pallas kernels, finish(): pl.pallas_call(finish_kernel, grid_spec=pltpu.PrefetchScalarGridSpec(num_...  30.7 us
    pallas_call x1, Pallas kernels, attend_back(): pl.pallas_call(attend_back_kernel, in_specs=[pl.BlockSpec(memory_space=pl...  23.9 us
    pallas_call x1, Pallas kernels, experts_backward(): pl.pallas_call(backward_kernel, grid_spec=pltpu.PrefetchScalarGridSpec(nu...  22.7 us
    pallas_call x1, Pallas kernels, expert_moments(): pl.pallas_call(moments_kernel, grid_spec=pltpu.PrefetchScalarGridSpec(num...  21.2 us
    pallas_call x1, Pallas kernels, experts_forward(): pl.pallas_call(forward_kernel, grid_spec=pltpu.PrefetchScalarGridSpec(num...  15.3 us
  transfers between devices with their start and end apart: 2, of which 1 were waited for; matrix products, arithmetic and copies ran while one was open for 3% of the time, Pallas kernels for 11%

profile of v6, /device:TPU:0, one launch (start us, length us, event | category | flops | bytes accessed | tf_op | source)
XLA Modules:
  0.0 709.7 jit_solution(11354654229086167080)
XLA Ops:
  2.1 1.1 convert.20
  5.2 0.8 dynamic_slice.20
  6.0 11.9 %exchange_0.1 = s32[4,8,8,128]{3,2,1,0:T(8,128)S(1)} custom-call(s32[8,128]{1,0:T(8,128)S(1)} %add_bitcast_fusion.refs_0_), custom_call_target="tpu_custom_call" | custom-call | bytes 2703360 | tf_op jit(solution)/shard_map/exchange_0/pallas_call | solution.py:429
  18.0 1.0 convert.23
  19.1 1.3 broadcast_in_dim.45
  20.4 4.3 all-to-all-start
  25.2 0.8 select_reduce_fusion.1
  26.2 1.1 reshape.236.routes_ref
  27.3 6.4 convert_element_type.38.refs_3_.refs_1_
  33.8 4.8 select_reduce_fusion
  38.7 12.4 %gather_rows.1 = bf16[32,256,384]{2,1,0:T(8,128)(2,1)S(1)} custom-call(s32[32,256]{1,0:T(8,128)S(1)} %fusion.12.list_ref, s32[32]{0:T(128)S(1)} %get-tuple-element.245.count_ref, f32[6144,384]{1,0:T(8,128)} %refs_0_.1), custom_call_target="tpu_custom_call" | custom-call | tf_op jit(solution)/shard_map/gather_rows/pallas_call | solution.py:943
  51.1 2.7 copy-done.5
  54.5 9.5 %all-to-all-done = bf16[4,96,2176]{2,1,0:T(8,128)(2,1)S(1)} async-done(((bf16[4,96,2176]{2,1,0:T(8,128)(2,1)}), bf16[4,96,2176]{2,1,0:T(8,128)(2,1)S(1)}, u32[]{:S(2)}, u32[]{:S(2)}) %all-to-all-start) | async-done | bytes 1671200 | tf_op jit(solution)/shard_map/all_to_all | solution.py:1303
  64.1 95.7 %exchange_1.1 = (bf16[4,2,2,2,48,2176]{5,4,3,2,1,0:T(8,128)(2,1)}, bf16[4,2,2,2,48,2176]{5,4,3,2,1,0:T(8,128)(2,1)}, bf16[4,256,384]{2,1,0:T(8,128)(2,1)S(1)}, bf16[1536,1536]{1,0:T(8,128)(2,1)S(1)}) custom-call(bf16[4,48,2176]{2,1,0:T(8,128)(2,1)S(1)} %get-tuple-element.248.refs_0_, bf16[4,48,2176]{2,1,0:T(8,128)(2,1)S(1)} %get-tuple-element.247.refs_1_, ...), custom_call_target="tpu_custom_call" | custom-call | bytes 631111680 | tf_op jit(solution)/shard_map/exchange_1/pallas_call | solution.py:429
  159.9 2.2 copy-done.6
  162.0 0.9 copy-done.23
  162.9 12.2 %attend.1 = (bf16[32,1536]{1,0:T(8,128)(2,1)}, f32[32,1536]{1,0:T(8,128)}, f32[8,96,256]{2,1,0:T(8,128)}, bf16[32,1536]{1,0:T(8,128)(2,1)}, bf16[256,512]{1,0:T(...) custom-call(s32[1]{0:T(128)} %bitcast.128, ...), custom_call_target="tpu_custom_call" | custom-call | tf_op jit(solution)/shard_map/attend/pallas_call | solution.py:797
  175.2 2.3 copy-done.7
  177.5 0.9 copy-done.36
  178.4 26.1 %exchange_2.1 = (bf16[4,2,2,2,32,1536]{5,4,3,2,1,0:T(8,128)(2,1)S(1)}, bf16[1536,1536]{1,0:T(8,128)(2,1)S(1)}) custom-call(bf16[32,1536]{1,0:T(8,128)(2,1)S(1)} %copy-done.36, bf16[6144,384]{1,0:T(8,128)(2,1)S(1)} %bitcast.81, bf16[1536,1536]{1,0:T(8,128)(2,1)S(1)} %copy-done.7), custom_call_target="tpu_custom_call", output_to_operand_aliasing={{1}: (2, {})} | custom-call | bytes 347996160 | tf_op jit(solution)/shard_map/exchange_2/pallas_call | solution.py:429
  204.6 2.2 copy-done.8
  206.8 1.7 copy-done.21
  208.4 15.3 %experts_forward.1 = (bf16[1024,1536]{1,0:T(8,128)(2,1)S(1)}, f32[1024,1024]{1,0:T(8,128)}, f32[1024,128]{1,0:T(8,128)S(1)}, bf16[1536,1024]{1,0:T(8,128)(2,1)S(...) custom-call(s32[4]{0:T(128)S(1)} %iota_add_fusion.1.lane_ref, bf16[1024,1536]{1,0:T(8,128)(2,1)} %bitcast.97, ...), custom_call_target="tpu_custom_call" | custom-call | tf_op jit(solution)/shard_map/experts_forward/pallas_call | solution.py:513
  223.8 54.3 %exchange_3.1 = (bf16[4,2,2,2,32,1536]{5,4,3,2,1,0:T(8,128)(2,1)S(1)}, f32[32,1536]{1,0:T(8,128)S(1)}, bf16[1536,1536]{1,0:T(8,128)(2,1)S(1)}) custom-call(bf16[4,2,2,2,32,1536]{5,4,3,2,1,0:T(8,128)(2,1)S(1)} %bitcast.95, f32[32,1536]{1,0:T(8,128)S(1)} %copy-done.30, f32[8,1536]{1,0:T(8,128)S(1)} %copy-done.35, ...), custom_call_target="tpu_custom_call", output_to_operand_aliasing={{2}: (4, {})} | custom-call | bytes 417792000 | tf_op jit(solution)/shard_map/exchange_3/pallas_call | solution.py:429
  278.1 5.1 multiply_reduce_fusion
  283.3 3.0 exponential_reduce_fusion
  286.4 11.7 %exchange_5.1 = f32[4,8,8,384]{3,2,1,0:T(8,128)S(1)} custom-call(f32[8,384]{1,0:T(8,128)S(1)} %reshape.240.refs_0_), custom_call_target="tpu_custom_call" | custom-call | bytes 8110080 | tf_op jit(solution)/shard_map/exchange_5/pallas_call | solution.py:429
  300.0 4.0 fusion.5
  304.1 5.3 multiply_convert_fusion
  309.4 5.4 fusion.1.refs_3_.refs_1_
  315.4 53.5 %exchange_6.1 = (bf16[4,2,2,2,32,1536]{5,4,3,2,1,0:T(8,128)(2,1)S(1)}, f32[32,1536]{1,0:T(8,128)S(1)}, f32[1,1536]{1,0:T(1,128)S(1)}, bf16[4,1536,384]{2,1,0:T(8,128)(2,1)S(1)}) custom-call(bf16[4,2,2,2,32,1536]{5,4,3,2,1,0:T(8,128)(2,1)S(1)} %bitcast.96, f32[32,1536]{1,0:T(8,128)S(1)} %get-tuple-element.98.refs_1_, f32[8,1536]{1,0:T(8,128)S(1)} %copy-done.35, ...), custom_call_target="tpu_custom_call" | custom-call | bytes 323543040 | tf_op jit(solution)/shard_map/exchange_6/pallas_call | solution.py:429
  368.9 1.7 copy-done.18
  371.2 22.7 %experts_backward.1 = (bf16[1024,1664]{1,0:T(8,128)(2,1)}, bf16[1024,1024]{1,0:T(8,128)(2,1)}) custom-call(s32[4]{0:T(128)S(1)} %iota_add_fusion.1.lane_ref, bf16[1024,1536]{1,0:T(8,128)(2,1)} %bitcast.93, f32[1024,1024]{1,0:T(8,128)} %get-tuple-element.100.mid_ref, f32[1024,128]{1,0:T(8,128)S(1)} %get-tuple-element.101.gates_ref, ...), custom_call_target="tpu_custom_call" | custom-call | tf_op jit(solution)/shard_map/experts_backward/pallas_call | solution.py:592
  393.9 2.0 copy-done.13
  395.8 32.5 %exchange_8.1 = (f32[32,1664]{1,0:T(8,128)S(1)}, bf16[4,1536,384]{2,1,0:T(8,128)(2,1)S(1)}) custom-call(bf16[4,2,2,2,32,1664]{5,4,3,2,1,0:T(8,128)(2,1)S(1)} %bitcast.88, bf16[1536,1536]{1,0:T(8,128)(2,1)S(1)} %fusion.1.refs_3_.refs_1_, bf16[4,1536,384]{2,1,0:T(8,128)(2,1)S(1)} %get-tuple-element.108.refs_2_), custom_call_target="tpu_custom_call", output_to_operand_aliasing={{1}: (2, {})} | custom-call | bytes 355532800 | tf_op jit(solution)/shard_map/exchange_8/pallas_call | solution.py:429
  428.4 2.1 copy-done.2
  431.2 23.9 %attend_back.1 = (bf16[4,256,384]{2,1,0:T(8,128)(2,1)}, bf16[1536,2176]{1,0:T(8,128)(2,1)}, bf16[1536,2176]{1,0:T(8,128)(2,1)}) custom-call(s32[1]{0:T(128)} %bitcast.129, f32[32,1664]{1,0:T(8,128)} %copy-done.42, f32[32,128]{1,0:T(8,128)} %constant_dynamic-slice_fusion.gates_ref, f32[32,1536]{1,0:T(8,128)} %copy-done.43, f32[1,1536]{1,0:T(1,128)} %copy-done.48, ...), custom_call_target="tpu_custom_call" | custom-call | tf_op jit(solution)/shard_map/attend_back/pallas_call | solution.py:885
  455.1 96.2 %exchange_9.1 = (bf16[4,48,2176]{2,1,0:T(8,128)(2,1)}, bf16[4,48,2176]{2,1,0:T(8,128)(2,1)}, bf16[4,2,2,2,256,384]{5,4,3,2,1,0:T(8,128)(2,1)}, bf16[4,1536,384]{2,1,0:T(8,128)(2,1)}) custom-call(bf16[4,2,2,2,48,2176]{5,4,3,2,1,0:T(8,128)(2,1)} %bitcast.110, bf16[4,2,2,2,48,2176]{5,4,3,2,1,0:T(8,128)(2,1)} %bitcast.111, ...), custom_call_target="tpu_custom_call", output_to_operand_aliasing={{3}: (4, {})} | custom-call | bytes 725483520 | tf_op jit(solution)/shard_map/exchange_9/pallas_call | solution.py:429
  551.3 2.7 pad_maximum_fusion
  554.0 5.0 all-to-all-start.1
  561.4 43.9 %table_moments.1 = (f32[6144,384]{1,0:T(8,128)}, f32[6144,384]{1,0:T(8,128)}, f32[8,128]{1,0:T(8,128)}) custom-call(s32[32,256]{1,0:T(8,128)} %copy-done.39, s32[32]{0:T(128)} %copy-done.46, f32[2]{0:T(128)} %pad_maximum_fusion.4.scale_ref, bf16[32,256,384]{2,1,0:T(8,128)(2,1)} %bitcast.116, bf16[6144,384]{1,0:T(8,128)(2,1)} %bitcast.82, ...), custom_call_target="tpu_custom_call" | custom-call | tf_op jit(solution)/shard_map/table_moments/pallas_call | solution.py:1041
  605.3 1.9 fusion.20.down_grad
  607.8 5.4 fusion.19.grad_ref
  613.3 21.2 %expert_moments.1 = (f32[12288,128]{1,0:T(8,128)}, f32[12288,128]{1,0:T(8,128)}, f32[512,1536]{1,0:T(8,128)}, f32[512,1536]{1,0:T(8,128)}, f32[8,128]{1,0:T(8,128)S(1)}) custom-call(f32[2]{0:T(128)S(1)} %copy-done.47, f32[1536,1024]{1,0:T(8,128)} %fusion.19.grad_ref, f32[12288,128]{1,0:T(8,128)} %bitcast.106, f32[12288,128]{1,0:T(8,128)} %bitcast.112, ...), custom_call_target="tpu_custom_call" | custom-call | tf_op jit(solution)/shard_map/expert_moments/pallas_call | solution.py:662
  634.5 1.0 copy-done.11
  635.5 1.0 copy-done.33
  636.6 1.0 copy-done.34
  637.6 1.0 copy-done.40
  638.5 1.0 copy-done.41
  640.9 3.5 small_moments.1
  645.6 1.4 copy.119
  647.8 13.1 %exchange_10.1 = f32[4,8,8,128]{3,2,1,0:T(8,128)S(1)} custom-call(f32[8,128]{1,0:T(8,128)S(1)} %add_add_fusion.refs_0_), custom_call_target="tpu_custom_call" | custom-call | bytes 2703360 | tf_op jit(solution)/shard_map/exchange_10/pallas_call | solution.py:429
  661.6 0.9 reduce_sum.119
  664.5 0.8 multiply_subtract_fusion
  666.6 1.3 multiply_subtract_fusion.1
  667.9 1.0 copy-done.12
  668.9 1.9 copy-done.14
  670.8 1.9 copy-done.15
  672.7 0.9 copy-done.29
  673.6 1.0 copy-done.31
  674.7 1.0 copy-done.32
  675.7 1.0 copy-done.37
  676.7 1.0 copy-done.38
  677.6 30.7 %finish.1 = (f32[6144,384]{1,0:T(8,128)}, f32[12288,128]{1,0:T(8,128)}, f32[512,1536]{1,0:T(8,128)}, f32[48,2560]{1,0:T(8,128)}, f32[48,1536]{1,0:T(8,128)}) custom-call(f32[2]{0:T(128)S(1)} %copy-done.47, f32[32,8,128]{2,1,0:T(8,128)S(1)} %bitcast.99, f32[6144,384]{1,0:T(8,128)} %refs_0_.1, f32[6144,384]{1,0:T(8,128)} %get-tuple-element.218.refs_1_, ...), custom_call_target="tpu_custom_call" | custom-call | tf_op jit(solution)/shard_map/finish/pallas_call | solution.py:1152
  (180 shorter events, 16.6 us)
Async XLA Ops:
  0.7 4.2 copy-start
  2.1 22.9 %copy-start.60 = (s32[1,32]{1,0:T(1,128)}, s32[1,32]{1,0:T(1,128)S(1)}, u32[]{:S(2)}) copy-start(s32[1,32]{1,0:T(1,128)S(1)} %constant_dynamic-slice_fusion.4) | copy-start | bytes 388
  20.4 43.6 %all-to-all-start = ((bf16[4,96,2176]{2,1,0:T(8,128)(2,1)}), bf16[4,96,2176]{2,1,0:T(8,128)(2,1)S(1)}, u32[]{:S(2)}, u32[]{:S(2)}) async-start(bf16[4,96,2176]{2,1,0:T(8,128)(2,1)} %broadcast_in_dim.45), calls=%async_computation | async-start | bytes 3342336 | tf_op jit(solution)/shard_map/all_to_all | solution.py:1303
  25.0 28.8 %copy-start.55 = (f32[256,128]{1,0:T(8,128)}, f32[256,128]{1,0:T(8,128)S(1)}, u32[]{:S(2)}) copy-start(f32[256,128]{1,0:T(8,128)S(1)} %copy.108.sin_ref) | copy-start | bytes 393220
  25.2 13.5 %copy-start.46 = (s32[32]{0:T(128)}, s32[32]{0:T(128)S(1)}, u32[]{:S(2)}) copy-start(s32[32]{0:T(128)S(1)} %get-tuple-element.245.count_ref) | copy-start | bytes 388
  26.2 27.6 %copy-start.56 = (f32[256,128]{1,0:T(8,128)}, f32[256,128]{1,0:T(8,128)S(1)}, u32[]{:S(2)}) copy-start(f32[256,128]{1,0:T(8,128)S(1)} %copy.107.cos_ref) | copy-start | bytes 393220
  38.7 12.4 %copy-start.39 = (s32[32,256]{1,0:T(8,128)}, s32[32,256]{1,0:T(8,128)S(1)}, u32[]{:S(2)}) copy-start(s32[32,256]{1,0:T(8,128)S(1)} %fusion.12.list_ref) | copy-start | bytes 98308
  38.7 15.8 %copy-start.61 = (s32[16,2]{0,1:T(2,128)S(1)}, s32[16,2]{0,1:T(2,128)}, u32[]{:S(2)}) copy-start(s32[16,2]{0,1:T(2,128)} %param.29) | copy-start | bytes 388
  51.1 2.7 copy-start.5
  64.1 111.0 %slice-start = ((s8[4718592]{0:T(1024)(128)(4,1)}), s8[4194304]{0:T(1024)(128)(4,1)S(1)}, s32[]{:S(2)}) async-start(s8[4718592]{0:T(1024)(128)(4,1)} %bitcast.80), calls=%async_computation.2 | async-start | bytes 8388608
  159.9 2.2 copy-start.6
  162.0 0.9 copy-start.23
  162.9 12.3 %slice-start.1 = ((s8[4718592]{0:T(1024)(128)(4,1)}), s8[524288]{0:T(1024)(128)(4,1)S(1)}, s32[]{:S(2)}) async-start(s8[4718592]{0:T(1024)(128)(4,1)} %bitcast.80), calls=%async_computation.3 | async-start | bytes 1048576
  175.2 2.3 copy-start.7
  177.5 0.9 copy-start.36
  178.4 30.0 %copy-start.25 = (s32[1024,8]{1,0:T(8,128)S(1)}, s32[1024,8]{1,0:T(8,128)}, u32[]{:S(2)}) copy-start(s32[1024,8]{1,0:T(8,128)} %reshape.236.routes_ref) | copy-start | bytes 98308
  204.6 2.2 copy-start.8
  206.8 1.7 copy-start.21
  208.4 15.3 %copy-start.9 = (bf16[1536,1536]{1,0:T(8,128)(2,1)S(1)}, bf16[1536,1536]{1,0:T(8,128)(2,1)}, u32[]{:S(2)}) copy-start(bf16[1536,1536]{1,0:T(8,128)(2,1)} %copy-done.8) | copy-start | bytes 14155780
  208.4 15.3 %copy-start.30 = (f32[32,1536]{1,0:T(8,128)S(1)}, f32[32,1536]{1,0:T(8,128)}, u32[]{:S(2)}) copy-start(f32[32,1536]{1,0:T(8,128)} %get-tuple-element.93.refs_1_.resid_ref) | copy-start | bytes 589828
  208.4 15.3 %copy-start.35 = (f32[8,1536]{1,0:T(8,128)S(1)}, f32[8,1536]{1,0:T(8,128)}, u32[]{:S(2)}) copy-start(f32[8,1536]{1,0:T(8,128)} %get-tuple-element.94.refs_2_.gains_ref) | copy-start | bytes 147460
  223.8 54.3 %copy-start.20 = (bf16[1536,1024]{1,0:T(8,128)(2,1)}, bf16[1536,1024]{1,0:T(8,128)(2,1)S(1)}, u32[]{:S(2)}) copy-start(bf16[1536,1024]{1,0:T(8,128)(2,1)S(1)} %get-tuple-element.102.cat_ref) | copy-start | bytes 9437188
  223.8 54.3 %copy-start.26 = (bf16[512,1536]{1,0:T(8,128)(2,1)}, bf16[512,1536]{1,0:T(8,128)(2,1)S(1)}, u32[]{:S(2)}) copy-start(bf16[512,1536]{1,0:T(8,128)(2,1)S(1)} %get-tuple-element.103.down_ref) | copy-start | bytes 4718596
  278.1 5.2 copy-start.10
  278.1 5.2 copy-start.52
  283.3 3.1 copy-start.54
  283.3 15.6 %copy-start.63 = (f32[32]{0:T(128)S(1)}, f32[32]{0:T(128)}, u32[]{:S(2)}) copy-start(f32[32]{0:T(128)} %param.30) | copy-start | bytes 388
  298.7 5.4 slice-start.2
  300.0 4.1 slice-start.3
  304.1 5.3 copy-start.53
  314.8 79.1 %copy-start.3 = (bf16[1536,1536]{1,0:T(8,128)(2,1)}, bf16[1536,1536]{1,0:T(8,128)(2,1)S(1)}, u32[]{:S(2)}) copy-start(bf16[1536,1536]{1,0:T(8,128)(2,1)S(1)} %fusion.1.refs_3_.refs_1_) | copy-start | bytes 14155780
  314.8 56.4 %copy-start.27 = (bf16[512,1536]{1,0:T(8,128)(2,1)S(1)}, bf16[512,1536]{1,0:T(8,128)(2,1)}, u32[]{:S(2)}) copy-start(bf16[512,1536]{1,0:T(8,128)(2,1)} %copy-done.26) | copy-start | bytes 4718596
  368.9 1.7 copy-start.18
  371.2 22.7 %copy-start.43 = (f32[32,1536]{1,0:T(8,128)}, f32[32,1536]{1,0:T(8,128)S(1)}, u32[]{:S(2)}) copy-start(f32[32,1536]{1,0:T(8,128)S(1)} %get-tuple-element.110.grad_two_ref) | copy-start | bytes 589828
  393.9 2.0 copy-start.13
  428.4 2.1 copy-start.2
  551.3 7.8 %copy-start.57 = (f32[48,32]{0,1:T(8,128)S(1)}, f32[48,32]{0,1:T(8,128)}, u32[]{:S(2)}) copy-start(f32[48,32]{0,1:T(8,128)} %param.42) | copy-start | bytes 18436
  551.3 8.7 %copy-start.58 = (f32[48,32]{0,1:T(8,128)S(1)}, f32[48,32]{0,1:T(8,128)}, u32[]{:S(2)}) copy-start(f32[48,32]{0,1:T(8,128)} %param.43) | copy-start | bytes 18436
  551.3 8.7 %copy-start.59 = (f32[48,32]{0,1:T(8,128)S(1)}, f32[48,32]{0,1:T(8,128)}, u32[]{:S(2)}) copy-start(f32[48,32]{0,1:T(8,128)} %param.44) | copy-start | bytes 18436
  554.0 80.4 %all-to-all-start.1 = ((bf16[4,96,2176]{2,1,0:T(8,128)(2,1)}), bf16[4,96,2176]{2,1,0:T(8,128)(2,1)}, u32[]{:S(2)}, u32[]{:S(2)}) async-start(bf16[4,96,2176]{2,1,0:T(8,128)(2,1)} %pad_maximum_fusion), calls=%async_computation.1 | async-start | bytes 3342336 | tf_op jit(solution)/shard_map/all_to_all | solution.py:1430
  561.3 43.9 %copy-start.19 = (bf16[4,2,2,2,32,1536]{5,4,3,2,1,0:T(8,128)(2,1)S(1)}, bf16[4,2,2,2,32,1536]{5,4,3,2,1,0:T(8,128)(2,1)}, u32[]{:S(2)}) copy-start(bf16[4,2,2,2,32,1536]{5,4,3,2,1,0:T(8,128)(2,1)} %copy-done.18) | copy-start | bytes 9437188
  605.3 1.9 copy-start.22
  605.3 2.5 copy-start.62
  607.8 5.4 copy-start.4
  607.8 5.4 copy-start.16
  607.8 5.4 copy-start.17
  607.8 5.4 copy-start.47
  613.3 21.2 %copy-start.24 = (f32[48,1536]{1,0:T(8,128)S(1)}, f32[48,1536]{1,0:T(8,128)}, u32[]{:S(2)}) copy-start(f32[48,1536]{1,0:T(8,128)} %refs_12_.1) | copy-start | bytes 884740
  613.3 21.2 %copy-start.45 = (f32[3,48]{1,0:T(4,128)S(1)}, f32[3,48]{1,0:T(4,128)}, u32[]{:S(2)}) copy-start(f32[3,48]{1,0:T(4,128)} %gains.1) | copy-start | bytes 1732
  634.5 1.0 copy-start.11
  635.5 1.0 copy-start.33
  636.5 1.0 copy-start.34
  637.6 1.0 copy-start.40
  638.5 1.0 copy-start.41
  645.0 2.1 copy-start.49
  667.9 1.0 copy-start.12
  668.9 1.9 copy-start.14
  670.8 1.9 copy-start.15
  672.7 0.9 copy-start.29
  673.6 1.0 copy-start.31
  674.7 1.0 copy-start.32
  675.7 1.0 copy-start.37
  676.7 1.0 copy-start.38
  677.6 30.7 %copy-start.1 = (s32[256,8]{0,1:T(8,128)S(1)}, s32[256,8]{0,1:T(8,128)}, u32[]{:S(2)}) copy-start(s32[256,8]{0,1:T(8,128)} %param.31) | copy-start | bytes 24580
  (6 other events, 3.9 us)

commit v7 on v6

--- a/solution.py
+++ b/solution.py
@@ -318,7 +318,7 @@
     def __init__(self, x, turns, planes, side, back=False, held=None):
         self.planes, self.side = planes, side
         self.inputs = [x] if held is None else [x, held]
-        self.in_spaces, self.out_spaces = (pl.ANY,) * len(self.inputs), (pl.ANY,)
+        self.in_spaces, self.out_spaces = (pltpu.HBM,) * len(self.inputs), (pltpu.HBM,)
         self.aliases = {} if held is None else {1: 0}
         self.turns, self.back = turns, back
         self.scratch = [pltpu.SemaphoreType.DMA((len(turns),))]
@@ -617,8 +617,8 @@
 
 
 def moments_kernel(
-    scale_ref, grad_ref, w_ref, first_ref, second_ref, down_grad, down_w, down_first, down_second,
-    new_first, new_second, new_down_first, new_down_second, norms, sums, down_sums,
+    scale_ref, other_norms, grad_ref, w_ref, first_ref, second_ref, down_grad, down_w, down_first, down_second,
+    new_first, new_second, updates, new_down_first, new_down_second, down_updates, norms, sums, down_sums,
 ):
     units = w_ref.shape[1]
     part = w_ref.shape[0] // 2
@@ -637,26 +637,30 @@
         one, two, update = lamb_parts(weight, first_ref[here, :], second_ref[here, :], grad, scales)
         new_first[here, :] = one
         new_second[here, :] = two
+        updates[here, :] = update
         sums[0] += fold(weight * weight)
         sums[1] += fold(update * update)
     weight = down_w[...]
     one, two, update = lamb_parts(weight, down_first[...], down_second[...], down_grad[...], scales)
     new_down_first[...] = one
     new_down_second[...] = two
+    down_updates[...] = update
     down_sums[0] += fold(weight * weight)
     down_sums[1] += fold(update * update)
 
     @pl.when(step == pl.num_programs(0) * pl.num_programs(1) - 1)
     def _():
-        norms[...] = norm_cells(5, total_of(sums[0]), total_of(sums[1])) + norm_cells(
-            6, total_of(down_sums[0]), total_of(down_sums[1])
-        )
-
-
-def expert_moments(scales, grad, weight, first, second, down_grad, down, down_first, down_second):
+        block = norm_cells(5, total_of(sums[0]), total_of(sums[1]))
+        block += norm_cells(6, total_of(down_sums[0]), total_of(down_sums[1]))
+        norms[...] = other_norms[...] + block
+
+
+def expert_moments(scales, norms, grad, weight, first, second, *down_state):
     units = weight.shape[1]
+    down = down_state[1]
     number = grad.shape[1] // (2 * units)
     parts = 2
+    cells = pl.BlockSpec((8, 128), lambda e, p, *_: (0, 0))
     row = pl.BlockSpec((2 * D // parts, units), lambda e, p, *_: (e * parts + p, 0))
     down_row = pl.BlockSpec((units // parts, D), lambda e, p, *_: (e * parts + p, 0))
     return pl.pallas_call(
@@ -664,17 +668,18 @@
         grid_spec=pltpu.PrefetchScalarGridSpec(
             num_scalar_prefetch=1,
             grid=(number, parts),
-            in_specs=[pl.BlockSpec((D // parts, 2 * units), lambda e, p, *_: (p, e)), row, row, row]
+            in_specs=[cells, pl.BlockSpec((D // parts, 2 * units), lambda e, p, *_: (p, e))]
+            + [row] * 3
             + [down_row] * 4,
-            out_specs=[row, row, down_row, down_row, pl.BlockSpec((8, 128), lambda e, p, *_: (0, 0))],
+            out_specs=[row] * 3 + [down_row] * 3 + [cells],
             scratch_shapes=[pltpu.VMEM((2, 8, units), f32), pltpu.VMEM((2, 8, D), f32)],
         ),
-        out_shape=[jax.ShapeDtypeStruct(weight.shape, f32)] * 2
-        + [jax.ShapeDtypeStruct(down.shape, f32)] * 2
+        out_shape=[jax.ShapeDtypeStruct(weight.shape, f32)] * 3
+        + [jax.ShapeDtypeStruct(down.shape, f32)] * 3
         + [jax.ShapeDtypeStruct((8, 128), f32)],
-        compiler_params=pltpu.CompilerParams(vmem_limit_bytes=36 << 20),
+        compiler_params=pltpu.CompilerParams(vmem_limit_bytes=62 << 20),
         name="expert_moments",
-    )(scales, grad, weight, first, second, down_grad, down, down_first, down_second)
+    )(scales, norms, grad, weight, first, second, *down_state)
 
 
 HEAD_COLS = QUERY_HEADS * HEAD_WIDTH
@@ -810,7 +815,7 @@
             jax.ShapeDtypeStruct((8, D), f32),
         ],
         scratch_shapes=[pltpu.VMEM((SEQUENCE_TOKENS, D), f32)],
-        compiler_params=pltpu.CompilerParams(vmem_limit_bytes=56 << 20),
+        compiler_params=pltpu.CompilerParams(vmem_limit_bytes=28 << 20),
         name="attend",
     )(start, picked, one, two, *tables)
 
@@ -892,7 +897,7 @@
             jax.ShapeDtypeStruct((D, PACK), bf16),
         ],
         scratch_shapes=[pltpu.VMEM((SEQUENCE_TOKENS, D), f32)],
-        compiler_params=pltpu.CompilerParams(vmem_limit_bytes=60 << 20),
+        compiler_params=pltpu.CompilerParams(vmem_limit_bytes=44 << 20),
         name="attend_back",
     )(start, *operands)
 
@@ -908,6 +913,7 @@
 
 
 STEPS = 4
+TOGETHER = 4
 
 
 def row_lists(tokens, base, rows):
@@ -924,17 +930,18 @@
 
 
 def gather_kernel(list_ref, count_ref, table_ref, out_ref, rows_ref):
-    b = pl.program_id(0)
-    rows_ref[...] = jnp.zeros_like(rows_ref)
-
-    def step(k, carry):
-        for j in range(STEPS):
-            entry = list_ref[b, k * STEPS + j]
-            rows_ref[pl.ds(entry >> 16, 1), :] = table_ref[pl.ds(entry & 65535, 1), :]
-        return carry
-
-    lax.fori_loop(0, (count_ref[b] + STEPS - 1) // STEPS, step, 0)
-    out_ref[0] = rows_ref[:SEQUENCE_TOKENS].astype(bf16)
+    for n in range(TOGETHER):
+        b = pl.program_id(0) * TOGETHER + n
+        rows_ref[n] = jnp.zeros(rows_ref.shape[1:], f32)
+
+        def step(k, carry, n=n, b=b):
+            for j in range(STEPS):
+                entry = list_ref[b, k * STEPS + j]
+                rows_ref[n, pl.ds(entry >> 16, 1), :] = table_ref[pl.ds(entry & 65535, 1), :]
+            return carry
+
+        lax.fori_loop(0, (count_ref[b] + STEPS - 1) // STEPS, step, 0)
+        out_ref[n] = rows_ref[n, :SEQUENCE_TOKENS].astype(bf16)
 
 
 def gather_rows(lists, counts, table):
@@ -944,13 +951,13 @@
         gather_kernel,
         grid_spec=pltpu.PrefetchScalarGridSpec(
             num_scalar_prefetch=2,
-            grid=(blocks,),
+            grid=(blocks // TOGETHER,),
             in_specs=[pl.BlockSpec((rows, columns), lambda b, *_: (0, 0))],
-            out_specs=pl.BlockSpec((1, SEQUENCE_TOKENS, columns), lambda b, *_: (b, 0, 0)),
-            scratch_shapes=[pltpu.VMEM((SEQUENCE_TOKENS + 8, columns), f32)],
+            out_specs=pl.BlockSpec((TOGETHER, SEQUENCE_TOKENS, columns), lambda b, *_: (b, 0, 0)),
+            scratch_shapes=[pltpu.VMEM((TOGETHER, SEQUENCE_TOKENS + 8, columns), f32)],
         ),
         out_shape=jax.ShapeDtypeStruct((blocks, SEQUENCE_TOKENS, columns), bf16),
-        compiler_params=pltpu.CompilerParams(vmem_limit_bytes=40 << 20),
+        compiler_params=pltpu.CompilerParams(vmem_limit_bytes=22 << 20),
         name="gather_rows",
     )(lists, counts, table)
 
@@ -975,7 +982,7 @@
 
 def table_kernel(
     list_ref, count_ref, scale_ref, grad_ref, head_ref, w_in, first_in, second_in,
-    new_first, new_second, norms,
+    new_first, new_second, updates, norms,
     rows_ref, acc, w, first, second, sums, sems,
 ):
     b = pl.program_id(0)
@@ -994,22 +1001,24 @@
 
     @pl.when(b < blocks)
     def _():
-        rows_ref[:SEQUENCE_TOKENS] = grad_ref[0].astype(f32)
-        rows_ref[SEQUENCE_TOKENS:] = jnp.zeros((8, rows_ref.shape[1]), f32)
-
-        def step(k, carry):
-            entries = [list_ref[b, k * STEPS + j] for j in range(STEPS)]
-            spots = [entry & 65535 for entry in entries]
-            grads = [rows_ref[pl.ds(entry >> 16, 1), :] for entry in entries]
-            olds = [acc[pl.ds(spot, 1), :] for spot in spots]
-            for j in range(STEPS):
-                total = olds[j] + grads[j]
-                for i in range(j):
-                    total += jnp.where(spots[i] == spots[j], grads[i], 0.0)
-                acc[pl.ds(spots[j], 1), :] = total
-            return carry
-
-        lax.fori_loop(0, (count_ref[b] + STEPS - 1) // STEPS, step, 0)
+        for n in range(TOGETHER):
+            rows_ref[n, :SEQUENCE_TOKENS] = grad_ref[n].astype(f32)
+            rows_ref[n, SEQUENCE_TOKENS:] = jnp.zeros((8, rows_ref.shape[2]), f32)
+            own = b * TOGETHER + n
+
+            def step(k, carry, n=n, own=own):
+                entries = [list_ref[own, k * STEPS + j] for j in range(STEPS)]
+                spots = [entry & 65535 for entry in entries]
+                grads = [rows_ref[n, pl.ds(entry >> 16, 1), :] for entry in entries]
+                olds = [acc[pl.ds(spot, 1), :] for spot in spots]
+                for j in range(STEPS):
+                    total = olds[j] + grads[j]
+                    for i in range(j):
+                        total += jnp.where(spots[i] == spots[j], grads[i], 0.0)
+                    acc[pl.ds(spots[j], 1), :] = total
+                return carry
+
+            lax.fori_loop(0, (count_ref[own] + STEPS - 1) // STEPS, step, 0)
 
     @pl.when(b == blocks)
     def _():
@@ -1025,6 +1034,7 @@
         )
         new_first[...] = one
         new_second[...] = two
+        updates[...] = update
         sums[0] += fold(w[here, :] * w[here, :])
         sums[1] += fold(update * update)
 
@@ -1034,7 +1044,7 @@
 
 
 def table_moments(lists, counts, scales, grads, head, weight, first, second):
-    blocks = lists.shape[0]
+    blocks = lists.shape[0] // TOGETHER
     rows, columns = weight.shape
     part = rows // TABLE_PARTS
     out = pl.BlockSpec((part, columns), lambda b, *_: (jnp.maximum(b - blocks, 0), 0))
@@ -1045,7 +1055,7 @@
             grid=(blocks + TABLE_PARTS,),
             in_specs=[
                 pl.BlockSpec(
-                    (1, SEQUENCE_TOKENS, columns),
+                    (TOGETHER, SEQUENCE_TOKENS, columns),
                     lambda b, *_: (jnp.minimum(b, blocks - 1), 0, 0),
                 ),
                 pl.BlockSpec(
@@ -1053,14 +1063,14 @@
                 ),
             ]
             + [pl.BlockSpec(memory_space=pl.ANY)] * 3,
-            out_specs=[out, out, pl.BlockSpec((8, 128), lambda b, *_: (0, 0))],
-            scratch_shapes=[pltpu.VMEM((SEQUENCE_TOKENS + 8, columns), f32)]
+            out_specs=[out, out, out, pl.BlockSpec((8, 128), lambda b, *_: (0, 0))],
+            scratch_shapes=[pltpu.VMEM((TOGETHER, SEQUENCE_TOKENS + 8, columns), f32)]
             + [pltpu.VMEM((rows, columns), f32)] * 4
             + [pltpu.VMEM((2, 8, columns), f32), pltpu.SemaphoreType.DMA((3,))],
         ),
-        out_shape=[jax.ShapeDtypeStruct((rows, columns), f32)] * 2
+        out_shape=[jax.ShapeDtypeStruct((rows, columns), f32)] * 3
         + [jax.ShapeDtypeStruct((8, 128), f32)],
-        compiler_params=pltpu.CompilerParams(vmem_limit_bytes=54 << 20),
+        compiler_params=pltpu.CompilerParams(vmem_limit_bytes=52 << 20),
         name="table_moments",
     )(lists, counts, scales, grads, head, weight, first, second)
 
@@ -1096,10 +1106,11 @@
     ]
     for n, (weight, first, second, grad) in enumerate(sets):
         one, two, update = lamb_parts(weight[...], first[...], second[...], grad, scales)
-        results[2 * n][...] = one
-        results[2 * n + 1][...] = two
+        results[3 * n][...] = one
+        results[3 * n + 1][...] = two
+        results[3 * n + 2][...] = update
         block += norm_cells(n + 1, total_of(weight[...] * weight[...]), total_of(update * update))
-    results[8][...] = block
+    results[12][...] = block
 
 
 def small_moments(scales, sums, *state):
@@ -1107,10 +1118,10 @@
     return pl.pallas_call(
         small_kernel,
         in_specs=[pl.BlockSpec(memory_space=pltpu.SMEM)] + [vm] * (1 + len(state)),
-        out_specs=[vm] * 9,
-        out_shape=[jax.ShapeDtypeStruct(x.shape, f32) for x in state[::3] for _ in range(2)]
+        out_specs=[vm] * 13,
+        out_shape=[jax.ShapeDtypeStruct(x.shape, f32) for x in state[::3] for _ in range(3)]
         + [jax.ShapeDtypeStruct((8, 128), f32)],
-        compiler_params=pltpu.CompilerParams(vmem_limit_bytes=16 << 20),
+        compiler_params=pltpu.CompilerParams(vmem_limit_bytes=62 << 20),
         name="small_moments",
     )(scales, sums, *state)
 
@@ -1118,17 +1129,13 @@
 FINISH_PARTS = 16
 
 
-def finish_kernel(scale_ref, norms_ref, *refs):
+def finish_kernel(norms_ref, *refs):
     norms = jnp.sqrt(jnp.sum(norms_ref[...], axis=0))
-    count = len(refs) // 4
+    count = len(refs) // 3
 
     def apply(n, row):
-        weight = refs[3 * n][...]
-        update = lamb_update(
-            weight, refs[3 * n + 1][...], refs[3 * n + 2][...], scale_ref[0], scale_ref[1]
-        )
         ratio = norms[row : row + 1, 0:1] / norms[row : row + 1, 1:2]
-        refs[3 * count + n][...] = weight - (STEP_RATE * ratio) * update
+        refs[2 * count + n][...] = refs[2 * n][...] - (STEP_RATE * ratio) * refs[2 * n + 1][...]
 
     apply(0, 0)
     apply(1, 5)
@@ -1140,28 +1147,25 @@
         apply(4, 2)
 
 
-def finish(scales, norms, *state):
-    weights = state[::3]
+def finish(norms, *state):
+    weights = state[::2]
 
     def spec(n):
         rows, columns = weights[n].shape
         if n < 3:
-            return pl.BlockSpec((rows // FINISH_PARTS, columns), lambda i, *_: (i, 0))
-        return pl.BlockSpec((rows, columns), lambda i, *_: (0, 0))
+            return pl.BlockSpec((rows // FINISH_PARTS, columns), lambda i: (i, 0))
+        return pl.BlockSpec((rows, columns), lambda i: (0, 0))
 
     return pl.pallas_call(
         finish_kernel,
-        grid_spec=pltpu.PrefetchScalarGridSpec(
-            num_scalar_prefetch=1,
-            grid=(FINISH_PARTS,),
-            in_specs=[pl.BlockSpec(norms.shape, lambda i, *_: (0, 0, 0))]
-            + [spec(n) for n in range(5) for _ in range(3)],
-            out_specs=[spec(n) for n in range(5)],
-        ),
+        grid=(FINISH_PARTS,),
+        in_specs=[pl.BlockSpec(norms.shape, lambda i: (0, 0, 0))]
+        + [spec(n) for n in range(5) for _ in range(2)],
+        out_specs=[spec(n) for n in range(5)],
         out_shape=[jax.ShapeDtypeStruct(x.shape, f32) for x in weights],
-        compiler_params=pltpu.CompilerParams(vmem_limit_bytes=40 << 20),
+        compiler_params=pltpu.CompilerParams(vmem_limit_bytes=62 << 20),
         name="finish",
-    )(scales, norms, *state)
+    )(norms, *state)
 
 
 def on_device(
@@ -1440,18 +1444,7 @@
     grad_in = jnp.einsum("td,tk->dk", expert_rows, mid_grad, preferred_element_type=f32)
     grad_down = jnp.einsum("tk,td->kd", gated_hidden, grad_all, preferred_element_type=f32)
     down_rows = down_weight.reshape(-1, D)
-    in_one, in_two, down_one, down_two, expert_norms = expert_moments(
-        scales,
-        grad_in,
-        in_rows,
-        in_first.reshape(in_rows.shape),
-        in_second.reshape(in_rows.shape),
-        grad_down,
-        down_rows,
-        down_first.reshape(down_rows.shape),
-        down_second.reshape(down_rows.shape),
-    )
-    table_one, table_two, table_norms = table_moments(
+    table_one, table_two, table_update, table_norms = table_moments(
         lists,
         counts,
         scales,
@@ -1477,35 +1470,36 @@
         gains_first,
         gains_second,
     )
-    norm_blocks = gather_tiny(expert_norms + table_norms + small_norms, 10)
+    in_one, in_two, in_update, down_one, down_two, down_update, expert_norms = expert_moments(
+        scales,
+        table_norms + small_norms,
+        grad_in,
+        in_rows,
+        in_first.reshape(in_rows.shape),
+        in_second.reshape(in_rows.shape),
+        grad_down,
+        down_rows,
+        down_first.reshape(down_rows.shape),
+        down_second.reshape(down_rows.shape),
+    )
+    norm_blocks = gather_tiny(expert_norms, 10)
     norm_values = jnp.sqrt(jnp.sum(norm_blocks, axis=0))[:7, :2]
     trust_ratio = norm_values[:, 0] / norm_values[:, 1]
     new_table, new_in, new_down, new_qkv, new_out = finish(
-        scales,
         norm_blocks,
         embed_table,
-        table_one,
-        table_two,
+        table_update,
         in_rows,
-        in_one,
-        in_two,
+        in_update,
         down_rows,
-        down_one,
-        down_two,
+        down_update,
         qkv_weight,
-        small[0],
-        small[1],
+        small[2],
         out_weight,
-        small[2],
-        small[3],
-    )
-
-    def renew(place, weight, one, two):
-        update = lamb_update(weight, one, two, scales[0], scales[1])
-        return weight - STEP_RATE * trust_ratio[place] * update
-
-    new_router = renew(3, router_weight, small[4], small[5])
-    new_gains = renew(4, norm_gains, small[6], small[7])
+        small[5],
+    )
+    new_router = router_weight - STEP_RATE * trust_ratio[3] * small[8]
+    new_gains = norm_gains - STEP_RATE * trust_ratio[4] * small[11]
     stats = jnp.stack([norm_values[:, 0], norm_values[:, 1], trust_ratio], axis=1)
     return (
         loss_value,
@@ -1516,14 +1510,14 @@
         small[0],
         small[1],
         new_out,
-        small[2],
         small[3],
+        small[4],
         new_router,
-        small[4],
-        small[5],
-        new_gains,
         small[6],
         small[7],
+        new_gains,
+        small[9],
+        small[10],
         new_in.reshape(in_weight.shape),
         in_one.reshape(in_weight.shape),
         in_two.reshape(in_weight.shape),

time: 714 us -> 676 us (0.947)
  Pallas kernels: 581 us -> 557 us
  local copies, waits for them, and re-layouts: 49.4 us -> 35.2 us
    unnamed x145 -> x153, local copies, waits for them, and re-layouts: 41.7 us -> 27.6 us
    pallas_call x1, Pallas kernels: 22.7 us -> 12.5 us  [experts_backward(): pl.pallas_call(backward_kernel, grid_spec=pltpu.PrefetchScalarGridSpec(nu...]
    pallas_call x1, Pallas kernels: 43.9 us -> 36.1 us  [table_moments(): pl.pallas_call(table_kernel, grid_spec=pltpu.PrefetchScalarGridSpec(num_s...]
  transfers between devices with their start and end apart: 2 -> 2, of which waited for: 1 -> 1; matrix products, arithmetic and copies ran while one was open for 3% -> 4% of each run, Pallas kernels for 11% -> 7%
where the time goes in v7:
time: 676 us; the launch traced here: 669 us
  Pallas kernels  557 us (82%)
  local copies, waits for them, and re-layouts  35.2 us (5%)
  other arithmetic  29.9 us (4%)
  matrix products  24.9 us (4%)
  starting transfers between devices  8.85 us (1%)
  waiting for transfers between devices  6.8 us (1%)
    pallas_call x9, Pallas kernels, communicate(): pl.pallas_call(kernel, out_shape=[x for p in parts for x in p.outputs], i...  397 us
    pallas_call x1, Pallas kernels, table_moments(): pl.pallas_call(table_kernel, grid_spec=pltpu.PrefetchScalarGridSpec(num_s...  36.1 us
    pallas_call x1, Pallas kernels, expert_moments(): pl.pallas_call(moments_kernel, grid_spec=pltpu.PrefetchScalarGridSpec(num...  27.9 us
    unnamed x153, local copies, waits for them, and re-layouts  27.6 us
    pallas_call x1, Pallas kernels, finish(): pl.pallas_call(finish_kernel, grid=(FINISH_PARTS,), in_specs=[pl.BlockSpe...  24.7 us
    pallas_call x1, Pallas kernels, attend_back(): pl.pallas_call(attend_back_kernel, in_specs=[pl.BlockSpec(memory_space=pl...  23.6 us
    pallas_call x1, Pallas kernels, experts_forward(): pl.pallas_call(forward_kernel, grid_spec=pltpu.PrefetchScalarGridSpec(num...  15 us
  transfers between devices with their start and end apart: 2, of which 1 were waited for; matrix products, arithmetic and copies ran while one was open for 4% of the time, Pallas kernels for 7%

profile of v7, /device:TPU:0, one launch (start us, length us, event | category | flops | bytes accessed | tf_op | source)
XLA Modules:
  0.0 668.8 jit_solution(1795853272878395432)
XLA Ops:
  0.7 0.7 constant_dynamic-slice_fusion.4
  1.5 0.7 fusion.32
  2.2 1.1 convert.20
  3.5 0.8 dynamic_slice.20
  4.4 11.9 %exchange_0.1 = s32[4,8,8,128]{3,2,1,0:T(8,128)S(1)} custom-call(s32[8,128]{1,0:T(8,128)S(1)} %add_bitcast_fusion.refs_0_), custom_call_target="tpu_custom_call" | custom-call | bytes 2703360 | tf_op jit(solution)/shard_map/exchange_0/pallas_call | solution.py:429
  16.3 0.7 convert.21
  17.2 0.7 convert_bitcast_fusion
  18.0 1.0 convert.23
  19.1 1.3 broadcast_in_dim.45
  20.4 4.3 all-to-all-start
  24.8 6.4 convert_element_type.38.refs_3_.refs_1_
  31.3 4.8 select_reduce_fusion
  36.2 3.7 copy-done.2
  39.9 10.4 %gather_rows.1 = bf16[32,256,384]{2,1,0:T(8,128)(2,1)S(1)} custom-call(s32[32,256]{1,0:T(8,128)S(1)} %fusion.12.list_ref, s32[32]{0:T(128)S(1)} %get-tuple-element.259.count_ref, f32[6144,384]{1,0:T(8,128)S(1)} %copy-done.2), custom_call_target="tpu_custom_call" | custom-call | tf_op jit(solution)/shard_map/gather_rows/pallas_call | solution.py:950
  50.3 2.7 copy-done.7
  53.4 1.1 reshape.236.routes_ref
  54.6 0.8 select_reduce_fusion.1
  55.4 0.7 eq.85
  56.0 0.6 iota_add_fusion
  57.2 6.8 %all-to-all-done = bf16[4,96,2176]{2,1,0:T(8,128)(2,1)S(1)} async-done(((bf16[4,96,2176]{2,1,0:T(8,128)(2,1)}), bf16[4,96,2176]{2,1,0:T(8,128)(2,1)S(1)}, u32[]{:S(2)}, u32[]{:S(2)}) %all-to-all-start) | async-done | bytes 1671200 | tf_op jit(solution)/shard_map/all_to_all | solution.py:1307
  64.1 95.6 %exchange_1.1 = (bf16[4,2,2,2,48,2176]{5,4,3,2,1,0:T(8,128)(2,1)}, bf16[4,2,2,2,48,2176]{5,4,3,2,1,0:T(8,128)(2,1)}, bf16[4,256,384]{2,1,0:T(8,128)(2,1)S(1)}, bf16[1536,1536]{1,0:T(8,128)(2,1)S(1)}) custom-call(bf16[4,48,2176]{2,1,0:T(8,128)(2,1)S(1)} %get-tuple-element.262.refs_0_, bf16[4,48,2176]{2,1,0:T(8,128)(2,1)S(1)} %get-tuple-element.261.refs_1_, ...), custom_call_target="tpu_custom_call" | custom-call | bytes 631111680 | tf_op jit(solution)/shard_map/exchange_1/pallas_call | solution.py:429
  159.8 3.2 copy-done.3
  163.0 2.9 copy-done.6
  165.9 5.6 attend.1
  171.5 0.9 copy-done.24
  172.4 0.7 copy-done.26
  173.2 26.2 %exchange_2.1 = (bf16[4,2,2,2,32,1536]{5,4,3,2,1,0:T(8,128)(2,1)S(1)}, bf16[1536,1536]{1,0:T(8,128)(2,1)S(1)}) custom-call(bf16[32,1536]{1,0:T(8,128)(2,1)S(1)} %get-tuple-element.96.refs_0_.c_ref, bf16[6144,384]{1,0:T(8,128)(2,1)S(1)} %bitcast.81, bf16[1536,1536]{1,0:T(8,128)(2,1)S(1)} %get-tuple-element.97.refs_2_), custom_call_target="tpu_custom_call", output_to_operand_aliasing={{1}: (2, {})} | custom-call | bytes 347996160 | tf_op jit(solution)/shard_map/exchange_2/pallas_call | solution.py:429
  199.4 1.7 copy-done.13
  201.1 15.0 %experts_forward.1 = (bf16[1024,1536]{1,0:T(8,128)(2,1)S(1)}, f32[1024,1024]{1,0:T(8,128)}, f32[1024,128]{1,0:T(8,128)S(1)}, bf16[1536,1024]{1,0:T(8,128)(2,1)S(...) custom-call(s32[4]{0:T(128)S(1)} %iota_add_fusion.1.lane_ref, bf16[1024,1536]{1,0:T(8,128)(2,1)} %bitcast.96, ...), custom_call_target="tpu_custom_call" | custom-call | tf_op jit(solution)/shard_map/experts_forward/pallas_call | solution.py:513
  216.1 1.7 copy-done.12
  217.8 54.5 %exchange_3.1 = (bf16[4,2,2,2,32,1536]{5,4,3,2,1,0:T(8,128)(2,1)S(1)}, f32[32,1536]{1,0:T(8,128)S(1)}, bf16[1536,1536]{1,0:T(8,128)(2,1)S(1)}) custom-call(bf16[4,2,2,2,32,1536]{5,4,3,2,1,0:T(8,128)(2,1)S(1)} %bitcast.94, f32[32,1536]{1,0:T(8,128)S(1)} %copy-done.27, ...), custom_call_target="tpu_custom_call", output_to_operand_aliasing={{2}: (4, {})} | custom-call | bytes 417792000 | tf_op jit(solution)/shard_map/exchange_3/pallas_call | solution.py:429
  272.4 5.1 multiply_reduce_fusion
  277.6 3.1 exponential_reduce_fusion
  280.7 11.4 %exchange_5.1 = f32[4,8,8,384]{3,2,1,0:T(8,128)S(1)} custom-call(f32[8,384]{1,0:T(8,128)S(1)} %reshape.240.refs_0_), custom_call_target="tpu_custom_call" | custom-call | bytes 8110080 | tf_op jit(solution)/shard_map/exchange_5/pallas_call | solution.py:429
  293.1 0.6 divide_multiply_fusion
  294.0 4.0 fusion.5
  298.1 5.4 fusion.1.refs_3_.refs_1_
  303.6 5.3 multiply_convert_fusion
  308.9 54.0 %exchange_6.1 = (bf16[4,2,2,2,32,1536]{5,4,3,2,1,0:T(8,128)(2,1)S(1)}, f32[32,1536]{1,0:T(8,128)S(1)}, f32[1,1536]{1,0:T(1,128)S(1)}, bf16[4,1536,384]{2,1,0:T(8,128)(2,1)S(1)}) custom-call(bf16[4,2,2,2,32,1536]{5,4,3,2,1,0:T(8,128)(2,1)S(1)} %bitcast.95, f32[32,1536]{1,0:T(8,128)S(1)} %copy-done.36, f32[8,1536]{1,0:T(8,128)S(1)} %get-tuple-element.101.refs_2_.gains_ref, ...), custom_call_target="tpu_custom_call" | custom-call | bytes 323543040 | tf_op jit(solution)/shard_map/exchange_6/pallas_call | solution.py:429
  362.9 1.7 copy-done.10
  364.6 12.5 %experts_backward.1 = (bf16[1024,1664]{1,0:T(8,128)(2,1)}, bf16[1024,1024]{1,0:T(8,128)(2,1)}) custom-call(s32[4]{0:T(128)S(1)} %iota_add_fusion.1.lane_ref, bf16[1024,1536]{1,0:T(8,128)(2,1)} %bitcast.92, f32[1024,1024]{1,0:T(8,128)} %get-tuple-element.107.mid_ref, f32[1024,128]{1,0:T(8,128)S(1)} %copy-done.30, bf16[1536,1024]{1,0:T(8,128)(2,1)} %copy-done.12, ...), custom_call_target="tpu_custom_call" | custom-call | tf_op jit(solution)/shard_map/experts_backward/pallas_call | solution.py:592
  377.1 2.0 copy-done.9
  379.1 32.3 %exchange_8.1 = (f32[32,1664]{1,0:T(8,128)S(1)}, bf16[4,1536,384]{2,1,0:T(8,128)(2,1)S(1)}) custom-call(bf16[4,2,2,2,32,1664]{5,4,3,2,1,0:T(8,128)(2,1)S(1)} %bitcast.91, bf16[1536,1536]{1,0:T(8,128)(2,1)S(1)} %fusion.1.refs_3_.refs_1_, bf16[4,1536,384]{2,1,0:T(8,128)(2,1)S(1)} %get-tuple-element.112.refs_2_), custom_call_target="tpu_custom_call", output_to_operand_aliasing={{1}: (2, {})} | custom-call | bytes 355532800 | tf_op jit(solution)/shard_map/exchange_8/pallas_call | solution.py:429
  411.5 23.6 %attend_back.1 = (bf16[4,256,384]{2,1,0:T(8,128)(2,1)S(1)}, bf16[1536,2176]{1,0:T(8,128)(2,1)}, bf16[1536,2176]{1,0:T(8,128)(2,1)}) custom-call(s32[1]{0:T(128)S(1)} %bitcast.103, f32[32,1664]{1,0:T(8,128)S(1)} %get-tuple-element.113.back_ref, f32[32,128]{1,0:T(8,128)S(1)} %constant_dynamic-slice_fusion.gates_ref, ...), custom_call_target="tpu_custom_call" | custom-call | tf_op jit(solution)/shard_map/attend_back/pallas_call | solution.py:890
  435.2 0.9 copy-done.21
  436.1 96.6 %exchange_9.1 = (bf16[4,48,2176]{2,1,0:T(8,128)(2,1)}, bf16[4,48,2176]{2,1,0:T(8,128)(2,1)}, bf16[4,2,2,2,256,384]{5,4,3,2,1,0:T(8,128)(2,1)}, bf16[4,1536,384]{2,1,0:T(8,128)(2,1)}) custom-call(bf16[4,2,2,2,48,2176]{5,4,3,2,1,0:T(8,128)(2,1)} %bitcast.111, bf16[4,2,2,2,48,2176]{5,4,3,2,1,0:T(8,128)(2,1)} %bitcast.112, ...), custom_call_target="tpu_custom_call", output_to_operand_aliasing={{3}: (4, {})} | custom-call | bytes 725483520 | tf_op jit(solution)/shard_map/exchange_9/pallas_call | solution.py:429
  532.7 2.7 pad_maximum_fusion
  535.4 4.6 all-to-all-start.1
  540.1 0.7 copy.109.router
  541.6 0.7 copy.110.router_one
  542.3 0.7 copy.111.router_two
  543.7 36.1 %table_moments.1 = (f32[6144,384]{1,0:T(8,128)}, f32[6144,384]{1,0:T(8,128)}, f32[6144,384]{1,0:T(8,128)}, f32[8,128]{1,0:T(8,128)S(1)}) custom-call(s32[32,256]{1,0:T(8,128)S(1)} %fusion.12.list_ref, s32[32]{0:T(128)S(1)} %get-tuple-element.259.count_ref, f32[2]{0:T(128)S(1)} %pad_maximum_fusion.4.scale_ref, bf16[32,256,384]{2,1,0:T(8,128)(2,1)} %bitcast.113, ...), custom_call_target="tpu_custom_call" | custom-call | tf_op jit(solution)/shard_map/table_moments/pallas_call | solution.py:1051
  579.9 3.5 fusion.20.down_grad
  583.4 5.4 fusion.19.grad_ref
  588.8 4.4 small_moments.1
  593.2 1.3 add.98.other_norms
  594.5 27.9 %expert_moments.1 = (f32[12288,128]{1,0:T(8,128)}, f32[12288,128]{1,0:T(8,128)}, f32[12288,128]{1,0:T(8,128)}, f32[512,1536]{1,0:T(8,128)}, f32[512,1536]{1,0:T(...) custom-call(f32[2]{0:T(128)} %copy-done.45, f32[8,128]{1,0:T(8,128)} %add.98.other_norms, f32[1536,1024]{1,0:T(8,128)} %fusion.19.grad_ref, ...), custom_call_target="tpu_custom_call" | custom-call | tf_op jit(solution)/shard_map/expert_moments/pallas_call | solution.py:666
  622.4 0.7 copy-done.46
  623.1 14.2 %exchange_10.1 = f32[4,8,8,128]{3,2,1,0:T(8,128)S(1)} custom-call(f32[8,128]{1,0:T(8,128)S(1)} %copy-done.46), custom_call_target="tpu_custom_call" | custom-call | bytes 2703360 | tf_op jit(solution)/shard_map/exchange_10/pallas_call | solution.py:429
  638.0 0.7 copy.116
  640.0 0.7 copy.113
  640.7 0.7 copy.114
  641.4 0.7 copy.115
  642.7 24.7 %finish.1 = (f32[6144,384]{1,0:T(8,128)}, f32[12288,128]{1,0:T(8,128)}, f32[512,1536]{1,0:T(8,128)}, f32[48,2560]{1,0:T(8,128)}, f32[48,1536]{1,0:T(8,128)}) custom-call(f32[32,8,128]{2,1,0:T(8,128)} %bitcast.98, f32[6144,384]{1,0:T(8,128)} %refs_0_.1, f32[6144,384]{1,0:T(8,128)} %get-tuple-element.135.refs_1_, f32[12288,128]{1,0:T(8,128)} %bitcast.108, ...), custom_call_target="tpu_custom_call" | custom-call | tf_op jit(solution)/shard_map/finish/pallas_call | solution.py:1159
  (188 shorter events, 5.1 us)
Async XLA Ops:
  20.4 43.6 %all-to-all-start = ((bf16[4,96,2176]{2,1,0:T(8,128)(2,1)}), bf16[4,96,2176]{2,1,0:T(8,128)(2,1)S(1)}, u32[]{:S(2)}, u32[]{:S(2)}) async-start(bf16[4,96,2176]{2,1,0:T(8,128)(2,1)} %broadcast_in_dim.45), calls=%async_computation | async-start | bytes 3342336 | tf_op jit(solution)/shard_map/all_to_all | solution.py:1307
  36.2 3.7 copy-start.2
  39.8 16.8 %copy-start.65 = (s32[16,2]{0,1:T(2,128)S(1)}, s32[16,2]{0,1:T(2,128)}, u32[]{:S(2)}) copy-start(s32[16,2]{0,1:T(2,128)} %param.29) | copy-start | bytes 388
  56.7 103.1 %copy-start.37 = (f32[32,128]{1,0:T(8,128)}, f32[32,128]{1,0:T(8,128)S(1)}, u32[]{:S(2)}) copy-start(f32[32,128]{1,0:T(8,128)S(1)} %get-tuple-element.281.sin_rows) | copy-start | bytes 49156
  56.7 103.1 %copy-start.39 = (f32[32,128]{1,0:T(8,128)}, f32[32,128]{1,0:T(8,128)S(1)}, u32[]{:S(2)}) copy-start(f32[32,128]{1,0:T(8,128)S(1)} %get-tuple-element.282.cos_rows) | copy-start | bytes 49156
  64.1 109.0 %slice-start = ((s8[4718592]{0:T(1024)(128)(4,1)}), s8[524288]{0:T(1024)(128)(4,1)S(1)}, s32[]{:S(2)}) async-start(s8[4718592]{0:T(1024)(128)(4,1)} %bitcast.80), calls=%async_computation.2 | async-start | bytes 1048576
  159.8 11.8 %copy-start.15 = (bf16[4,256,384]{2,1,0:T(8,128)(2,1)}, bf16[4,256,384]{2,1,0:T(8,128)(2,1)S(1)}, u32[]{:S(2)}) copy-start(bf16[4,256,384]{2,1,0:T(8,128)(2,1)S(1)} %get-tuple-element.93.picked_ref) | copy-start | bytes 2359300
  159.8 3.2 copy-start.3
  163.0 2.9 copy-start.6
  165.9 7.3 %slice-start.1 = ((s8[4718592]{0:T(1024)(128)(4,1)}), s8[4194304]{0:T(1024)(128)(4,1)S(1)}, s32[]{:S(2)}) async-start(s8[4718592]{0:T(1024)(128)(4,1)} %bitcast.80), calls=%async_computation.3 | async-start | bytes 8388608
  173.1 26.3 %copy-start.22 = (f32[8,96,256]{2,1,0:T(8,128)}, f32[8,96,256]{2,1,0:T(8,128)S(1)}, u32[]{:S(2)}) copy-start(f32[8,96,256]{2,1,0:T(8,128)S(1)} %get-tuple-element.116.probs_ref) | copy-start | bytes 2359300
  173.1 26.3 %copy-start.31 = (bf16[256,512]{1,0:T(8,128)(2,1)}, bf16[256,512]{1,0:T(8,128)(2,1)S(1)}, u32[]{:S(2)}) copy-start(bf16[256,512]{1,0:T(8,128)(2,1)S(1)} %get-tuple-element.118.key_ref) | copy-start | bytes 786436
  173.1 26.3 %copy-start.33 = (bf16[256,512]{1,0:T(8,128)(2,1)}, bf16[256,512]{1,0:T(8,128)(2,1)S(1)}, u32[]{:S(2)}) copy-start(bf16[256,512]{1,0:T(8,128)(2,1)S(1)} %get-tuple-element.119.value_ref) | copy-start | bytes 786436
  173.1 26.3 %copy-start.41 = (bf16[32,1536]{1,0:T(8,128)(2,1)}, bf16[32,1536]{1,0:T(8,128)(2,1)S(1)}, u32[]{:S(2)}) copy-start(bf16[32,1536]{1,0:T(8,128)(2,1)S(1)} %get-tuple-element.117.query_ref) | copy-start | bytes 294916
  173.1 26.3 %copy-start.43 = (bf16[32,1536]{1,0:T(8,128)(2,1)}, bf16[32,1536]{1,0:T(8,128)(2,1)S(1)}, u32[]{:S(2)}) copy-start(bf16[32,1536]{1,0:T(8,128)(2,1)S(1)} %get-tuple-element.120.mixed_ref) | copy-start | bytes 294916
  173.1 27.9 %copy-start.17 = (s32[1024,8]{1,0:T(8,128)S(1)}, s32[1024,8]{1,0:T(8,128)}, u32[]{:S(2)}) copy-start(s32[1024,8]{1,0:T(8,128)} %reshape.236.routes_ref) | copy-start | bytes 98308
  201.1 16.7 %copy-start.27 = (f32[32,1536]{1,0:T(8,128)S(1)}, f32[32,1536]{1,0:T(8,128)}, u32[]{:S(2)}) copy-start(f32[32,1536]{1,0:T(8,128)} %copy-done.26) | copy-start | bytes 589828
  217.8 54.5 %copy-start.18 = (bf16[512,1536]{1,0:T(8,128)(2,1)}, bf16[512,1536]{1,0:T(8,128)(2,1)S(1)}, u32[]{:S(2)}) copy-start(bf16[512,1536]{1,0:T(8,128)(2,1)S(1)} %get-tuple-element.110.down_ref) | copy-start | bytes 4718596
  217.8 54.5 %copy-start.29 = (f32[1024,128]{1,0:T(8,128)}, f32[1024,128]{1,0:T(8,128)S(1)}, u32[]{:S(2)}) copy-start(f32[1024,128]{1,0:T(8,128)S(1)} %get-tuple-element.108.gates_ref) | copy-start | bytes 1572868
  217.8 54.5 %copy-start.49 = (bf16[1024,512]{1,0:T(8,128)(2,1)}, bf16[1024,512]{1,0:T(8,128)(2,1)S(1)}, u32[]{:S(2)}) copy-start(bf16[1024,512]{1,0:T(8,128)(2,1)S(1)} %get-tuple-element.133) | copy-start | bytes 3145732
  272.3 5.2 copy-start.8
  272.3 5.2 copy-start.35
  272.3 5.2 copy-start.47
  272.3 5.2 copy-start.53
  272.3 5.2 copy-start.55
  277.5 3.1 copy-start.51
  277.5 15.4 %copy-start.67 = (f32[32]{0:T(128)S(1)}, f32[32]{0:T(128)}, u32[]{:S(2)}) copy-start(f32[32]{0:T(128)} %param.30) | copy-start | bytes 388
  277.6 15.4 %copy-start.62 = (s32[16]{0:T(128)S(1)}, s32[16]{0:T(128)}, u32[]{:S(2)}) copy-start(s32[16]{0:T(128)} %get-tuple-element.272) | copy-start | bytes 196
  277.6 15.4 %copy-start.63 = (s32[16]{0:T(128)S(1)}, s32[16]{0:T(128)}, u32[]{:S(2)}) copy-start(s32[16]{0:T(128)} %get-tuple-element.273) | copy-start | bytes 196
  294.0 4.0 copy-start.48
  294.0 9.5 %slice-start.2 = ((s8[4718592]{0:T(1024)(128)(4,1)}), s8[4194304]{0:T(1024)(128)(4,1)S(1)}, s32[]{:S(2)}) async-start(s8[4718592]{0:T(1024)(128)(4,1)} %bitcast.89), calls=%async_computation.4 | async-start | bytes 8388608
  298.1 5.5 slice-start.3
  303.5 73.6 %copy-start.5 = (bf16[1536,1536]{1,0:T(8,128)(2,1)}, bf16[1536,1536]{1,0:T(8,128)(2,1)S(1)}, u32[]{:S(2)}) copy-start(bf16[1536,1536]{1,0:T(8,128)(2,1)S(1)} %fusion.1.refs_3_.refs_1_) | copy-start | bytes 14155780
  303.5 5.3 copy-start.30
  303.6 5.3 copy-start.36
  308.8 55.7 %copy-start.19 = (bf16[512,1536]{1,0:T(8,128)(2,1)S(1)}, bf16[512,1536]{1,0:T(8,128)(2,1)}, u32[]{:S(2)}) copy-start(bf16[512,1536]{1,0:T(8,128)(2,1)} %copy-done.18) | copy-start | bytes 4718596
  379.1 32.4 %copy-start.16 = (bf16[4,256,384]{2,1,0:T(8,128)(2,1)S(1)}, bf16[4,256,384]{2,1,0:T(8,128)(2,1)}, u32[]{:S(2)}) copy-start(bf16[4,256,384]{2,1,0:T(8,128)(2,1)} %copy-done.15) | copy-start | bytes 2359300
  379.1 32.4 %copy-start.23 = (f32[8,96,256]{2,1,0:T(8,128)S(1)}, f32[8,96,256]{2,1,0:T(8,128)}, u32[]{:S(2)}) copy-start(f32[8,96,256]{2,1,0:T(8,128)} %copy-done.22) | copy-start | bytes 2359300
  379.1 32.4 %copy-start.25 = (bf16[256,1536]{1,0:T(8,128)(2,1)S(1)}, bf16[256,1536]{1,0:T(8,128)(2,1)}, u32[]{:S(2)}) copy-start(bf16[256,1536]{1,0:T(8,128)(2,1)} %copy-done.24) | copy-start | bytes 2359300
  379.1 32.4 %copy-start.28 = (f32[32,1536]{1,0:T(8,128)S(1)}, f32[32,1536]{1,0:T(8,128)}, u32[]{:S(2)}) copy-start(f32[32,1536]{1,0:T(8,128)} %copy-done.26) | copy-start | bytes 589828
  379.1 32.4 %copy-start.32 = (bf16[256,512]{1,0:T(8,128)(2,1)S(1)}, bf16[256,512]{1,0:T(8,128)(2,1)}, u32[]{:S(2)}) copy-start(bf16[256,512]{1,0:T(8,128)(2,1)} %copy-done.31) | copy-start | bytes 786436
  379.1 32.4 %copy-start.34 = (bf16[256,512]{1,0:T(8,128)(2,1)S(1)}, bf16[256,512]{1,0:T(8,128)(2,1)}, u32[]{:S(2)}) copy-start(bf16[256,512]{1,0:T(8,128)(2,1)} %copy-done.33) | copy-start | bytes 786436
  379.1 32.4 %copy-start.38 = (f32[32,128]{1,0:T(8,128)S(1)}, f32[32,128]{1,0:T(8,128)}, u32[]{:S(2)}) copy-start(f32[32,128]{1,0:T(8,128)} %copy-done.37) | copy-start | bytes 49156
  379.1 32.4 %copy-start.40 = (f32[32,128]{1,0:T(8,128)S(1)}, f32[32,128]{1,0:T(8,128)}, u32[]{:S(2)}) copy-start(f32[32,128]{1,0:T(8,128)} %copy-done.39) | copy-start | bytes 49156
  379.1 32.4 %copy-start.42 = (bf16[32,1536]{1,0:T(8,128)(2,1)S(1)}, bf16[32,1536]{1,0:T(8,128)(2,1)}, u32[]{:S(2)}) copy-start(bf16[32,1536]{1,0:T(8,128)(2,1)} %copy-done.41) | copy-start | bytes 294916
  379.1 32.4 %copy-start.44 = (bf16[32,1536]{1,0:T(8,128)(2,1)S(1)}, bf16[32,1536]{1,0:T(8,128)(2,1)}, u32[]{:S(2)}) copy-start(bf16[32,1536]{1,0:T(8,128)(2,1)} %copy-done.43) | copy-start | bytes 294916
  411.4 23.7 %copy-start.4 = (bf16[4,1536,384]{2,1,0:T(8,128)(2,1)}, bf16[4,1536,384]{2,1,0:T(8,128)(2,1)S(1)}, u32[]{:S(2)}) copy-start(bf16[4,1536,384]{2,1,0:T(8,128)(2,1)S(1)} %get-tuple-element.125.refs_4_) | copy-start | bytes 14155780
  532.7 7.3 %copy-start.54 = (f32[48,32]{0,1:T(8,128)S(1)}, f32[48,32]{0,1:T(8,128)}, u32[]{:S(2)}) copy-start(f32[48,32]{0,1:T(8,128)} %param.42) | copy-start | bytes 18436
  532.7 8.8 %copy-start.60 = (f32[48,32]{0,1:T(8,128)S(1)}, f32[48,32]{0,1:T(8,128)}, u32[]{:S(2)}) copy-start(f32[48,32]{0,1:T(8,128)} %param.43) | copy-start | bytes 18436
  532.7 9.5 %copy-start.61 = (f32[48,32]{0,1:T(8,128)S(1)}, f32[48,32]{0,1:T(8,128)}, u32[]{:S(2)}) copy-start(f32[48,32]{0,1:T(8,128)} %param.44) | copy-start | bytes 18436
  535.4 53.4 %all-to-all-start.1 = ((bf16[4,96,2176]{2,1,0:T(8,128)(2,1)}), bf16[4,96,2176]{2,1,0:T(8,128)(2,1)}, u32[]{:S(2)}, u32[]{:S(2)}) async-start(bf16[4,96,2176]{2,1,0:T(8,128)(2,1)} %pad_maximum_fusion), calls=%async_computation.1 | async-start | bytes 3342336 | tf_op jit(solution)/shard_map/all_to_all | solution.py:1434
  543.0 36.8 %copy-start.45 = (f32[2]{0:T(128)}, f32[2]{0:T(128)S(1)}, u32[]{:S(2)}) copy-start(f32[2]{0:T(128)S(1)} %pad_maximum_fusion.4.scale_ref) | copy-start | bytes 28
  543.7 36.2 %copy-start.11 = (bf16[4,2,2,2,32,1536]{5,4,3,2,1,0:T(8,128)(2,1)S(1)}, bf16[4,2,2,2,32,1536]{5,4,3,2,1,0:T(8,128)(2,1)}, u32[]{:S(2)}) copy-start(bf16[4,2,2,2,32,1536]{5,4,3,2,1,0:T(8,128)(2,1)} %copy-done.10) | copy-start | bytes 9437188
  543.7 36.2 %copy-start.50 = (bf16[1024,512]{1,0:T(8,128)(2,1)S(1)}, bf16[1024,512]{1,0:T(8,128)(2,1)}, u32[]{:S(2)}) copy-start(bf16[1024,512]{1,0:T(8,128)(2,1)} %copy-done.49) | copy-start | bytes 3145732
  579.9 3.5 copy-start.14
  579.9 3.5 copy-start.66
  594.5 45.5 %copy-start.52 = (f32[48,32]{1,0:T(8,128)S(1)}, f32[48,32]{1,0:T(8,128)}, u32[]{:S(2)}) copy-start(f32[48,32]{1,0:T(8,128)} %copy.109.router) | copy-start | bytes 18436
  594.5 45.5 %copy-start.58 = (f32[48,32]{1,0:T(8,128)S(1)}, f32[48,32]{1,0:T(8,128)}, u32[]{:S(2)}) copy-start(f32[48,32]{1,0:T(8,128)} %get-tuple-element.149) | copy-start | bytes 18436
  594.5 46.2 %copy-start.57 = (f32[48,32]{1,0:T(8,128)S(1)}, f32[48,32]{1,0:T(8,128)}, u32[]{:S(2)}) copy-start(f32[48,32]{1,0:T(8,128)} %get-tuple-element.241) | copy-start | bytes 18436
  594.5 46.9 %copy-start.56 = (f32[48,32]{1,0:T(8,128)S(1)}, f32[48,32]{1,0:T(8,128)}, u32[]{:S(2)}) copy-start(f32[48,32]{1,0:T(8,128)} %get-tuple-element.242) | copy-start | bytes 18436
  594.5 47.6 %copy-start.59 = (f32[3,48]{1,0:T(4,128)S(1)}, f32[3,48]{1,0:T(4,128)}, u32[]{:S(2)}) copy-start(f32[3,48]{1,0:T(4,128)} %gains.1) | copy-start | bytes 1732
  594.5 47.6 %copy-start.64 = (f32[3,48]{1,0:T(4,128)S(1)}, f32[3,48]{1,0:T(4,128)}, u32[]{:S(2)}) copy-start(f32[3,48]{1,0:T(4,128)} %get-tuple-element.152) | copy-start | bytes 1732
  637.3 5.4 copy-start.20
  642.7 24.7 %copy-start.1 = (s32[256,8]{0,1:T(8,128)S(1)}, s32[256,8]{0,1:T(8,128)}, u32[]{:S(2)}) copy-start(s32[256,8]{0,1:T(8,128)} %param.31) | copy-start | bytes 24580
  (10 other events, 15.4 us)

commit v8 on v7

--- a/solution.py
+++ b/solution.py
@@ -158,20 +158,27 @@
     flat = False
     scratch = ()
 
-    def __init__(self, xs, groups, planes, side, exchange=False, prior=False):
+    def __init__(self, xs, groups, planes, side, exchange=False, prior=None):
         self.planes, self.side, self.inputs, self.groups = planes, side, xs, groups
         self.exchange, self.prior = exchange, prior
         grid = (planes, side, side, 2)
-        self.outputs = [jax.ShapeDtypeStruct(grid + x.shape[-2:], x.dtype) for x in xs]
+        shapes = [x.shape[-2:] for x in xs]
+        if prior:
+            shapes = [xs[0].shape[-2:-1] + (width,) for width in prior]
+        self.outputs = [jax.ShapeDtypeStruct(grid + shape, xs[0].dtype) for shape in shapes]
         self.copies = sum(map(len, groups)) * (planes - 1 + 2 * (side - 1) + 1)
 
     def steps(self, spot, mail, *refs):
         xs, outs = refs[: len(self.inputs)], refs[len(self.inputs) :]
         z, a, b, core = spot.z, spot.a, spot.b, spot.core
-        for x, out in zip(xs, outs):
-            if self.prior:
-                out[:, a, b, core] = x[...]
-            else:
+        if self.prior:
+            low = 0
+            for width, out in zip(self.prior, outs):
+                out[:, a, b, core] = xs[0][:, :, low : low + width]
+                low += width
+            xs = [None] * len(outs)
+        else:
+            for x, out in zip(xs, outs):
                 out[z, a, b, core] = x[z] if self.exchange else x[...]
 
         def stage(step, key, cut):
@@ -218,6 +225,9 @@
             else jax.ShapeDtypeStruct(x.shape[-2:], f32)
             for x in xs
         ]
+        if partial:
+            shape = (planes, xs[0].shape[-2], sum(x.shape[-1] for x in xs))
+            self.outputs = [jax.ShapeDtypeStruct(shape, xs[0].dtype)]
         self.scratch = []
         for i, rows, columns, _ in [cut for group in groups for cut in group]:
             block = (rows.stop - rows.start, columns.stop - columns.start)
@@ -236,7 +246,12 @@
 
     def steps(self, spot, mail, *refs):
         planes, side, number = self.planes, self.side, len(self.inputs)
-        xs, outs, rest = refs[:number], refs[number : 2 * number], refs[2 * number :]
+        made = number + len(self.outputs)
+        xs, outs, rest = refs[:number], refs[number:made], refs[made:]
+        lows = [0] * number
+        if self.partial:
+            outs = [outs[0]] * number
+            lows = [sum(x.shape[-1] for x in self.inputs[:n]) for n in range(number)]
         each = 5 if self.exchange else 6
         order = [(t, n) for t, group in enumerate(self.groups) for n in range(len(group))]
         held = {key: rest[each * p : each * (p + 1)] for p, key in enumerate(order)}
@@ -286,7 +301,8 @@
                     for k in range(side - 1):
                         total += hop_three[k, iz].astype(f32)
                     if self.partial:
-                        out[iz, rows, columns] = total.astype(out.dtype)
+                        place = slice(lows[i] + columns.start, lows[i] + columns.stop)
+                        out[iz, rows, place] = total.astype(out.dtype)
                     else:
                         three[iz] = total.astype(three.dtype)
                     return carry
@@ -586,7 +602,7 @@
 def experts_backward(lanes, grad, mid, gates, cat, down):
     number = lanes.shape[0]
     total = grad.shape[0]
-    block = min(total, BLOCK)
+    block = CHUNK
     row = lambda r, *_: (r, 0)
     still = lambda r, *_: (0, 0)
     return pl.pallas_call(
@@ -611,14 +627,14 @@
             jax.ShapeDtypeStruct((total, D + 128), bf16),
             jax.ShapeDtypeStruct(mid.shape, bf16),
         ],
-        compiler_params=pltpu.CompilerParams(vmem_limit_bytes=50 << 20),
+        compiler_params=pltpu.CompilerParams(vmem_limit_bytes=36 << 20),
         name="experts_backward",
     )(lanes, grad, mid, gates, cat, down)
 
 
 def moments_kernel(
     scale_ref, other_norms, grad_ref, w_ref, first_ref, second_ref, down_grad, down_w, down_first, down_second,
-    new_first, new_second, updates, new_down_first, new_down_second, down_updates, norms, sums, down_sums,
+    new_first, new_second, updates, new_down_first, new_down_second, down_updates, norms, sums, down_sums, turned,
 ):
     units = w_ref.shape[1]
     part = w_ref.shape[0] // 2
@@ -631,15 +647,14 @@
         down_sums[...] = jnp.zeros_like(down_sums)
 
     for j in range(2):
-        here = pl.ds(j, part, stride=2)
-        grad = grad_ref[:, j * units : (j + 1) * units]
-        weight = w_ref[here, :]
-        one, two, update = lamb_parts(weight, first_ref[here, :], second_ref[here, :], grad, scales)
-        new_first[here, :] = one
-        new_second[here, :] = two
-        updates[here, :] = update
-        sums[0] += fold(weight * weight)
-        sums[1] += fold(update * update)
+        turned[pl.ds(j, part, stride=2), :] = grad_ref[:, j * units : (j + 1) * units]
+    weight = w_ref[...]
+    one, two, update = lamb_parts(weight, first_ref[...], second_ref[...], turned[...], scales)
+    new_first[...] = one
+    new_second[...] = two
+    updates[...] = update
+    sums[0] += fold(weight * weight)
+    sums[1] += fold(update * update)
     weight = down_w[...]
     one, two, update = lamb_parts(weight, down_first[...], down_second[...], down_grad[...], scales)
     new_down_first[...] = one
@@ -672,7 +687,11 @@
             + [row] * 3
             + [down_row] * 4,
             out_specs=[row] * 3 + [down_row] * 3 + [cells],
-            scratch_shapes=[pltpu.VMEM((2, 8, units), f32), pltpu.VMEM((2, 8, D), f32)],
+            scratch_shapes=[
+                pltpu.VMEM((2, 8, units), f32),
+                pltpu.VMEM((2, 8, D), f32),
+                pltpu.VMEM((2 * D // parts, units), f32),
+            ],
         ),
         out_shape=[jax.ShapeDtypeStruct(weight.shape, f32)] * 3
         + [jax.ShapeDtypeStruct(down.shape, f32)] * 3
@@ -685,6 +704,7 @@
 HEAD_COLS = QUERY_HEADS * HEAD_WIDTH
 KEY_COLS = KEY_VALUE_HEADS * HEAD_WIDTH
 PACK = HEAD_COLS + KEY_COLS + 128
+PACK_TWO = KEY_COLS + D
 ROOT = HEAD_WIDTH ** (-0.5)
 
 
@@ -873,7 +893,6 @@
     grad_pack_ref[:, KEY_COLS : KEY_COLS + D] = dot(
         mixed_ref[...].astype(f32).T.astype(bf16), branch
     ).astype(bf16)
-    grad_pack_ref[:, KEY_COLS + D :] = jnp.zeros((D, PACK - KEY_COLS - D), bf16)
     left = jnp.concatenate(
         [c_ref[...].astype(f32), gain_one, gain_two, gain_three_ref[...], jnp.zeros((5, D), f32)],
         axis=0,
@@ -894,7 +913,7 @@
         out_shape=[
             jax.ShapeDtypeStruct(picked.shape, bf16),
             jax.ShapeDtypeStruct((D, PACK), bf16),
-            jax.ShapeDtypeStruct((D, PACK), bf16),
+            jax.ShapeDtypeStruct((D, PACK_TWO), bf16),
         ],
         scratch_shapes=[pltpu.VMEM((SEQUENCE_TOKENS, D), f32)],
         compiler_params=pltpu.CompilerParams(vmem_limit_bytes=44 << 20),
@@ -929,7 +948,10 @@
     return jnp.where(place[None, :] < count[:, None], entry, empty), count
 
 
-def gather_kernel(list_ref, count_ref, table_ref, out_ref, rows_ref):
+def gather_kernel(list_ref, count_ref, table_ref, out_ref, table_out, rows_ref):
+    part = table_out.shape[0]
+    here = pl.ds(pl.multiple_of(pl.program_id(0) * part, 16), part)
+    table_out[...] = table_ref[here, :].astype(bf16)
     for n in range(TOGETHER):
         b = pl.program_id(0) * TOGETHER + n
         rows_ref[n] = jnp.zeros(rows_ref.shape[1:], f32)
@@ -953,16 +975,22 @@
             num_scalar_prefetch=2,
             grid=(blocks // TOGETHER,),
             in_specs=[pl.BlockSpec((rows, columns), lambda b, *_: (0, 0))],
-            out_specs=pl.BlockSpec((TOGETHER, SEQUENCE_TOKENS, columns), lambda b, *_: (b, 0, 0)),
+            out_specs=[
+                pl.BlockSpec((TOGETHER, SEQUENCE_TOKENS, columns), lambda b, *_: (b, 0, 0)),
+                pl.BlockSpec((rows * TOGETHER // blocks, columns), lambda b, *_: (b, 0)),
+            ],
             scratch_shapes=[pltpu.VMEM((TOGETHER, SEQUENCE_TOKENS + 8, columns), f32)],
         ),
-        out_shape=jax.ShapeDtypeStruct((blocks, SEQUENCE_TOKENS, columns), bf16),
-        compiler_params=pltpu.CompilerParams(vmem_limit_bytes=22 << 20),
+        out_shape=[
+            jax.ShapeDtypeStruct((blocks, SEQUENCE_TOKENS, columns), bf16),
+            jax.ShapeDtypeStruct((rows, columns), bf16),
+        ],
+        compiler_params=pltpu.CompilerParams(vmem_limit_bytes=26 << 20),
         name="gather_rows",
     )(lists, counts, table)
 
 
-TABLE_PARTS = 16
+TABLE_PARTS = 8
 
 
 def norm_cells(row, weight_sum, update_sum):
@@ -1070,7 +1098,7 @@
         ),
         out_shape=[jax.ShapeDtypeStruct((rows, columns), f32)] * 3
         + [jax.ShapeDtypeStruct((8, 128), f32)],
-        compiler_params=pltpu.CompilerParams(vmem_limit_bytes=52 << 20),
+        compiler_params=pltpu.CompilerParams(vmem_limit_bytes=58 << 20),
         name="table_moments",
     )(lists, counts, scales, grads, head, weight, first, second)
 
@@ -1081,12 +1109,10 @@
 ):
     scales = (scale_ref[0], scale_ref[1])
     planes = grad_ref.shape[0]
-    packs = []
-    for n in range(2):
-        pack = grad_ref[0, n].astype(f32)
-        for z in range(1, planes):
-            pack += grad_ref[z, n].astype(f32)
-        packs.append(pack)
+    total = grad_ref[0].astype(f32)
+    for z in range(1, planes):
+        total += grad_ref[z].astype(f32)
+    packs = (total[:, :PACK], total[:, PACK:])
     wide = HEAD_COLS + KEY_COLS
     pick = lax.broadcasted_iota(jnp.int32, (8, 128), 0) + EXPERTS
     pick = (pick == lax.broadcasted_iota(jnp.int32, (8, 128), 1)).astype(f32)
@@ -1126,7 +1152,7 @@
     )(scales, sums, *state)
 
 
-FINISH_PARTS = 16
+FINISH_PARTS = 8
 
 
 def finish_kernel(norms_ref, *refs):
@@ -1232,8 +1258,17 @@
         return Gather([rows], split(0, COMP, rows.shape[1], 2, 2), planes, side)
 
     def reduce_part(rows, cuts):
-        rows = rows.reshape(grid + (COMP, rows.shape[1]))
-        return Reduce([rows], split(0, COMP, rows.shape[-1], 2, cuts), planes, side)
+        width = rows.shape[1]
+        rows = rows.reshape(grid + (COMP, width))
+        edges = [width * n // (128 * cuts) * 128 for n in range(cuts + 1)]
+        groups = [
+            [
+                (0, slice(i * COMP // 2, (i + 1) * COMP // 2), slice(low, high), i == 0)
+                for i in range(2)
+            ]
+            for low, high in zip(edges, edges[1:])
+        ]
+        return Reduce([rows], groups, planes, side)
 
     def chain(rows, extra, extra_out, middle, beside, ident):
         gather = gather_part(jax.ShapeDtypeStruct((COMP, D), bf16))
@@ -1245,12 +1280,12 @@
         return communicate([Tiny(block, planes, side)], ident)[0].reshape((devices,) + block.shape)
 
     weight_rows = qkv_weight.shape[0]
-    weight_cols = PACK
     cuts = 3 if weight_rows % 48 == 0 else 1
+    widths = (PACK, PACK_TWO)
     weight_groups = [
         [
-            (i, slice(n * (weight_rows // cuts), (n + 1) * (weight_rows // cuts)), slice(0, weight_cols), i == 0)
-            for i in range(2)
+            (i, slice(n * (weight_rows // cuts), (n + 1) * (weight_rows // cuts)), slice(0, width), i == 0)
+            for i, width in enumerate(widths)
         ]
         for n in range(cuts)
     ]
@@ -1281,28 +1316,19 @@
     ).reshape(-1)
 
     lists, counts = row_lists(tokens_all, vocab_base, vocab_rows)
-    picked = gather_rows(lists, counts, embed_table).reshape(grid + (SEQUENCE_TOKENS, columns))
-    packs = [
-        jnp.concatenate(
-            [
-                qkv_weight[:, : head_cols + key_cols],
-                router_weight,
-                norm_gains.T,
-                jnp.zeros((weight_rows, 128 - EXPERTS - 3), f32),
-            ],
-            axis=1,
-        ).astype(bf16),
-        jnp.concatenate(
-            [
-                qkv_weight[:, head_cols + key_cols :],
-                out_weight,
-                jnp.zeros((weight_rows, 128), f32),
-            ],
-            axis=1,
-        ).astype(bf16),
-    ]
-    table_b = embed_table.astype(bf16)
-    packs = jnp.concatenate(packs, axis=0)
+    picked, table_b = gather_rows(lists, counts, embed_table)
+    picked = picked.reshape(grid + (SEQUENCE_TOKENS, columns))
+    packs = jnp.concatenate(
+        [
+            qkv_weight[:, : head_cols + key_cols],
+            router_weight,
+            norm_gains.T,
+            jnp.zeros((weight_rows, 128 - EXPERTS - 3), f32),
+            qkv_weight[:, head_cols + key_cols :],
+            out_weight,
+        ],
+        axis=1,
+    ).astype(bf16)
     packs, sheets = lax.optimization_barrier((packs, sheets))
     packs = lax.all_to_all(
         jnp.broadcast_to(packs[None], (planes,) + packs.shape),
@@ -1311,23 +1337,16 @@
         concat_axis=0,
         tiled=True,
     )
-    table_b = embed_table.astype(bf16)
     first_pack, second_pack, picked, table_own = send(
         [
-            Gather(
-                [packs[:, :weight_rows], packs[:, weight_rows:]],
-                weight_groups,
-                planes,
-                side,
-                prior=True,
-            ),
+            Gather([packs], weight_groups, planes, side, prior=widths),
             Reduce([picked], embed_groups, planes, side, exchange=True),
             swap(table_b, (0, 16, 0)),
         ],
         1,
     )
-    first_pack = first_pack.reshape(D, weight_cols)
-    second_pack = second_pack.reshape(D, weight_cols)
+    first_pack = first_pack.reshape(D, PACK)
+    second_pack = second_pack.reshape(D, PACK_TWO)
 
     start_at = start.reshape(1)
     tables = rotary_tables()
@@ -1398,7 +1417,7 @@
 
     back, mid_grad = experts_backward(lanes, grad_all, mid, gates, in_cat, down_b)
     back, head_back = communicate(
-        [reduce_part(back, 1), swap(head_grad, (6, 3, 0), back=True, held=head_back)], 8
+        [reduce_part(back, 2), swap(head_grad, (6, 3, 0), back=True, held=head_back)], 8
     )
 
     grad_embedded, *grad_packs = attend_back(
@@ -1421,9 +1440,9 @@
         second_pack,
         *tables,
     )
-    grad_packs = [pack.reshape(grid + (weight_rows, weight_cols)) for pack in grad_packs]
+    grad_packs = [pack.reshape(grid + (weight_rows, pack.shape[1])) for pack in grad_packs]
     wide = head_cols + key_cols
-    first_grad, second_grad, sent, head_back = send(
+    plane_sums, sent, head_back = send(
         [
             Reduce(grad_packs, weight_groups, planes, side, partial=True),
             Gather([grad_embedded], embed_groups, planes, side, exchange=True),
@@ -1432,12 +1451,8 @@
         9,
     )
     plane_sums = lax.all_to_all(
-        jnp.concatenate([first_grad, second_grad], axis=1),
-        "expert",
-        split_axis=0,
-        concat_axis=0,
-        tiled=True,
-    ).reshape(planes, 2, weight_rows, weight_cols)
+        plane_sums, "expert", split_axis=0, concat_axis=0, tiled=True
+    )
 
     step_value = step_count.astype(f32)
     scales = jnp.stack([1.0 / (1.0 - RATE_ONE**step_value), 1.0 / (1.0 - RATE_TWO**step_value)])

time: 676 us -> 664 us (0.982)
  other arithmetic: 29.9 us -> 20.7 us
  Pallas kernels: 557 us -> 548 us
    pallas_call x9, Pallas kernels: 397 us -> 387 us  [communicate(): pl.pallas_call(kernel, out_shape=[x for p in parts for x in p.outputs], i...]
    unnamed x153 -> x155, local copies, waits for them, and re-layouts: 27.6 us -> 34.1 us
  transfers between devices with their start and end apart: 2 -> 2, of which waited for: 1 -> 1; matrix products, arithmetic and copies ran while one was open for 4% -> 3% of each run, Pallas kernels for 7% -> 7%
where the time goes in v8:
time: 664 us; the launch traced here: 660 us
  Pallas kernels  548 us (83%)
  local copies, waits for them, and re-layouts  40.2 us (6%)
  matrix products  24.9 us (4%)
  other arithmetic  20.7 us (3%)
  waiting for transfers between devices  11.2 us (2%)
  starting transfers between devices  9.3 us (1%)
    pallas_call x9, Pallas kernels, communicate(): pl.pallas_call(kernel, out_shape=[x for p in parts for x in p.outputs], i...  387 us
    pallas_call x1, Pallas kernels, table_moments(): pl.pallas_call(table_kernel, grid_spec=pltpu.PrefetchScalarGridSpec(num_s...  35.1 us
    unnamed x155, local copies, waits for them, and re-layouts  34.1 us
    pallas_call x1, Pallas kernels, expert_moments(): pl.pallas_call(moments_kernel, grid_spec=pltpu.PrefetchScalarGridSpec(num...  28.3 us
    pallas_call x1, Pallas kernels, attend_back(): pl.pallas_call(attend_back_kernel, in_specs=[pl.BlockSpec(memory_space=pl...  23.4 us
    pallas_call x1, Pallas kernels, finish(): pl.pallas_call(finish_kernel, grid=(FINISH_PARTS,), in_specs=[pl.BlockSpe...  20.8 us
    pallas_call x1, Pallas kernels, experts_backward(): pl.pallas_call(backward_kernel, grid_spec=pltpu.PrefetchScalarGridSpec(nu...  17.1 us
    pallas_call x1, Pallas kernels, experts_forward(): pl.pallas_call(forward_kernel, grid_spec=pltpu.PrefetchScalarGridSpec(num...  15 us
  transfers between devices with their start and end apart: 2, of which 1 were waited for; matrix products, arithmetic and copies ran while one was open for 3% of the time, Pallas kernels for 7%

profile of v8, /device:TPU:0, one launch (start us, length us, event | category | flops | bytes accessed | tf_op | source)
XLA Modules:
  0.0 660.1 jit_solution(14640302745794991098)
XLA Ops:
  0.7 0.7 constant_dynamic-slice_fusion.4
  1.5 0.7 fusion.31
  2.2 1.1 convert.18
  3.5 0.8 dynamic_slice.20
  4.4 11.9 %exchange_0.1 = s32[4,8,8,128]{3,2,1,0:T(8,128)S(1)} custom-call(s32[8,128]{1,0:T(8,128)S(1)} %add_bitcast_fusion.refs_0_), custom_call_target="tpu_custom_call" | custom-call | bytes 2703360 | tf_op jit(solution)/shard_map/exchange_0/pallas_call | solution.py:445
  16.3 1.0 convert.21
  17.3 0.7 convert.19
  18.1 0.7 convert_bitcast_fusion
  19.0 1.3 broadcast_in_dim.42
  20.3 4.3 all-to-all-start
  25.5 0.8 select_reduce_fusion.1
  26.6 4.8 select_reduce_fusion
  31.4 3.7 copy-done.2
  35.1 11.6 %gather_rows.1 = (bf16[32,256,384]{2,1,0:T(8,128)(2,1)S(1)}, bf16[6144,384]{1,0:T(8,128)(2,1)S(1)}) custom-call(s32[32,256]{1,0:T(8,128)S(1)} %fusion.12.list_ref, s32[32]{0:T(128)S(1)} %get-tuple-element.261.count_ref, f32[6144,384]{1,0:T(8,128)S(1)} %copy-done.2), custom_call_target="tpu_custom_call" | custom-call | tf_op jit(solution)/shard_map/gather_rows/pallas_call | solution.py:972
  46.8 2.2 copy-done.5
  48.9 2.7 copy-done.9
  51.7 11.2 %all-to-all-done.refs_0_ = bf16[4,48,4224]{2,1,0:T(8,128)(2,1)S(1)} async-done(((bf16[4,48,4224]{2,1,0:T(8,128)(2,1)}), bf16[4,48,4224]{2,1,0:T(8,128)(2,1)S(1)}, u32[]{:S(2)}, u32[]{:S(2)}) %all-to-all-start) | async-done | bytes 1622048 | tf_op jit(solution)/shard_map/all_to_all | solution.py:1333
  62.9 95.5 %exchange_1.1 = (bf16[4,2,2,2,48,2176]{5,4,3,2,1,0:T(8,128)(2,1)}, bf16[4,2,2,2,48,2048]{5,4,3,2,1,0:T(8,128)(2,1)}, bf16[4,256,384]{2,1,0:T(8,128)(2,1)S(1)}, bf16[1536,1536]{1,0:T(8,128)(2,1)S(1)}) custom-call(bf16[4,48,4224]{2,1,0:T(8,128)(2,1)S(1)} %all-to-all-done.refs_0_, bf16[4,2,2,2,256,384]{5,4,3,2,1,0:T(8,128)(2,1)} %bitcast.89, ...), custom_call_target="tpu_custom_call" | custom-call | bytes 622264320 | tf_op jit(solution)/shard_map/exchange_1/pallas_call | solution.py:445
  158.4 2.9 copy-done.3
  161.3 2.8 copy-done.7
  164.1 5.6 attend.1
  169.9 26.2 %exchange_2.1 = (bf16[4,2,2,2,32,1536]{5,4,3,2,1,0:T(8,128)(2,1)S(1)}, bf16[1536,1536]{1,0:T(8,128)(2,1)S(1)}) custom-call(bf16[32,1536]{1,0:T(8,128)(2,1)S(1)} %get-tuple-element.99.refs_0_.c_ref, bf16[6144,384]{1,0:T(8,128)(2,1)S(1)} %bitcast.84, bf16[1536,1536]{1,0:T(8,128)(2,1)S(1)} %get-tuple-element.100.refs_2_), custom_call_target="tpu_custom_call", output_to_operand_aliasing={{1}: (2, {})} | custom-call | bytes 347996160 | tf_op jit(solution)/shard_map/exchange_2/pallas_call | solution.py:445
  196.1 1.7 copy-done.17
  197.8 15.0 %experts_forward.1 = (bf16[1024,1536]{1,0:T(8,128)(2,1)S(1)}, f32[1024,1024]{1,0:T(8,128)}, f32[1024,128]{1,0:T(8,128)S(1)}, bf16[1536,1024]{1,0:T(8,128)(2,1)S(...) custom-call(s32[4]{0:T(128)S(1)} %iota_add_fusion.1.lane_ref, bf16[1024,1536]{1,0:T(8,128)(2,1)} %bitcast.95, ...), custom_call_target="tpu_custom_call" | custom-call | tf_op jit(solution)/shard_map/experts_forward/pallas_call | solution.py:529
  212.8 1.7 copy-done.13
  214.5 1.7 copy-done.15
  216.2 0.8 copy-done.29
  217.0 2.8 copy-done.16
  219.8 54.3 %exchange_3.1 = (bf16[4,2,2,2,32,1536]{5,4,3,2,1,0:T(8,128)(2,1)S(1)}, f32[32,1536]{1,0:T(8,128)S(1)}, bf16[1536,1536]{1,0:T(8,128)(2,1)S(1)}) custom-call(bf16[4,2,2,2,32,1536]{5,4,3,2,1,0:T(8,128)(2,1)S(1)} %bitcast.93, f32[32,1536]{1,0:T(8,128)S(1)} %get-tuple-element.103.refs_1_.resid_ref, ...), custom_call_target="tpu_custom_call", output_to_operand_aliasing={{2}: (4, {})} | custom-call | bytes 417792000 | tf_op jit(solution)/shard_map/exchange_3/pallas_call | solution.py:445
  274.1 5.2 multiply_reduce_fusion
  279.3 3.0 exponential_reduce_fusion
  282.4 11.7 %exchange_5.1 = f32[4,8,8,384]{3,2,1,0:T(8,128)S(1)} custom-call(f32[8,384]{1,0:T(8,128)S(1)} %reshape.237.refs_0_), custom_call_target="tpu_custom_call" | custom-call | bytes 8110080 | tf_op jit(solution)/shard_map/exchange_5/pallas_call | solution.py:445
  295.1 0.6 divide_multiply_fusion
  296.0 4.0 fusion.5
  300.1 5.4 fusion.1.refs_3_.refs_1_
  305.5 5.3 multiply_convert_fusion
  310.8 0.6 constant_dynamic-slice_fusion.gates_ref
  311.5 54.0 %exchange_6.1 = (bf16[4,2,2,2,32,1536]{5,4,3,2,1,0:T(8,128)(2,1)S(1)}, f32[32,1536]{1,0:T(8,128)S(1)}, f32[1,1536]{1,0:T(1,128)S(1)}, bf16[4,1536,384]{2,1,0:T(8,128)(2,1)S(1)}) custom-call(bf16[4,2,2,2,32,1536]{5,4,3,2,1,0:T(8,128)(2,1)S(1)} %bitcast.94, f32[32,1536]{1,0:T(8,128)S(1)} %copy-done.39, f32[8,1536]{1,0:T(8,128)S(1)} %get-tuple-element.104.refs_2_.gains_ref, ...), custom_call_target="tpu_custom_call" | custom-call | bytes 323543040 | tf_op jit(solution)/shard_map/exchange_6/pallas_call | solution.py:445
  365.5 3.3 copy-done.10
  368.9 17.1 %experts_backward.1 = (bf16[1024,1664]{1,0:T(8,128)(2,1)S(1)}, bf16[1024,1024]{1,0:T(8,128)(2,1)S(1)}) custom-call(s32[4]{0:T(128)S(1)} %copy-done.48, bf16[1024,1536]{1,0:T(8,128)(2,1)S(1)} %bitcast.91, f32[1024,1024]{1,0:T(8,128)S(1)} %copy-done.10, f32[1024,128]{1,0:T(8,128)S(1)} %copy-done.30, bf16[1536,1024]{1,0:T(8,128)(2,1)S(1)} %copy-done.14, ...), custom_call_target="tpu_custom_call" | custom-call | tf_op jit(solution)/shard_map/experts_backward/pallas_call | solution.py:608
  386.1 29.0 %exchange_8.1 = (f32[32,1664]{1,0:T(8,128)S(1)}, bf16[4,1536,384]{2,1,0:T(8,128)(2,1)S(1)}) custom-call(bf16[4,2,2,2,32,1664]{5,4,3,2,1,0:T(8,128)(2,1)S(1)} %bitcast.90, bf16[1536,1536]{1,0:T(8,128)(2,1)S(1)} %fusion.1.refs_3_.refs_1_, bf16[4,1536,384]{2,1,0:T(8,128)(2,1)S(1)} %get-tuple-element.115.refs_2_), custom_call_target="tpu_custom_call", output_to_operand_aliasing={{1}: (2, {})} | custom-call | bytes 355532800 | tf_op jit(solution)/shard_map/exchange_8/pallas_call | solution.py:445
  415.2 23.4 %attend_back.1 = (bf16[4,256,384]{2,1,0:T(8,128)(2,1)S(1)}, bf16[1536,2176]{1,0:T(8,128)(2,1)}, bf16[1536,2048]{1,0:T(8,128)(2,1)}) custom-call(s32[1]{0:T(128)S(1)} %bitcast.102, f32[32,1664]{1,0:T(8,128)S(1)} %get-tuple-element.116.back_ref, f32[32,128]{1,0:T(8,128)S(1)} %copy-done.44, f32[32,1536]{1,0:T(8,128)S(1)} %copy-done.37, ...), custom_call_target="tpu_custom_call" | custom-call | tf_op jit(solution)/shard_map/attend_back/pallas_call | solution.py:909
  438.6 0.9 copy-done.26
  439.5 93.0 %exchange_9.1 = (bf16[4,48,4224]{2,1,0:T(8,128)(2,1)}, bf16[4,2,2,2,256,384]{5,4,3,2,1,0:T(8,128)(2,1)}, bf16[4,1536,384]{2,1,0:T(8,128)(2,1)}) custom-call(bf16[4,2,2,2,48,2176]{5,4,3,2,1,0:T(8,128)(2,1)} %bitcast.110, bf16[4,2,2,2,48,2048]{5,4,3,2,1,0:T(8,128)(2,1)} %bitcast.112, bf16[4,256,384]{2,1,0:T(8,128)(2,1)} %copy-done.26, ...), custom_call_target="tpu_custom_call", output_to_operand_aliasing={{2}: (4, {})} | custom-call | bytes 716636160 | tf_op jit(solution)/shard_map/exchange_9/pallas_call | solution.py:445
  532.5 5.0 all-to-all-start.1
  537.6 0.7 copy.109.router
  539.1 0.7 copy.110.router_one
  539.8 0.7 copy.111.router_two
  540.5 0.6 pad_maximum_fusion.3.scale_ref
  541.8 35.1 %table_moments.1 = (f32[6144,384]{1,0:T(8,128)}, f32[6144,384]{1,0:T(8,128)}, f32[6144,384]{1,0:T(8,128)}, f32[8,128]{1,0:T(8,128)}) custom-call(s32[32,256]{1,0:T(8,128)} %copy-done.31, s32[32]{0:T(128)} %copy-done.45, f32[2]{0:T(128)} %pad_maximum_fusion.3.scale_ref, bf16[32,256,384]{2,1,0:T(8,128)(2,1)} %bitcast.111, bf16[6144,384]{1,0:T(8,128)(2,1)} %bitcast.82, ...), custom_call_target="tpu_custom_call" | custom-call | tf_op jit(solution)/shard_map/table_moments/pallas_call | solution.py:1079
  576.9 3.5 fusion.19.down_grad
  580.4 5.4 fusion.18.grad_ref
  585.8 1.2 copy-done.56
  587.0 4.3 small_moments.1
  591.3 1.3 add.98.other_norms
  592.6 28.3 %expert_moments.1 = (f32[12288,128]{1,0:T(8,128)}, f32[12288,128]{1,0:T(8,128)}, f32[12288,128]{1,0:T(8,128)}, f32[512,1536]{1,0:T(8,128)}, f32[512,1536]{1,0:T(...) custom-call(f32[2]{0:T(128)} %pad_maximum_fusion.3.scale_ref, f32[8,128]{1,0:T(8,128)} %add.98.other_norms, ...), custom_call_target="tpu_custom_call" | custom-call | tf_op jit(solution)/shard_map/expert_moments/pallas_call | solution.py:681
  620.9 0.7 copy-done.46
  621.6 10.9 %exchange_10.1 = f32[4,8,8,128]{3,2,1,0:T(8,128)S(1)} custom-call(f32[8,128]{1,0:T(8,128)S(1)} %copy-done.46), custom_call_target="tpu_custom_call" | custom-call | bytes 2703360 | tf_op jit(solution)/shard_map/exchange_10/pallas_call | solution.py:445
  633.3 0.7 copy.116
  635.3 0.7 copy.113
  636.0 0.7 copy.114
  636.6 0.7 copy.115
  637.3 0.6 multiply_subtract_fusion.1
  637.9 20.8 %finish.1 = (f32[6144,384]{1,0:T(8,128)}, f32[12288,128]{1,0:T(8,128)}, f32[512,1536]{1,0:T(8,128)}, f32[48,2560]{1,0:T(8,128)}, f32[48,1536]{1,0:T(8,128)}) custom-call(f32[32,8,128]{2,1,0:T(8,128)} %bitcast.97, f32[6144,384]{1,0:T(8,128)} %refs_0_.1, f32[6144,384]{1,0:T(8,128)} %get-tuple-element.137.refs_1_, f32[12288,128]{1,0:T(8,128)} %bitcast.107, ...), custom_call_target="tpu_custom_call" | custom-call | tf_op jit(solution)/shard_map/finish/pallas_call | solution.py:1185
  (185 shorter events, 4.2 us)
Async XLA Ops:
  20.3 42.6 %all-to-all-start = ((bf16[4,48,4224]{2,1,0:T(8,128)(2,1)}), bf16[4,48,4224]{2,1,0:T(8,128)(2,1)S(1)}, u32[]{:S(2)}, u32[]{:S(2)}) async-start(bf16[4,48,4224]{2,1,0:T(8,128)(2,1)} %broadcast_in_dim.42), calls=%async_computation | async-start | bytes 3244032 | tf_op jit(solution)/shard_map/all_to_all | solution.py:1333
  24.7 22.0 %copy-start.45 = (s32[32]{0:T(128)}, s32[32]{0:T(128)S(1)}, u32[]{:S(2)}) copy-start(s32[32]{0:T(128)S(1)} %get-tuple-element.261.count_ref) | copy-start | bytes 388
  31.4 3.7 copy-start.2
  35.1 11.6 %copy-start.31 = (s32[32,256]{1,0:T(8,128)}, s32[32,256]{1,0:T(8,128)S(1)}, u32[]{:S(2)}) copy-start(s32[32,256]{1,0:T(8,128)S(1)} %fusion.12.list_ref) | copy-start | bytes 98308
  35.1 16.6 %copy-start.67 = (s32[16,2]{0,1:T(2,128)S(1)}, s32[16,2]{0,1:T(2,128)}, u32[]{:S(2)}) copy-start(s32[16,2]{0,1:T(2,128)} %param.29) | copy-start | bytes 388
  51.6 146.2 %copy-start.47 = (s32[4]{0:T(128)}, s32[4]{0:T(128)S(1)}, u32[]{:S(2)}) copy-start(s32[4]{0:T(128)S(1)} %iota_add_fusion.1.lane_ref) | copy-start | bytes 52
  62.9 107.0 %slice-start = ((s8[4718592]{0:T(1024)(128)(4,1)}), s8[524288]{0:T(1024)(128)(4,1)S(1)}, s32[]{:S(2)}) async-start(s8[4718592]{0:T(1024)(128)(4,1)} %bitcast.83), calls=%async_computation.2 | async-start | bytes 1048576
  158.4 2.9 copy-start.3
  164.1 5.7 slice-start.1
  169.8 26.3 %copy-start.22 = (f32[8,96,256]{2,1,0:T(8,128)}, f32[8,96,256]{2,1,0:T(8,128)S(1)}, u32[]{:S(2)}) copy-start(f32[8,96,256]{2,1,0:T(8,128)S(1)} %get-tuple-element.119.probs_ref) | copy-start | bytes 2359300
  169.8 26.3 %copy-start.24 = (bf16[256,1536]{1,0:T(8,128)(2,1)}, bf16[256,1536]{1,0:T(8,128)(2,1)S(1)}, u32[]{:S(2)}) copy-start(bf16[256,1536]{1,0:T(8,128)(2,1)S(1)} %get-tuple-element.124.normed_ref) | copy-start | bytes 2359300
  169.8 26.3 %copy-start.32 = (bf16[256,512]{1,0:T(8,128)(2,1)}, bf16[256,512]{1,0:T(8,128)(2,1)S(1)}, u32[]{:S(2)}) copy-start(bf16[256,512]{1,0:T(8,128)(2,1)S(1)} %get-tuple-element.121.key_ref) | copy-start | bytes 786436
  169.8 26.3 %copy-start.34 = (bf16[256,512]{1,0:T(8,128)(2,1)}, bf16[256,512]{1,0:T(8,128)(2,1)S(1)}, u32[]{:S(2)}) copy-start(bf16[256,512]{1,0:T(8,128)(2,1)S(1)} %get-tuple-element.122.value_ref) | copy-start | bytes 786436
  169.8 26.3 %copy-start.40 = (bf16[32,1536]{1,0:T(8,128)(2,1)}, bf16[32,1536]{1,0:T(8,128)(2,1)S(1)}, u32[]{:S(2)}) copy-start(bf16[32,1536]{1,0:T(8,128)(2,1)S(1)} %get-tuple-element.120.query_ref) | copy-start | bytes 294916
  169.8 26.3 %copy-start.42 = (bf16[32,1536]{1,0:T(8,128)(2,1)}, bf16[32,1536]{1,0:T(8,128)(2,1)S(1)}, u32[]{:S(2)}) copy-start(bf16[32,1536]{1,0:T(8,128)(2,1)S(1)} %get-tuple-element.123.mixed_ref) | copy-start | bytes 294916
  169.8 47.1 %copy-start.27 = (f32[32,1536]{1,0:T(8,128)}, f32[32,1536]{1,0:T(8,128)S(1)}, u32[]{:S(2)}) copy-start(f32[32,1536]{1,0:T(8,128)S(1)} %get-tuple-element.103.refs_1_.resid_ref) | copy-start | bytes 589828
  217.0 57.1 %copy-start.19 = (bf16[512,1536]{1,0:T(8,128)(2,1)}, bf16[512,1536]{1,0:T(8,128)(2,1)S(1)}, u32[]{:S(2)}) copy-start(bf16[512,1536]{1,0:T(8,128)(2,1)S(1)} %get-tuple-element.113.down_ref) | copy-start | bytes 4718596
  217.0 57.1 %copy-start.53 = (bf16[1024,512]{1,0:T(8,128)(2,1)}, bf16[1024,512]{1,0:T(8,128)(2,1)S(1)}, u32[]{:S(2)}) copy-start(bf16[1024,512]{1,0:T(8,128)(2,1)S(1)} %get-tuple-element.135) | copy-start | bytes 3145732
  217.0 2.8 copy-start.16
  274.1 5.2 copy-start.8
  274.1 5.2 copy-start.38
  274.1 5.2 copy-start.49
  279.3 3.1 copy-start.55
  279.3 15.6 %copy-start.68 = (f32[32]{0:T(128)S(1)}, f32[32]{0:T(128)}, u32[]{:S(2)}) copy-start(f32[32]{0:T(128)} %param.30) | copy-start | bytes 388
  296.0 4.1 copy-start.50
  296.0 9.5 %slice-start.2 = ((s8[4718592]{0:T(1024)(128)(4,1)}), s8[4194304]{0:T(1024)(128)(4,1)S(1)}, s32[]{:S(2)}) async-start(s8[4718592]{0:T(1024)(128)(4,1)} %bitcast.87), calls=%async_computation.4 | async-start | bytes 8388608
  300.0 5.4 slice-start.3
  305.5 80.5 %copy-start.6 = (bf16[1536,1536]{1,0:T(8,128)(2,1)}, bf16[1536,1536]{1,0:T(8,128)(2,1)S(1)}, u32[]{:S(2)}) copy-start(bf16[1536,1536]{1,0:T(8,128)(2,1)S(1)} %fusion.1.refs_3_.refs_1_) | copy-start | bytes 14155780
  305.5 5.3 copy-start.30
  305.5 5.9 copy-start.39
  310.8 54.7 %copy-start.14 = (bf16[1536,1024]{1,0:T(8,128)(2,1)S(1)}, bf16[1536,1024]{1,0:T(8,128)(2,1)}, u32[]{:S(2)}) copy-start(bf16[1536,1024]{1,0:T(8,128)(2,1)} %copy-done.13) | copy-start | bytes 9437188
  310.8 54.7 %copy-start.20 = (bf16[512,1536]{1,0:T(8,128)(2,1)S(1)}, bf16[512,1536]{1,0:T(8,128)(2,1)}, u32[]{:S(2)}) copy-start(bf16[512,1536]{1,0:T(8,128)(2,1)} %copy-done.19) | copy-start | bytes 4718596
  310.8 54.7 %copy-start.48 = (s32[4]{0:T(128)S(1)}, s32[4]{0:T(128)}, u32[]{:S(2)}) copy-start(s32[4]{0:T(128)} %copy-done.47) | copy-start | bytes 52
  365.5 20.5 %copy-start.11 = (bf16[4,2,2,2,32,1536]{5,4,3,2,1,0:T(8,128)(2,1)}, bf16[4,2,2,2,32,1536]{5,4,3,2,1,0:T(8,128)(2,1)S(1)}, u32[]{:S(2)}) copy-start(bf16[4,2,2,2,32,1536]{5,4,3,2,1,0:T(8,128)(2,1)S(1)} %get-tuple-element.109) | copy-start | bytes 9437188
  365.5 20.5 %copy-start.36 = (f32[32,1536]{1,0:T(8,128)}, f32[32,1536]{1,0:T(8,128)S(1)}, u32[]{:S(2)}) copy-start(f32[32,1536]{1,0:T(8,128)S(1)} %get-tuple-element.117.grad_two_ref) | copy-start | bytes 589828
  365.5 3.4 copy-start.10
  386.0 29.2 %copy-start.51 = (bf16[1024,1024]{1,0:T(8,128)(2,1)}, bf16[1024,1024]{1,0:T(8,128)(2,1)S(1)}, u32[]{:S(2)}) copy-start(bf16[1024,1024]{1,0:T(8,128)(2,1)S(1)} %get-tuple-element.134) | copy-start | bytes 6291460
  386.0 29.1 %copy-start.23 = (f32[8,96,256]{2,1,0:T(8,128)S(1)}, f32[8,96,256]{2,1,0:T(8,128)}, u32[]{:S(2)}) copy-start(f32[8,96,256]{2,1,0:T(8,128)} %copy-done.22) | copy-start | bytes 2359300
  386.0 29.1 %copy-start.25 = (bf16[256,1536]{1,0:T(8,128)(2,1)S(1)}, bf16[256,1536]{1,0:T(8,128)(2,1)}, u32[]{:S(2)}) copy-start(bf16[256,1536]{1,0:T(8,128)(2,1)} %copy-done.24) | copy-start | bytes 2359300
  386.0 29.1 %copy-start.28 = (f32[32,1536]{1,0:T(8,128)S(1)}, f32[32,1536]{1,0:T(8,128)}, u32[]{:S(2)}) copy-start(f32[32,1536]{1,0:T(8,128)} %copy-done.27) | copy-start | bytes 589828
  386.0 29.1 %copy-start.33 = (bf16[256,512]{1,0:T(8,128)(2,1)S(1)}, bf16[256,512]{1,0:T(8,128)(2,1)}, u32[]{:S(2)}) copy-start(bf16[256,512]{1,0:T(8,128)(2,1)} %copy-done.32) | copy-start | bytes 786436
  386.1 29.1 %copy-start.35 = (bf16[256,512]{1,0:T(8,128)(2,1)S(1)}, bf16[256,512]{1,0:T(8,128)(2,1)}, u32[]{:S(2)}) copy-start(bf16[256,512]{1,0:T(8,128)(2,1)} %copy-done.34) | copy-start | bytes 786436
  386.1 29.1 %copy-start.37 = (f32[32,1536]{1,0:T(8,128)S(1)}, f32[32,1536]{1,0:T(8,128)}, u32[]{:S(2)}) copy-start(f32[32,1536]{1,0:T(8,128)} %copy-done.36) | copy-start | bytes 589828
  386.1 29.1 %copy-start.41 = (bf16[32,1536]{1,0:T(8,128)(2,1)S(1)}, bf16[32,1536]{1,0:T(8,128)(2,1)}, u32[]{:S(2)}) copy-start(bf16[32,1536]{1,0:T(8,128)(2,1)} %copy-done.40) | copy-start | bytes 294916
  386.1 29.1 %copy-start.43 = (bf16[32,1536]{1,0:T(8,128)(2,1)S(1)}, bf16[32,1536]{1,0:T(8,128)(2,1)}, u32[]{:S(2)}) copy-start(bf16[32,1536]{1,0:T(8,128)(2,1)} %copy-done.42) | copy-start | bytes 294916
  386.1 29.1 %copy-start.44 = (f32[32,128]{1,0:T(8,128)S(1)}, f32[32,128]{1,0:T(8,128)}, u32[]{:S(2)}) copy-start(f32[32,128]{1,0:T(8,128)} %constant_dynamic-slice_fusion.gates_ref) | copy-start | bytes 49156
  415.1 23.5 %copy-start.4 = (bf16[4,1536,384]{2,1,0:T(8,128)(2,1)}, bf16[4,1536,384]{2,1,0:T(8,128)(2,1)S(1)}, u32[]{:S(2)}) copy-start(bf16[4,1536,384]{2,1,0:T(8,128)(2,1)S(1)} %get-tuple-element.128.refs_4_) | copy-start | bytes 14155780
  439.5 98.1 %copy-start.58 = (f32[48,32]{0,1:T(8,128)S(1)}, f32[48,32]{0,1:T(8,128)}, u32[]{:S(2)}) copy-start(f32[48,32]{0,1:T(8,128)} %param.42) | copy-start | bytes 18436
  439.5 99.6 %copy-start.63 = (f32[48,32]{0,1:T(8,128)S(1)}, f32[48,32]{0,1:T(8,128)}, u32[]{:S(2)}) copy-start(f32[48,32]{0,1:T(8,128)} %param.43) | copy-start | bytes 18436
  439.5 100.3 %copy-start.64 = (f32[48,32]{0,1:T(8,128)S(1)}, f32[48,32]{0,1:T(8,128)}, u32[]{:S(2)}) copy-start(f32[48,32]{0,1:T(8,128)} %param.44) | copy-start | bytes 18436
  532.5 53.3 %all-to-all-start.1 = ((bf16[4,48,4224]{2,1,0:T(8,128)(2,1)}), bf16[4,48,4224]{2,1,0:T(8,128)(2,1)S(1)}, u32[]{:S(2)}, u32[]{:S(2)}) async-start(bf16[4,48,4224]{2,1,0:T(8,128)(2,1)} %get-tuple-element.132), calls=%async_computation.1 | async-start | bytes 3244032 | tf_op jit(solution)/shard_map/all_to_all | solution.py:1453
  541.7 35.1 %copy-start.12 = (bf16[4,2,2,2,32,1536]{5,4,3,2,1,0:T(8,128)(2,1)S(1)}, bf16[4,2,2,2,32,1536]{5,4,3,2,1,0:T(8,128)(2,1)}, u32[]{:S(2)}) copy-start(bf16[4,2,2,2,32,1536]{5,4,3,2,1,0:T(8,128)(2,1)} %copy-done.11) | copy-start | bytes 9437188
  541.7 35.1 %copy-start.54 = (bf16[1024,512]{1,0:T(8,128)(2,1)S(1)}, bf16[1024,512]{1,0:T(8,128)(2,1)}, u32[]{:S(2)}) copy-start(bf16[1024,512]{1,0:T(8,128)(2,1)} %copy-done.53) | copy-start | bytes 3145732
  576.9 3.5 copy-start.18
  576.9 3.5 copy-start.52
  580.4 10.9 %copy-start.65 = (f32[8,128]{1,0:T(8,128)S(1)}, f32[8,128]{1,0:T(8,128)}, u32[]{:S(2)}) copy-start(f32[8,128]{1,0:T(8,128)} %get-tuple-element.131) | copy-start | bytes 12292
  592.6 42.6 %copy-start.57 = (f32[48,32]{1,0:T(8,128)S(1)}, f32[48,32]{1,0:T(8,128)}, u32[]{:S(2)}) copy-start(f32[48,32]{1,0:T(8,128)} %copy.109.router) | copy-start | bytes 18436
  592.6 42.6 %copy-start.61 = (f32[48,32]{1,0:T(8,128)S(1)}, f32[48,32]{1,0:T(8,128)}, u32[]{:S(2)}) copy-start(f32[48,32]{1,0:T(8,128)} %get-tuple-element.151) | copy-start | bytes 18436
  592.6 43.3 %copy-start.60 = (f32[48,32]{1,0:T(8,128)S(1)}, f32[48,32]{1,0:T(8,128)}, u32[]{:S(2)}) copy-start(f32[48,32]{1,0:T(8,128)} %get-tuple-element.243) | copy-start | bytes 18436
  592.6 44.0 %copy-start.59 = (f32[48,32]{1,0:T(8,128)S(1)}, f32[48,32]{1,0:T(8,128)}, u32[]{:S(2)}) copy-start(f32[48,32]{1,0:T(8,128)} %get-tuple-element.244) | copy-start | bytes 18436
  592.6 44.7 %copy-start.62 = (f32[3,48]{1,0:T(4,128)S(1)}, f32[3,48]{1,0:T(4,128)}, u32[]{:S(2)}) copy-start(f32[3,48]{1,0:T(4,128)} %gains.1) | copy-start | bytes 1732
  592.6 44.7 %copy-start.66 = (f32[3,48]{1,0:T(4,128)S(1)}, f32[3,48]{1,0:T(4,128)}, u32[]{:S(2)}) copy-start(f32[3,48]{1,0:T(4,128)} %get-tuple-element.154) | copy-start | bytes 1732
  632.5 5.4 copy-start.21
  637.9 20.8 %copy-start.1 = (s32[256,8]{0,1:T(8,128)S(1)}, s32[256,8]{0,1:T(8,128)}, u32[]{:S(2)}) copy-start(s32[256,8]{0,1:T(8,128)} %param.31) | copy-start | bytes 24580
  (11 other events, 18.8 us)

commit v9 on v8

--- a/solution.py
+++ b/solution.py
@@ -436,11 +436,17 @@
         mail.finish()
 
     size = sum(x.size * x.dtype.itemsize for p in parts for x in p.inputs + p.outputs)
-    need = size + sum(
+    need = sum(
         math.prod(x.shape) * x.dtype.itemsize
         for p in parts
         for x in p.scratch
         if x.memory_space == pltpu.VMEM
+    )
+    need += sum(
+        x.size * x.dtype.itemsize
+        for p in parts
+        if not isinstance(p, Swap)
+        for x in p.inputs + p.outputs
     )
     out = pl.pallas_call(
         kernel,
@@ -754,6 +760,10 @@
 def spread(start, rows):
     pick = selector(start, (SEQUENCE_TOKENS, COMP), 0)
     return jnp.dot(pick, rows, preferred_element_type=f32, precision=lax.Precision.HIGHEST)
+
+
+def dot_down(a, b):
+    return lax.dot_general(a, b, (((0,), (0,)), ((), ())), preferred_element_type=f32)
 
 
 def head_rows(ref_value, h):
@@ -868,9 +878,9 @@
         grad_probs = dot_across(grad_head, value[:, lanes]).astype(bf16).astype(f32)
         inner = jnp.sum(grad_probs * probs, axis=-1, keepdims=True)
         grad_scores = probs * (grad_probs - inner)
-        value_parts.append(dot(probs.T.astype(bf16), grad_head))
+        value_parts.append(dot_down(probs.astype(bf16), grad_head))
         query_parts.append(dot(grad_scores.astype(bf16), key[:, lanes]) * ROOT)
-        key_parts.append(dot(grad_scores.T.astype(bf16), head_rows(query, h)) * ROOT)
+        key_parts.append(dot_down(grad_scores.astype(bf16), head_rows(query, h)) * ROOT)
     grad_query = turn(head_lanes(query_parts), cos_rows[...], -sin_rows[...]).astype(bf16)
     grad_key = jnp.concatenate(key_parts, axis=1)
     grad_key = turn(grad_key, cos_ref[...], -sin_ref[...]).astype(bf16)
@@ -886,13 +896,11 @@
         out_ref[p] = total[:, p * columns : (p + 1) * columns].astype(bf16)
     pick_rows = selector(start, (COMP, SEQUENCE_TOKENS), 1).astype(bf16)
     a_rows = dot(pick_rows, normed_ref[...])
-    turned = normed_ref[...].astype(f32).T.astype(bf16)
-    grad_one_ref[:, HEAD_COLS:wide] = dot(turned, grad_key).astype(bf16)
-    grad_pack_ref[:, :KEY_COLS] = dot(turned, grad_value).astype(bf16)
-    grad_one_ref[:, :HEAD_COLS] = dot(a_rows.T.astype(bf16), grad_query).astype(bf16)
-    grad_pack_ref[:, KEY_COLS : KEY_COLS + D] = dot(
-        mixed_ref[...].astype(f32).T.astype(bf16), branch
-    ).astype(bf16)
+    turned = normed_ref[...]
+    grad_one_ref[:, HEAD_COLS:wide] = dot_down(turned, grad_key).astype(bf16)
+    grad_pack_ref[:, :KEY_COLS] = dot_down(turned, grad_value).astype(bf16)
+    grad_one_ref[:, :HEAD_COLS] = dot_down(a_rows.astype(bf16), grad_query).astype(bf16)
+    grad_pack_ref[:, KEY_COLS : KEY_COLS + D] = dot_down(mixed_ref[...], branch).astype(bf16)
     left = jnp.concatenate(
         [c_ref[...].astype(f32), gain_one, gain_two, gain_three_ref[...], jnp.zeros((5, D), f32)],
         axis=0,
@@ -900,7 +908,7 @@
     lane = lax.broadcasted_iota(jnp.int32, (8, 128), 0) + EXPERTS
     lane = (lane == lax.broadcasted_iota(jnp.int32, (8, 128), 1)).astype(f32)
     right = jnp.concatenate([router_grad.astype(f32), lane], axis=0).astype(bf16)
-    grad_one_ref[:, wide:] = dot(left.T.astype(bf16), right).astype(bf16)
+    grad_one_ref[:, wide:] = dot_down(left.astype(bf16), right).astype(bf16)
 
 
 def attend_back(start, *operands):
@@ -922,7 +930,8 @@
 
 
 def lamb_update(weight, moment_one, moment_two, scale_one, scale_two):
-    return (moment_one * scale_one) / (jnp.sqrt(moment_two * scale_two) + EPSILON) + DECAY * weight
+    square = moment_two * scale_two
+    return (moment_one * scale_one) / (square * lax.rsqrt(square) + EPSILON) + DECAY * weight
 
 
 def lamb_parts(weight, moment_one, moment_two, gradient, scales):

time: 664 us -> 657 us (0.989)
  Pallas kernels: 548 us -> 537 us
    pallas_call x1, Pallas kernels: 17.1 us -> 6.88 us  [experts_backward(): pl.pallas_call(backward_kernel, grid_spec=pltpu.PrefetchScalarGridSpec(nu...]
    pallas_call x9, Pallas kernels: 387 us -> 394 us  [communicate(): pl.pallas_call(kernel, out_shape=[x for p in parts for x in p.outputs], i...]
    unnamed x155 -> x177, local copies, waits for them, and re-layouts: 34.1 us -> 35.9 us
  transfers between devices with their start and end apart: 2 -> 2, of which waited for: 1 -> 1; matrix products, arithmetic and copies ran while one was open for 3% -> 3% of each run, Pallas kernels for 7% -> 6%
where the time goes in v9:
time: 657 us; the launch traced here: 652 us
  Pallas kernels  537 us (82%)
  local copies, waits for them, and re-layouts  42.8 us (7%)
  matrix products  25 us (4%)
  other arithmetic  21.3 us (3%)
  waiting for transfers between devices  11.1 us (2%)
  starting transfers between devices  8.78 us (1%)
    pallas_call x9, Pallas kernels, communicate(): pl.pallas_call(kernel, out_shape=[x for p in parts for x in p.outputs], i...  394 us
    unnamed x177, local copies, waits for them, and re-layouts  35.9 us
    pallas_call x1, Pallas kernels, table_moments(): pl.pallas_call(table_kernel, grid_spec=pltpu.PrefetchScalarGridSpec(num_s...  32 us
    pallas_call x1, Pallas kernels, expert_moments(): pl.pallas_call(moments_kernel, grid_spec=pltpu.PrefetchScalarGridSpec(num...  27.1 us
    pallas_call x1, Pallas kernels, attend_back(): pl.pallas_call(attend_back_kernel, in_specs=[pl.BlockSpec(memory_space=pl...  21.6 us
    pallas_call x1, Pallas kernels, finish(): pl.pallas_call(finish_kernel, grid=(FINISH_PARTS,), in_specs=[pl.BlockSpe...  20.8 us
    pallas_call x1, Pallas kernels, experts_forward(): pl.pallas_call(forward_kernel, grid_spec=pltpu.PrefetchScalarGridSpec(num...  15.3 us
  transfers between devices with their start and end apart: 2, of which 1 were waited for; matrix products, arithmetic and copies ran while one was open for 3% of the time, Pallas kernels for 6%

profile of v9, /device:TPU:0, one launch (start us, length us, event | category | flops | bytes accessed | tf_op | source)
XLA Modules:
  0.0 652.1 jit_solution(9249163376880567748)
XLA Ops:
  0.7 0.7 constant_dynamic-slice_fusion.4
  1.5 0.7 fusion.31
  2.2 1.1 convert.18
  3.5 0.8 dynamic_slice.20
  4.4 11.9 %exchange_0.1 = s32[4,8,8,128]{3,2,1,0:T(8,128)S(1)} custom-call(s32[8,128]{1,0:T(8,128)S(1)} %add_bitcast_fusion.refs_0_), custom_call_target="tpu_custom_call" | custom-call | bytes 2703360 | tf_op jit(solution)/shard_map/exchange_0/pallas_call | solution.py:451
  16.3 1.0 convert.21
  17.3 0.7 convert.19
  18.1 0.7 convert_bitcast_fusion
  19.0 1.3 broadcast_in_dim.42
  20.3 4.3 all-to-all-start
  25.2 1.1 reshape.233.routes_ref
  26.3 0.8 select_reduce_fusion.1
  27.3 4.8 select_reduce_fusion
  32.2 3.7 copy-done.2
  35.9 9.2 %gather_rows.1 = (bf16[32,256,384]{2,1,0:T(8,128)(2,1)S(1)}, bf16[6144,384]{1,0:T(8,128)(2,1)S(1)}) custom-call(s32[32,256]{1,0:T(8,128)S(1)} %fusion.12.list_ref, s32[32]{0:T(128)S(1)} %get-tuple-element.261.count_ref, f32[6144,384]{1,0:T(8,128)S(1)} %copy-done.2), custom_call_target="tpu_custom_call" | custom-call | tf_op jit(solution)/shard_map/gather_rows/pallas_call | solution.py:981
  45.1 2.2 copy-done.5
  47.3 2.7 copy-done.14
  50.0 0.6 copy-done.38
  51.7 11.1 %all-to-all-done.refs_0_ = bf16[4,48,4224]{2,1,0:T(8,128)(2,1)S(1)} async-done(((bf16[4,48,4224]{2,1,0:T(8,128)(2,1)}), bf16[4,48,4224]{2,1,0:T(8,128)(2,1)S(1)}, u32[]{:S(2)}, u32[]{:S(2)}) %all-to-all-start) | async-done | bytes 1622048 | tf_op jit(solution)/shard_map/all_to_all | solution.py:1342
  62.9 2.3 copy-done.6
  65.2 93.3 %exchange_1.1 = (bf16[4,2,2,2,48,2176]{5,4,3,2,1,0:T(8,128)(2,1)}, bf16[4,2,2,2,48,2048]{5,4,3,2,1,0:T(8,128)(2,1)S(1)}, bf16[4,256,384]{2,1,0:T(8,128)(2,1)S(1)}, bf16[1536,1536]{1,0:T(8,128)(2,1)S(1)}) custom-call(bf16[4,48,4224]{2,1,0:T(8,128)(2,1)S(1)} %all-to-all-done.refs_0_, bf16[4,2,2,2,256,384]{5,4,3,2,1,0:T(8,128)(2,1)} %bitcast.89, ...), custom_call_target="tpu_custom_call" | custom-call | bytes 622264320 | tf_op jit(solution)/shard_map/exchange_1/pallas_call | solution.py:451
  158.5 2.2 copy-done.9
  160.8 5.4 copy-done.3
  166.2 5.7 attend.1
  171.9 0.9 copy-done.28
  172.7 0.6 copy-done.51
  173.5 26.2 %exchange_2.1 = (bf16[4,2,2,2,32,1536]{5,4,3,2,1,0:T(8,128)(2,1)S(1)}, bf16[1536,1536]{1,0:T(8,128)(2,1)S(1)}) custom-call(bf16[32,1536]{1,0:T(8,128)(2,1)S(1)} %get-tuple-element.99.refs_0_.c_ref, bf16[6144,384]{1,0:T(8,128)(2,1)S(1)} %bitcast.84, bf16[1536,1536]{1,0:T(8,128)(2,1)S(1)} %copy-done.10), custom_call_target="tpu_custom_call", output_to_operand_aliasing={{1}: (2, {})} | custom-call | bytes 347996160 | tf_op jit(solution)/shard_map/exchange_2/pallas_call | solution.py:451
  199.7 2.2 copy-done.11
  201.9 1.7 copy-done.22
  203.6 15.3 %experts_forward.1 = (bf16[1024,1536]{1,0:T(8,128)(2,1)S(1)}, f32[1024,1024]{1,0:T(8,128)}, f32[1024,128]{1,0:T(8,128)S(1)}, bf16[1536,1024]{1,0:T(8,128)(2,1)S(...) custom-call(s32[4]{0:T(128)S(1)} %iota_add_fusion.1.lane_ref, bf16[1024,1536]{1,0:T(8,128)(2,1)} %bitcast.95, ...), custom_call_target="tpu_custom_call" | custom-call | tf_op jit(solution)/shard_map/experts_forward/pallas_call | solution.py:535
  218.9 1.0 copy-done.61
  219.9 54.1 %exchange_3.1 = (bf16[4,2,2,2,32,1536]{5,4,3,2,1,0:T(8,128)(2,1)S(1)}, f32[32,1536]{1,0:T(8,128)S(1)}, bf16[1536,1536]{1,0:T(8,128)(2,1)S(1)}) custom-call(bf16[4,2,2,2,32,1536]{5,4,3,2,1,0:T(8,128)(2,1)S(1)} %bitcast.93, f32[32,1536]{1,0:T(8,128)S(1)} %get-tuple-element.103.refs_1_.resid_ref, ...), custom_call_target="tpu_custom_call", output_to_operand_aliasing={{2}: (4, {})} | custom-call | bytes 417792000 | tf_op jit(solution)/shard_map/exchange_3/pallas_call | solution.py:451
  274.1 5.2 multiply_reduce_fusion
  279.3 3.0 exponential_reduce_fusion
  282.4 11.7 %exchange_5.1 = f32[4,8,8,384]{3,2,1,0:T(8,128)S(1)} custom-call(f32[8,384]{1,0:T(8,128)S(1)} %reshape.237.refs_0_), custom_call_target="tpu_custom_call" | custom-call | bytes 8110080 | tf_op jit(solution)/shard_map/exchange_5/pallas_call | solution.py:451
  295.2 0.6 divide_multiply_fusion
  296.1 4.0 fusion.5
  300.1 5.5 fusion.1.refs_3_.refs_1_
  305.7 5.3 multiply_convert_fusion
  311.1 60.7 %exchange_6.1 = (bf16[4,2,2,2,32,1536]{5,4,3,2,1,0:T(8,128)(2,1)S(1)}, f32[32,1536]{1,0:T(8,128)S(1)}, f32[1,1536]{1,0:T(1,128)S(1)}, bf16[4,1536,384]{2,1,0:T(8,128)(2,1)S(1)}) custom-call(bf16[4,2,2,2,32,1536]{5,4,3,2,1,0:T(8,128)(2,1)S(1)} %bitcast.94, f32[32,1536]{1,0:T(8,128)S(1)} %copy-done.46, f32[8,1536]{1,0:T(8,128)S(1)} %get-tuple-element.104.refs_2_.gains_ref, ...), custom_call_target="tpu_custom_call" | custom-call | bytes 323543040 | tf_op jit(solution)/shard_map/exchange_6/pallas_call | solution.py:451
  371.8 6.9 %experts_backward.1 = (bf16[1024,1664]{1,0:T(8,128)(2,1)S(1)}, bf16[1024,1024]{1,0:T(8,128)(2,1)S(1)}) custom-call(s32[4]{0:T(128)S(1)} %iota_add_fusion.1.lane_ref, bf16[1024,1536]{1,0:T(8,128)(2,1)S(1)} %bitcast.91, f32[1024,1024]{1,0:T(8,128)S(1)} %copy-done.15, f32[1024,128]{1,0:T(8,128)S(1)} %copy-done.35, bf16[1536,1024]{1,0:T(8,128)(2,1)S(1)} %copy-done.21, ...), custom_call_target="tpu_custom_call" | custom-call | tf_op jit(solution)/shard_map/experts_backward/pallas_call | solution.py:614
  378.8 1.3 copy-done.59
  380.2 30.6 %exchange_8.1 = (f32[32,1664]{1,0:T(8,128)S(1)}, bf16[4,1536,384]{2,1,0:T(8,128)(2,1)S(1)}) custom-call(bf16[4,2,2,2,32,1664]{5,4,3,2,1,0:T(8,128)(2,1)S(1)} %bitcast.90, bf16[1536,1536]{1,0:T(8,128)(2,1)S(1)} %fusion.1.refs_3_.refs_1_, bf16[4,1536,384]{2,1,0:T(8,128)(2,1)S(1)} %get-tuple-element.115.refs_2_), custom_call_target="tpu_custom_call", output_to_operand_aliasing={{1}: (2, {})} | custom-call | bytes 355532800 | tf_op jit(solution)/shard_map/exchange_8/pallas_call | solution.py:451
  410.9 21.6 %attend_back.1 = (bf16[4,256,384]{2,1,0:T(8,128)(2,1)S(1)}, bf16[1536,2176]{1,0:T(8,128)(2,1)}, bf16[1536,2048]{1,0:T(8,128)(2,1)}) custom-call(s32[1]{0:T(128)S(1)} %bitcast.102, f32[32,1664]{1,0:T(8,128)S(1)} %get-tuple-element.116.back_ref, f32[32,128]{1,0:T(8,128)S(1)} %constant_dynamic-slice_fusion.gates_ref, f32[32,1536]{1,0:T(8,128)S(1)} %copy-done.44, ...), custom_call_target="tpu_custom_call" | custom-call | tf_op jit(solution)/shard_map/attend_back/pallas_call | solution.py:917
  432.5 91.2 %exchange_9.1 = (bf16[4,48,4224]{2,1,0:T(8,128)(2,1)}, bf16[4,2,2,2,256,384]{5,4,3,2,1,0:T(8,128)(2,1)}, bf16[4,1536,384]{2,1,0:T(8,128)(2,1)S(1)}) custom-call(bf16[4,2,2,2,48,2176]{5,4,3,2,1,0:T(8,128)(2,1)} %bitcast.110, bf16[4,2,2,2,48,2048]{5,4,3,2,1,0:T(8,128)(2,1)} %bitcast.112, ...), custom_call_target="tpu_custom_call", output_to_operand_aliasing={{2}: (4, {})} | custom-call | bytes 716636160 | tf_op jit(solution)/shard_map/exchange_9/pallas_call | solution.py:451
  523.8 2.2 copy-done.4
  525.9 4.5 all-to-all-start.1
  530.5 0.7 copy.109.router
  532.0 0.7 copy.110.router_one
  532.7 0.7 copy.111.router_two
  534.6 32.0 %table_moments.1 = (f32[6144,384]{1,0:T(8,128)}, f32[6144,384]{1,0:T(8,128)}, f32[6144,384]{1,0:T(8,128)}, f32[8,128]{1,0:T(8,128)}) custom-call(s32[32,256]{1,0:T(8,128)} %copy-done.38, s32[32]{0:T(128)} %copy-done.55, f32[2]{0:T(128)} %pad_maximum_fusion.3.scale_ref, bf16[32,256,384]{2,1,0:T(8,128)(2,1)} %bitcast.111, bf16[6144,384]{1,0:T(8,128)(2,1)} %bitcast.82, ...), custom_call_target="tpu_custom_call" | custom-call | tf_op jit(solution)/shard_map/table_moments/pallas_call | solution.py:1088
  566.7 3.5 fusion.19.down_grad
  570.2 5.4 fusion.18.grad_ref
  575.6 1.2 copy-done.64
  576.8 4.3 small_moments.1
  581.1 1.3 add.98.other_norms
  582.4 27.1 %expert_moments.1 = (f32[12288,128]{1,0:T(8,128)}, f32[12288,128]{1,0:T(8,128)}, f32[12288,128]{1,0:T(8,128)}, f32[512,1536]{1,0:T(8,128)}, f32[512,1536]{1,0:T(...) custom-call(f32[2]{0:T(128)} %pad_maximum_fusion.3.scale_ref, f32[8,128]{1,0:T(8,128)} %add.98.other_norms, ...), custom_call_target="tpu_custom_call" | custom-call | tf_op jit(solution)/shard_map/expert_moments/pallas_call | solution.py:687
  609.5 0.7 copy-done.56
  610.2 14.4 %exchange_10.1 = f32[4,8,8,128]{3,2,1,0:T(8,128)S(1)} custom-call(f32[8,128]{1,0:T(8,128)S(1)} %copy-done.56), custom_call_target="tpu_custom_call" | custom-call | bytes 2703360 | tf_op jit(solution)/shard_map/exchange_10/pallas_call | solution.py:451
  625.3 0.7 copy.116
  627.3 0.7 copy.113
  628.0 0.7 copy.114
  628.6 0.7 copy.115
  629.9 20.8 %finish.1 = (f32[6144,384]{1,0:T(8,128)}, f32[12288,128]{1,0:T(8,128)}, f32[512,1536]{1,0:T(8,128)}, f32[48,2560]{1,0:T(8,128)}, f32[48,1536]{1,0:T(8,128)}) custom-call(f32[32,8,128]{2,1,0:T(8,128)} %bitcast.97, f32[6144,384]{1,0:T(8,128)} %refs_0_.1, f32[6144,384]{1,0:T(8,128)} %get-tuple-element.137.refs_1_, f32[12288,128]{1,0:T(8,128)} %bitcast.107, ...), custom_call_target="tpu_custom_call" | custom-call | tf_op jit(solution)/shard_map/finish/pallas_call | solution.py:1194
  (207 shorter events, 6.2 us)
Async XLA Ops:
  20.3 42.6 %all-to-all-start = ((bf16[4,48,4224]{2,1,0:T(8,128)(2,1)}), bf16[4,48,4224]{2,1,0:T(8,128)(2,1)S(1)}, u32[]{:S(2)}, u32[]{:S(2)}) async-start(bf16[4,48,4224]{2,1,0:T(8,128)(2,1)} %broadcast_in_dim.42), calls=%async_computation | async-start | bytes 3244032 | tf_op jit(solution)/shard_map/all_to_all | solution.py:1342
  24.7 20.4 %copy-start.55 = (s32[32]{0:T(128)}, s32[32]{0:T(128)S(1)}, u32[]{:S(2)}) copy-start(s32[32]{0:T(128)S(1)} %get-tuple-element.261.count_ref) | copy-start | bytes 388
  25.2 135.5 %copy-start.25 = (f32[256,128]{1,0:T(8,128)}, f32[256,128]{1,0:T(8,128)S(1)}, u32[]{:S(2)}) copy-start(f32[256,128]{1,0:T(8,128)S(1)} %copy.104.cos_ref) | copy-start | bytes 393220
  35.9 15.3 %copy-start.78 = (s32[16,2]{0,1:T(2,128)S(1)}, s32[16,2]{0,1:T(2,128)}, u32[]{:S(2)}) copy-start(s32[16,2]{0,1:T(2,128)} %param.29) | copy-start | bytes 388
  51.2 109.5 %copy-start.47 = (f32[32,128]{1,0:T(8,128)}, f32[32,128]{1,0:T(8,128)S(1)}, u32[]{:S(2)}) copy-start(f32[32,128]{1,0:T(8,128)S(1)} %get-tuple-element.281.sin_rows) | copy-start | bytes 49156
  51.2 109.5 %copy-start.49 = (f32[32,128]{1,0:T(8,128)}, f32[32,128]{1,0:T(8,128)S(1)}, u32[]{:S(2)}) copy-start(f32[32,128]{1,0:T(8,128)S(1)} %get-tuple-element.282.cos_rows) | copy-start | bytes 49156
  65.2 108.2 %slice-start = ((s8[4718592]{0:T(1024)(128)(4,1)}), s8[524288]{0:T(1024)(128)(4,1)S(1)}, s32[]{:S(2)}) async-start(s8[4718592]{0:T(1024)(128)(4,1)} %bitcast.83), calls=%async_computation.2 | async-start | bytes 1048576
  160.7 11.1 %copy-start.8 = (bf16[4,2,2,2,48,2048]{5,4,3,2,1,0:T(8,128)(2,1)}, bf16[4,2,2,2,48,2048]{5,4,3,2,1,0:T(8,128)(2,1)S(1)}, u32[]{:S(2)}) copy-start(bf16[4,2,2,2,48,2048]{5,4,3,2,1,0:T(8,128)(2,1)S(1)} %get-tuple-element.98) | copy-start | bytes 18874372
  160.7 11.1 %copy-start.16 = (bf16[4,256,384]{2,1,0:T(8,128)(2,1)}, bf16[4,256,384]{2,1,0:T(8,128)(2,1)S(1)}, u32[]{:S(2)}) copy-start(bf16[4,256,384]{2,1,0:T(8,128)(2,1)S(1)} %get-tuple-element.96.picked_ref) | copy-start | bytes 2359300
  160.7 5.4 copy-start.3
  166.2 7.2 %slice-start.1 = ((s8[4718592]{0:T(1024)(128)(4,1)}), s8[4194304]{0:T(1024)(128)(4,1)S(1)}, s32[]{:S(2)}) async-start(s8[4718592]{0:T(1024)(128)(4,1)} %bitcast.83), calls=%async_computation.3 | async-start | bytes 8388608
  166.2 7.3 %copy-start.10 = (bf16[1536,1536]{1,0:T(8,128)(2,1)S(1)}, bf16[1536,1536]{1,0:T(8,128)(2,1)}, u32[]{:S(2)}) copy-start(bf16[1536,1536]{1,0:T(8,128)(2,1)} %copy-done.9) | copy-start | bytes 14155780
  173.4 26.3 %copy-start.30 = (bf16[256,1536]{1,0:T(8,128)(2,1)}, bf16[256,1536]{1,0:T(8,128)(2,1)S(1)}, u32[]{:S(2)}) copy-start(bf16[256,1536]{1,0:T(8,128)(2,1)S(1)} %get-tuple-element.124.normed_ref) | copy-start | bytes 2359300
  173.4 26.3 %copy-start.36 = (bf16[32,1536]{1,0:T(8,128)(2,1)}, bf16[32,1536]{1,0:T(8,128)(2,1)S(1)}, u32[]{:S(2)}) copy-start(bf16[32,1536]{1,0:T(8,128)(2,1)S(1)} %get-tuple-element.99.refs_0_.c_ref) | copy-start | bytes 294916
  173.4 26.3 %copy-start.39 = (bf16[256,512]{1,0:T(8,128)(2,1)}, bf16[256,512]{1,0:T(8,128)(2,1)S(1)}, u32[]{:S(2)}) copy-start(bf16[256,512]{1,0:T(8,128)(2,1)S(1)} %get-tuple-element.121.key_ref) | copy-start | bytes 786436
  173.4 26.3 %copy-start.41 = (bf16[256,512]{1,0:T(8,128)(2,1)}, bf16[256,512]{1,0:T(8,128)(2,1)S(1)}, u32[]{:S(2)}) copy-start(bf16[256,512]{1,0:T(8,128)(2,1)S(1)} %get-tuple-element.122.value_ref) | copy-start | bytes 786436
  173.4 26.3 %copy-start.53 = (bf16[32,1536]{1,0:T(8,128)(2,1)}, bf16[32,1536]{1,0:T(8,128)(2,1)S(1)}, u32[]{:S(2)}) copy-start(bf16[32,1536]{1,0:T(8,128)(2,1)S(1)} %get-tuple-element.123.mixed_ref) | copy-start | bytes 294916
  173.4 46.5 %copy-start.32 = (f32[32,1536]{1,0:T(8,128)}, f32[32,1536]{1,0:T(8,128)S(1)}, u32[]{:S(2)}) copy-start(f32[32,1536]{1,0:T(8,128)S(1)} %get-tuple-element.103.refs_1_.resid_ref) | copy-start | bytes 589828
  173.4 30.1 %copy-start.24 = (s32[1024,8]{1,0:T(8,128)S(1)}, s32[1024,8]{1,0:T(8,128)}, u32[]{:S(2)}) copy-start(s32[1024,8]{1,0:T(8,128)} %reshape.233.routes_ref) | copy-start | bytes 98308
  203.6 16.3 %copy-start.12 = (bf16[1536,1536]{1,0:T(8,128)(2,1)S(1)}, bf16[1536,1536]{1,0:T(8,128)(2,1)}, u32[]{:S(2)}) copy-start(bf16[1536,1536]{1,0:T(8,128)(2,1)} %copy-done.11) | copy-start | bytes 14155780
  219.9 54.2 %copy-start.20 = (bf16[1536,1024]{1,0:T(8,128)(2,1)}, bf16[1536,1024]{1,0:T(8,128)(2,1)S(1)}, u32[]{:S(2)}) copy-start(bf16[1536,1024]{1,0:T(8,128)(2,1)S(1)} %get-tuple-element.112.cat_ref) | copy-start | bytes 9437188
  219.9 54.2 %copy-start.34 = (f32[1024,128]{1,0:T(8,128)}, f32[1024,128]{1,0:T(8,128)S(1)}, u32[]{:S(2)}) copy-start(f32[1024,128]{1,0:T(8,128)S(1)} %get-tuple-element.111.gates_ref) | copy-start | bytes 1572868
  274.0 5.2 copy-start.13
  274.1 5.2 copy-start.66
  279.3 15.7 %copy-start.79 = (f32[32]{0:T(128)S(1)}, f32[32]{0:T(128)}, u32[]{:S(2)}) copy-start(f32[32]{0:T(128)} %param.30) | copy-start | bytes 388
  279.3 15.7 %copy-start.74 = (s32[16]{0:T(128)S(1)}, s32[16]{0:T(128)}, u32[]{:S(2)}) copy-start(s32[16]{0:T(128)} %get-tuple-element.272) | copy-start | bytes 196
  279.3 15.7 %copy-start.75 = (s32[16]{0:T(128)S(1)}, s32[16]{0:T(128)}, u32[]{:S(2)}) copy-start(s32[16]{0:T(128)} %get-tuple-element.273) | copy-start | bytes 196
  296.1 9.6 %slice-start.2 = ((s8[4718592]{0:T(1024)(128)(4,1)}), s8[4194304]{0:T(1024)(128)(4,1)S(1)}, s32[]{:S(2)}) async-start(s8[4718592]{0:T(1024)(128)(4,1)} %bitcast.87), calls=%async_computation.4 | async-start | bytes 8388608
  300.1 5.6 slice-start.3
  305.7 74.4 %copy-start.7 = (bf16[1536,1536]{1,0:T(8,128)(2,1)}, bf16[1536,1536]{1,0:T(8,128)(2,1)S(1)}, u32[]{:S(2)}) copy-start(bf16[1536,1536]{1,0:T(8,128)(2,1)S(1)} %fusion.1.refs_3_.refs_1_) | copy-start | bytes 14155780
  305.7 5.3 copy-start.35
  305.7 5.3 copy-start.46
  311.0 60.8 %copy-start.15 = (f32[1024,1024]{1,0:T(8,128)S(1)}, f32[1024,1024]{1,0:T(8,128)}, u32[]{:S(2)}) copy-start(f32[1024,1024]{1,0:T(8,128)} %get-tuple-element.110.mid_ref) | copy-start | bytes 12582916
  311.0 60.8 %copy-start.21 = (bf16[1536,1024]{1,0:T(8,128)(2,1)S(1)}, bf16[1536,1024]{1,0:T(8,128)(2,1)}, u32[]{:S(2)}) copy-start(bf16[1536,1024]{1,0:T(8,128)(2,1)} %copy-done.20) | copy-start | bytes 9437188
  371.8 6.9 %copy-start.18 = (bf16[4,2,2,2,32,1536]{5,4,3,2,1,0:T(8,128)(2,1)}, bf16[4,2,2,2,32,1536]{5,4,3,2,1,0:T(8,128)(2,1)S(1)}, u32[]{:S(2)}) copy-start(bf16[4,2,2,2,32,1536]{5,4,3,2,1,0:T(8,128)(2,1)S(1)} %get-tuple-element.109) | copy-start | bytes 9437188
  371.8 6.9 %copy-start.43 = (f32[32,1536]{1,0:T(8,128)}, f32[32,1536]{1,0:T(8,128)S(1)}, u32[]{:S(2)}) copy-start(f32[32,1536]{1,0:T(8,128)S(1)} %get-tuple-element.117.grad_two_ref) | copy-start | bytes 589828
  380.1 30.7 %copy-start.17 = (bf16[4,256,384]{2,1,0:T(8,128)(2,1)S(1)}, bf16[4,256,384]{2,1,0:T(8,128)(2,1)}, u32[]{:S(2)}) copy-start(bf16[4,256,384]{2,1,0:T(8,128)(2,1)} %copy-done.16) | copy-start | bytes 2359300
  380.1 30.7 %copy-start.26 = (f32[256,128]{1,0:T(8,128)S(1)}, f32[256,128]{1,0:T(8,128)}, u32[]{:S(2)}) copy-start(f32[256,128]{1,0:T(8,128)} %copy-done.25) | copy-start | bytes 393220
  380.1 30.7 %copy-start.29 = (f32[8,96,256]{2,1,0:T(8,128)S(1)}, f32[8,96,256]{2,1,0:T(8,128)}, u32[]{:S(2)}) copy-start(f32[8,96,256]{2,1,0:T(8,128)} %copy-done.28) | copy-start | bytes 2359300
  380.1 30.7 %copy-start.31 = (bf16[256,1536]{1,0:T(8,128)(2,1)S(1)}, bf16[256,1536]{1,0:T(8,128)(2,1)}, u32[]{:S(2)}) copy-start(bf16[256,1536]{1,0:T(8,128)(2,1)} %copy-done.30) | copy-start | bytes 2359300
  380.1 30.7 %copy-start.33 = (f32[32,1536]{1,0:T(8,128)S(1)}, f32[32,1536]{1,0:T(8,128)}, u32[]{:S(2)}) copy-start(f32[32,1536]{1,0:T(8,128)} %copy-done.32) | copy-start | bytes 589828
  380.1 30.7 %copy-start.37 = (bf16[32,1536]{1,0:T(8,128)(2,1)S(1)}, bf16[32,1536]{1,0:T(8,128)(2,1)}, u32[]{:S(2)}) copy-start(bf16[32,1536]{1,0:T(8,128)(2,1)} %copy-done.36) | copy-start | bytes 294916
  380.1 30.7 %copy-start.40 = (bf16[256,512]{1,0:T(8,128)(2,1)S(1)}, bf16[256,512]{1,0:T(8,128)(2,1)}, u32[]{:S(2)}) copy-start(bf16[256,512]{1,0:T(8,128)(2,1)} %copy-done.39) | copy-start | bytes 786436
  380.1 30.7 %copy-start.42 = (bf16[256,512]{1,0:T(8,128)(2,1)S(1)}, bf16[256,512]{1,0:T(8,128)(2,1)}, u32[]{:S(2)}) copy-start(bf16[256,512]{1,0:T(8,128)(2,1)} %copy-done.41) | copy-start | bytes 786436
  380.1 30.7 %copy-start.44 = (f32[32,1536]{1,0:T(8,128)S(1)}, f32[32,1536]{1,0:T(8,128)}, u32[]{:S(2)}) copy-start(f32[32,1536]{1,0:T(8,128)} %copy-done.43) | copy-start | bytes 589828
  380.2 30.7 %copy-start.48 = (f32[32,128]{1,0:T(8,128)S(1)}, f32[32,128]{1,0:T(8,128)}, u32[]{:S(2)}) copy-start(f32[32,128]{1,0:T(8,128)} %copy-done.47) | copy-start | bytes 49156
  380.2 30.7 %copy-start.50 = (f32[32,128]{1,0:T(8,128)S(1)}, f32[32,128]{1,0:T(8,128)}, u32[]{:S(2)}) copy-start(f32[32,128]{1,0:T(8,128)} %copy-done.49) | copy-start | bytes 49156
  380.2 30.7 %copy-start.52 = (bf16[32,1536]{1,0:T(8,128)(2,1)S(1)}, bf16[32,1536]{1,0:T(8,128)(2,1)}, u32[]{:S(2)}) copy-start(bf16[32,1536]{1,0:T(8,128)(2,1)} %copy-done.51) | copy-start | bytes 294916
  380.2 30.7 %copy-start.54 = (bf16[32,1536]{1,0:T(8,128)(2,1)S(1)}, bf16[32,1536]{1,0:T(8,128)(2,1)}, u32[]{:S(2)}) copy-start(bf16[32,1536]{1,0:T(8,128)(2,1)} %copy-done.53) | copy-start | bytes 294916
  432.5 98.0 %copy-start.67 = (f32[48,32]{0,1:T(8,128)S(1)}, f32[48,32]{0,1:T(8,128)}, u32[]{:S(2)}) copy-start(f32[48,32]{0,1:T(8,128)} %param.42) | copy-start | bytes 18436
  432.5 99.5 %copy-start.72 = (f32[48,32]{0,1:T(8,128)S(1)}, f32[48,32]{0,1:T(8,128)}, u32[]{:S(2)}) copy-start(f32[48,32]{0,1:T(8,128)} %param.43) | copy-start | bytes 18436
  432.5 100.2 %copy-start.73 = (f32[48,32]{0,1:T(8,128)S(1)}, f32[48,32]{0,1:T(8,128)}, u32[]{:S(2)}) copy-start(f32[48,32]{0,1:T(8,128)} %param.44) | copy-start | bytes 18436
  525.9 49.7 %all-to-all-start.1 = ((bf16[4,48,4224]{2,1,0:T(8,128)(2,1)}), bf16[4,48,4224]{2,1,0:T(8,128)(2,1)S(1)}, u32[]{:S(2)}, u32[]{:S(2)}) async-start(bf16[4,48,4224]{2,1,0:T(8,128)(2,1)} %get-tuple-element.132), calls=%async_computation.1 | async-start | bytes 3244032 | tf_op jit(solution)/shard_map/all_to_all | solution.py:1462
  534.6 32.1 %copy-start.19 = (bf16[4,2,2,2,32,1536]{5,4,3,2,1,0:T(8,128)(2,1)S(1)}, bf16[4,2,2,2,32,1536]{5,4,3,2,1,0:T(8,128)(2,1)}, u32[]{:S(2)}) copy-start(bf16[4,2,2,2,32,1536]{5,4,3,2,1,0:T(8,128)(2,1)} %copy-done.18) | copy-start | bytes 9437188
  534.6 32.1 %copy-start.62 = (bf16[1024,512]{1,0:T(8,128)(2,1)S(1)}, bf16[1024,512]{1,0:T(8,128)(2,1)}, u32[]{:S(2)}) copy-start(bf16[1024,512]{1,0:T(8,128)(2,1)} %copy-done.61) | copy-start | bytes 3145732
  570.2 10.9 %copy-start.76 = (f32[8,128]{1,0:T(8,128)S(1)}, f32[8,128]{1,0:T(8,128)}, u32[]{:S(2)}) copy-start(f32[8,128]{1,0:T(8,128)} %get-tuple-element.131) | copy-start | bytes 12292
  582.3 44.9 %copy-start.65 = (f32[48,32]{1,0:T(8,128)S(1)}, f32[48,32]{1,0:T(8,128)}, u32[]{:S(2)}) copy-start(f32[48,32]{1,0:T(8,128)} %copy.109.router) | copy-start | bytes 18436
  582.3 44.9 %copy-start.70 = (f32[48,32]{1,0:T(8,128)S(1)}, f32[48,32]{1,0:T(8,128)}, u32[]{:S(2)}) copy-start(f32[48,32]{1,0:T(8,128)} %get-tuple-element.151) | copy-start | bytes 18436
  582.4 45.6 %copy-start.69 = (f32[48,32]{1,0:T(8,128)S(1)}, f32[48,32]{1,0:T(8,128)}, u32[]{:S(2)}) copy-start(f32[48,32]{1,0:T(8,128)} %get-tuple-element.243) | copy-start | bytes 18436
  582.4 46.3 %copy-start.68 = (f32[48,32]{1,0:T(8,128)S(1)}, f32[48,32]{1,0:T(8,128)}, u32[]{:S(2)}) copy-start(f32[48,32]{1,0:T(8,128)} %get-tuple-element.244) | copy-start | bytes 18436
  582.4 47.0 %copy-start.71 = (f32[3,48]{1,0:T(4,128)S(1)}, f32[3,48]{1,0:T(4,128)}, u32[]{:S(2)}) copy-start(f32[3,48]{1,0:T(4,128)} %gains.1) | copy-start | bytes 1732
  582.4 47.0 %copy-start.77 = (f32[3,48]{1,0:T(4,128)S(1)}, f32[3,48]{1,0:T(4,128)}, u32[]{:S(2)}) copy-start(f32[3,48]{1,0:T(4,128)} %get-tuple-element.154) | copy-start | bytes 1732
  624.5 5.4 copy-start.27
  629.9 20.8 %copy-start.1 = (s32[256,8]{0,1:T(8,128)S(1)}, s32[256,8]{0,1:T(8,128)}, u32[]{:S(2)}) copy-start(s32[256,8]{0,1:T(8,128)} %param.31) | copy-start | bytes 24580
  (22 other events, 52.6 us)

commit v10 on v9

--- a/solution.py
+++ b/solution.py
@@ -639,7 +639,7 @@
 
 
 def moments_kernel(
-    scale_ref, other_norms, grad_ref, w_ref, first_ref, second_ref, down_grad, down_w, down_first, down_second,
+    scale_ref, table_norms, small_norms, grad_ref, w_ref, first_ref, second_ref, down_grad, down_w, down_first, down_second,
     new_first, new_second, updates, new_down_first, new_down_second, down_updates, norms, sums, down_sums, turned,
 ):
     units = w_ref.shape[1]
@@ -673,10 +673,10 @@
     def _():
         block = norm_cells(5, total_of(sums[0]), total_of(sums[1]))
         block += norm_cells(6, total_of(down_sums[0]), total_of(down_sums[1]))
-        norms[...] = other_norms[...] + block
-
-
-def expert_moments(scales, norms, grad, weight, first, second, *down_state):
+        norms[...] = table_norms[...] + small_norms[...] + block
+
+
+def expert_moments(scales, table_norms, small_norms, grad, weight, first, second, *down_state):
     units = weight.shape[1]
     down = down_state[1]
     number = grad.shape[1] // (2 * units)
@@ -689,7 +689,7 @@
         grid_spec=pltpu.PrefetchScalarGridSpec(
             num_scalar_prefetch=1,
             grid=(number, parts),
-            in_specs=[cells, pl.BlockSpec((D // parts, 2 * units), lambda e, p, *_: (p, e))]
+            in_specs=[cells, cells, pl.BlockSpec((D // parts, 2 * units), lambda e, p, *_: (p, e))]
             + [row] * 3
             + [down_row] * 4,
             out_specs=[row] * 3 + [down_row] * 3 + [cells],
@@ -704,7 +704,7 @@
         + [jax.ShapeDtypeStruct((8, 128), f32)],
         compiler_params=pltpu.CompilerParams(vmem_limit_bytes=62 << 20),
         name="expert_moments",
-    )(scales, norms, grad, weight, first, second, *down_state)
+    )(scales, table_norms, small_norms, grad, weight, first, second, *down_state)
 
 
 HEAD_COLS = QUERY_HEADS * HEAD_WIDTH
@@ -1123,21 +1123,21 @@
         total += grad_ref[z].astype(f32)
     packs = (total[:, :PACK], total[:, PACK:])
     wide = HEAD_COLS + KEY_COLS
-    pick = lax.broadcasted_iota(jnp.int32, (8, 128), 0) + EXPERTS
-    pick = (pick == lax.broadcasted_iota(jnp.int32, (8, 128), 1)).astype(f32)
-    gains_grad = lax.dot_general(
+    pick = lax.broadcasted_iota(jnp.int32, (EXPERTS + 8, 128), 0)
+    pick = (pick == lax.broadcasted_iota(jnp.int32, (EXPERTS + 8, 128), 1)).astype(f32)
+    turned = lax.dot_general(
         pick,
         packs[0][:, wide:],
         ACROSS,
         preferred_element_type=f32,
         precision=lax.Precision.HIGHEST,
-    )[:3]
+    )
     block = jnp.zeros((8, 128), f32)
     sets = [
         (qkv, qkv_one, qkv_two, jnp.concatenate([packs[0][:, :wide], packs[1][:, :KEY_COLS]], axis=1)),
         (out, out_one, out_two, packs[1][:, KEY_COLS : KEY_COLS + D]),
-        (router, router_one, router_two, packs[0][:, wide : wide + EXPERTS]),
-        (gains, gains_one, gains_two, gains_grad),
+        (router, router_one, router_two, turned[:EXPERTS]),
+        (gains, gains_one, gains_two, turned[EXPERTS : EXPERTS + 3]),
     ]
     for n, (weight, first, second, grad) in enumerate(sets):
         one, two, update = lamb_parts(weight[...], first[...], second[...], grad, scales)
@@ -1487,16 +1487,17 @@
         out_weight,
         out_first,
         out_second,
-        router_weight,
-        router_first,
-        router_second,
+        router_weight.T,
+        router_first.T,
+        router_second.T,
         norm_gains,
         gains_first,
         gains_second,
     )
     in_one, in_two, in_update, down_one, down_two, down_update, expert_norms = expert_moments(
         scales,
-        table_norms + small_norms,
+        table_norms,
+        small_norms,
         grad_in,
         in_rows,
         in_first.reshape(in_rows.shape),
@@ -1522,7 +1523,7 @@
         out_weight,
         small[5],
     )
-    new_router = router_weight - STEP_RATE * trust_ratio[3] * small[8]
+    new_router = (router_weight.T - STEP_RATE * trust_ratio[3] * small[8]).T
     new_gains = norm_gains - STEP_RATE * trust_ratio[4] * small[11]
     stats = jnp.stack([norm_values[:, 0], norm_values[:, 1], trust_ratio], axis=1)
     return (
@@ -1537,8 +1538,8 @@
         small[3],
         small[4],
         new_router,
-        small[6],
-        small[7],
+        small[6].T,
+        small[7].T,
         new_gains,
         small[9],
         small[10],

time: 657 us -> 653 us (level)
    unnamed x177 -> x161, local copies, waits for them, and re-layouts: 35.9 us -> 31.2 us
where the time goes in v10:
time: 653 us; the launch traced here: 648 us
  Pallas kernels  536 us (82%)
  local copies, waits for them, and re-layouts  38.6 us (6%)
  matrix products  25 us (4%)
  other arithmetic  20.7 us (3%)
  waiting for transfers between devices  11.9 us (2%)
  starting transfers between devices  8.89 us (1%)
    pallas_call x9, Pallas kernels, communicate(): pl.pallas_call(kernel, out_shape=[x for p in parts for x in p.outputs], i...  395 us
    pallas_call x1, Pallas kernels, table_moments(): pl.pallas_call(table_kernel, grid_spec=pltpu.PrefetchScalarGridSpec(num_s...  31.6 us
    unnamed x161, local copies, waits for them, and re-layouts  31.2 us
    pallas_call x1, Pallas kernels, expert_moments(): pl.pallas_call(moments_kernel, grid_spec=pltpu.PrefetchScalarGridSpec(num...  27 us
    pallas_call x1, Pallas kernels, attend_back(): pl.pallas_call(attend_back_kernel, in_specs=[pl.BlockSpec(memory_space=pl...  21.6 us
    pallas_call x1, Pallas kernels, finish(): pl.pallas_call(finish_kernel, grid=(FINISH_PARTS,), in_specs=[pl.BlockSpe...  20.8 us
    pallas_call x1, Pallas kernels, experts_forward(): pl.pallas_call(forward_kernel, grid_spec=pltpu.PrefetchScalarGridSpec(num...  15.3 us
  transfers between devices with their start and end apart: 2, of which 1 were waited for; matrix products, arithmetic and copies ran while one was open for 3% of the time, Pallas kernels for 6%

profile of v10, /device:TPU:0, one launch (start us, length us, event | category | flops | bytes accessed | tf_op | source)
XLA Modules:
  0.0 647.6 jit_solution(5104173021492124216)
XLA Ops:
  0.7 0.7 fusion.31
  1.4 0.7 constant_dynamic-slice_fusion.4
  2.1 1.1 convert.18
  3.2 0.7 convert_bitcast_fusion
  3.9 0.7 convert.19
  5.2 0.8 dynamic_slice.20
  6.0 11.9 %exchange_0.1 = s32[4,8,8,128]{3,2,1,0:T(8,128)S(1)} custom-call(s32[8,128]{1,0:T(8,128)S(1)} %add_bitcast_fusion.refs_0_), custom_call_target="tpu_custom_call" | custom-call | bytes 2703360 | tf_op jit(solution)/shard_map/exchange_0/pallas_call | solution.py:451
  18.0 1.0 convert.21
  19.1 1.3 broadcast_in_dim.42
  20.3 4.3 all-to-all-start
  25.1 0.8 select_reduce_fusion.1
  25.9 0.7 eq.85
  26.7 1.1 reshape.233.routes_ref
  28.0 4.8 select_reduce_fusion
  32.8 3.7 copy-done.2
  36.5 8.4 %gather_rows.1 = (bf16[32,256,384]{2,1,0:T(8,128)(2,1)S(1)}, bf16[6144,384]{1,0:T(8,128)(2,1)S(1)}) custom-call(s32[32,256]{1,0:T(8,128)S(1)} %fusion.12.list_ref, s32[32]{0:T(128)S(1)} %get-tuple-element.215.count_ref, f32[6144,384]{1,0:T(8,128)S(1)} %copy-done.2), custom_call_target="tpu_custom_call" | custom-call | tf_op jit(solution)/shard_map/gather_rows/pallas_call | solution.py:981
  44.9 2.2 copy-done.5
  47.1 2.7 copy-done.14
  49.8 0.6 iota_add_fusion
  50.4 0.5 slice_bitcast_fusion.1
  51.0 11.9 %all-to-all-done.refs_0_ = bf16[4,48,4224]{2,1,0:T(8,128)(2,1)S(1)} async-done(((bf16[4,48,4224]{2,1,0:T(8,128)(2,1)}), bf16[4,48,4224]{2,1,0:T(8,128)(2,1)S(1)}, u32[]{:S(2)}, u32[]{:S(2)}) %all-to-all-start) | async-done | bytes 1622048 | tf_op jit(solution)/shard_map/all_to_all | solution.py:1342
  62.9 2.3 copy-done.6
  65.2 93.3 %exchange_1.1 = (bf16[4,2,2,2,48,2176]{5,4,3,2,1,0:T(8,128)(2,1)}, bf16[4,2,2,2,48,2048]{5,4,3,2,1,0:T(8,128)(2,1)S(1)}, bf16[4,256,384]{2,1,0:T(8,128)(2,1)S(1)}, bf16[1536,1536]{1,0:T(8,128)(2,1)S(1)}) custom-call(bf16[4,48,4224]{2,1,0:T(8,128)(2,1)S(1)} %all-to-all-done.refs_0_, bf16[4,2,2,2,256,384]{5,4,3,2,1,0:T(8,128)(2,1)} %bitcast.97, ...), custom_call_target="tpu_custom_call" | custom-call | bytes 622264320 | tf_op jit(solution)/shard_map/exchange_1/pallas_call | solution.py:451
  158.6 2.2 copy-done.9
  160.8 5.4 copy-done.3
  166.2 5.7 attend.1
  171.9 0.9 copy-done.28
  172.8 0.6 copy-done.51
  173.5 26.2 %exchange_2.1 = (bf16[4,2,2,2,32,1536]{5,4,3,2,1,0:T(8,128)(2,1)S(1)}, bf16[1536,1536]{1,0:T(8,128)(2,1)S(1)}) custom-call(bf16[32,1536]{1,0:T(8,128)(2,1)S(1)} %get-tuple-element.99.refs_0_.c_ref, bf16[6144,384]{1,0:T(8,128)(2,1)S(1)} %bitcast.92, bf16[1536,1536]{1,0:T(8,128)(2,1)S(1)} %copy-done.10), custom_call_target="tpu_custom_call", output_to_operand_aliasing={{1}: (2, {})} | custom-call | bytes 347996160 | tf_op jit(solution)/shard_map/exchange_2/pallas_call | solution.py:451
  199.8 2.2 copy-done.11
  201.9 1.7 copy-done.22
  203.6 15.3 %experts_forward.1 = (bf16[1024,1536]{1,0:T(8,128)(2,1)S(1)}, f32[1024,1024]{1,0:T(8,128)}, f32[1024,128]{1,0:T(8,128)S(1)}, bf16[1536,1024]{1,0:T(8,128)(2,1)S(...) custom-call(s32[4]{0:T(128)S(1)} %iota_add_fusion.1.lane_ref, bf16[1024,1536]{1,0:T(8,128)(2,1)} %bitcast.103, ...), custom_call_target="tpu_custom_call" | custom-call | tf_op jit(solution)/shard_map/experts_forward/pallas_call | solution.py:535
  218.9 1.0 copy-done.61
  219.9 54.2 %exchange_3.1 = (bf16[4,2,2,2,32,1536]{5,4,3,2,1,0:T(8,128)(2,1)S(1)}, f32[32,1536]{1,0:T(8,128)S(1)}, bf16[1536,1536]{1,0:T(8,128)(2,1)S(1)}) custom-call(bf16[4,2,2,2,32,1536]{5,4,3,2,1,0:T(8,128)(2,1)S(1)} %bitcast.101, f32[32,1536]{1,0:T(8,128)S(1)} %get-tuple-element.103.refs_1_.resid_ref, ...), custom_call_target="tpu_custom_call", output_to_operand_aliasing={{2}: (4, {})} | custom-call | bytes 417792000 | tf_op jit(solution)/shard_map/exchange_3/pallas_call | solution.py:451
  274.2 5.2 multiply_reduce_fusion
  279.4 3.0 exponential_reduce_fusion
  282.5 11.7 %exchange_5.1 = f32[4,8,8,384]{3,2,1,0:T(8,128)S(1)} custom-call(f32[8,384]{1,0:T(8,128)S(1)} %reshape.237.refs_0_), custom_call_target="tpu_custom_call" | custom-call | bytes 8110080 | tf_op jit(solution)/shard_map/exchange_5/pallas_call | solution.py:451
  294.4 0.3 fusion.16
  295.3 0.6 divide_multiply_fusion
  296.1 4.0 fusion.5
  300.2 5.3 multiply_convert_fusion
  305.5 5.5 fusion.1.refs_3_.refs_1_
  311.1 60.7 %exchange_6.1 = (bf16[4,2,2,2,32,1536]{5,4,3,2,1,0:T(8,128)(2,1)S(1)}, f32[32,1536]{1,0:T(8,128)S(1)}, f32[1,1536]{1,0:T(1,128)S(1)}, bf16[4,1536,384]{2,1,0:T(8,128)(2,1)S(1)}) custom-call(bf16[4,2,2,2,32,1536]{5,4,3,2,1,0:T(8,128)(2,1)S(1)} %bitcast.102, f32[32,1536]{1,0:T(8,128)S(1)} %copy-done.46, f32[8,1536]{1,0:T(8,128)S(1)} %get-tuple-element.104.refs_2_.gains_ref, ...), custom_call_target="tpu_custom_call" | custom-call | bytes 323543040 | tf_op jit(solution)/shard_map/exchange_6/pallas_call | solution.py:451
  371.9 6.9 %experts_backward.1 = (bf16[1024,1664]{1,0:T(8,128)(2,1)S(1)}, bf16[1024,1024]{1,0:T(8,128)(2,1)S(1)}) custom-call(s32[4]{0:T(128)S(1)} %iota_add_fusion.1.lane_ref, bf16[1024,1536]{1,0:T(8,128)(2,1)S(1)} %bitcast.99, f32[1024,1024]{1,0:T(8,128)S(1)} %copy-done.15, f32[1024,128]{1,0:T(8,128)S(1)} %copy-done.35, bf16[1536,1024]{1,0:T(8,128)(2,1)S(1)} %copy-done.21, ...), custom_call_target="tpu_custom_call" | custom-call | tf_op jit(solution)/shard_map/experts_backward/pallas_call | solution.py:614
  378.8 1.3 copy-done.59
  380.2 30.1 %exchange_8.1 = (f32[32,1664]{1,0:T(8,128)S(1)}, bf16[4,1536,384]{2,1,0:T(8,128)(2,1)S(1)}) custom-call(bf16[4,2,2,2,32,1664]{5,4,3,2,1,0:T(8,128)(2,1)S(1)} %bitcast.98, bf16[1536,1536]{1,0:T(8,128)(2,1)S(1)} %fusion.1.refs_3_.refs_1_, bf16[4,1536,384]{2,1,0:T(8,128)(2,1)S(1)} %get-tuple-element.115.refs_2_), custom_call_target="tpu_custom_call", output_to_operand_aliasing={{1}: (2, {})} | custom-call | bytes 355532800 | tf_op jit(solution)/shard_map/exchange_8/pallas_call | solution.py:451
  410.5 21.6 %attend_back.1 = (bf16[4,256,384]{2,1,0:T(8,128)(2,1)S(1)}, bf16[1536,2176]{1,0:T(8,128)(2,1)}, bf16[1536,2048]{1,0:T(8,128)(2,1)}) custom-call(s32[1]{0:T(128)S(1)} %bitcast.110, f32[32,1664]{1,0:T(8,128)S(1)} %get-tuple-element.116.back_ref, f32[32,128]{1,0:T(8,128)S(1)} %constant_dynamic-slice_fusion.gates_ref, f32[32,1536]{1,0:T(8,128)S(1)} %copy-done.44, ...), custom_call_target="tpu_custom_call" | custom-call | tf_op jit(solution)/shard_map/attend_back/pallas_call | solution.py:917
  432.1 91.5 %exchange_9.1 = (bf16[4,48,4224]{2,1,0:T(8,128)(2,1)}, bf16[4,2,2,2,256,384]{5,4,3,2,1,0:T(8,128)(2,1)}, bf16[4,1536,384]{2,1,0:T(8,128)(2,1)S(1)}) custom-call(bf16[4,2,2,2,48,2176]{5,4,3,2,1,0:T(8,128)(2,1)} %bitcast.118, bf16[4,2,2,2,48,2048]{5,4,3,2,1,0:T(8,128)(2,1)} %bitcast.120, ...), custom_call_target="tpu_custom_call", output_to_operand_aliasing={{2}: (4, {})} | custom-call | bytes 716636160 | tf_op jit(solution)/shard_map/exchange_9/pallas_call | solution.py:451
  523.6 2.2 copy-done.4
  525.8 4.6 all-to-all-start.1
  531.2 0.6 pad_maximum_fusion.3.scale_ref
  532.5 31.6 %table_moments.1 = (f32[6144,384]{1,0:T(8,128)}, f32[6144,384]{1,0:T(8,128)}, f32[6144,384]{1,0:T(8,128)}, f32[8,128]{1,0:T(8,128)}) custom-call(s32[32,256]{1,0:T(8,128)} %copy-done.38, s32[32]{0:T(128)} %copy-done.55, f32[2]{0:T(128)} %pad_maximum_fusion.3.scale_ref, bf16[32,256,384]{2,1,0:T(8,128)(2,1)} %bitcast.119, bf16[6144,384]{1,0:T(8,128)(2,1)} %bitcast.90, ...), custom_call_target="tpu_custom_call" | custom-call | tf_op jit(solution)/shard_map/table_moments/pallas_call | solution.py:1088
  564.2 3.5 fusion.19.down_grad
  567.7 5.4 fusion.18.grad_ref
  573.1 1.2 copy-done.64
  574.2 4.2 small_moments.1
  578.5 27.0 %expert_moments.1 = (f32[12288,128]{1,0:T(8,128)}, f32[12288,128]{1,0:T(8,128)}, f32[12288,128]{1,0:T(8,128)}, f32[512,1536]{1,0:T(8,128)}, f32[512,1536]{1,0:T(...) custom-call(f32[2]{0:T(128)} %pad_maximum_fusion.3.scale_ref, f32[8,128]{1,0:T(8,128)} %get-tuple-element.131.table_norms, ...), custom_call_target="tpu_custom_call" | custom-call | tf_op jit(solution)/shard_map/expert_moments/pallas_call | solution.py:687
  605.6 0.7 copy-done.56
  606.2 15.2 %exchange_10.1 = f32[4,8,8,128]{3,2,1,0:T(8,128)S(1)} custom-call(f32[8,128]{1,0:T(8,128)S(1)} %copy-done.56), custom_call_target="tpu_custom_call" | custom-call | bytes 2703360 | tf_op jit(solution)/shard_map/exchange_10/pallas_call | solution.py:451
  621.6 0.5 fusion.17
  623.5 0.7 copy.88
  624.2 0.6 multiply_subtract_fusion
  624.8 0.6 subtract_bitcast_fusion
  625.4 20.8 %finish.1 = (f32[6144,384]{1,0:T(8,128)}, f32[12288,128]{1,0:T(8,128)}, f32[512,1536]{1,0:T(8,128)}, f32[48,2560]{1,0:T(8,128)}, f32[48,1536]{1,0:T(8,128)}) custom-call(f32[32,8,128]{2,1,0:T(8,128)} %bitcast.105, f32[6144,384]{1,0:T(8,128)} %refs_0_.1, f32[6144,384]{1,0:T(8,128)} %get-tuple-element.137.refs_1_, f32[12288,128]{1,0:T(8,128)} %bitcast.115, ...), custom_call_target="tpu_custom_call" | custom-call | tf_op jit(solution)/shard_map/finish/pallas_call | solution.py:1194
  (190 shorter events, 3.0 us)
Async XLA Ops:
  0.7 4.2 copy-start
  20.3 42.6 %all-to-all-start = ((bf16[4,48,4224]{2,1,0:T(8,128)(2,1)}), bf16[4,48,4224]{2,1,0:T(8,128)(2,1)S(1)}, u32[]{:S(2)}, u32[]{:S(2)}) async-start(bf16[4,48,4224]{2,1,0:T(8,128)(2,1)} %broadcast_in_dim.42), calls=%async_computation | async-start | bytes 3244032 | tf_op jit(solution)/shard_map/all_to_all | solution.py:1342
  25.1 19.8 %copy-start.55 = (s32[32]{0:T(128)}, s32[32]{0:T(128)S(1)}, u32[]{:S(2)}) copy-start(s32[32]{0:T(128)S(1)} %get-tuple-element.215.count_ref) | copy-start | bytes 388
  26.7 134.1 %copy-start.25 = (f32[256,128]{1,0:T(8,128)}, f32[256,128]{1,0:T(8,128)S(1)}, u32[]{:S(2)}) copy-start(f32[256,128]{1,0:T(8,128)S(1)} %copy.83.cos_ref) | copy-start | bytes 393220
  36.5 8.4 %copy-start.38 = (s32[32,256]{1,0:T(8,128)}, s32[32,256]{1,0:T(8,128)S(1)}, u32[]{:S(2)}) copy-start(s32[32,256]{1,0:T(8,128)S(1)} %fusion.12.list_ref) | copy-start | bytes 98308
  36.5 13.9 %copy-start.73 = (s32[16,2]{0,1:T(2,128)S(1)}, s32[16,2]{0,1:T(2,128)}, u32[]{:S(2)}) copy-start(s32[16,2]{0,1:T(2,128)} %param.29) | copy-start | bytes 388
  50.4 110.3 %copy-start.47 = (f32[32,128]{1,0:T(8,128)}, f32[32,128]{1,0:T(8,128)S(1)}, u32[]{:S(2)}) copy-start(f32[32,128]{1,0:T(8,128)S(1)} %get-tuple-element.235.sin_rows) | copy-start | bytes 49156
  50.4 110.3 %copy-start.49 = (f32[32,128]{1,0:T(8,128)}, f32[32,128]{1,0:T(8,128)S(1)}, u32[]{:S(2)}) copy-start(f32[32,128]{1,0:T(8,128)S(1)} %get-tuple-element.236.cos_rows) | copy-start | bytes 49156
  65.2 108.2 %slice-start = ((s8[4718592]{0:T(1024)(128)(4,1)}), s8[524288]{0:T(1024)(128)(4,1)S(1)}, s32[]{:S(2)}) async-start(s8[4718592]{0:T(1024)(128)(4,1)} %bitcast.91), calls=%async_computation.2 | async-start | bytes 1048576
  160.7 11.1 %copy-start.8 = (bf16[4,2,2,2,48,2048]{5,4,3,2,1,0:T(8,128)(2,1)}, bf16[4,2,2,2,48,2048]{5,4,3,2,1,0:T(8,128)(2,1)S(1)}, u32[]{:S(2)}) copy-start(bf16[4,2,2,2,48,2048]{5,4,3,2,1,0:T(8,128)(2,1)S(1)} %get-tuple-element.98) | copy-start | bytes 18874372
  160.7 11.1 %copy-start.16 = (bf16[4,256,384]{2,1,0:T(8,128)(2,1)}, bf16[4,256,384]{2,1,0:T(8,128)(2,1)S(1)}, u32[]{:S(2)}) copy-start(bf16[4,256,384]{2,1,0:T(8,128)(2,1)S(1)} %get-tuple-element.96.picked_ref) | copy-start | bytes 2359300
  160.8 5.4 copy-start.3
  166.2 7.3 %slice-start.1 = ((s8[4718592]{0:T(1024)(128)(4,1)}), s8[4194304]{0:T(1024)(128)(4,1)S(1)}, s32[]{:S(2)}) async-start(s8[4718592]{0:T(1024)(128)(4,1)} %bitcast.91), calls=%async_computation.3 | async-start | bytes 8388608
  166.2 7.3 %copy-start.10 = (bf16[1536,1536]{1,0:T(8,128)(2,1)S(1)}, bf16[1536,1536]{1,0:T(8,128)(2,1)}, u32[]{:S(2)}) copy-start(bf16[1536,1536]{1,0:T(8,128)(2,1)} %copy-done.9) | copy-start | bytes 14155780
  173.4 26.3 %copy-start.30 = (bf16[256,1536]{1,0:T(8,128)(2,1)}, bf16[256,1536]{1,0:T(8,128)(2,1)S(1)}, u32[]{:S(2)}) copy-start(bf16[256,1536]{1,0:T(8,128)(2,1)S(1)} %get-tuple-element.124.normed_ref) | copy-start | bytes 2359300
  173.4 26.3 %copy-start.36 = (bf16[32,1536]{1,0:T(8,128)(2,1)}, bf16[32,1536]{1,0:T(8,128)(2,1)S(1)}, u32[]{:S(2)}) copy-start(bf16[32,1536]{1,0:T(8,128)(2,1)S(1)} %get-tuple-element.99.refs_0_.c_ref) | copy-start | bytes 294916
  173.4 26.3 %copy-start.39 = (bf16[256,512]{1,0:T(8,128)(2,1)}, bf16[256,512]{1,0:T(8,128)(2,1)S(1)}, u32[]{:S(2)}) copy-start(bf16[256,512]{1,0:T(8,128)(2,1)S(1)} %get-tuple-element.121.key_ref) | copy-start | bytes 786436
  173.4 26.3 %copy-start.41 = (bf16[256,512]{1,0:T(8,128)(2,1)}, bf16[256,512]{1,0:T(8,128)(2,1)S(1)}, u32[]{:S(2)}) copy-start(bf16[256,512]{1,0:T(8,128)(2,1)S(1)} %get-tuple-element.122.value_ref) | copy-start | bytes 786436
  173.4 26.3 %copy-start.53 = (bf16[32,1536]{1,0:T(8,128)(2,1)}, bf16[32,1536]{1,0:T(8,128)(2,1)S(1)}, u32[]{:S(2)}) copy-start(bf16[32,1536]{1,0:T(8,128)(2,1)S(1)} %get-tuple-element.123.mixed_ref) | copy-start | bytes 294916
  173.4 46.5 %copy-start.32 = (f32[32,1536]{1,0:T(8,128)}, f32[32,1536]{1,0:T(8,128)S(1)}, u32[]{:S(2)}) copy-start(f32[32,1536]{1,0:T(8,128)S(1)} %get-tuple-element.103.refs_1_.resid_ref) | copy-start | bytes 589828
  173.5 30.1 %copy-start.24 = (s32[1024,8]{1,0:T(8,128)S(1)}, s32[1024,8]{1,0:T(8,128)}, u32[]{:S(2)}) copy-start(s32[1024,8]{1,0:T(8,128)} %reshape.233.routes_ref) | copy-start | bytes 98308
  203.6 16.3 %copy-start.12 = (bf16[1536,1536]{1,0:T(8,128)(2,1)S(1)}, bf16[1536,1536]{1,0:T(8,128)(2,1)}, u32[]{:S(2)}) copy-start(bf16[1536,1536]{1,0:T(8,128)(2,1)} %copy-done.11) | copy-start | bytes 14155780
  219.9 54.2 %copy-start.20 = (bf16[1536,1024]{1,0:T(8,128)(2,1)}, bf16[1536,1024]{1,0:T(8,128)(2,1)S(1)}, u32[]{:S(2)}) copy-start(bf16[1536,1024]{1,0:T(8,128)(2,1)S(1)} %get-tuple-element.112.cat_ref) | copy-start | bytes 9437188
  219.9 54.2 %copy-start.34 = (f32[1024,128]{1,0:T(8,128)}, f32[1024,128]{1,0:T(8,128)S(1)}, u32[]{:S(2)}) copy-start(f32[1024,128]{1,0:T(8,128)S(1)} %get-tuple-element.111.gates_ref) | copy-start | bytes 1572868
  274.1 5.2 copy-start.13
  274.1 5.2 copy-start.45
  274.1 5.2 copy-start.57
  274.1 5.3 copy-start.66
  274.1 5.3 copy-start.67
  279.4 15.7 %copy-start.74 = (f32[32]{0:T(128)S(1)}, f32[32]{0:T(128)}, u32[]{:S(2)}) copy-start(f32[32]{0:T(128)} %param.30) | copy-start | bytes 388
  279.4 15.7 %copy-start.70 = (s32[16]{0:T(128)S(1)}, s32[16]{0:T(128)}, u32[]{:S(2)}) copy-start(s32[16]{0:T(128)} %get-tuple-element.226) | copy-start | bytes 196
  279.4 15.7 %copy-start.71 = (s32[16]{0:T(128)S(1)}, s32[16]{0:T(128)}, u32[]{:S(2)}) copy-start(s32[16]{0:T(128)} %get-tuple-element.227) | copy-start | bytes 196
  294.8 5.4 slice-start.2
  296.1 4.1 slice-start.3
  300.2 5.3 copy-start.58
  305.5 5.6 copy-start.35
  305.5 5.6 copy-start.46
  311.1 69.0 %copy-start.7 = (bf16[1536,1536]{1,0:T(8,128)(2,1)}, bf16[1536,1536]{1,0:T(8,128)(2,1)S(1)}, u32[]{:S(2)}) copy-start(bf16[1536,1536]{1,0:T(8,128)(2,1)S(1)} %fusion.1.refs_3_.refs_1_) | copy-start | bytes 14155780
  311.1 60.8 %copy-start.15 = (f32[1024,1024]{1,0:T(8,128)S(1)}, f32[1024,1024]{1,0:T(8,128)}, u32[]{:S(2)}) copy-start(f32[1024,1024]{1,0:T(8,128)} %get-tuple-element.110.mid_ref) | copy-start | bytes 12582916
  311.1 60.8 %copy-start.21 = (bf16[1536,1024]{1,0:T(8,128)(2,1)S(1)}, bf16[1536,1024]{1,0:T(8,128)(2,1)}, u32[]{:S(2)}) copy-start(bf16[1536,1024]{1,0:T(8,128)(2,1)} %copy-done.20) | copy-start | bytes 9437188
  371.8 6.9 %copy-start.18 = (bf16[4,2,2,2,32,1536]{5,4,3,2,1,0:T(8,128)(2,1)}, bf16[4,2,2,2,32,1536]{5,4,3,2,1,0:T(8,128)(2,1)S(1)}, u32[]{:S(2)}) copy-start(bf16[4,2,2,2,32,1536]{5,4,3,2,1,0:T(8,128)(2,1)S(1)} %get-tuple-element.109) | copy-start | bytes 9437188
  371.8 6.9 %copy-start.43 = (f32[32,1536]{1,0:T(8,128)}, f32[32,1536]{1,0:T(8,128)S(1)}, u32[]{:S(2)}) copy-start(f32[32,1536]{1,0:T(8,128)S(1)} %get-tuple-element.117.grad_two_ref) | copy-start | bytes 589828
  380.1 30.3 %copy-start.17 = (bf16[4,256,384]{2,1,0:T(8,128)(2,1)S(1)}, bf16[4,256,384]{2,1,0:T(8,128)(2,1)}, u32[]{:S(2)}) copy-start(bf16[4,256,384]{2,1,0:T(8,128)(2,1)} %copy-done.16) | copy-start | bytes 2359300
  380.1 30.3 %copy-start.26 = (f32[256,128]{1,0:T(8,128)S(1)}, f32[256,128]{1,0:T(8,128)}, u32[]{:S(2)}) copy-start(f32[256,128]{1,0:T(8,128)} %copy-done.25) | copy-start | bytes 393220
  380.1 30.3 %copy-start.29 = (f32[8,96,256]{2,1,0:T(8,128)S(1)}, f32[8,96,256]{2,1,0:T(8,128)}, u32[]{:S(2)}) copy-start(f32[8,96,256]{2,1,0:T(8,128)} %copy-done.28) | copy-start | bytes 2359300
  380.1 30.3 %copy-start.31 = (bf16[256,1536]{1,0:T(8,128)(2,1)S(1)}, bf16[256,1536]{1,0:T(8,128)(2,1)}, u32[]{:S(2)}) copy-start(bf16[256,1536]{1,0:T(8,128)(2,1)} %copy-done.30) | copy-start | bytes 2359300
  380.1 30.3 %copy-start.33 = (f32[32,1536]{1,0:T(8,128)S(1)}, f32[32,1536]{1,0:T(8,128)}, u32[]{:S(2)}) copy-start(f32[32,1536]{1,0:T(8,128)} %copy-done.32) | copy-start | bytes 589828
  380.1 30.3 %copy-start.37 = (bf16[32,1536]{1,0:T(8,128)(2,1)S(1)}, bf16[32,1536]{1,0:T(8,128)(2,1)}, u32[]{:S(2)}) copy-start(bf16[32,1536]{1,0:T(8,128)(2,1)} %copy-done.36) | copy-start | bytes 294916
  380.1 30.3 %copy-start.40 = (bf16[256,512]{1,0:T(8,128)(2,1)S(1)}, bf16[256,512]{1,0:T(8,128)(2,1)}, u32[]{:S(2)}) copy-start(bf16[256,512]{1,0:T(8,128)(2,1)} %copy-done.39) | copy-start | bytes 786436
  380.2 30.3 %copy-start.42 = (bf16[256,512]{1,0:T(8,128)(2,1)S(1)}, bf16[256,512]{1,0:T(8,128)(2,1)}, u32[]{:S(2)}) copy-start(bf16[256,512]{1,0:T(8,128)(2,1)} %copy-done.41) | copy-start | bytes 786436
  380.2 30.3 %copy-start.44 = (f32[32,1536]{1,0:T(8,128)S(1)}, f32[32,1536]{1,0:T(8,128)}, u32[]{:S(2)}) copy-start(f32[32,1536]{1,0:T(8,128)} %copy-done.43) | copy-start | bytes 589828
  380.2 30.3 %copy-start.48 = (f32[32,128]{1,0:T(8,128)S(1)}, f32[32,128]{1,0:T(8,128)}, u32[]{:S(2)}) copy-start(f32[32,128]{1,0:T(8,128)} %copy-done.47) | copy-start | bytes 49156
  380.2 30.3 %copy-start.50 = (f32[32,128]{1,0:T(8,128)S(1)}, f32[32,128]{1,0:T(8,128)}, u32[]{:S(2)}) copy-start(f32[32,128]{1,0:T(8,128)} %copy-done.49) | copy-start | bytes 49156
  380.2 30.3 %copy-start.52 = (bf16[32,1536]{1,0:T(8,128)(2,1)S(1)}, bf16[32,1536]{1,0:T(8,128)(2,1)}, u32[]{:S(2)}) copy-start(bf16[32,1536]{1,0:T(8,128)(2,1)} %copy-done.51) | copy-start | bytes 294916
  380.2 30.3 %copy-start.54 = (bf16[32,1536]{1,0:T(8,128)(2,1)S(1)}, bf16[32,1536]{1,0:T(8,128)(2,1)}, u32[]{:S(2)}) copy-start(bf16[32,1536]{1,0:T(8,128)(2,1)} %copy-done.53) | copy-start | bytes 294916
  525.8 47.3 %all-to-all-start.1 = ((bf16[4,48,4224]{2,1,0:T(8,128)(2,1)}), bf16[4,48,4224]{2,1,0:T(8,128)(2,1)S(1)}, u32[]{:S(2)}, u32[]{:S(2)}) async-start(bf16[4,48,4224]{2,1,0:T(8,128)(2,1)} %get-tuple-element.132), calls=%async_computation.1 | async-start | bytes 3244032 | tf_op jit(solution)/shard_map/all_to_all | solution.py:1462
  532.5 31.6 %copy-start.19 = (bf16[4,2,2,2,32,1536]{5,4,3,2,1,0:T(8,128)(2,1)S(1)}, bf16[4,2,2,2,32,1536]{5,4,3,2,1,0:T(8,128)(2,1)}, u32[]{:S(2)}) copy-start(bf16[4,2,2,2,32,1536]{5,4,3,2,1,0:T(8,128)(2,1)} %copy-done.18) | copy-start | bytes 9437188
  532.5 31.6 %copy-start.62 = (bf16[1024,512]{1,0:T(8,128)(2,1)S(1)}, bf16[1024,512]{1,0:T(8,128)(2,1)}, u32[]{:S(2)}) copy-start(bf16[1024,512]{1,0:T(8,128)(2,1)} %copy-done.61) | copy-start | bytes 3145732
  578.5 45.7 %copy-start.68 = (f32[3,48]{1,0:T(4,128)S(1)}, f32[3,48]{1,0:T(4,128)}, u32[]{:S(2)}) copy-start(f32[3,48]{1,0:T(4,128)} %gains.1) | copy-start | bytes 1732
  578.5 45.7 %copy-start.72 = (f32[3,48]{1,0:T(4,128)S(1)}, f32[3,48]{1,0:T(4,128)}, u32[]{:S(2)}) copy-start(f32[3,48]{1,0:T(4,128)} %get-tuple-element.154) | copy-start | bytes 1732
  578.5 46.3 %copy-start.65 = (f32[48,32]{0,1:T(8,128)S(1)}, f32[48,32]{0,1:T(8,128)}, u32[]{:S(2)}) copy-start(f32[48,32]{0,1:T(8,128)} %param.42) | copy-start | bytes 18436
  578.5 46.3 %copy-start.69 = (f32[32,48]{1,0:T(8,128)S(1)}, f32[32,48]{1,0:T(8,128)}, u32[]{:S(2)}) copy-start(f32[32,48]{1,0:T(8,128)} %get-tuple-element.151) | copy-start | bytes 18436
  621.5 3.9 copy-start.27
  625.4 20.8 %copy-start.1 = (s32[256,8]{0,1:T(8,128)S(1)}, s32[256,8]{0,1:T(8,128)}, u32[]{:S(2)}) copy-start(s32[256,8]{0,1:T(8,128)} %param.31) | copy-start | bytes 24580
  (17 other events, 34.9 us)
